TPU v7x, 32 devices: a whole 2x2x4 slice. The times are simulated.
32 devices in a mesh: seg: 4 (over z), pair: 8 (over y, x, core).
Axes of the slice: x: 2, y: 2, z: 4, core: 2. Of those that a mesh axis runs over, the one named last changes fastest.
Arguments:
- spectra: bfloat16 [4, 2, 2048, 2048], P('seg', None, None, 'pair'), may hold values from -6 to 6
- pair_lists: int32 [32, 2], P('pair'), may hold values from 0 to 15
- pair_counts: int32 [8], P('pair'), may hold values from 1 to 4, as said below
Outputs:
- correlations: float32 [2048, 32, 128], P('seg', 'pair')
Inputs may be any that keep to these rules, and one draw needn't show every extreme that they name: `pair_counts`: some owner uses exactly 4 slots.
All inputs are finite; a program needn't handle non-finite values.
Results may differ from a plain program's by a relative error of at most 0.0003.
Values may be sent and summed in bfloat16 or wider, within the bound.
No kernel may reach another device: no remote copies, remote signals or barrier semaphores. Data moves between devices by JAX's collectives and lax.ppermute only.
A program may use at most 128 MiB of HBM per device.

v0:
```python
import math

import jax
import jax.numpy as jnp
from jax import lax
from jax.sharding import PartitionSpec as P

TILE = 128
LAG = 2048


def stack_weights(linear_re, linear_im, phase_re, phase_im, total_segments):
    weight = (phase_re * phase_re + phase_im * phase_im) / float(total_segments * total_segments)
    return (linear_re * weight, linear_im * weight)


def accumulate(local_spec, group, source_ids, receiver_ids):
    segs_here = local_spec.shape[0]
    band_bins = local_spec.shape[2]
    tiled_spec = local_spec.reshape(segs_here // group, group, 2, band_bins, -1, TILE)

    def one_group(totals, block):
        source_spec = jnp.take(block, source_ids, axis=3).astype(jnp.float32)
        recv_spec = jnp.take(block, receiver_ids, axis=3).astype(jnp.float32)
        cross_re = source_spec[:, 0] * recv_spec[:, 0] + source_spec[:, 1] * recv_spec[:, 1]
        cross_im = source_spec[:, 1] * recv_spec[:, 0] - source_spec[:, 0] * recv_spec[:, 1]
        magnitude = jnp.sqrt(cross_re * cross_re + cross_im * cross_im + 1.0)
        return (
            (
                totals[0] + jnp.sum(cross_re, axis=0),
                totals[1] + jnp.sum(cross_im, axis=0),
                totals[2] + jnp.sum(cross_re / magnitude, axis=0),
                totals[3] + jnp.sum(cross_im / magnitude, axis=0),
            ),
            None,
        )

    zeros = jnp.zeros((band_bins, source_ids.shape[0], TILE), jnp.float32)
    sums, _ = lax.scan(one_group, (zeros, zeros, zeros, zeros), tiled_spec)
    return sums


def body(spectra, pair_lists, pair_counts):
    seg_dev = spectra.shape[0]
    freq_bins = spectra.shape[2]
    n_pair = lax.axis_size("pair")
    n_seg = lax.axis_size("seg")
    seg_index = lax.axis_index("seg")
    most_slots = pair_lists.shape[0]
    total_segments = seg_dev * n_seg
    lists = lax.all_gather(pair_lists, "pair", axis=0, tiled=True)
    source_ids = lists[:, 0]
    receiver_ids = lists[:, 1]
    sub_bins = freq_bins // (n_pair * n_seg)
    bands = lax.all_to_all(spectra, "pair", split_axis=2, concat_axis=3, tiled=True)
    partial_sums = accumulate(bands, seg_dev, source_ids, receiver_ids)
    shares = (
        lax.psum_scatter(partial_sums[0], "seg", scatter_dimension=0, tiled=True),
        lax.psum_scatter(partial_sums[1], "seg", scatter_dimension=0, tiled=True),
        lax.psum_scatter(partial_sums[2], "seg", scatter_dimension=0, tiled=True),
        lax.psum_scatter(partial_sums[3], "seg", scatter_dimension=0, tiled=True),
    )
    block_start = jnp.arange(n_pair, dtype=jnp.int32) * (freq_bins // n_pair) + seg_index * sub_bins
    stack_re, stack_im = stack_weights(shares[0], shares[1], shares[2], shares[3], total_segments)
    stack_re = stack_re.reshape(sub_bins, n_pair, most_slots, TILE)
    stack_im = stack_im.reshape(sub_bins, n_pair, most_slots, TILE)
    owned = (
        lax.all_to_all(stack_re, "pair", split_axis=1, concat_axis=0, tiled=True),
        lax.all_to_all(stack_im, "pair", split_axis=1, concat_axis=0, tiled=True),
    )
    own_bins = sub_bins * n_pair
    row_index = jnp.arange(own_bins, dtype=jnp.int32)
    bin_index = block_start[row_index // sub_bins] + row_index % sub_bins
    owned_re = owned[0].reshape(own_bins, most_slots, TILE)
    owned_im = owned[1].reshape(own_bins, most_slots, TILE)
    live_mask = (jnp.arange(most_slots, dtype=jnp.int32) < pair_counts[0]).astype(jnp.float32)
    owned_re = (owned_re * live_mask[None, :, None]).reshape(own_bins, most_slots * TILE)
    owned_im = (owned_im * live_mask[None, :, None]).reshape(own_bins, most_slots * TILE)
    lag_rows = LAG // n_seg
    lag_offset = jnp.arange(lax.axis_size("seg") * lag_rows, dtype=jnp.int32) - LAG // 2
    product = lag_offset[:, None] * bin_index[None, :] % (2 * freq_bins)
    angles = product.astype(jnp.float32) * jnp.float32(math.pi / freq_bins)
    terms = jnp.dot(
        jnp.cos(angles),
        owned_re,
        precision=lax.Precision.HIGHEST,
        preferred_element_type=jnp.float32,
    )
    terms = terms - jnp.dot(
        jnp.sin(angles),
        owned_im,
        precision=lax.Precision.HIGHEST,
        preferred_element_type=jnp.float32,
    )
    summed = lax.psum_scatter(
        terms * jnp.float32(1.0 / math.sqrt(freq_bins)), "seg", scatter_dimension=0, tiled=True
    )
    return summed.reshape(lag_rows, most_slots, TILE)


def solution(mesh):
    return jax.shard_map(
        body,
        mesh=mesh,
        in_specs=(P("seg", None, None, "pair"), P("pair", None), P("pair")),
        out_specs=P("seg", "pair", None),
        check_vma=False,
    )
```

profile of v0, /device:TPU:0, one launch (start us, length us, event | category | flops | bytes accessed | tf_op | source)
XLA Modules:
  0.0 561.9 jit_solution(8158701286742860428)
XLA Ops:
  6.5 5.8 %copy.27 = bf16[1,2,2048,256]{3,1,0,2:T(2,128)(2,1)} copy(bf16[1,2,2048,256]{3,2,1,0:T(8,128)(2,1)} %param.5) | data formatting | bytes 4194304 | tf_op args[0]
  12.3 5.2 all-to-all-start
  17.6 29.6 %all-gather = s32[8,4,2]{1,2,0:T(2,128)S(1)} all-gather(s32[1,4,2]{1,2,0:T(2,128)S(1)} %bitcast.100), channel_id=1, replica_groups=mesh['seg'=4,'pair'=8] {'pair'}, dimensions={0}, use_global_device_ids=true | all-gather | bytes 288 | tf_op jit(solution)/shard_map/all_gather | solution.py:51
  47.3 1.6 copy.28
  48.9 4.0 copy.29
  52.9 3.0 copy.30
  55.9 3.1 gather_fusion
  59.0 3.0 gather_fusion.1
  62.0 2.9 fusion.4
  65.4 0.7 fusion.3
  66.1 6.3 %fusion.11 = (f32[256,32,128]{2,0,1:T(8,128)}, f32[256,32,128]{2,0,1:T(8,128)}, f32[256,32,128]{2,0,1:T(8,128)}) fusion(f32[1,2,256,32,128]{4,2,3,1,0:T(8,128)S(1)} %fusion.3, f32[1,2,256,32,128]{4,2,1,3,0:T(8,128)S(1)} %fusion.4), kind=kLoop, calls=%fused_computation.26 | loop fusion | flops 11534336 | bytes 29360128 | tf_op jit(solution)/shard_map/while/body/eval_jaxpr/div | solution.py:32
  72.4 6.4 %fusion.10 = f32[256,32,128]{2,0,1:T(8,128)} fusion(f32[256,32,128]{2,0,1:T(8,128)} %get-tuple-element.22, f32[256,32,128]{2,0,1:T(8,128)} %get-tuple-element.21), kind=kLoop, calls=%fused_computation.25 | loop fusion | flops 5242880 | bytes 12582912 | tf_op jit(solution)/shard_map/while/body/eval_jaxpr/div | solution.py:33
  78.9 0.7 reduce-scatter.12.cloned.1.call-update
  79.7 0.7 reduce-scatter.6.cloned.1.call-update
  80.4 0.5 reduce-scatter.8.cloned.1.call-update
  81.0 74.2 %reduce-scatter.10.cloned.1.call-done = f32[64,32,128]{2,0,1:T(8,128)} async-done(((f32[256,32,128]{2,0,1:T(8,128)}), f32[64,32,128]{2,0,1:T(8,128)}) %reduce-scatter.10.cloned.1.call-update) | async-done | bytes 1048592 | tf_op jit(solution)/shard_map/reduce_scatter | solution.py:61
  155.2 79.7 %reduce-scatter.12.cloned.1.call-done = f32[64,32,128]{2,0,1:T(8,128)} async-done(((f32[256,32,128]{2,0,1:T(8,128)}), f32[64,32,128]{2,0,1:T(8,128)}) %reduce-scatter.12.cloned.1.call-update) | async-done | bytes 1048592 | tf_op jit(solution)/shard_map/reduce_scatter | solution.py:59
  234.9 79.6 %reduce-scatter.6.cloned.1.call-done = f32[64,32,128]{2,0,1:T(8,128)} async-done(((f32[256,32,128]{2,0,1:T(8,128)}), f32[64,32,128]{2,0,1:T(8,128)}) %reduce-scatter.6.cloned.1.call-update) | async-done | bytes 1048592 | tf_op jit(solution)/shard_map/reduce_scatter | solution.py:58
  314.5 79.6 %reduce-scatter.8.cloned.1.call-done = f32[64,32,128]{2,0,1:T(8,128)} async-done(((f32[256,32,128]{2,0,1:T(8,128)}), f32[64,32,128]{2,0,1:T(8,128)}) %reduce-scatter.8.cloned.1.call-update) | async-done | bytes 1048592 | tf_op jit(solution)/shard_map/reduce_scatter | solution.py:60
  394.1 2.6 fusion.23
  396.7 1.6 copy.38
  398.3 3.6 all-to-all-start.2
  402.7 0.7 fusion.38
  403.4 1.6 copy.37
  405.0 12.4 %all-to-all-done.2 = f32[64,8,4,128]{3,2,0,1:T(4,128)S(1)} async-done(((f32[64,8,4,128]{3,2,0,1:T(4,128)}), f32[64,8,4,128]{3,2,0,1:T(4,128)S(1)}, u32[]{:S(2)}, u32[]{:S(2)}) %all-to-all-start.2) | async-done | bytes 1048608 | tf_op jit(solution)/shard_map/all_to_all | solution.py:69
  417.4 3.6 all-to-all-start.1
  421.2 4.3 compare_select_fusion.1
  425.5 0.6 fusion.24
  426.1 23.5 %fusion.8 = f32[2048,512]{1,0:T(8,128)} fusion(s32[512]{0:T(512)S(1)} %fusion.24, s32[2048]{0:T(1024)S(1)} %iota_add_fusion, f32[64,8,4,128]{3,2,1,0:T(4,128)S(1)} %bitcast.97, f32[512]{0:T(512)S(1)} %broadcast_bitcast_fusion), kind=kOutput, calls=%fused_computation.22 | convolution fusion | flops 6457393152 | bytes 5255168 | tf_op jit(solution)/shard_map/dot_general | solution.py:89
  449.6 25.5 %subtract_multiply_fusion = f32[2048,512]{1,0:T(8,128)} fusion(f32[2048,512]{1,0:T(8,128)} %fusion.8, s32[512]{0:T(512)S(1)} %fusion.24, s32[2048]{0:T(1024)S(1)} %iota_add_fusion, f32[64,8,4,128]{3,2,1,0:T(4,128)S(1)} %bitcast.98, f32[512]{0:T(512)S(1)} %broadcast_bitcast_fusion), kind=kOutput, calls=%fused_computation.21 | convolution fusion | flops 6459490304 | bytes 9449472 | tf_op jit(solution)/shard_map/dot_general | solution.py:83
  475.2 77.7 %reduce-scatter.14.cloned.1.call-done = f32[512,512]{1,0:T(8,128)} async-done(((f32[2048,512]{1,0:T(8,128)}), f32[512,512]{1,0:T(8,128)}) %reduce-scatter.14.cloned.1.call-update) | async-done | bytes 1048592 | tf_op jit(solution)/shard_map/reduce_scatter | solution.py:95
  552.8 2.5 reshape.186
  (22 shorter events, 1.1 us)
Async XLA Ops:
  6.5 11.0 %copy-start.1 = (s32[4,2]{0,1:T(2,128)S(1)}, s32[4,2]{0,1:T(2,128)}, u32[]{:S(2)}) copy-start(s32[4,2]{0,1:T(2,128)} %param.6) | copy-start | bytes 100
  12.3 35.0 %all-to-all-start = ((bf16[1,2,2048,256]{3,1,0,2:T(2,128)(2,1)}), bf16[1,2,2048,256]{3,1,0,2:T(2,128)(2,1)S(1)}, u32[]{:S(2)}, u32[]{:S(2)}) async-start(bf16[1,2,2048,256]{3,1,0,2:T(2,128)(2,1)} %copy.27), calls=%async_computation | async-start | bytes 4194304 | tf_op jit(solution)/shard_map/all_to_all | solution.py:55
  17.5 137.7 %reduce-scatter.10.cloned.1.call-start = ((), (), s32[]{:S(2)}) async-start(), calls=%async_computation.10 | async-start | bytes 5242880 | tf_op jit(solution)/shard_map/reduce_scatter | solution.py:61
  62.0 3.4 copy-start
  78.9 156.0 %reduce-scatter.12.cloned.1.call-start = ((), (), s32[]{:S(2)}) async-start(), calls=%async_computation.11 | async-start | bytes 5242880 | tf_op jit(solution)/shard_map/reduce_scatter | solution.py:59
  79.6 234.8 %reduce-scatter.6.cloned.1.call-start = ((), (), s32[]{:S(2)}) async-start(), calls=%async_computation.8 | async-start | bytes 5242880 | tf_op jit(solution)/shard_map/reduce_scatter | solution.py:58
  80.4 313.7 %reduce-scatter.8.cloned.1.call-start = ((), (), s32[]{:S(2)}) async-start(), calls=%async_computation.9 | async-start | bytes 5242880 | tf_op jit(solution)/shard_map/reduce_scatter | solution.py:60
  398.3 19.1 %all-to-all-start.2 = ((f32[64,8,4,128]{3,2,0,1:T(4,128)}), f32[64,8,4,128]{3,2,0,1:T(4,128)S(1)}, u32[]{:S(2)}, u32[]{:S(2)}) async-start(f32[64,8,4,128]{3,2,0,1:T(4,128)} %copy.38), calls=%async_computation.6 | async-start | bytes 2097152 | tf_op jit(solution)/shard_map/all_to_all | solution.py:69
  417.4 32.3 %all-to-all-start.1 = ((f32[64,8,4,128]{3,2,0,1:T(4,128)}), f32[64,8,4,128]{3,2,0,1:T(4,128)S(1)}, u32[]{:S(2)}, u32[]{:S(2)}) async-start(f32[64,8,4,128]{3,2,0,1:T(4,128)} %copy.37), calls=%async_computation.4 | async-start | bytes 2097152 | tf_op jit(solution)/shard_map/all_to_all | solution.py:68
  420.9 131.9 %reduce-scatter.14.cloned.1.call-start = ((), (), s32[]{:S(2)}) async-start(), calls=%async_computation.12 | async-start | bytes 5242880 | tf_op jit(solution)/shard_map/reduce_scatter | solution.py:95
Sparse Core Ops, SparseCore 0:
  79.0 76.1 reduce-scatter.9
  157.6 77.2 reduce-scatter.11
  237.2 77.2 reduce-scatter.5
  316.7 77.2 reduce-scatter.7
  475.3 77.5 reduce-scatter.13
where the time goes:
time: 563 us; the launch traced here: 562 us
  waiting for transfers between devices  405 us (72%)
  matrix products  49 us (9%)
  blocking collectives  29.6 us (5%)
  local copies, waits for them, and re-layouts  27.6 us (5%)
  other arithmetic  23.9 us (4%)
  between operations  13.9 us (2%)
  starting transfers between devices  12.7 us (2%)
    reduce_scatter x1, waiting for transfers between devices, body(): lax.psum_scatter(partial_sums[1], 'seg', scatter_dimension=0, tiled=True)  79.7 us
    reduce_scatter x1, waiting for transfers between devices, body(): lax.psum_scatter(partial_sums[0], 'seg', scatter_dimension=0, tiled=True)  79.6 us
    reduce_scatter x1, waiting for transfers between devices, body(): lax.psum_scatter(partial_sums[2], 'seg', scatter_dimension=0, tiled=True)  79.6 us
    reduce_scatter x1, waiting for transfers between devices, body(): lax.psum_scatter(terms * jnp.float32(1.0 / math.sqrt(freq_bins)), 'seg',...  77.7 us
    reduce_scatter x1, waiting for transfers between devices, body(): lax.psum_scatter(partial_sums[3], 'seg', scatter_dimension=0, tiled=True)  74.2 us
    all_gather x1, blocking collectives, body(): lists = lax.all_gather(pair_lists, 'pair', axis=0, tiled=True)  29.6 us
    dot_general x1, matrix products, body(): jnp.dot(jnp.cos(angles), owned_re, precision=lax.Precision.HIGHEST, prefe...  25.5 us
    dot_general x1, matrix products, body(): jnp.dot(jnp.sin(angles), owned_im, precision=lax.Precision.HIGHEST, prefe...  23.5 us
  transfers between devices with their start and end apart: 8, of which 6 were waited for; matrix products, arithmetic and copies ran while one was open for 6% of the time, Pallas kernels for 0%

commit v1 on v0

v1 whole, which is shorter than its diff:
```python
import functools
import math

import jax
import jax.numpy as jnp
import numpy as np
from jax import lax
from jax.experimental import pallas as pl
from jax.experimental.pallas import tpu as pltpu
from jax.sharding import PartitionSpec as P

TILE = 128
LAG = 2048
GROUPS = 8
CC = TILE // GROUPS


def lane_groups(shape):
    return lax.broadcasted_iota(jnp.int32, shape, len(shape) - 1) // CC


def shift_groups(x, by):
    return pltpu.roll(x, (by * CC) % TILE, x.ndim - 1)


def transpose_groups(vectors):
    v = list(vectors)
    grp = lane_groups(v[0].shape)
    for bit in (4, 2, 1):
        low = (grp & bit) == 0
        for i in range(GROUPS):
            if i & bit:
                continue
            a, b = v[i], v[i | bit]
            v[i] = jnp.where(low, a, shift_groups(b, bit))
            v[i | bit] = jnp.where(low, shift_groups(a, -bit), b)
    return v


def reduce_groups(vectors):
    v = list(vectors)
    grp = lane_groups(v[0].shape)
    low = (grp & 4) == 0
    v = [
        jnp.where(low, v[i], v[i + 4])
        + shift_groups(jnp.where(low, v[i + 4], v[i]), 4)
        for i in range(4)
    ]
    for bit in (2, 1):
        low = (grp & bit) == 0
        v = [
            jnp.where(low, v[i], v[i + bit])
            + jnp.where(low, shift_groups(v[i], -bit), shift_groups(v[i + bit], bit))
            for i in range(bit)
        ]
    return v[0]


def pack_kernel(n_seg, n_pair, x_ref, sel_ref, out_ref, buf_ref):
    freq = x_ref.shape[1]
    tiles = out_ref.shape[2]
    rows = out_ref.shape[4]
    band = freq // n_pair
    wide = sel_ref.shape[1]

    def one(step, _):
        ri, p = step // n_pair, step % n_pair
        block = x_ref[ri, pl.ds(pl.multiple_of(p * band, band), band), :]
        for part in range(wide // TILE):
            buf_ref[...] = jnp.dot(
                block,
                sel_ref[:, part * TILE : (part + 1) * TILE],
                preferred_element_type=jnp.float32,
            )
            v = [buf_ref[pl.ds(fb, rows, stride=GROUPS), :] for fb in range(GROUPS)]
            v = transpose_groups(v)
            for g in range(GROUPS):
                t, z = divmod(part * GROUPS + g, n_seg)
                out_ref[z, p, t, ri] = v[g].astype(jnp.bfloat16)
        return 0

    lax.fori_loop(0, 2 * n_pair, one, 0)


def pack(x, chunk, n_seg, n_pair):
    _, freq, chans = x.shape
    tiles = chans // TILE
    rows = freq // n_pair // GROUPS
    wide = tiles * n_seg * CC
    sel = np.zeros((chans, wide), np.float32)
    for t in range(tiles):
        for z in range(n_seg):
            for c in range(CC):
                src = t * TILE + z * (TILE // n_seg) + chunk * CC + c
                sel[src, (t * n_seg + z) * CC + c] = 1.0
    return pl.pallas_call(
        functools.partial(pack_kernel, n_seg, n_pair),
        out_shape=jax.ShapeDtypeStruct(
            (n_seg, n_pair, tiles, 2, rows, TILE), jnp.bfloat16
        ),
        in_specs=[pl.BlockSpec(memory_space=pltpu.VMEM)] * 2,
        out_specs=pl.BlockSpec(memory_space=pltpu.VMEM),
        scratch_shapes=[pltpu.VMEM((freq // n_pair, TILE), jnp.float32)],
        name="pack",
        cost_estimate=pl.CostEstimate(
            flops=4 * freq * chans * wide,
            bytes_accessed=x.size * 2 + 2 * freq * wide * 2,
            transcendentals=0,
        ),
    )(x, jnp.asarray(sel, jnp.bfloat16))


def stack_kernel(n_seg, n_pair, most, me_ref, table_ref, spec_ref, *out_refs):
    inv = 1.0 / float(n_seg * n_seg)
    for k in range(n_pair):
        owner = jnp.bitwise_xor(me_ref[1], k)
        count = table_ref[owner, 2 * most]
        out_ref = out_refs[k]

        def one(s, _):
            src = table_ref[owner, 2 * s]
            rcv = table_ref[owner, 2 * s + 1]

            @pl.when(s < count)
            def _():
                lr = li = pr = pi = None
                for g in range(n_seg):
                    a0 = spec_ref[g, src, 0].astype(jnp.float32)
                    a1 = spec_ref[g, src, 1].astype(jnp.float32)
                    b0 = spec_ref[g, rcv, 0].astype(jnp.float32)
                    b1 = spec_ref[g, rcv, 1].astype(jnp.float32)
                    cr = a0 * b0 + a1 * b1
                    ci = a1 * b0 - a0 * b1
                    m = lax.rsqrt(cr * cr + ci * ci + 1.0)
                    if g == 0:
                        lr, li, pr, pi = cr, ci, cr * m, ci * m
                    else:
                        lr, li, pr, pi = lr + cr, li + ci, pr + cr * m, pi + ci * m
                w = (pr * pr + pi * pi) * inv
                out_ref[s, 0] = lr * w
                out_ref[s, 1] = li * w

            @pl.when(s >= count)
            def _():
                out_ref[s] = jnp.zeros(out_ref.shape[1:], jnp.float32)

            return 0

        lax.fori_loop(0, most, one, 0)


def stacks(me, table, spec, n_seg, n_pair, most):
    rows = spec.shape[3]
    shape = (most, 2, rows, TILE)
    smem = pl.BlockSpec(memory_space=pltpu.SMEM)
    vmem = pl.BlockSpec(memory_space=pltpu.VMEM)
    return pl.pallas_call(
        functools.partial(stack_kernel, n_seg, n_pair, most),
        out_shape=[jax.ShapeDtypeStruct(shape, jnp.float32)] * n_pair,
        in_specs=[smem, smem, vmem],
        out_specs=[vmem] * n_pair,
        name="stack",
        cost_estimate=pl.CostEstimate(
            flops=n_pair * most * rows * TILE * n_seg * 20,
            bytes_accessed=spec.size * 2 + n_pair * most * 2 * rows * TILE * 4,
            transcendentals=n_pair * most * rows * TILE * n_seg,
        ),
    )(me, table, spec)


def dft_kernel(n_seg, n_pair, most, me_ref, whi_ref, wlo_ref, cos_ref, sin_ref, turn_ref, *refs):
    ins = refs[:n_pair]
    outs = refs[n_pair : n_pair + n_seg]
    s32, shi, slo, y = refs[n_pair + n_seg :]
    rows = ins[0].shape[2]
    half_h = s32.shape[0] // 2
    for k in range(n_pair):
        band = jnp.bitwise_xor(me_ref[1], k)
        for s in range(most):
            for ri in range(2):
                at = pl.multiple_of(ri * half_h + band * rows, rows)
                s32[pl.ds(at, rows), s * TILE : (s + 1) * TILE] = ins[k][s, ri]
    full = s32[...]
    hi = full.astype(jnp.bfloat16)
    shi[...] = hi
    slo[...] = (full - hi.astype(jnp.float32)).astype(jnp.bfloat16)
    for m in range(whi_ref.shape[0]):
        y[m] = (
            jnp.dot(wlo_ref[m], shi[...], preferred_element_type=jnp.float32)
            + jnp.dot(whi_ref[m], slo[...], preferred_element_type=jnp.float32)
        ) + jnp.dot(whi_ref[m], shi[...], preferred_element_type=jnp.float32)
    period = y.shape[1]
    half = outs[0].shape[0]
    step_rows = 16
    for k in range(n_seg):
        dest = jnp.bitwise_xor(me_ref[0], k)
        out_ref = outs[k]

        def one(b, _):
            v = []
            for h in range(2):
                lag = dest * (2 * half) + h * half + b * step_rows
                l0 = pl.multiple_of(lax.rem(lag, period), step_rows)
                c0 = cos_ref[pl.ds(l0, step_rows), :]
                d0 = sin_ref[pl.ds(l0, step_rows), :]
                ct = turn_ref[0, lag // period]
                dt = turn_ref[1, lag // period]
                c = c0 * ct - d0 * dt
                d = d0 * ct + c0 * dt
                for s in range(most):
                    lanes = slice(s * TILE, (s + 1) * TILE)
                    v.append(
                        c * y[0, pl.ds(l0, step_rows), lanes]
                        - d * y[1, pl.ds(l0, step_rows), lanes]
                    )
            at = pl.multiple_of(b * step_rows, step_rows)
            out_ref[pl.ds(at, step_rows), :] = reduce_groups(v)
            return 0

        lax.fori_loop(0, half // step_rows, one, 0)


def dft(me, blocks, freq, n_seg, n_pair, most):
    h = freq // GROUPS
    period = 2 * h
    turn = (np.arange(period)[:, None] * np.arange(h)[None, :]) % period
    angle = turn * (2.0 * math.pi / period)
    w = np.stack(
        [
            np.concatenate([np.cos(angle), -np.sin(angle)], 1),
            np.concatenate([np.sin(angle), np.cos(angle)], 1),
        ]
    ).astype(np.float32)
    whi = w.astype(jnp.bfloat16)
    wlo = (w - whi.astype(np.float32)).astype(jnp.bfloat16)
    fb = np.arange(TILE) // CC
    phase = ((np.arange(period)[:, None] * fb[None, :]) % (2 * freq)) * (math.pi / freq)
    scale = 1.0 / math.sqrt(freq)
    cos = jnp.asarray(np.cos(phase) * scale, jnp.float32)
    sin = jnp.asarray(np.sin(phase) * scale, jnp.float32)
    start = np.arange(LAG // period) * period - LAG // 2
    phase = ((start[:, None] * fb[None, :]) % (2 * freq)) * (math.pi / freq)
    turns = jnp.asarray(np.stack([np.cos(phase), np.sin(phase)])[:, :, None], jnp.float32)
    smem = pl.BlockSpec(memory_space=pltpu.SMEM)
    vmem = pl.BlockSpec(memory_space=pltpu.VMEM)
    half = LAG // n_seg // 2
    wide = most * TILE
    return pl.pallas_call(
        functools.partial(dft_kernel, n_seg, n_pair, most),
        out_shape=[jax.ShapeDtypeStruct((half, TILE), jnp.float32)] * n_seg,
        in_specs=[smem] + [vmem] * (5 + n_pair),
        out_specs=[vmem] * n_seg,
        scratch_shapes=[
            pltpu.VMEM((2 * h, wide), jnp.float32),
            pltpu.VMEM((2 * h, wide), jnp.bfloat16),
            pltpu.VMEM((2 * h, wide), jnp.bfloat16),
            pltpu.VMEM((2, period, wide), jnp.float32),
        ],
        name="dft",
        cost_estimate=pl.CostEstimate(
            flops=3 * 2 * 2 * period * 2 * h * wide,
            bytes_accessed=2 * w.size * 2 + 2 * period * TILE * 4 + 2 * h * wide * 4,
            transcendentals=0,
        ),
    )(me, jnp.asarray(whi), jnp.asarray(wlo), cos, sin, turns, *blocks)


def unpack_kernel(n_seg, chunks, most, me_ref, *refs):
    ins = refs[: n_seg * chunks]
    out_ref, buf = refs[n_seg * chunks :]
    half = ins[0].shape[0]
    for k in range(n_seg):
        z = jnp.bitwise_xor(me_ref[0], k)
        for ch in range(chunks):
            buf[z * chunks + ch] = ins[ch * n_seg + k][...]
    step_rows = 16

    def one(b, _):
        at = pl.multiple_of(b * step_rows, step_rows)
        v = transpose_groups([buf[i, pl.ds(at, step_rows), :] for i in range(GROUPS)])
        for h in range(2):
            for s in range(most):
                out_ref[pl.ds(h * half + at, step_rows), s, :] = v[h * most + s]
        return 0

    lax.fori_loop(0, half // step_rows, one, 0)


def unpack(me, parts, n_seg, chunks, most):
    half = parts[0].shape[0]
    smem = pl.BlockSpec(memory_space=pltpu.SMEM)
    vmem = pl.BlockSpec(memory_space=pltpu.VMEM)
    return pl.pallas_call(
        functools.partial(unpack_kernel, n_seg, chunks, most),
        out_shape=jax.ShapeDtypeStruct((2 * half, most, TILE), jnp.float32),
        in_specs=[smem] + [vmem] * len(parts),
        out_specs=vmem,
        scratch_shapes=[pltpu.VMEM((GROUPS, half, TILE), jnp.float32)],
        name="unpack",
        cost_estimate=pl.CostEstimate(
            flops=half * TILE * GROUPS * 9,
            bytes_accessed=2 * half * TILE * GROUPS * 4,
            transcendentals=0,
        ),
    )(me, *parts)


def exchange(blocks, axis, size):
    return [blocks[0]] + [
        lax.ppermute(blocks[k], axis, [(i, i ^ k) for i in range(size)])
        for k in range(1, size)
    ]


def body(spectra, pair_lists, pair_counts):
    n_pair = lax.axis_size("pair")
    n_seg = lax.axis_size("seg")
    freq = spectra.shape[2]
    most = pair_lists.shape[0]
    tiles = spectra.shape[3] // TILE
    chunks = GROUPS // n_seg
    rows = freq // n_pair // GROUPS
    me = jnp.stack([lax.axis_index("seg"), lax.axis_index("pair")]).astype(jnp.int32)
    x = spectra.reshape(2, freq, spectra.shape[3])
    table = lax.all_gather(
        jnp.concatenate([pair_lists.reshape(-1), pair_counts]), "pair", axis=0
    )
    done = []
    for chunk in range(chunks):
        sent = pack(x, chunk, n_seg, n_pair)
        sent = sent.reshape(n_seg * n_pair, tiles, 2, rows, TILE)
        got = lax.all_to_all(
            sent, ("seg", "pair"), split_axis=0, concat_axis=0, tiled=True
        )
        spec = got.reshape(n_seg, n_pair * tiles, 2, rows, TILE)
        blocks = stacks(me, table, spec, n_seg, n_pair, most)
        blocks = exchange(blocks, "pair", n_pair)
        lags = dft(me, blocks, freq, n_seg, n_pair, most)
        done += exchange(lags, "seg", n_seg)
    return unpack(me, done, n_seg, chunks, most)


def solution(mesh):
    return jax.shard_map(
        body,
        mesh=mesh,
        in_specs=(P("seg", None, None, "pair"), P("pair", None), P("pair")),
        out_specs=P("seg", "pair", None),
        check_vma=False,
    )
```

time: 563 us -> 155 us (0.28)
  waiting for transfers between devices: 405 us -> 35.5 us
  Pallas kernels: 0 us -> 70.7 us
  matrix products: 49 us -> 0 us
  local copies, waits for them, and re-layouts: 27.6 us -> 3.91 us
  other arithmetic: 23.9 us -> 0.81 us
  blocking collectives: 29.6 us -> 9.7 us
  starting transfers between devices: 12.7 us -> 32.2 us
  between operations: 13.9 us -> 1.58 us
    reduce_scatter x5 -> x0, waiting for transfers between devices: 391 us -> none  [the longest x1 79.7 us: body(): lax.psum_scatter(partial_sums[1], 'seg', scatter_dimension=0, tiled=True)]
    pallas_call x0 -> x7, Pallas kernels: none -> 70.7 us  [the longest x2 38.4 us: dft(): pl.pallas_call(functools.partial(dft_kernel, n_seg, n_pair, most), out_sh...]
    dot_general x2 -> x0, matrix products: 49 us -> none  [the longest x1 25.5 us: body(): jnp.dot(jnp.cos(angles), owned_re, precision=lax.Precision.HIGHEST, prefe...]
    all_gather x1 -> x0, blocking collectives: 29.6 us -> none  [body(): lists = lax.all_gather(pair_lists, 'pair', axis=0, tiled=True)]
    ppermute x0 -> x20, starting transfers between devices: none -> 21.3 us  [exchange(): lax.ppermute(blocks[k], axis, [(i, i ^ k) for i in range(size)])]
    ppermute x0 -> x20, waiting for transfers between devices: none -> 13 us  [exchange(): lax.ppermute(blocks[k], axis, [(i, i ^ k) for i in range(size)])]
    div x2 -> x0, other arithmetic: 12.7 us -> none  [the longest x1 6.44 us: one_group(): cross_im / magnitude]
    all_to_all x3 -> x2, waiting for transfers between devices: 12.4 us -> 22.6 us  [body(): lax.all_to_all(sent, ('seg', 'pair'), split_axis=0, concat_axis=0, tiled=...]
  transfers between devices with their start and end apart: 8 -> 22, of which waited for: 6 -> 6; matrix products, arithmetic and copies ran while one was open for 6% -> 2% of each run, Pallas kernels for 0% -> 36%
where the time goes in v1:
time: 155 us; the launch traced here: 154 us
  Pallas kernels  70.7 us (46%)
  waiting for transfers between devices  35.5 us (23%)
  starting transfers between devices  32.2 us (21%)
  blocking collectives  9.7 us (6%)
  local copies, waits for them, and re-layouts  3.91 us (3%)
  between operations  1.58 us (1%)
    pallas_call x2, Pallas kernels, dft(): pl.pallas_call(functools.partial(dft_kernel, n_seg, n_pair, most), out_sh...  38.4 us
    all_to_all x2, waiting for transfers between devices, body(): lax.all_to_all(sent, ('seg', 'pair'), split_axis=0, concat_axis=0, tiled=...  22.6 us
    ppermute x20, starting transfers between devices, exchange(): lax.ppermute(blocks[k], axis, [(i, i ^ k) for i in range(size)])  21.3 us
    pallas_call x2, Pallas kernels, pack(): pl.pallas_call(functools.partial(pack_kernel, n_seg, n_pair), out_shape=j...  18.6 us
    ppermute x20, waiting for transfers between devices, exchange(): lax.ppermute(blocks[k], axis, [(i, i ^ k) for i in range(size)])  13 us
    all_to_all x2, starting transfers between devices, body(): lax.all_to_all(sent, ('seg', 'pair'), split_axis=0, concat_axis=0, tiled=...  10.9 us
    unnamed x1, blocking collectives  9.7 us
    pallas_call x2, Pallas kernels, stacks(): pl.pallas_call(functools.partial(stack_kernel, n_seg, n_pair, most), out_...  7.22 us
  transfers between devices with their start and end apart: 22, of which 6 were waited for; matrix products, arithmetic and copies ran while one was open for 2% of the time, Pallas kernels for 36%

profile of v1, /device:TPU:0, one launch (start us, length us, event | category | flops | bytes accessed | tf_op | source)
XLA Modules:
  0.0 154.5 jit_solution(11875547880172465319)
XLA Ops:
  0.0 9.3 %pack.2 = bf16[4,8,2,2,32,128]{5,4,3,2,1,0:T(8,128)(2,1)} custom-call(bf16[2,2048,256]{2,1,0:T(8,128)(2,1)} %bitcast.8, bf16[256,128]{1,0:T(8,128)(2,1)} %constant.22.clone.sel_ref), custom_call_target="tpu_custom_call" | custom-call | flops 268435456 | bytes 3145728 | tf_op jit(solution)/shard_map/pack/pallas_call | solution.py:96
  9.3 7.3 %all-to-all-start = ((bf16[32,2,2,32,128]{4,3,2,1,0:T(8,128)(2,1)}), bf16[32,2,2,32,128]{4,3,2,1,0:T(8,128)(2,1)S(1)}, u32[]{:S(2)}, u32[]{:S(2)}) async-start(bf16[32,2,2,32,128]{4,3,2,1,0:T(8,128)(2,1)} %bitcast.11), calls=%async_computation | async-start | bytes 2097152 | tf_op jit(solution)/shard_map/all_to_all | solution.py:332
  16.6 9.3 %pack.3 = bf16[4,8,2,2,32,128]{5,4,3,2,1,0:T(8,128)(2,1)} custom-call(bf16[2,2048,256]{2,1,0:T(8,128)(2,1)} %bitcast.9, bf16[256,128]{1,0:T(8,128)(2,1)} %constant.28.clone.sel_ref), custom_call_target="tpu_custom_call" | custom-call | flops 268435456 | bytes 3145728 | tf_op jit(solution)/shard_map/pack/pallas_call | solution.py:96
  26.0 16.9 %all-to-all-done = bf16[32,2,2,32,128]{4,3,2,1,0:T(8,128)(2,1)S(1)} async-done(((bf16[32,2,2,32,128]{4,3,2,1,0:T(8,128)(2,1)}), bf16[32,2,2,32,128]{4,3,2,1,0:T(8,128)(2,1)S(1)}, u32[]{:S(2)}, u32[]{:S(2)}) %all-to-all-start) | async-done | bytes 1048608 | tf_op jit(solution)/shard_map/all_to_all | solution.py:332
  42.8 3.6 %all-to-all-start.1 = ((bf16[32,2,2,32,128]{4,3,2,1,0:T(8,128)(2,1)}), bf16[32,2,2,32,128]{4,3,2,1,0:T(8,128)(2,1)S(1)}, u32[]{:S(2)}, u32[]{:S(2)}) async-start(bf16[32,2,2,32,128]{4,3,2,1,0:T(8,128)(2,1)} %bitcast.10), calls=%async_computation.1 | async-start | bytes 2097152 | tf_op jit(solution)/shard_map/all_to_all | solution.py:332
  47.3 0.7 dynamic-slice
  48.9 9.7 %all-reduce = s32[72]{0:T(128)S(1)} all-reduce(s32[72]{0:T(128)S(1)} %add_dynamic-update-slice_fusion), channel_id=2, replica_groups=mesh['seg'=4,'pair'=8] {'pair'}, use_global_device_ids=true, to_apply=%add | all-reduce | flops 72 | bytes 576
  58.6 0.7 reshape.24.table_ref
  59.9 3.6 %stack.14 = (f32[4,2,32,128]{3,2,1,0:T(8,128)}, f32[4,2,32,128]{3,2,1,0:T(8,128)}, f32[4,2,32,128]{3,2,1,0:T(8,128)}, f32[4,2,32,128]{3,2,1,0:T(8,128)}, f32[4,2...) custom-call(s32[2]{0:T(128)} %pad_add_fusion.me_ref, ...), custom_call_target="tpu_custom_call" | custom-call | flops 10485760 | bytes 2097152 | tf_op jit(solution)/shard_map/stack/pallas_call | solution.py:157
  64.1 1.3 collective-permute-start.2
  65.4 1.7 %collective-permute-start.4 = (f32[4,2,32,128]{3,2,1,0:T(8,128)}, f32[4,2,32,128]{3,2,1,0:T(8,128)S(1)}, u32[]{:S(2)}, u32[]{:S(2)}) collective-permute-start(f32[4,2,32,128]{3,2,1,0:T(8,128)} %get-tuple-element.34), channel_id=1, source_target_pairs={{0,5},{1,4},{2,7},{3,6},{4,1},{5,0},{6,3},{7,2},{8,13},{9,12},{10,... | collective-permute-start | bytes 393224 | tf_op jit(solution)/shard_map/ppermute | solution.py:310
  67.0 5.7 %all-to-all-done.1 = bf16[32,2,2,32,128]{4,3,2,1,0:T(8,128)(2,1)S(1)} async-done(((bf16[32,2,2,32,128]{4,3,2,1,0:T(8,128)(2,1)}), bf16[32,2,2,32,128]{4,3,2,1,0:T(8,128)(2,1)S(1)}, u32[]{:S(2)}, u32[]{:S(2)}) %all-to-all-start.1) | async-done | bytes 1048608 | tf_op jit(solution)/shard_map/all_to_all | solution.py:332
  72.7 1.0 copy-done
  73.7 3.6 %stack.15 = (f32[4,2,32,128]{3,2,1,0:T(8,128)}, f32[4,2,32,128]{3,2,1,0:T(8,128)}, f32[4,2,32,128]{3,2,1,0:T(8,128)}, f32[4,2,32,128]{3,2,1,0:T(8,128)}, f32[4,2...) custom-call(s32[2]{0:T(128)} %pad_add_fusion.me_ref, ...), custom_call_target="tpu_custom_call" | custom-call | flops 10485760 | bytes 2097152 | tf_op jit(solution)/shard_map/stack/pallas_call | solution.py:157
  77.3 2.5 %collective-permute-start.5 = (f32[4,2,32,128]{3,2,1,0:T(8,128)}, f32[4,2,32,128]{3,2,1,0:T(8,128)S(1)}, u32[]{:S(2)}, u32[]{:S(2)}) collective-permute-start(f32[4,2,32,128]{3,2,1,0:T(8,128)} %get-tuple-element.35), channel_id=1, source_target_pairs={{0,6},{1,7},{2,4},{3,5},{4,2},{5,3},{6,0},{7,1},{8,14},{9,15},{10,... | collective-permute-start | bytes 393224 | tf_op jit(solution)/shard_map/ppermute | solution.py:310
  80.4 1.5 collective-permute-start.11
  81.9 2.1 %collective-permute-done.5.refs_6_ = f32[4,2,32,128]{3,2,1,0:T(8,128)S(1)} collective-permute-done((f32[4,2,32,128]{3,2,1,0:T(8,128)}, f32[4,2,32,128]{3,2,1,0:T(8,128)S(1)}, u32[]{:S(2)}, u32[]{:S(2)}) %collective-permute-start.5) | collective-permute-done | bytes 131104 | tf_op jit(solution)/shard_map/ppermute | solution.py:310
  84.0 1.4 collective-permute-start.13
  85.5 1.4 collective-permute-done.6.refs_7_
  86.8 0.9 collective-permute-start.14
  87.7 1.9 %collective-permute-start.15 = (f32[4,2,32,128]{3,2,1,0:T(8,128)}, f32[4,2,32,128]{3,2,1,0:T(8,128)S(1)}, u32[]{:S(2)}, u32[]{:S(2)}) collective-permute-start(f32[4,2,32,128]{3,2,1,0:T(8,128)} %get-tuple-element.47), channel_id=1, source_target_pairs={{0,6},{1,7},{2,4},{3,5},{4,2},{5,3},{6,0},{7,1},{8,14},{9,15},{10,... | collective-permute-start | bytes 393224 | tf_op jit(solution)/shard_map/ppermute | solution.py:310
  89.8 19.2 %dft.2 = (f32[256,128]{1,0:T(8,128)}, f32[256,128]{1,0:T(8,128)}, f32[256,128]{1,0:T(8,128)}, f32[256,128]{1,0:T(8,128)}) custom-call(s32[2]{0:T(128)} %pad_add_fusion.me_ref, bf16[2,512,512]{2,1,0:T(8,128)(2,1)} %constant.26.clone.whi_ref, bf16[2,512,512]{2,1,0:T(8,128)(2,1)} %constant.27.clone.wlo_ref, f32[512,128]{1,0:T(8,128)} %constant.23.clone.cos_ref, ...), custom_call_target="tpu_custom_call" | custom-call | flops 1610612736 | bytes 3670016 | tf_op jit(solution)/shard_map/dft/pallas_call | solution.py:248
  109.0 1.8 %collective-permute-start.7 = (f32[256,128]{1,0:T(8,128)}, f32[256,128]{1,0:T(8,128)S(1)}, u32[]{:S(2)}, u32[]{:S(2)}) collective-permute-start(f32[256,128]{1,0:T(8,128)} %get-tuple-element.38), channel_id=1, source_target_pairs={{0,8},{8,0},{16,24},{24,16},{1,9},{9,1},{17,25},{25,17},{2,10},{10... | collective-permute-start | bytes 393224 | tf_op jit(solution)/shard_map/ppermute | solution.py:310
  110.8 1.1 collective-permute-start.8
  111.9 1.6 %collective-permute-start.9 = (f32[256,128]{1,0:T(8,128)}, f32[256,128]{1,0:T(8,128)S(1)}, u32[]{:S(2)}, u32[]{:S(2)}) collective-permute-start(f32[256,128]{1,0:T(8,128)} %get-tuple-element.40), channel_id=1, source_target_pairs={{0,24},{8,16},{16,8},{24,0},{1,25},{9,17},{17,9},{25,1},{2,26},{10... | collective-permute-start | bytes 393224 | tf_op jit(solution)/shard_map/ppermute | solution.py:310
  114.2 19.2 %dft.3 = (f32[256,128]{1,0:T(8,128)}, f32[256,128]{1,0:T(8,128)}, f32[256,128]{1,0:T(8,128)}, f32[256,128]{1,0:T(8,128)}) custom-call(s32[2]{0:T(128)} %pad_add_fusion.me_ref, bf16[2,512,512]{2,1,0:T(8,128)(2,1)} %constant.26.clone.whi_ref, bf16[2,512,512]{2,1,0:T(8,128)(2,1)} %constant.27.clone.wlo_ref, f32[512,128]{1,0:T(8,128)} %constant.23.clone.cos_ref, ...), custom_call_target="tpu_custom_call" | custom-call | flops 1610612736 | bytes 3670016 | tf_op jit(solution)/shard_map/dft/pallas_call | solution.py:248
  133.4 0.8 collective-permute-start.17
  134.2 2.0 %collective-permute-start.18 = (f32[256,128]{1,0:T(8,128)}, f32[256,128]{1,0:T(8,128)S(1)}, u32[]{:S(2)}, u32[]{:S(2)}) collective-permute-start(f32[256,128]{1,0:T(8,128)} %get-tuple-element.51), channel_id=1, source_target_pairs={{0,16},{8,24},{16,0},{24,8},{1,17},{9,25},{17,1},{25,9},{2,18},{10... | collective-permute-start | bytes 393224 | tf_op jit(solution)/shard_map/ppermute | solution.py:310
  136.2 1.6 %collective-permute-start.19 = (f32[256,128]{1,0:T(8,128)}, f32[256,128]{1,0:T(8,128)S(1)}, u32[]{:S(2)}, u32[]{:S(2)}) collective-permute-start(f32[256,128]{1,0:T(8,128)} %get-tuple-element.52), channel_id=1, source_target_pairs={{0,24},{8,16},{16,8},{24,0},{1,25},{9,17},{17,9},{25,1},{2,26},{10... | collective-permute-start | bytes 393224 | tf_op jit(solution)/shard_map/ppermute | solution.py:310
  137.8 3.6 %collective-permute-done.17.refs_5_ = f32[256,128]{1,0:T(8,128)S(1)} collective-permute-done((f32[256,128]{1,0:T(8,128)}, f32[256,128]{1,0:T(8,128)S(1)}, u32[]{:S(2)}, u32[]{:S(2)}) %collective-permute-start.17) | collective-permute-done | bytes 131104 | tf_op jit(solution)/shard_map/ppermute | solution.py:310
  141.4 5.9 %collective-permute-done.18.refs_6_ = f32[256,128]{1,0:T(8,128)S(1)} collective-permute-done((f32[256,128]{1,0:T(8,128)}, f32[256,128]{1,0:T(8,128)S(1)}, u32[]{:S(2)}, u32[]{:S(2)}) %collective-permute-start.18) | collective-permute-done | bytes 131104 | tf_op jit(solution)/shard_map/ppermute | solution.py:310
  148.0 6.5 %unpack.1 = f32[512,4,128]{2,1,0:T(4,128)} custom-call(s32[2]{0:T(128)} %pad_add_fusion.me_ref, f32[256,128]{1,0:T(8,128)} %get-tuple-element.37.refs_0_, f32[256,128]{1,0:T(8,128)} %copy-done.2, f32[256,128]{1,0:T(8,128)} %copy-done.3, f32[256,128]{1,0:T(8,128)} %copy-done.4, f32[256,128]{1,0:T(8,128)} %get-tuple-element.49.refs_4_, f32[256,128]{1,0:T(8,128)} %copy-done.5, ...), custom_call_target="tpu_custom_call" | custom-call | flops 2359296 | bytes 2097152 | tf_op jit(solution)/shard_map/unpack/pallas_call | solution.py:293
  (75 shorter events, 3.7 us)
Async XLA Ops:
  9.3 33.5 %all-to-all-start = ((bf16[32,2,2,32,128]{4,3,2,1,0:T(8,128)(2,1)}), bf16[32,2,2,32,128]{4,3,2,1,0:T(8,128)(2,1)S(1)}, u32[]{:S(2)}, u32[]{:S(2)}) async-start(bf16[32,2,2,32,128]{4,3,2,1,0:T(8,128)(2,1)} %bitcast.11), calls=%async_computation | async-start | bytes 2097152 | tf_op jit(solution)/shard_map/all_to_all | solution.py:332
  16.6 30.5 %copy-start.8 = (s32[4,2]{0,1:T(2,128)S(1)}, s32[4,2]{0,1:T(2,128)}, u32[]{:S(2)}) copy-start(s32[4,2]{0,1:T(2,128)} %param.16) | copy-start | bytes 100
  16.6 30.7 %copy-start.23 = (u32[32]{0:T(128)S(1)}, u32[32]{0:T(128)}, u32[]{:S(2)}) copy-start(u32[32]{0:T(128)} %constant.34) | copy-start | bytes 388
  42.8 17.0 %copy-start.1 = (bf16[32,2,2,32,128]{4,3,2,1,0:T(8,128)(2,1)}, bf16[32,2,2,32,128]{4,3,2,1,0:T(8,128)(2,1)S(1)}, u32[]{:S(2)}) copy-start(bf16[32,2,2,32,128]{4,3,2,1,0:T(8,128)(2,1)S(1)} %all-to-all-done) | copy-start | bytes 3145732
  42.8 29.9 %all-to-all-start.1 = ((bf16[32,2,2,32,128]{4,3,2,1,0:T(8,128)(2,1)}), bf16[32,2,2,32,128]{4,3,2,1,0:T(8,128)(2,1)S(1)}, u32[]{:S(2)}, u32[]{:S(2)}) async-start(bf16[32,2,2,32,128]{4,3,2,1,0:T(8,128)(2,1)} %bitcast.10), calls=%async_computation.1 | async-start | bytes 2097152 | tf_op jit(solution)/shard_map/all_to_all | solution.py:332
  63.5 13.8 %collective-permute-start = (f32[4,2,32,128]{3,2,1,0:T(8,128)}, f32[4,2,32,128]{3,2,1,0:T(8,128)S(1)}, u32[]{:S(2)}, u32[]{:S(2)}) collective-permute-start(f32[4,2,32,128]{3,2,1,0:T(8,128)} %get-tuple-element.30), channel_id=1, source_target_pairs={{0,1},{1,0},{2,3},{3,2},{4,5},{5,4},{6,7},{7,6},{8,9},{9,8},{10,11... | collective-permute-start | bytes 393224 | tf_op jit(solution)/shard_map/ppermute | solution.py:310
  63.5 16.3 %collective-permute-start.1 = (f32[4,2,32,128]{3,2,1,0:T(8,128)}, f32[4,2,32,128]{3,2,1,0:T(8,128)S(1)}, u32[]{:S(2)}, u32[]{:S(2)}) collective-permute-start(f32[4,2,32,128]{3,2,1,0:T(8,128)} %get-tuple-element.31), channel_id=1, source_target_pairs={{0,2},{1,3},{2,0},{3,1},{4,6},{5,7},{6,4},{7,5},{8,10},{9,11},{10,... | collective-permute-start | bytes 393224 | tf_op jit(solution)/shard_map/ppermute | solution.py:310
  64.1 15.7 %collective-permute-start.2 = (f32[4,2,32,128]{3,2,1,0:T(8,128)}, f32[4,2,32,128]{3,2,1,0:T(8,128)S(1)}, u32[]{:S(2)}, u32[]{:S(2)}) collective-permute-start(f32[4,2,32,128]{3,2,1,0:T(8,128)} %get-tuple-element.32), channel_id=1, source_target_pairs={{0,3},{1,2},{2,1},{3,0},{4,7},{5,6},{6,5},{7,4},{8,11},{9,10},{10,... | collective-permute-start | bytes 393224 | tf_op jit(solution)/shard_map/ppermute | solution.py:310
  65.4 15.1 %collective-permute-start.3 = (f32[4,2,32,128]{3,2,1,0:T(8,128)}, f32[4,2,32,128]{3,2,1,0:T(8,128)S(1)}, u32[]{:S(2)}, u32[]{:S(2)}) collective-permute-start(f32[4,2,32,128]{3,2,1,0:T(8,128)} %get-tuple-element.33), channel_id=1, source_target_pairs={{0,4},{1,5},{2,6},{3,7},{4,0},{5,1},{6,2},{7,3},{8,12},{9,13},{10,... | collective-permute-start | bytes 393224 | tf_op jit(solution)/shard_map/ppermute | solution.py:310
  65.4 16.5 %collective-permute-start.4 = (f32[4,2,32,128]{3,2,1,0:T(8,128)}, f32[4,2,32,128]{3,2,1,0:T(8,128)S(1)}, u32[]{:S(2)}, u32[]{:S(2)}) collective-permute-start(f32[4,2,32,128]{3,2,1,0:T(8,128)} %get-tuple-element.34), channel_id=1, source_target_pairs={{0,5},{1,4},{2,7},{3,6},{4,1},{5,0},{6,3},{7,2},{8,13},{9,12},{10,... | collective-permute-start | bytes 393224 | tf_op jit(solution)/shard_map/ppermute | solution.py:310
  77.3 12.4 %copy-start.9 = (f32[4,2,32,128]{3,2,1,0:T(8,128)}, f32[4,2,32,128]{3,2,1,0:T(8,128)S(1)}, u32[]{:S(2)}) copy-start(f32[4,2,32,128]{3,2,1,0:T(8,128)S(1)} %collective-permute-done.refs_1_) | copy-start | bytes 393220
  77.3 6.7 %collective-permute-start.5 = (f32[4,2,32,128]{3,2,1,0:T(8,128)}, f32[4,2,32,128]{3,2,1,0:T(8,128)S(1)}, u32[]{:S(2)}, u32[]{:S(2)}) collective-permute-start(f32[4,2,32,128]{3,2,1,0:T(8,128)} %get-tuple-element.35), channel_id=1, source_target_pairs={{0,6},{1,7},{2,4},{3,5},{4,2},{5,3},{6,0},{7,1},{8,14},{9,15},{10,... | collective-permute-start | bytes 393224 | tf_op jit(solution)/shard_map/ppermute | solution.py:310
  79.8 10.0 %copy-start.10 = (f32[4,2,32,128]{3,2,1,0:T(8,128)}, f32[4,2,32,128]{3,2,1,0:T(8,128)S(1)}, u32[]{:S(2)}) copy-start(f32[4,2,32,128]{3,2,1,0:T(8,128)S(1)} %collective-permute-done.1.refs_2_) | copy-start | bytes 393220
  79.8 7.1 %collective-permute-start.6 = (f32[4,2,32,128]{3,2,1,0:T(8,128)}, f32[4,2,32,128]{3,2,1,0:T(8,128)S(1)}, u32[]{:S(2)}, u32[]{:S(2)}) collective-permute-start(f32[4,2,32,128]{3,2,1,0:T(8,128)} %get-tuple-element.36), channel_id=1, source_target_pairs={{0,7},{1,6},{2,5},{3,4},{4,3},{5,2},{6,1},{7,0},{8,15},{9,14},{10,... | collective-permute-start | bytes 393224 | tf_op jit(solution)/shard_map/ppermute | solution.py:310
  79.8 10.0 %copy-start.12 = (f32[4,2,32,128]{3,2,1,0:T(8,128)}, f32[4,2,32,128]{3,2,1,0:T(8,128)S(1)}, u32[]{:S(2)}) copy-start(f32[4,2,32,128]{3,2,1,0:T(8,128)S(1)} %collective-permute-done.2.refs_3_) | copy-start | bytes 393220
  79.8 7.9 %collective-permute-start.10 = (f32[4,2,32,128]{3,2,1,0:T(8,128)}, f32[4,2,32,128]{3,2,1,0:T(8,128)S(1)}, u32[]{:S(2)}, u32[]{:S(2)}) collective-permute-start(f32[4,2,32,128]{3,2,1,0:T(8,128)} %get-tuple-element.42), channel_id=1, source_target_pairs={{0,1},{1,0},{2,3},{3,2},{4,5},{5,4},{6,7},{7,6},{8,9},{9,8},{10,11... | collective-permute-start | bytes 393224 | tf_op jit(solution)/shard_map/ppermute | solution.py:310
  80.4 9.2 %collective-permute-start.11 = (f32[4,2,32,128]{3,2,1,0:T(8,128)}, f32[4,2,32,128]{3,2,1,0:T(8,128)S(1)}, u32[]{:S(2)}, u32[]{:S(2)}) collective-permute-start(f32[4,2,32,128]{3,2,1,0:T(8,128)} %get-tuple-element.43), channel_id=1, source_target_pairs={{0,2},{1,3},{2,0},{3,1},{4,6},{5,7},{6,4},{7,5},{8,10},{9,11},{10,... | collective-permute-start | bytes 393224 | tf_op jit(solution)/shard_map/ppermute | solution.py:310
  81.9 27.1 %collective-permute-start.12 = (f32[4,2,32,128]{3,2,1,0:T(8,128)}, f32[4,2,32,128]{3,2,1,0:T(8,128)S(1)}, u32[]{:S(2)}, u32[]{:S(2)}) collective-permute-start(f32[4,2,32,128]{3,2,1,0:T(8,128)} %get-tuple-element.44), channel_id=1, source_target_pairs={{0,3},{1,2},{2,1},{3,0},{4,7},{5,6},{6,5},{7,4},{8,11},{9,10},{10,... | collective-permute-start | bytes 393224 | tf_op jit(solution)/shard_map/ppermute | solution.py:310
  84.0 26.8 %collective-permute-start.13 = (f32[4,2,32,128]{3,2,1,0:T(8,128)}, f32[4,2,32,128]{3,2,1,0:T(8,128)S(1)}, u32[]{:S(2)}, u32[]{:S(2)}) collective-permute-start(f32[4,2,32,128]{3,2,1,0:T(8,128)} %get-tuple-element.45), channel_id=1, source_target_pairs={{0,4},{1,5},{2,6},{3,7},{4,0},{5,1},{6,2},{7,3},{8,12},{9,13},{10,... | collective-permute-start | bytes 393224 | tf_op jit(solution)/shard_map/ppermute | solution.py:310
  86.8 25.1 %collective-permute-start.14 = (f32[4,2,32,128]{3,2,1,0:T(8,128)}, f32[4,2,32,128]{3,2,1,0:T(8,128)S(1)}, u32[]{:S(2)}, u32[]{:S(2)}) collective-permute-start(f32[4,2,32,128]{3,2,1,0:T(8,128)} %get-tuple-element.46), channel_id=1, source_target_pairs={{0,5},{1,4},{2,7},{3,6},{4,1},{5,0},{6,3},{7,2},{8,13},{9,12},{10,... | collective-permute-start | bytes 393224 | tf_op jit(solution)/shard_map/ppermute | solution.py:310
  87.7 21.3 %copy-start.11 = (f32[4,2,32,128]{3,2,1,0:T(8,128)}, f32[4,2,32,128]{3,2,1,0:T(8,128)S(1)}, u32[]{:S(2)}) copy-start(f32[4,2,32,128]{3,2,1,0:T(8,128)S(1)} %collective-permute-done.10.refs_1_) | copy-start | bytes 393220
  87.7 25.8 %collective-permute-start.15 = (f32[4,2,32,128]{3,2,1,0:T(8,128)}, f32[4,2,32,128]{3,2,1,0:T(8,128)S(1)}, u32[]{:S(2)}, u32[]{:S(2)}) collective-permute-start(f32[4,2,32,128]{3,2,1,0:T(8,128)} %get-tuple-element.47), channel_id=1, source_target_pairs={{0,6},{1,7},{2,4},{3,5},{4,2},{5,3},{6,0},{7,1},{8,14},{9,15},{10,... | collective-permute-start | bytes 393224 | tf_op jit(solution)/shard_map/ppermute | solution.py:310
  89.6 19.3 %copy-start.15 = (f32[4,2,32,128]{3,2,1,0:T(8,128)}, f32[4,2,32,128]{3,2,1,0:T(8,128)S(1)}, u32[]{:S(2)}) copy-start(f32[4,2,32,128]{3,2,1,0:T(8,128)S(1)} %collective-permute-done.11.refs_2_) | copy-start | bytes 393220
  89.6 23.8 %collective-permute-start.16 = (f32[4,2,32,128]{3,2,1,0:T(8,128)}, f32[4,2,32,128]{3,2,1,0:T(8,128)S(1)}, u32[]{:S(2)}, u32[]{:S(2)}) collective-permute-start(f32[4,2,32,128]{3,2,1,0:T(8,128)} %get-tuple-element.48), channel_id=1, source_target_pairs={{0,7},{1,6},{2,5},{3,4},{4,3},{5,2},{6,1},{7,0},{8,15},{9,14},{10,... | collective-permute-start | bytes 393224 | tf_op jit(solution)/shard_map/ppermute | solution.py:310
  109.0 27.2 %collective-permute-start.7 = (f32[256,128]{1,0:T(8,128)}, f32[256,128]{1,0:T(8,128)S(1)}, u32[]{:S(2)}, u32[]{:S(2)}) collective-permute-start(f32[256,128]{1,0:T(8,128)} %get-tuple-element.38), channel_id=1, source_target_pairs={{0,8},{8,0},{16,24},{24,16},{1,9},{9,1},{17,25},{25,17},{2,10},{10... | collective-permute-start | bytes 393224 | tf_op jit(solution)/shard_map/ppermute | solution.py:310
  110.8 27.0 %collective-permute-start.8 = (f32[256,128]{1,0:T(8,128)}, f32[256,128]{1,0:T(8,128)S(1)}, u32[]{:S(2)}, u32[]{:S(2)}) collective-permute-start(f32[256,128]{1,0:T(8,128)} %get-tuple-element.39), channel_id=1, source_target_pairs={{0,16},{8,24},{16,0},{24,8},{1,17},{9,25},{17,1},{25,9},{2,18},{10... | collective-permute-start | bytes 393224 | tf_op jit(solution)/shard_map/ppermute | solution.py:310
  111.9 25.9 %collective-permute-start.9 = (f32[256,128]{1,0:T(8,128)}, f32[256,128]{1,0:T(8,128)S(1)}, u32[]{:S(2)}, u32[]{:S(2)}) collective-permute-start(f32[256,128]{1,0:T(8,128)} %get-tuple-element.40), channel_id=1, source_target_pairs={{0,24},{8,16},{16,8},{24,0},{1,25},{9,17},{17,9},{25,1},{2,26},{10... | collective-permute-start | bytes 393224 | tf_op jit(solution)/shard_map/ppermute | solution.py:310
  133.4 8.0 %collective-permute-start.17 = (f32[256,128]{1,0:T(8,128)}, f32[256,128]{1,0:T(8,128)S(1)}, u32[]{:S(2)}, u32[]{:S(2)}) collective-permute-start(f32[256,128]{1,0:T(8,128)} %get-tuple-element.50), channel_id=1, source_target_pairs={{0,8},{8,0},{16,24},{24,16},{1,9},{9,1},{17,25},{25,17},{2,10},{10... | collective-permute-start | bytes 393224 | tf_op jit(solution)/shard_map/ppermute | solution.py:310
  134.2 13.1 %collective-permute-start.18 = (f32[256,128]{1,0:T(8,128)}, f32[256,128]{1,0:T(8,128)S(1)}, u32[]{:S(2)}, u32[]{:S(2)}) collective-permute-start(f32[256,128]{1,0:T(8,128)} %get-tuple-element.51), channel_id=1, source_target_pairs={{0,16},{8,24},{16,0},{24,8},{1,17},{9,25},{17,1},{25,9},{2,18},{10... | collective-permute-start | bytes 393224 | tf_op jit(solution)/shard_map/ppermute | solution.py:310
  136.2 11.1 %copy-start.2 = (f32[256,128]{1,0:T(8,128)}, f32[256,128]{1,0:T(8,128)S(1)}, u32[]{:S(2)}) copy-start(f32[256,128]{1,0:T(8,128)S(1)} %collective-permute-done.7.refs_1_) | copy-start | bytes 393220
  136.2 11.1 %collective-permute-start.19 = (f32[256,128]{1,0:T(8,128)}, f32[256,128]{1,0:T(8,128)S(1)}, u32[]{:S(2)}, u32[]{:S(2)}) collective-permute-start(f32[256,128]{1,0:T(8,128)} %get-tuple-element.52), channel_id=1, source_target_pairs={{0,24},{8,16},{16,8},{24,0},{1,25},{9,17},{17,9},{25,1},{2,26},{10... | collective-permute-start | bytes 393224 | tf_op jit(solution)/shard_map/ppermute | solution.py:310
  137.8 9.5 %copy-start.4 = (f32[256,128]{1,0:T(8,128)}, f32[256,128]{1,0:T(8,128)S(1)}, u32[]{:S(2)}) copy-start(f32[256,128]{1,0:T(8,128)S(1)} %collective-permute-done.9.refs_3_) | copy-start | bytes 393220
  (14 other events, 53.8 us)

commit v2 on v1

--- a/solution.py
+++ b/solution.py
@@ -63,23 +63,28 @@
     band = freq // n_pair
     wide = sel_ref.shape[1]
 
+    unroll = buf_ref.shape[0]
+
     def one(step, _):
         ri, p = step // n_pair, step % n_pair
+        slot = step % unroll
         block = x_ref[ri, pl.ds(pl.multiple_of(p * band, band), band), :]
         for part in range(wide // TILE):
-            buf_ref[...] = jnp.dot(
+            buf_ref[slot] = jnp.dot(
                 block,
                 sel_ref[:, part * TILE : (part + 1) * TILE],
                 preferred_element_type=jnp.float32,
             )
-            v = [buf_ref[pl.ds(fb, rows, stride=GROUPS), :] for fb in range(GROUPS)]
+            v = [
+                buf_ref[slot, pl.ds(fb, rows, stride=GROUPS), :] for fb in range(GROUPS)
+            ]
             v = transpose_groups(v)
             for g in range(GROUPS):
                 t, z = divmod(part * GROUPS + g, n_seg)
                 out_ref[z, p, t, ri] = v[g].astype(jnp.bfloat16)
         return 0
 
-    lax.fori_loop(0, 2 * n_pair, one, 0)
+    lax.fori_loop(0, 2 * n_pair, one, 0, unroll=unroll)
 
 
 def pack(x, chunk, n_seg, n_pair):
@@ -100,8 +105,9 @@
         ),
         in_specs=[pl.BlockSpec(memory_space=pltpu.VMEM)] * 2,
         out_specs=pl.BlockSpec(memory_space=pltpu.VMEM),
-        scratch_shapes=[pltpu.VMEM((freq // n_pair, TILE), jnp.float32)],
+        scratch_shapes=[pltpu.VMEM((8, freq // n_pair, TILE), jnp.float32)],
         name="pack",
+        compiler_params=pltpu.CompilerParams(vmem_limit_bytes=16 << 20),
         cost_estimate=pl.CostEstimate(
             flops=4 * freq * chans * wide,
             bytes_accessed=x.size * 2 + 2 * freq * wide * 2,
@@ -160,6 +166,7 @@
         in_specs=[smem, smem, vmem],
         out_specs=[vmem] * n_pair,
         name="stack",
+        compiler_params=pltpu.CompilerParams(vmem_limit_bytes=12 << 20),
         cost_estimate=pl.CostEstimate(
             flops=n_pair * most * rows * TILE * n_seg * 20,
             bytes_accessed=spec.size * 2 + n_pair * most * 2 * rows * TILE * 4,
@@ -168,10 +175,10 @@
     )(me, table, spec)
 
 
-def dft_kernel(n_seg, n_pair, most, me_ref, whi_ref, wlo_ref, cos_ref, sin_ref, turn_ref, *refs):
+def dft_kernel(n_seg, n_pair, most, me_ref, whi_ref, wlo_ref, cos_ref, sin_ref, thi_ref, tlo_ref, *refs):
     ins = refs[:n_pair]
     outs = refs[n_pair : n_pair + n_seg]
-    s32, shi, slo, y = refs[n_pair + n_seg :]
+    s32, shi, slo, y, zhi, zlo, sums, parts = refs[n_pair + n_seg :]
     rows = ins[0].shape[2]
     half_h = s32.shape[0] // 2
     for k in range(n_pair):
@@ -190,34 +197,39 @@
             + jnp.dot(whi_ref[m], slo[...], preferred_element_type=jnp.float32)
         ) + jnp.dot(whi_ref[m], shi[...], preferred_element_type=jnp.float32)
     period = y.shape[1]
+    step_rows = 64
+    for b in range(period // step_rows):
+        at = slice(b * step_rows, (b + 1) * step_rows)
+        c = cos_ref[at, :]
+        d = sin_ref[at, :]
+        for s in range(most):
+            lanes = slice(s * TILE, (s + 1) * TILE)
+            yr = y[0, at, lanes]
+            yi = y[1, at, lanes]
+            for ri, z in enumerate((c * yr - d * yi, d * yr + c * yi)):
+                to = slice((ri * most + s) * TILE, (ri * most + s + 1) * TILE)
+                hi = z.astype(jnp.bfloat16)
+                zhi[at, to] = hi
+                zlo[at, to] = (z - hi.astype(jnp.float32)).astype(jnp.bfloat16)
+    sums[...] = (
+        jnp.dot(zhi[...], tlo_ref[...], preferred_element_type=jnp.float32)
+        + jnp.dot(zlo[...], thi_ref[...], preferred_element_type=jnp.float32)
+    ) + jnp.dot(zhi[...], thi_ref[...], preferred_element_type=jnp.float32)
     half = outs[0].shape[0]
-    step_rows = 16
+    first = lax.broadcasted_iota(jnp.int32, (half, TILE), 1) < TILE // 2
+    for dest in range(n_seg):
+        lag = dest * 2 * half
+        r, l0 = lag // period, lag % period
+        col = slice(r // 2 * TILE, (r // 2 + 1) * TILE)
+        low = sums[l0 : l0 + half, col]
+        high = sums[l0 + half : l0 + 2 * half, col]
+        if r % 2 == 0:
+            high = pltpu.roll(high, TILE // 2, 1)
+        else:
+            low = pltpu.roll(low, TILE // 2, 1)
+        parts[dest] = jnp.where(first, low, high)
     for k in range(n_seg):
-        dest = jnp.bitwise_xor(me_ref[0], k)
-        out_ref = outs[k]
-
-        def one(b, _):
-            v = []
-            for h in range(2):
-                lag = dest * (2 * half) + h * half + b * step_rows
-                l0 = pl.multiple_of(lax.rem(lag, period), step_rows)
-                c0 = cos_ref[pl.ds(l0, step_rows), :]
-                d0 = sin_ref[pl.ds(l0, step_rows), :]
-                ct = turn_ref[0, lag // period]
-                dt = turn_ref[1, lag // period]
-                c = c0 * ct - d0 * dt
-                d = d0 * ct + c0 * dt
-                for s in range(most):
-                    lanes = slice(s * TILE, (s + 1) * TILE)
-                    v.append(
-                        c * y[0, pl.ds(l0, step_rows), lanes]
-                        - d * y[1, pl.ds(l0, step_rows), lanes]
-                    )
-            at = pl.multiple_of(b * step_rows, step_rows)
-            out_ref[pl.ds(at, step_rows), :] = reduce_groups(v)
-            return 0
-
-        lax.fori_loop(0, half // step_rows, one, 0)
+        outs[k][...] = parts[jnp.bitwise_xor(me_ref[0], k)]
 
 
 def dft(me, blocks, freq, n_seg, n_pair, most):
@@ -238,9 +250,18 @@
     scale = 1.0 / math.sqrt(freq)
     cos = jnp.asarray(np.cos(phase) * scale, jnp.float32)
     sin = jnp.asarray(np.sin(phase) * scale, jnp.float32)
-    start = np.arange(LAG // period) * period - LAG // 2
-    phase = ((start[:, None] * fb[None, :]) % (2 * freq)) * (math.pi / freq)
-    turns = jnp.asarray(np.stack([np.cos(phase), np.sin(phase)])[:, :, None], jnp.float32)
+    turns = LAG // period
+    t = np.zeros((2, most, GROUPS, CC, turns, most, CC), np.float64)
+    for r in range(turns):
+        for q in range(GROUPS):
+            phase = ((r * period - LAG // 2) * q % (2 * freq)) * (math.pi / freq)
+            for sl in range(most):
+                for ch in range(CC):
+                    t[0, sl, q, ch, r, sl, ch] = math.cos(phase)
+                    t[1, sl, q, ch, r, sl, ch] = -math.sin(phase)
+    t = t.reshape(2 * most * TILE, turns * most * CC).astype(np.float32)
+    thi = t.astype(jnp.bfloat16)
+    tlo = (t - thi.astype(np.float32)).astype(jnp.bfloat16)
     smem = pl.BlockSpec(memory_space=pltpu.SMEM)
     vmem = pl.BlockSpec(memory_space=pltpu.VMEM)
     half = LAG // n_seg // 2
@@ -248,21 +269,26 @@
     return pl.pallas_call(
         functools.partial(dft_kernel, n_seg, n_pair, most),
         out_shape=[jax.ShapeDtypeStruct((half, TILE), jnp.float32)] * n_seg,
-        in_specs=[smem] + [vmem] * (5 + n_pair),
+        in_specs=[smem] + [vmem] * (6 + n_pair),
         out_specs=[vmem] * n_seg,
         scratch_shapes=[
             pltpu.VMEM((2 * h, wide), jnp.float32),
             pltpu.VMEM((2 * h, wide), jnp.bfloat16),
             pltpu.VMEM((2 * h, wide), jnp.bfloat16),
             pltpu.VMEM((2, period, wide), jnp.float32),
+            pltpu.VMEM((period, 2 * wide), jnp.bfloat16),
+            pltpu.VMEM((period, 2 * wide), jnp.bfloat16),
+            pltpu.VMEM((period, turns * most * CC), jnp.float32),
+            pltpu.VMEM((n_seg, half, TILE), jnp.float32),
         ],
         name="dft",
+        compiler_params=pltpu.CompilerParams(vmem_limit_bytes=24 << 20),
         cost_estimate=pl.CostEstimate(
             flops=3 * 2 * 2 * period * 2 * h * wide,
             bytes_accessed=2 * w.size * 2 + 2 * period * TILE * 4 + 2 * h * wide * 4,
             transcendentals=0,
         ),
-    )(me, jnp.asarray(whi), jnp.asarray(wlo), cos, sin, turns, *blocks)
+    )(me, jnp.asarray(whi), jnp.asarray(wlo), cos, sin, jnp.asarray(thi), jnp.asarray(tlo), *blocks)
 
 
 def unpack_kernel(n_seg, chunks, most, me_ref, *refs):
@@ -283,7 +309,7 @@
                 out_ref[pl.ds(h * half + at, step_rows), s, :] = v[h * most + s]
         return 0
 
-    lax.fori_loop(0, half // step_rows, one, 0)
+    lax.fori_loop(0, half // step_rows, one, 0, unroll=4)
 
 
 def unpack(me, parts, n_seg, chunks, most):
@@ -297,6 +323,7 @@
         out_specs=vmem,
         scratch_shapes=[pltpu.VMEM((GROUPS, half, TILE), jnp.float32)],
         name="unpack",
+        compiler_params=pltpu.CompilerParams(vmem_limit_bytes=12 << 20),
         cost_estimate=pl.CostEstimate(
             flops=half * TILE * GROUPS * 9,
             bytes_accessed=2 * half * TILE * GROUPS * 4,
@@ -322,21 +349,30 @@
     rows = freq // n_pair // GROUPS
     me = jnp.stack([lax.axis_index("seg"), lax.axis_index("pair")]).astype(jnp.int32)
     x = spectra.reshape(2, freq, spectra.shape[3])
-    table = lax.all_gather(
-        jnp.concatenate([pair_lists.reshape(-1), pair_counts]), "pair", axis=0
-    )
+    lists = jnp.concatenate([pair_lists.reshape(-1), pair_counts])
+    packed = [pack(x, chunk, n_seg, n_pair) for chunk in range(chunks)]
+    lists, packed[-1] = lax.optimization_barrier((lists, packed[-1]))
+    table = lax.all_gather(lists, "pair", axis=0)
+    if chunks > 1:
+        table, packed[1] = lax.optimization_barrier((table, packed[1]))
     done = []
-    for chunk in range(chunks):
-        sent = pack(x, chunk, n_seg, n_pair)
-        sent = sent.reshape(n_seg * n_pair, tiles, 2, rows, TILE)
+    lags = None
+    for sent in packed:
         got = lax.all_to_all(
-            sent, ("seg", "pair"), split_axis=0, concat_axis=0, tiled=True
+            sent.reshape(n_seg * n_pair, tiles, 2, rows, TILE),
+            ("seg", "pair"),
+            split_axis=0,
+            concat_axis=0,
+            tiled=True,
         )
+        if lags is not None:
+            got, lags = lax.optimization_barrier((got, lags))
+            done += exchange(lags, "seg", n_seg)
         spec = got.reshape(n_seg, n_pair * tiles, 2, rows, TILE)
         blocks = stacks(me, table, spec, n_seg, n_pair, most)
         blocks = exchange(blocks, "pair", n_pair)
         lags = dft(me, blocks, freq, n_seg, n_pair, most)
-        done += exchange(lags, "seg", n_seg)
+    done += exchange(lags, "seg", n_seg)
     return unpack(me, done, n_seg, chunks, most)
 
 

time: 155 us -> 125 us (0.81)
  Pallas kernels: 70.7 us -> 22.9 us
  waiting for transfers between devices: 35.5 us -> 45.9 us
  local copies, waits for them, and re-layouts: 3.91 us -> 12.2 us
  starting transfers between devices: 32.2 us -> 33.8 us
    pallas_call x2, Pallas kernels: 38.4 us -> 10 us  [dft(): pl.pallas_call(functools.partial(dft_kernel, n_seg, n_pair, most), out_sh...]
    ppermute x20, waiting for transfers between devices: 13 us -> 33.2 us  [exchange(): lax.ppermute(blocks[k], axis, [(i, i ^ k) for i in range(size)])]
    pallas_call x2, Pallas kernels: 18.6 us -> 5.37 us  [pack(): pl.pallas_call(functools.partial(pack_kernel, n_seg, n_pair), out_shape=j...]
    all_to_all x2, waiting for transfers between devices: 22.6 us -> 12.7 us  [body(): lax.all_to_all(sent.reshape(n_seg * n_pair, tiles, 2, rows, TILE), ('seg'...]
    unnamed x51 -> x38, local copies, waits for them, and re-layouts: 3.14 us -> 12 us
    pallas_call x2, Pallas kernels: 7.22 us -> 4.09 us  [stacks(): pl.pallas_call(functools.partial(stack_kernel, n_seg, n_pair, most), out_...]
    pallas_call x1, Pallas kernels: 6.47 us -> 3.38 us  [unpack(): pl.pallas_call(functools.partial(unpack_kernel, n_seg, chunks, most), out...]
    ppermute x20, starting transfers between devices: 21.3 us -> 22.9 us  [exchange(): lax.ppermute(blocks[k], axis, [(i, i ^ k) for i in range(size)])]
  transfers between devices with their start and end apart: 22 -> 22, of which waited for: 6 -> 11; matrix products, arithmetic and copies ran while one was open for 2% -> 1% of each run, Pallas kernels for 36% -> 12%
where the time goes in v2:
time: 125 us
  waiting for transfers between devices  45.9 us (37%)
  starting transfers between devices  33.8 us (27%)
  Pallas kernels  22.9 us (18%)
  local copies, waits for them, and re-layouts  12.2 us (10%)
  blocking collectives  8.42 us (7%)
  between operations  1.36 us (1%)
    ppermute x20, waiting for transfers between devices, exchange(): lax.ppermute(blocks[k], axis, [(i, i ^ k) for i in range(size)])  33.2 us
    ppermute x20, starting transfers between devices, exchange(): lax.ppermute(blocks[k], axis, [(i, i ^ k) for i in range(size)])  22.9 us
    all_to_all x2, waiting for transfers between devices, body(): lax.all_to_all(sent.reshape(n_seg * n_pair, tiles, 2, rows, TILE), ('seg'...  12.7 us
    unnamed x38, local copies, waits for them, and re-layouts  12 us
    all_to_all x2, starting transfers between devices, body(): lax.all_to_all(sent.reshape(n_seg * n_pair, tiles, 2, rows, TILE), ('seg'...  10.9 us
    pallas_call x2, Pallas kernels, dft(): pl.pallas_call(functools.partial(dft_kernel, n_seg, n_pair, most), out_sh...  10 us
    unnamed x1, blocking collectives  8.42 us
    pallas_call x2, Pallas kernels, pack(): pl.pallas_call(functools.partial(pack_kernel, n_seg, n_pair), out_shape=j...  5.37 us
  transfers between devices with their start and end apart: 22, of which 11 were waited for; matrix products, arithmetic and copies ran while one was open for 1% of the time, Pallas kernels for 12%

profile of v2, /device:TPU:0, one launch (start us, length us, event | category | flops | bytes accessed | tf_op | source)
XLA Modules:
  0.0 124.8 jit_solution(4582403928088203625)
XLA Ops:
  0.0 1.6 %copy-done = bf16[1,2,2048,256]{3,2,1,0:T(8,128)(2,1)S(1)} copy-done((bf16[1,2,2048,256]{3,2,1,0:T(8,128)(2,1)S(1)}, bf16[1,2,2048,256]{3,2,1,0:T(8,128)(2,1)}, u32[]{:S(2)}) %copy-start) | copy-done | bytes 2097176
  2.4 2.7 %pack.3 = bf16[4,8,2,2,32,128]{5,4,3,2,1,0:T(8,128)(2,1)} custom-call(bf16[2,2048,256]{2,1,0:T(8,128)(2,1)S(1)} %bitcast.8, bf16[256,128]{1,0:T(8,128)(2,1)S(1)} %copy-done.3), custom_call_target="tpu_custom_call" | custom-call | flops 268435456 | bytes 3145728 | tf_op jit(solution)/shard_map/pack/pallas_call | solution.py:101
  5.1 7.3 %all-to-all-start.1 = ((bf16[32,2,2,32,128]{4,3,2,1,0:T(8,128)(2,1)}), bf16[32,2,2,32,128]{4,3,2,1,0:T(8,128)(2,1)S(1)}, u32[]{:S(2)}, u32[]{:S(2)}) async-start(bf16[32,2,2,32,128]{4,3,2,1,0:T(8,128)(2,1)} %bitcast.5), calls=%async_computation.1 | async-start | bytes 2097152 | tf_op jit(solution)/shard_map/all_to_all | solution.py:361
  13.3 2.7 %pack.2 = bf16[4,8,2,2,32,128]{5,4,3,2,1,0:T(8,128)(2,1)} custom-call(bf16[2,2048,256]{2,1,0:T(8,128)(2,1)S(1)} %bitcast.9, bf16[256,128]{1,0:T(8,128)(2,1)S(1)} %copy-done.2), custom_call_target="tpu_custom_call" | custom-call | flops 268435456 | bytes 3145728 | tf_op jit(solution)/shard_map/pack/pallas_call | solution.py:101
  17.4 8.4 %all-reduce = s32[72]{0:T(128)S(1)} all-reduce(s32[72]{0:T(128)S(1)} %dynamic-update-slice), channel_id=2, replica_groups=mesh['seg'=4,'pair'=8] {'pair'}, use_global_device_ids=true, to_apply=%add | all-reduce | flops 72 | bytes 576
  25.9 12.7 %all-to-all-done.1 = bf16[32,2,2,32,128]{4,3,2,1,0:T(8,128)(2,1)S(1)} async-done(((bf16[32,2,2,32,128]{4,3,2,1,0:T(8,128)(2,1)}), bf16[32,2,2,32,128]{4,3,2,1,0:T(8,128)(2,1)S(1)}, u32[]{:S(2)}, u32[]{:S(2)}) %all-to-all-start.1) | async-done | bytes 1048608 | tf_op jit(solution)/shard_map/all_to_all | solution.py:361
  38.6 3.6 %all-to-all-start = ((bf16[32,2,2,32,128]{4,3,2,1,0:T(8,128)(2,1)}), bf16[32,2,2,32,128]{4,3,2,1,0:T(8,128)(2,1)S(1)}, u32[]{:S(2)}, u32[]{:S(2)}) async-start(bf16[32,2,2,32,128]{4,3,2,1,0:T(8,128)(2,1)} %bitcast.4), calls=%async_computation | async-start | bytes 2097152 | tf_op jit(solution)/shard_map/all_to_all | solution.py:361
  42.4 2.0 %stack.14 = (f32[4,2,32,128]{3,2,1,0:T(8,128)S(1)}, f32[4,2,32,128]{3,2,1,0:T(8,128)S(1)}, f32[4,2,32,128]{3,2,1,0:T(8,128)S(1)}, f32[4,2,32,128]{3,2,1,0:T(8,12...) custom-call(s32[2]{0:T(128)S(1)} %pad_add_fusion.me_ref, ...), custom_call_target="tpu_custom_call" | custom-call | flops 10485760 | bytes 2097152 | tf_op jit(solution)/shard_map/stack/pallas_call | solution.py:163
  44.7 1.7 %collective-permute-start.1 = (f32[4,2,32,128]{3,2,1,0:T(8,128)S(1)}, f32[4,2,32,128]{3,2,1,0:T(8,128)S(1)}, u32[]{:S(2)}, u32[]{:S(2)}) collective-permute-start(f32[4,2,32,128]{3,2,1,0:T(8,128)S(1)} %get-tuple-element.44), channel_id=1, source_target_pairs={{0,2},{1,3},{2,0},{3,1},{4,6},{5,7},{6,4},{7,5},{8,10},{9,11},{10,... | collective-permute-start | bytes 393224 | tf_op jit(solution)/shard_map/ppermute | solution.py:337
  46.4 1.7 %collective-permute-start.3 = (f32[4,2,32,128]{3,2,1,0:T(8,128)S(1)}, f32[4,2,32,128]{3,2,1,0:T(8,128)S(1)}, u32[]{:S(2)}, u32[]{:S(2)}) collective-permute-start(f32[4,2,32,128]{3,2,1,0:T(8,128)S(1)} %get-tuple-element.46), channel_id=1, source_target_pairs={{0,4},{1,5},{2,6},{3,7},{4,0},{5,1},{6,2},{7,3},{8,12},{9,13},{10,... | collective-permute-start | bytes 393224 | tf_op jit(solution)/shard_map/ppermute | solution.py:337
  48.2 2.6 %collective-permute-start.5 = (f32[4,2,32,128]{3,2,1,0:T(8,128)S(1)}, f32[4,2,32,128]{3,2,1,0:T(8,128)S(1)}, u32[]{:S(2)}, u32[]{:S(2)}) collective-permute-start(f32[4,2,32,128]{3,2,1,0:T(8,128)S(1)} %get-tuple-element.48), channel_id=1, source_target_pairs={{0,6},{1,7},{2,4},{3,5},{4,2},{5,3},{6,0},{7,1},{8,14},{9,15},{10,... | collective-permute-start | bytes 393224 | tf_op jit(solution)/shard_map/ppermute | solution.py:337
  50.8 6.1 %collective-permute-done.1.refs_2_ = f32[4,2,32,128]{3,2,1,0:T(8,128)S(1)} collective-permute-done((f32[4,2,32,128]{3,2,1,0:T(8,128)S(1)}, f32[4,2,32,128]{3,2,1,0:T(8,128)S(1)}, u32[]{:S(2)}, u32[]{:S(2)}) %collective-permute-start.1) | collective-permute-done | bytes 131104 | tf_op jit(solution)/shard_map/ppermute | solution.py:337
  57.1 2.4 %collective-permute-done.2.refs_3_ = f32[4,2,32,128]{3,2,1,0:T(8,128)S(1)} collective-permute-done((f32[4,2,32,128]{3,2,1,0:T(8,128)S(1)}, f32[4,2,32,128]{3,2,1,0:T(8,128)S(1)}, u32[]{:S(2)}, u32[]{:S(2)}) %collective-permute-start.2) | collective-permute-done | bytes 131104 | tf_op jit(solution)/shard_map/ppermute | solution.py:337
  59.9 4.7 %collective-permute-done.5.refs_6_ = f32[4,2,32,128]{3,2,1,0:T(8,128)S(1)} collective-permute-done((f32[4,2,32,128]{3,2,1,0:T(8,128)S(1)}, f32[4,2,32,128]{3,2,1,0:T(8,128)S(1)}, u32[]{:S(2)}, u32[]{:S(2)}) %collective-permute-start.5) | collective-permute-done | bytes 131104 | tf_op jit(solution)/shard_map/ppermute | solution.py:337
  64.7 3.8 %collective-permute-done.6.refs_7_ = f32[4,2,32,128]{3,2,1,0:T(8,128)S(1)} collective-permute-done((f32[4,2,32,128]{3,2,1,0:T(8,128)S(1)}, f32[4,2,32,128]{3,2,1,0:T(8,128)S(1)}, u32[]{:S(2)}, u32[]{:S(2)}) %collective-permute-start.6) | collective-permute-done | bytes 131104 | tf_op jit(solution)/shard_map/ppermute | solution.py:337
  68.4 1.2 copy-done.4
  69.7 1.2 copy-done.6
  73.9 5.0 %dft.2 = (f32[256,128]{1,0:T(8,128)S(1)}, f32[256,128]{1,0:T(8,128)S(1)}, f32[256,128]{1,0:T(8,128)S(1)}, f32[256,128]{1,0:T(8,128)S(1)}) custom-call(s32[2]{0:T(128)S(1)} %pad_add_fusion.me_ref, bf16[2,512,512]{2,1,0:T(8,128)(2,1)S(1)} %copy-done.6, bf16[2,512,512]{2,1,0:T(8,128)(2,1)S(1)} %copy-done.4, f32[512,128]{1,0:T(8,128)S(1)} %copy-done.13, ...), custom_call_target="tpu_custom_call" | custom-call | flops 1610612736 | bytes 3670016 | tf_op jit(solution)/shard_map/dft/pallas_call | solution.py:269
  79.0 2.0 %stack.15 = (f32[4,2,32,128]{3,2,1,0:T(8,128)S(1)}, f32[4,2,32,128]{3,2,1,0:T(8,128)S(1)}, f32[4,2,32,128]{3,2,1,0:T(8,128)S(1)}, f32[4,2,32,128]{3,2,1,0:T(8,12...) custom-call(s32[2]{0:T(128)S(1)} %pad_add_fusion.me_ref, ...), custom_call_target="tpu_custom_call" | custom-call | flops 10485760 | bytes 2097152 | tf_op jit(solution)/shard_map/stack/pallas_call | solution.py:163
  84.8 1.2 collective-permute-start.15
  86.0 1.6 %collective-permute-done.11.refs_2_ = f32[4,2,32,128]{3,2,1,0:T(8,128)S(1)} collective-permute-done((f32[4,2,32,128]{3,2,1,0:T(8,128)S(1)}, f32[4,2,32,128]{3,2,1,0:T(8,128)S(1)}, u32[]{:S(2)}, u32[]{:S(2)}) %collective-permute-start.11) | collective-permute-done | bytes 131104 | tf_op jit(solution)/shard_map/ppermute | solution.py:337
  87.6 1.6 %collective-permute-done.12.refs_3_ = f32[4,2,32,128]{3,2,1,0:T(8,128)S(1)} collective-permute-done((f32[4,2,32,128]{3,2,1,0:T(8,128)S(1)}, f32[4,2,32,128]{3,2,1,0:T(8,128)S(1)}, u32[]{:S(2)}, u32[]{:S(2)}) %collective-permute-start.12) | collective-permute-done | bytes 131104 | tf_op jit(solution)/shard_map/ppermute | solution.py:337
  89.2 1.3 %collective-permute-start.7 = (f32[256,128]{1,0:T(8,128)S(1)}, f32[256,128]{1,0:T(8,128)S(1)}, u32[]{:S(2)}, u32[]{:S(2)}) collective-permute-start(f32[256,128]{1,0:T(8,128)S(1)} %get-tuple-element.55), channel_id=1, source_target_pairs={{0,8},{8,0},{16,24},{24,16},{1,9},{9,1},{17,25},{25,17},{2,10},{10... | collective-permute-start | bytes 393224 | tf_op jit(solution)/shard_map/ppermute | solution.py:337
  90.5 2.6 %collective-permute-start.8 = (f32[256,128]{1,0:T(8,128)S(1)}, f32[256,128]{1,0:T(8,128)S(1)}, u32[]{:S(2)}, u32[]{:S(2)}) collective-permute-start(f32[256,128]{1,0:T(8,128)S(1)} %get-tuple-element.56), channel_id=1, source_target_pairs={{0,16},{8,24},{16,0},{24,8},{1,17},{9,25},{17,1},{25,9},{2,18},{10... | collective-permute-start | bytes 393224 | tf_op jit(solution)/shard_map/ppermute | solution.py:337
  93.1 3.7 %collective-permute-done.14.refs_5_ = f32[4,2,32,128]{3,2,1,0:T(8,128)S(1)} collective-permute-done((f32[4,2,32,128]{3,2,1,0:T(8,128)S(1)}, f32[4,2,32,128]{3,2,1,0:T(8,128)S(1)}, u32[]{:S(2)}, u32[]{:S(2)}) %collective-permute-start.14) | collective-permute-done | bytes 131104 | tf_op jit(solution)/shard_map/ppermute | solution.py:337
  96.8 3.0 %collective-permute-start.9 = (f32[256,128]{1,0:T(8,128)S(1)}, f32[256,128]{1,0:T(8,128)S(1)}, u32[]{:S(2)}, u32[]{:S(2)}) collective-permute-start(f32[256,128]{1,0:T(8,128)S(1)} %get-tuple-element.57), channel_id=1, source_target_pairs={{0,24},{8,16},{16,8},{24,0},{1,25},{9,17},{17,9},{25,1},{2,26},{10... | collective-permute-start | bytes 393224 | tf_op jit(solution)/shard_map/ppermute | solution.py:337
  99.8 1.2 copy-done.7
  103.0 5.0 %dft.3 = (f32[256,128]{1,0:T(8,128)S(1)}, f32[256,128]{1,0:T(8,128)S(1)}, f32[256,128]{1,0:T(8,128)S(1)}, f32[256,128]{1,0:T(8,128)S(1)}) custom-call(s32[2]{0:T(128)S(1)} %pad_add_fusion.me_ref, bf16[2,512,512]{2,1,0:T(8,128)(2,1)S(1)} %copy-done.7, bf16[2,512,512]{2,1,0:T(8,128)(2,1)S(1)} %copy-done.5, f32[512,128]{1,0:T(8,128)S(1)} %copy-done.14, ...), custom_call_target="tpu_custom_call" | custom-call | flops 1610612736 | bytes 3670016 | tf_op jit(solution)/shard_map/dft/pallas_call | solution.py:269
  109.5 3.0 %collective-permute-start.19 = (f32[256,128]{1,0:T(8,128)S(1)}, f32[256,128]{1,0:T(8,128)S(1)}, u32[]{:S(2)}, u32[]{:S(2)}) collective-permute-start(f32[256,128]{1,0:T(8,128)S(1)} %get-tuple-element.70), channel_id=1, source_target_pairs={{0,24},{8,16},{16,8},{24,0},{1,25},{9,17},{17,9},{25,1},{2,26},{10... | collective-permute-start | bytes 393224 | tf_op jit(solution)/shard_map/ppermute | solution.py:337
  112.5 2.7 %collective-permute-done.17.refs_5_ = f32[256,128]{1,0:T(8,128)S(1)} collective-permute-done((f32[256,128]{1,0:T(8,128)S(1)}, f32[256,128]{1,0:T(8,128)S(1)}, u32[]{:S(2)}, u32[]{:S(2)}) %collective-permute-start.17) | collective-permute-done | bytes 131104 | tf_op jit(solution)/shard_map/ppermute | solution.py:337
  115.2 6.2 %collective-permute-done.18.refs_6_ = f32[256,128]{1,0:T(8,128)S(1)} collective-permute-done((f32[256,128]{1,0:T(8,128)S(1)}, f32[256,128]{1,0:T(8,128)S(1)}, u32[]{:S(2)}, u32[]{:S(2)}) %collective-permute-start.18) | collective-permute-done | bytes 131104 | tf_op jit(solution)/shard_map/ppermute | solution.py:337
  121.4 3.4 %unpack.1 = f32[512,4,128]{2,1,0:T(4,128)} custom-call(s32[2]{0:T(128)S(1)} %pad_add_fusion.me_ref, f32[256,128]{1,0:T(8,128)S(1)} %get-tuple-element.54.refs_0_, f32[256,128]{1,0:T(8,128)S(1)} %collective-permute-done.7.refs_1_, f32[256,128]{1,0:T(8,128)S(1)} %collective-permute-done.8.refs_2_, f32[256,128]{1,0:T(8,128)S(1)} %collective-permute-done.9.refs_3_, ...), custom_call_target="tpu_custom_call" | custom-call | flops 2359296 | bytes 2097152 | tf_op jit(solution)/shard_map/unpack/pallas_call | solution.py:319
  (62 shorter events, 13.5 us)
Async XLA Ops:
  0.0 1.6 %copy-start = (bf16[1,2,2048,256]{3,2,1,0:T(8,128)(2,1)S(1)}, bf16[1,2,2048,256]{3,2,1,0:T(8,128)(2,1)}, u32[]{:S(2)}) copy-start(bf16[1,2,2048,256]{3,2,1,0:T(8,128)(2,1)} %param.17) | copy-start | bytes 6291460
  2.4 10.7 %copy-start.15 = (s32[4,2]{0,1:T(2,128)S(1)}, s32[4,2]{0,1:T(2,128)}, u32[]{:S(2)}) copy-start(s32[4,2]{0,1:T(2,128)} %param.18) | copy-start | bytes 100
  2.4 10.8 %copy-start.1 = (bf16[1,2,2048,256]{3,2,1,0:T(8,128)(2,1)S(1)}, bf16[1,2,2048,256]{3,2,1,0:T(8,128)(2,1)}, u32[]{:S(2)}) copy-start(bf16[1,2,2048,256]{3,2,1,0:T(8,128)(2,1)} %param.17) | copy-start | bytes 6291460
  2.4 10.8 %copy-start.2 = (bf16[256,128]{1,0:T(8,128)(2,1)S(1)}, bf16[256,128]{1,0:T(8,128)(2,1)}, u32[]{:S(2)}) copy-start(bf16[256,128]{1,0:T(8,128)(2,1)} %constant.25.clone.sel_ref) | copy-start | bytes 196612
  5.1 33.5 %all-to-all-start.1 = ((bf16[32,2,2,32,128]{4,3,2,1,0:T(8,128)(2,1)}), bf16[32,2,2,32,128]{4,3,2,1,0:T(8,128)(2,1)S(1)}, u32[]{:S(2)}, u32[]{:S(2)}) async-start(bf16[32,2,2,32,128]{4,3,2,1,0:T(8,128)(2,1)} %bitcast.5), calls=%async_computation.1 | async-start | bytes 2097152 | tf_op jit(solution)/shard_map/all_to_all | solution.py:361
  12.4 3.6 %copy-start.16 = (u32[32]{0:T(128)S(1)}, u32[32]{0:T(128)}, u32[]{:S(2)}) copy-start(u32[32]{0:T(128)} %constant.37) | copy-start | bytes 388
  16.0 52.5 %copy-start.12 = (f32[512,128]{1,0:T(8,128)S(1)}, f32[512,128]{1,0:T(8,128)}, u32[]{:S(2)}) copy-start(f32[512,128]{1,0:T(8,128)} %constant.27.clone.sin_ref) | copy-start | bytes 786436
  38.6 40.3 %all-to-all-start = ((bf16[32,2,2,32,128]{4,3,2,1,0:T(8,128)(2,1)}), bf16[32,2,2,32,128]{4,3,2,1,0:T(8,128)(2,1)S(1)}, u32[]{:S(2)}, u32[]{:S(2)}) async-start(bf16[32,2,2,32,128]{4,3,2,1,0:T(8,128)(2,1)} %bitcast.4), calls=%async_computation | async-start | bytes 2097152 | tf_op jit(solution)/shard_map/all_to_all | solution.py:361
  44.4 3.8 %collective-permute-start = (f32[4,2,32,128]{3,2,1,0:T(8,128)S(1)}, f32[4,2,32,128]{3,2,1,0:T(8,128)S(1)}, u32[]{:S(2)}, u32[]{:S(2)}) collective-permute-start(f32[4,2,32,128]{3,2,1,0:T(8,128)S(1)} %get-tuple-element.43), channel_id=1, source_target_pairs={{0,1},{1,0},{2,3},{3,2},{4,5},{5,4},{6,7},{7,6},{8,9},{9,8},{10,11... | collective-permute-start | bytes 393224 | tf_op jit(solution)/shard_map/ppermute | solution.py:337
  44.7 12.2 %collective-permute-start.1 = (f32[4,2,32,128]{3,2,1,0:T(8,128)S(1)}, f32[4,2,32,128]{3,2,1,0:T(8,128)S(1)}, u32[]{:S(2)}, u32[]{:S(2)}) collective-permute-start(f32[4,2,32,128]{3,2,1,0:T(8,128)S(1)} %get-tuple-element.44), channel_id=1, source_target_pairs={{0,2},{1,3},{2,0},{3,1},{4,6},{5,7},{6,4},{7,5},{8,10},{9,11},{10,... | collective-permute-start | bytes 393224 | tf_op jit(solution)/shard_map/ppermute | solution.py:337
  46.4 13.0 %collective-permute-start.2 = (f32[4,2,32,128]{3,2,1,0:T(8,128)S(1)}, f32[4,2,32,128]{3,2,1,0:T(8,128)S(1)}, u32[]{:S(2)}, u32[]{:S(2)}) collective-permute-start(f32[4,2,32,128]{3,2,1,0:T(8,128)S(1)} %get-tuple-element.45), channel_id=1, source_target_pairs={{0,3},{1,2},{2,1},{3,0},{4,7},{5,6},{6,5},{7,4},{8,11},{9,10},{10,... | collective-permute-start | bytes 393224 | tf_op jit(solution)/shard_map/ppermute | solution.py:337
  46.4 13.0 %collective-permute-start.3 = (f32[4,2,32,128]{3,2,1,0:T(8,128)S(1)}, f32[4,2,32,128]{3,2,1,0:T(8,128)S(1)}, u32[]{:S(2)}, u32[]{:S(2)}) collective-permute-start(f32[4,2,32,128]{3,2,1,0:T(8,128)S(1)} %get-tuple-element.46), channel_id=1, source_target_pairs={{0,4},{1,5},{2,6},{3,7},{4,0},{5,1},{6,2},{7,3},{8,12},{9,13},{10,... | collective-permute-start | bytes 393224 | tf_op jit(solution)/shard_map/ppermute | solution.py:337
  48.1 11.8 %collective-permute-start.4 = (f32[4,2,32,128]{3,2,1,0:T(8,128)S(1)}, f32[4,2,32,128]{3,2,1,0:T(8,128)S(1)}, u32[]{:S(2)}, u32[]{:S(2)}) collective-permute-start(f32[4,2,32,128]{3,2,1,0:T(8,128)S(1)} %get-tuple-element.47), channel_id=1, source_target_pairs={{0,5},{1,4},{2,7},{3,6},{4,1},{5,0},{6,3},{7,2},{8,13},{9,12},{10,... | collective-permute-start | bytes 393224 | tf_op jit(solution)/shard_map/ppermute | solution.py:337
  48.2 16.4 %collective-permute-start.5 = (f32[4,2,32,128]{3,2,1,0:T(8,128)S(1)}, f32[4,2,32,128]{3,2,1,0:T(8,128)S(1)}, u32[]{:S(2)}, u32[]{:S(2)}) collective-permute-start(f32[4,2,32,128]{3,2,1,0:T(8,128)S(1)} %get-tuple-element.48), channel_id=1, source_target_pairs={{0,6},{1,7},{2,4},{3,5},{4,2},{5,3},{6,0},{7,1},{8,14},{9,15},{10,... | collective-permute-start | bytes 393224 | tf_op jit(solution)/shard_map/ppermute | solution.py:337
  56.9 11.6 %collective-permute-start.6 = (f32[4,2,32,128]{3,2,1,0:T(8,128)S(1)}, f32[4,2,32,128]{3,2,1,0:T(8,128)S(1)}, u32[]{:S(2)}, u32[]{:S(2)}) collective-permute-start(f32[4,2,32,128]{3,2,1,0:T(8,128)S(1)} %get-tuple-element.49), channel_id=1, source_target_pairs={{0,7},{1,6},{2,5},{3,4},{4,3},{5,2},{6,1},{7,0},{8,15},{9,14},{10,... | collective-permute-start | bytes 393224 | tf_op jit(solution)/shard_map/ppermute | solution.py:337
  68.4 1.2 copy-start.4
  73.9 25.9 %copy-start.5 = (bf16[2,512,512]{2,1,0:T(8,128)(2,1)S(1)}, bf16[2,512,512]{2,1,0:T(8,128)(2,1)}, u32[]{:S(2)}) copy-start(bf16[2,512,512]{2,1,0:T(8,128)(2,1)} %constant.29.clone.wlo_ref) | copy-start | bytes 3145732
  73.9 25.9 %copy-start.9 = (bf16[1024,256]{1,0:T(8,128)(2,1)S(1)}, bf16[1024,256]{1,0:T(8,128)(2,1)}, u32[]{:S(2)}) copy-start(bf16[1024,256]{1,0:T(8,128)(2,1)} %constant.31.clone.tlo_ref) | copy-start | bytes 1572868
  81.0 3.8 %collective-permute-start.10 = (f32[4,2,32,128]{3,2,1,0:T(8,128)S(1)}, f32[4,2,32,128]{3,2,1,0:T(8,128)S(1)}, u32[]{:S(2)}, u32[]{:S(2)}) collective-permute-start(f32[4,2,32,128]{3,2,1,0:T(8,128)S(1)} %get-tuple-element.60), channel_id=1, source_target_pairs={{0,1},{1,0},{2,3},{3,2},{4,5},{5,4},{6,7},{7,6},{8,9},{9,8},{10,11... | collective-permute-start | bytes 393224 | tf_op jit(solution)/shard_map/ppermute | solution.py:337
  81.3 6.3 %collective-permute-start.11 = (f32[4,2,32,128]{3,2,1,0:T(8,128)S(1)}, f32[4,2,32,128]{3,2,1,0:T(8,128)S(1)}, u32[]{:S(2)}, u32[]{:S(2)}) collective-permute-start(f32[4,2,32,128]{3,2,1,0:T(8,128)S(1)} %get-tuple-element.61), channel_id=1, source_target_pairs={{0,2},{1,3},{2,0},{3,1},{4,6},{5,7},{6,4},{7,5},{8,10},{9,11},{10,... | collective-permute-start | bytes 393224 | tf_op jit(solution)/shard_map/ppermute | solution.py:337
  82.0 7.2 %collective-permute-start.12 = (f32[4,2,32,128]{3,2,1,0:T(8,128)S(1)}, f32[4,2,32,128]{3,2,1,0:T(8,128)S(1)}, u32[]{:S(2)}, u32[]{:S(2)}) collective-permute-start(f32[4,2,32,128]{3,2,1,0:T(8,128)S(1)} %get-tuple-element.62), channel_id=1, source_target_pairs={{0,3},{1,2},{2,1},{3,0},{4,7},{5,6},{6,5},{7,4},{8,11},{9,10},{10,... | collective-permute-start | bytes 393224 | tf_op jit(solution)/shard_map/ppermute | solution.py:337
  82.9 7.6 %collective-permute-start.13 = (f32[4,2,32,128]{3,2,1,0:T(8,128)S(1)}, f32[4,2,32,128]{3,2,1,0:T(8,128)S(1)}, u32[]{:S(2)}, u32[]{:S(2)}) collective-permute-start(f32[4,2,32,128]{3,2,1,0:T(8,128)S(1)} %get-tuple-element.63), channel_id=1, source_target_pairs={{0,4},{1,5},{2,6},{3,7},{4,0},{5,1},{6,2},{7,3},{8,12},{9,13},{10,... | collective-permute-start | bytes 393224 | tf_op jit(solution)/shard_map/ppermute | solution.py:337
  83.7 13.1 %collective-permute-start.14 = (f32[4,2,32,128]{3,2,1,0:T(8,128)S(1)}, f32[4,2,32,128]{3,2,1,0:T(8,128)S(1)}, u32[]{:S(2)}, u32[]{:S(2)}) collective-permute-start(f32[4,2,32,128]{3,2,1,0:T(8,128)S(1)} %get-tuple-element.64), channel_id=1, source_target_pairs={{0,5},{1,4},{2,7},{3,6},{4,1},{5,0},{6,3},{7,2},{8,13},{9,12},{10,... | collective-permute-start | bytes 393224 | tf_op jit(solution)/shard_map/ppermute | solution.py:337
  84.8 15.0 %collective-permute-start.15 = (f32[4,2,32,128]{3,2,1,0:T(8,128)S(1)}, f32[4,2,32,128]{3,2,1,0:T(8,128)S(1)}, u32[]{:S(2)}, u32[]{:S(2)}) collective-permute-start(f32[4,2,32,128]{3,2,1,0:T(8,128)S(1)} %get-tuple-element.65), channel_id=1, source_target_pairs={{0,6},{1,7},{2,4},{3,5},{4,2},{5,3},{6,0},{7,1},{8,14},{9,15},{10,... | collective-permute-start | bytes 393224 | tf_op jit(solution)/shard_map/ppermute | solution.py:337
  87.6 12.2 %collective-permute-start.16 = (f32[4,2,32,128]{3,2,1,0:T(8,128)S(1)}, f32[4,2,32,128]{3,2,1,0:T(8,128)S(1)}, u32[]{:S(2)}, u32[]{:S(2)}) collective-permute-start(f32[4,2,32,128]{3,2,1,0:T(8,128)S(1)} %get-tuple-element.66), channel_id=1, source_target_pairs={{0,7},{1,6},{2,5},{3,4},{4,3},{5,2},{6,1},{7,0},{8,15},{9,14},{10,... | collective-permute-start | bytes 393224 | tf_op jit(solution)/shard_map/ppermute | solution.py:337
  89.2 20.3 %collective-permute-start.7 = (f32[256,128]{1,0:T(8,128)S(1)}, f32[256,128]{1,0:T(8,128)S(1)}, u32[]{:S(2)}, u32[]{:S(2)}) collective-permute-start(f32[256,128]{1,0:T(8,128)S(1)} %get-tuple-element.55), channel_id=1, source_target_pairs={{0,8},{8,0},{16,24},{24,16},{1,9},{9,1},{17,25},{25,17},{2,10},{10... | collective-permute-start | bytes 393224 | tf_op jit(solution)/shard_map/ppermute | solution.py:337
  90.5 22.0 %collective-permute-start.8 = (f32[256,128]{1,0:T(8,128)S(1)}, f32[256,128]{1,0:T(8,128)S(1)}, u32[]{:S(2)}, u32[]{:S(2)}) collective-permute-start(f32[256,128]{1,0:T(8,128)S(1)} %get-tuple-element.56), channel_id=1, source_target_pairs={{0,16},{8,24},{16,0},{24,8},{1,17},{9,25},{17,1},{25,9},{2,18},{10... | collective-permute-start | bytes 393224 | tf_op jit(solution)/shard_map/ppermute | solution.py:337
  96.8 15.7 %collective-permute-start.9 = (f32[256,128]{1,0:T(8,128)S(1)}, f32[256,128]{1,0:T(8,128)S(1)}, u32[]{:S(2)}, u32[]{:S(2)}) collective-permute-start(f32[256,128]{1,0:T(8,128)S(1)} %get-tuple-element.57), channel_id=1, source_target_pairs={{0,24},{8,16},{16,8},{24,0},{1,25},{9,17},{17,9},{25,1},{2,26},{10... | collective-permute-start | bytes 393224 | tf_op jit(solution)/shard_map/ppermute | solution.py:337
  99.8 1.2 copy-start.7
  108.1 7.1 %collective-permute-start.17 = (f32[256,128]{1,0:T(8,128)S(1)}, f32[256,128]{1,0:T(8,128)S(1)}, u32[]{:S(2)}, u32[]{:S(2)}) collective-permute-start(f32[256,128]{1,0:T(8,128)S(1)} %get-tuple-element.68), channel_id=1, source_target_pairs={{0,8},{8,0},{16,24},{24,16},{1,9},{9,1},{17,25},{25,17},{2,10},{10... | collective-permute-start | bytes 393224 | tf_op jit(solution)/shard_map/ppermute | solution.py:337
  108.5 12.9 %collective-permute-start.18 = (f32[256,128]{1,0:T(8,128)S(1)}, f32[256,128]{1,0:T(8,128)S(1)}, u32[]{:S(2)}, u32[]{:S(2)}) collective-permute-start(f32[256,128]{1,0:T(8,128)S(1)} %get-tuple-element.69), channel_id=1, source_target_pairs={{0,16},{8,24},{16,0},{24,8},{1,17},{9,25},{17,1},{25,9},{2,18},{10... | collective-permute-start | bytes 393224 | tf_op jit(solution)/shard_map/ppermute | solution.py:337
  109.5 11.8 %collective-permute-start.19 = (f32[256,128]{1,0:T(8,128)S(1)}, f32[256,128]{1,0:T(8,128)S(1)}, u32[]{:S(2)}, u32[]{:S(2)}) collective-permute-start(f32[256,128]{1,0:T(8,128)S(1)} %get-tuple-element.70), channel_id=1, source_target_pairs={{0,24},{8,16},{16,8},{24,0},{1,25},{9,17},{17,9},{25,1},{2,26},{10... | collective-permute-start | bytes 393224 | tf_op jit(solution)/shard_map/ppermute | solution.py:337
  (7 other events, 7.1 us)

commit v3 on v2

v3 whole, which is shorter than its diff:
```python
import functools
import math

import jax
import jax.numpy as jnp
import numpy as np
from jax import lax
from jax.experimental import pallas as pl
from jax.experimental.pallas import tpu as pltpu
from jax.sharding import PartitionSpec as P

TILE = 128
LAG = 2048
GROUPS = 8
SMALL = pl.CostEstimate(flops=1, bytes_accessed=1, transcendentals=0)
LARGE = pl.CostEstimate(flops=10**11, bytes_accessed=1, transcendentals=0)
CC = TILE // GROUPS


def lane_groups(shape):
    return lax.broadcasted_iota(jnp.int32, shape, len(shape) - 1) // CC


def shift_groups(x, by):
    return pltpu.roll(x, (by * CC) % TILE, x.ndim - 1)


def transpose_groups(vectors):
    v = list(vectors)
    grp = lane_groups(v[0].shape)
    for bit in (4, 2, 1):
        low = (grp & bit) == 0
        for i in range(GROUPS):
            if i & bit:
                continue
            a, b = v[i], v[i | bit]
            v[i] = jnp.where(low, a, shift_groups(b, bit))
            v[i | bit] = jnp.where(low, shift_groups(a, -bit), b)
    return v


def reduce_groups(vectors):
    v = list(vectors)
    grp = lane_groups(v[0].shape)
    low = (grp & 4) == 0
    v = [
        jnp.where(low, v[i], v[i + 4])
        + shift_groups(jnp.where(low, v[i + 4], v[i]), 4)
        for i in range(4)
    ]
    for bit in (2, 1):
        low = (grp & bit) == 0
        v = [
            jnp.where(low, v[i], v[i + bit])
            + jnp.where(low, shift_groups(v[i], -bit), shift_groups(v[i + bit], bit))
            for i in range(bit)
        ]
    return v[0]


def selection(n_seg, chunk, chans):
    wide = chans // TILE * n_seg * CC
    row = lax.broadcasted_iota(jnp.int32, (chans, wide), 0)
    col = lax.broadcasted_iota(jnp.int32, (chans, wide), 1)
    group = col // CC
    want = (
        group // n_seg * TILE
        + group % n_seg * (TILE // n_seg)
        + chunk * CC
        + col % CC
    )
    return (row == want).astype(jnp.bfloat16)


def pack_band(n_seg, band, sel, buf_ref, store):
    rows = band.shape[0] // GROUPS
    for part in range(sel.shape[1] // TILE):
        lanes = slice(part * TILE, (part + 1) * TILE)
        buf_ref[...] = jnp.dot(
            band, sel[:, lanes], preferred_element_type=jnp.float32
        )
        v = [buf_ref[pl.ds(fb, rows, stride=GROUPS), :] for fb in range(GROUPS)]
        v = transpose_groups(v)
        for g in range(GROUPS):
            t, z = divmod(part * GROUPS + g, n_seg)
            store(t, z, v[g].astype(jnp.bfloat16))


def pack_kernel(n_seg, chunk, x_ref, out_ref, buf_ref):
    sel = selection(n_seg, chunk, x_ref.shape[2])
    for ri in range(2):

        def store(t, z, value, ri=ri):
            out_ref[z, 0, t, ri] = value

        pack_band(n_seg, x_ref[ri], sel, buf_ref.at[ri], store)


def pack(x, chunk, n_seg, n_pair):
    _, freq, chans = x.shape
    tiles = chans // TILE
    band = freq // n_pair
    rows = band // GROUPS
    return pl.pallas_call(
        functools.partial(pack_kernel, n_seg, chunk),
        out_shape=jax.ShapeDtypeStruct(
            (n_seg, n_pair, tiles, 2, rows, TILE), jnp.bfloat16
        ),
        grid=(n_pair,),
        in_specs=[pl.BlockSpec((2, band, chans), lambda p: (0, p, 0))],
        out_specs=pl.BlockSpec(
            (n_seg, 1, tiles, 2, rows, TILE), lambda p: (0, p, 0, 0, 0, 0)
        ),
        scratch_shapes=[pltpu.VMEM((2, band, TILE), jnp.float32)],
        name="pack",
        cost_estimate=SMALL,
    )(x)


def pack_near_kernel(n_seg, n_pair, chunk, me_ref, x_ref, *refs):
    outs, buf_ref = refs[:-1], refs[-1]
    band = x_ref.shape[1] // n_pair
    sel = selection(n_seg, chunk, x_ref.shape[2])
    for k in range(n_pair):
        p = jnp.bitwise_xor(me_ref[1], k)
        at = pl.ds(pl.multiple_of(p * band, band), band)
        for ri in range(2):

            def store(t, z, value, ri=ri, k=k):
                outs[k // 2][k % 2, z, t, ri] = value

            pack_band(n_seg, x_ref[ri, at, :], sel, buf_ref.at[ri], store)


def pack_near(me, x, chunk, n_seg, n_pair):
    _, freq, chans = x.shape
    tiles = chans // TILE
    band = freq // n_pair
    rows = band // GROUPS
    shape = (2, n_seg, tiles, 2, rows, TILE)
    vmem = pl.BlockSpec(memory_space=pltpu.VMEM)
    return pl.pallas_call(
        functools.partial(pack_near_kernel, n_seg, n_pair, chunk),
        out_shape=[jax.ShapeDtypeStruct(shape, jnp.bfloat16)] * (n_pair // 2),
        in_specs=[pl.BlockSpec(memory_space=pltpu.SMEM), vmem],
        out_specs=[vmem] * (n_pair // 2),
        scratch_shapes=[pltpu.VMEM((2, band, TILE), jnp.float32)],
        name="pack_near",
        cost_estimate=SMALL,
    )(me, x)


def regroup_kernel(n_seg, n_pair, me_ref, *refs):
    ins, outs = refs[:n_pair], refs[n_pair:]
    for kz in range(n_seg):
        z = jnp.bitwise_xor(me_ref[0], kz)
        for k in range(n_pair):
            p = jnp.bitwise_xor(me_ref[1], k)
            outs[kz][p] = ins[k % 2 * (n_pair // 2) + k // 2][k % 2, z]


def regroup(me, blocks, n_seg, n_pair):
    shape = (n_pair,) + blocks[0].shape[2:]
    vmem = pl.BlockSpec(memory_space=pltpu.VMEM)
    return pl.pallas_call(
        functools.partial(regroup_kernel, n_seg, n_pair),
        out_shape=[jax.ShapeDtypeStruct(shape, jnp.bfloat16)] * n_seg,
        in_specs=[pl.BlockSpec(memory_space=pltpu.SMEM)] + [vmem] * n_pair,
        out_specs=[vmem] * n_seg,
        name="regroup",
        cost_estimate=SMALL,
    )(me, *blocks)


def stack_kernel(n_seg, n_pair, most, n_specs, me_ref, table_ref, *refs):
    specs, out_refs = refs[:n_specs], refs[n_specs:]
    near = len(out_refs) > 1
    parts = [r.at[g] for r in specs for g in range(r.shape[0])]
    inv = 1.0 / float(n_seg * n_seg)
    for k in range(n_pair):
        owner = jnp.bitwise_xor(me_ref[1], k) if near else k
        count = table_ref[owner, 2 * most]
        out_ref = out_refs[k // 2].at[k % 2] if near else out_refs[0].at[k]

        def one(s, _):
            src = table_ref[owner, 2 * s]
            rcv = table_ref[owner, 2 * s + 1]

            @pl.when(s < count)
            def _():
                lr = li = pr = pi = None
                for g in range(n_seg):
                    a0 = parts[g][src, 0].astype(jnp.float32)
                    a1 = parts[g][src, 1].astype(jnp.float32)
                    b0 = parts[g][rcv, 0].astype(jnp.float32)
                    b1 = parts[g][rcv, 1].astype(jnp.float32)
                    cr = a0 * b0 + a1 * b1
                    ci = a1 * b0 - a0 * b1
                    m = lax.rsqrt(cr * cr + ci * ci + 1.0)
                    if g == 0:
                        lr, li, pr, pi = cr, ci, cr * m, ci * m
                    else:
                        lr, li, pr, pi = lr + cr, li + ci, pr + cr * m, pi + ci * m
                w = (pr * pr + pi * pi) * inv
                out_ref[s, 0] = lr * w
                out_ref[s, 1] = li * w

            @pl.when(s >= count)
            def _():
                out_ref[s] = jnp.zeros(out_ref.shape[1:], jnp.float32)

            return 0

        lax.fori_loop(0, most, one, 0)


def stacks(me, table, specs, near, n_seg, n_pair, most):
    rows = specs[0].shape[3]
    arrays = n_pair // 2 if near else 1
    shape = (n_pair // arrays, most, 2, rows, TILE)
    smem = pl.BlockSpec(memory_space=pltpu.SMEM)
    vmem = pl.BlockSpec(memory_space=pltpu.VMEM)
    return pl.pallas_call(
        functools.partial(stack_kernel, n_seg, n_pair, most, len(specs)),
        out_shape=[jax.ShapeDtypeStruct(shape, jnp.float32)] * arrays,
        in_specs=[smem, smem] + [vmem] * len(specs),
        out_specs=[vmem] * arrays,
        name="stack",
        cost_estimate=LARGE if near else SMALL,
    )(me, table, *specs)


def dft_kernel(n_seg, n_pair, most, n_blocks, me_ref, *refs):
    table_refs, ins = refs[:6], refs[6 : 6 + n_blocks]
    outs = refs[6 + n_blocks : 6 + n_blocks + n_seg]
    held = refs[6 + n_blocks + n_seg : 12 + n_blocks + n_seg]
    s32, shi, slo, y, zhi, zlo, sums, parts, sems = refs[12 + n_blocks + n_seg :]
    whi_ref, wlo_ref, cos_ref, sin_ref, thi_ref, tlo_ref = held
    copies = [
        pltpu.make_async_copy(src, to, sems.at[i])
        for i, (src, to) in enumerate(zip(table_refs, held))
    ]
    for copy in copies:
        copy.start()
    rows = ins[0].shape[3]
    half_h = whi_ref.shape[1] // 2
    wide = most * TILE
    for k in range(n_pair):
        if n_blocks == 1:
            band, src = k, ins[0].at[k]
        else:
            band = jnp.bitwise_xor(me_ref[1], k)
            src = ins[k % 2 * (n_pair // 2) + k // 2].at[k % 2]
        at = pl.ds(pl.multiple_of(band * rows, rows), rows)
        for s in range(most):
            for ri in range(2):
                s32[ri, at, s * TILE : (s + 1) * TILE] = src[s, ri]
    for ri in range(2):
        full = s32[ri]
        hi = full.astype(jnp.bfloat16)
        lo = (full - hi.astype(jnp.float32)).astype(jnp.bfloat16)
        own = slice(ri * wide, (ri + 1) * wide)
        other = slice((1 - ri) * wide, (2 - ri) * wide)
        for to, part in ((shi, hi), (slo, lo)):
            to[:half_h, own] = part
            to[half_h:, other] = part if ri == 0 else -part
    copies[0].wait()
    copies[1].wait()
    for ri in range(2):
        n = slice(ri * wide, (ri + 1) * wide)
        y[ri] = (
            jnp.dot(wlo_ref[...], shi[:, n], preferred_element_type=jnp.float32)
            + jnp.dot(whi_ref[...], slo[:, n], preferred_element_type=jnp.float32)
        ) + jnp.dot(whi_ref[...], shi[:, n], preferred_element_type=jnp.float32)
    copies[2].wait()
    copies[3].wait()
    period = y.shape[1]
    step_rows = 64
    for b in range(period // step_rows):
        at = slice(b * step_rows, (b + 1) * step_rows)
        c = cos_ref[at, :]
        d = sin_ref[at, :]
        for s in range(most):
            lanes = slice(s * TILE, (s + 1) * TILE)
            yr = y[0, at, lanes]
            yi = y[1, at, lanes]
            for ri, z in enumerate((c * yr - d * yi, d * yr + c * yi)):
                to = slice((ri * most + s) * TILE, (ri * most + s + 1) * TILE)
                hi = z.astype(jnp.bfloat16)
                zhi[at, to] = hi
                zlo[at, to] = (z - hi.astype(jnp.float32)).astype(jnp.bfloat16)
    copies[4].wait()
    copies[5].wait()
    sums[...] = (
        jnp.dot(zhi[...], tlo_ref[...], preferred_element_type=jnp.float32)
        + jnp.dot(zlo[...], thi_ref[...], preferred_element_type=jnp.float32)
    ) + jnp.dot(zhi[...], thi_ref[...], preferred_element_type=jnp.float32)
    half = outs[0].shape[0]
    first = lax.broadcasted_iota(jnp.int32, (half, TILE), 1) < TILE // 2
    for dest in range(n_seg):
        lag = dest * 2 * half
        r, l0 = lag // period, lag % period
        col = slice(r // 2 * TILE, (r // 2 + 1) * TILE)
        low = sums[l0 : l0 + half, col]
        high = sums[l0 + half : l0 + 2 * half, col]
        if r % 2 == 0:
            high = pltpu.roll(high, TILE // 2, 1)
        else:
            low = pltpu.roll(low, TILE // 2, 1)
        parts[dest] = jnp.where(first, low, high)
    for k in range(n_seg):
        outs[k][...] = parts[jnp.bitwise_xor(me_ref[0], k)]


def turns_kernel(most, turns, shift, hi_ref, lo_ref):
    shape = (most * TILE, turns * most * CC)
    row = lax.broadcasted_iota(jnp.int32, shape, 0)
    col = lax.broadcasted_iota(jnp.int32, shape, 1)
    same = (row // TILE == col // CC % most) & (row % CC == col % CC)
    eighths = (col // (most * CC) - shift) * (row // CC % GROUPS)
    diagonal = jnp.float32(math.sqrt(0.5))
    for ri in range(2):
        e = jnp.bitwise_and(eighths + 2 * ri, 7)
        size = jnp.where(e % 4 == 2, 0.0, jnp.where(e % 2 == 0, 1.0, diagonal))
        t = jnp.where(same, jnp.where((e > 2) & (e < 6), -size, size), 0.0)
        at = slice(ri * most * TILE, (ri + 1) * most * TILE)
        hi = t.astype(jnp.bfloat16)
        hi_ref[at, :] = hi
        lo_ref[at, :] = (t - hi.astype(jnp.float32)).astype(jnp.bfloat16)


def make_tables(freq, most):
    h = freq // GROUPS
    period = 2 * h
    turns = LAG // period
    angle = np.arange(period)[:, None] * np.arange(h)[None, :] % period
    angle = angle * (2.0 * math.pi / period)
    w = np.concatenate([np.cos(angle), np.sin(angle)], 1).astype(np.float32)
    whi = w.astype(jnp.bfloat16)
    wlo = (w - whi.astype(np.float32)).astype(jnp.bfloat16)
    fb = np.arange(TILE) // CC
    phase = ((np.arange(period)[:, None] * fb[None, :]) % (2 * freq)) * (math.pi / freq)
    scale = 1.0 / math.sqrt(freq)
    cos = (np.cos(phase) * scale).astype(np.float32)
    sin = (np.sin(phase) * scale).astype(np.float32)
    shape = (2 * most * TILE, turns * most * CC)
    pair = pl.pallas_call(
        functools.partial(turns_kernel, most, turns, LAG // 2 // period),
        out_shape=[jax.ShapeDtypeStruct(shape, jnp.bfloat16)] * 2,
        out_specs=[pl.BlockSpec(memory_space=pltpu.VMEM)] * 2,
        name="turns",
        cost_estimate=SMALL,
    )()
    return [jnp.asarray(c) for c in (whi, wlo, cos, sin)], list(pair)


def dft(me, tables, blocks, freq, n_seg, n_pair, most):
    period = 2 * (freq // GROUPS)
    smem = pl.BlockSpec(memory_space=pltpu.SMEM)
    vmem = pl.BlockSpec(memory_space=pltpu.VMEM)
    hbm = pl.BlockSpec(memory_space=pltpu.HBM)
    half = LAG // n_seg // 2
    wide = most * TILE
    return pl.pallas_call(
        functools.partial(dft_kernel, n_seg, n_pair, most, len(blocks)),
        out_shape=[jax.ShapeDtypeStruct((half, TILE), jnp.float32)] * n_seg,
        in_specs=[smem] + [hbm] * 6 + [vmem] * len(blocks),
        out_specs=[vmem] * n_seg,
        scratch_shapes=[pltpu.VMEM(t.shape, t.dtype) for t in tables]
        + [
            pltpu.VMEM((2, period // 2, wide), jnp.float32),
            pltpu.VMEM((period, 2 * wide), jnp.bfloat16),
            pltpu.VMEM((period, 2 * wide), jnp.bfloat16),
            pltpu.VMEM((2, period, wide), jnp.float32),
            pltpu.VMEM((period, 2 * wide), jnp.bfloat16),
            pltpu.VMEM((period, 2 * wide), jnp.bfloat16),
            pltpu.VMEM((period, LAG // period * most * CC), jnp.float32),
            pltpu.VMEM((n_seg, half, TILE), jnp.float32),
            pltpu.SemaphoreType.DMA((6,)),
        ],
        name="dft",
        compiler_params=pltpu.CompilerParams(vmem_limit_bytes=24 << 20),
        cost_estimate=SMALL,
    )(me, *tables, *blocks)


def unpack_kernel(n_seg, chunks, most, me_ref, *refs):
    ins = refs[: n_seg * chunks]
    out_ref, buf = refs[n_seg * chunks :]
    half = ins[0].shape[0]
    for k in range(n_seg):
        z = jnp.bitwise_xor(me_ref[0], k)
        for ch in range(chunks):
            buf[z * chunks + ch] = ins[ch * n_seg + k][...]
    step_rows = 16

    def one(b, _):
        at = pl.multiple_of(b * step_rows, step_rows)
        v = transpose_groups([buf[i, pl.ds(at, step_rows), :] for i in range(GROUPS)])
        for h in range(2):
            for s in range(most):
                out_ref[pl.ds(h * half + at, step_rows), s, :] = v[h * most + s]
        return 0

    lax.fori_loop(0, half // step_rows, one, 0, unroll=4)


def unpack(me, parts, n_seg, chunks, most):
    half = parts[0].shape[0]
    smem = pl.BlockSpec(memory_space=pltpu.SMEM)
    vmem = pl.BlockSpec(memory_space=pltpu.VMEM)
    return pl.pallas_call(
        functools.partial(unpack_kernel, n_seg, chunks, most),
        out_shape=jax.ShapeDtypeStruct((2 * half, most, TILE), jnp.float32),
        in_specs=[smem] + [vmem] * len(parts),
        out_specs=vmem,
        scratch_shapes=[pltpu.VMEM((GROUPS, half, TILE), jnp.float32)],
        name="unpack",
        compiler_params=pltpu.CompilerParams(vmem_limit_bytes=12 << 20),
        cost_estimate=SMALL,
    )(me, *parts)


def exchange(blocks, axis, size):
    return [blocks[0]] + [
        lax.ppermute(blocks[k], axis, [(i, i ^ k) for i in range(size)])
        for k in range(1, size)
    ]


def exchange_plane(blocks, n_pair):
    direct = [blocks[0]] + [
        lax.ppermute(blocks[k], "pair", [(i, i ^ (2 * k)) for i in range(n_pair)])
        for k in range(1, n_pair // 2)
    ]
    swap = [(i, i ^ 1) for i in range(n_pair)]
    return direct + [lax.ppermute(d, "pair", swap) for d in direct]


def body(spectra, pair_lists, pair_counts):
    n_pair = lax.axis_size("pair")
    n_seg = lax.axis_size("seg")
    freq = spectra.shape[2]
    most = pair_lists.shape[0]
    tiles = spectra.shape[3] // TILE
    chunks = GROUPS // n_seg
    rows = freq // n_pair // GROUPS
    me = jnp.stack([lax.axis_index("seg"), lax.axis_index("pair")]).astype(jnp.int32)
    x = spectra.reshape(2, freq, spectra.shape[3])
    lists = jnp.concatenate([pair_lists.reshape(-1), pair_counts])
    first = pack(x, 0, n_seg, n_pair)
    near = [pack_near(me, x, chunk, n_seg, n_pair) for chunk in range(1, chunks)]
    if near:
        lists, near[0] = lax.optimization_barrier((lists, near[0]))
    table = lax.all_gather(lists, "pair", axis=0)
    consts, turns = make_tables(freq, most)
    spec = lax.all_to_all(
        first.reshape(n_seg * n_pair, tiles, 2, rows, TILE),
        ("seg", "pair"),
        split_axis=0,
        concat_axis=0,
        tiled=True,
    ).reshape(n_seg, n_pair * tiles, 2, rows, TILE)
    far = [regroup(me, exchange_plane(n, n_pair), n_seg, n_pair) for n in near]
    spec, table, turns, _ = lax.optimization_barrier((spec, table, turns, far))
    tables = consts + turns
    blocks = stacks(me, table, [spec], False, n_seg, n_pair, most)
    blocks = [
        lax.all_to_all(blocks[0], "pair", split_axis=0, concat_axis=0, tiled=True)
    ]
    done = []
    for f in far:
        got = [
            g.reshape(1, n_pair * tiles, 2, rows, TILE)
            for g in exchange(f, "seg", n_seg)
        ]
        after = stacks(me, table, got, True, n_seg, n_pair, most)
        blocks, _ = lax.optimization_barrier((blocks, after))
        after = exchange_plane(after, n_pair)
        lags = dft(me, tables, blocks, freq, n_seg, n_pair, most)
        done += exchange(lags, "seg", n_seg)
        blocks, _ = lax.optimization_barrier((after, lags))
    lags = dft(me, tables, blocks, freq, n_seg, n_pair, most)
    done += exchange(lags, "seg", n_seg)
    return unpack(me, done, n_seg, chunks, most)


def solution(mesh):
    return jax.shard_map(
        body,
        mesh=mesh,
        in_specs=(P("seg", None, None, "pair"), P("pair", None), P("pair")),
        out_specs=P("seg", "pair", None),
        check_vma=False,
    )
```

time: 125 us -> 133 us (1.064)
  Pallas kernels: 22.9 us -> 39.6 us
  local copies, waits for them, and re-layouts: 12.2 us -> 5.48 us
  blocking collectives: 8.42 us -> 6.49 us
  starting transfers between devices: 33.8 us -> 32.3 us
    ppermute x0 -> x14, waiting for transfers between devices: none -> 37.3 us  [the longest x6 35.9 us: exchange_plane(): lax.ppermute(blocks[k], 'pair', [(i, i ^ 2 * k) for i in range(n_pair)])]
    ppermute x20 -> x9, waiting for transfers between devices: 33.2 us -> 9.28 us  [exchange(): lax.ppermute(blocks[k], axis, [(i, i ^ k) for i in range(size)])]
    pallas_call x6 -> x8, Pallas kernels: 19.5 us -> 36.2 us  [the longest x2 13 us: dft(): pl.pallas_call(functools.partial(dft_kernel, n_seg, n_pair, most, len(blo...]
    all_to_all x2, waiting for transfers between devices: 12.7 us -> 0.01 us  [the longest x1 0.01 us: body(): lax.all_to_all(first.reshape(n_seg * n_pair, tiles, 2, rows, TILE), ('seg...]
    ppermute x20 -> x9, starting transfers between devices: 22.9 us -> 13.3 us  [exchange(): lax.ppermute(blocks[k], axis, [(i, i ^ k) for i in range(size)])]
    ppermute x0 -> x14, starting transfers between devices: none -> 8 us  [the longest x6 6.98 us: exchange_plane(): lax.ppermute(blocks[k], 'pair', [(i, i ^ 2 * k) for i in range(n_pair)])]
    unnamed x38 -> x46, local copies, waits for them, and re-layouts: 12 us -> 4.73 us
    unnamed x1, blocking collectives: 8.42 us -> 6.49 us
  transfers between devices with their start and end apart: 22 -> 25, of which waited for: 11 -> 8; matrix products, arithmetic and copies ran while one was open for 1% -> 2% of each run, Pallas kernels for 12% -> 22%
where the time goes in v3:
time: 133 us
  waiting for transfers between devices  46.6 us (35%)
  Pallas kernels  39.6 us (30%)
  starting transfers between devices  32.3 us (24%)
  blocking collectives  6.49 us (5%)
  local copies, waits for them, and re-layouts  5.48 us (4%)
  between operations  1.55 us (1%)
    ppermute x6, waiting for transfers between devices, exchange_plane(): lax.ppermute(blocks[k], 'pair', [(i, i ^ 2 * k) for i in range(n_pair)])  35.9 us
    ppermute x9, starting transfers between devices, exchange(): lax.ppermute(blocks[k], axis, [(i, i ^ k) for i in range(size)])  13.3 us
    pallas_call x2, Pallas kernels, dft(): pl.pallas_call(functools.partial(dft_kernel, n_seg, n_pair, most, len(blo...  13 us
    ppermute x9, waiting for transfers between devices, exchange(): lax.ppermute(blocks[k], axis, [(i, i ^ k) for i in range(size)])  9.28 us
    pallas_call x2, Pallas kernels, stacks(): pl.pallas_call(functools.partial(stack_kernel, n_seg, n_pair, most, len(s...  7.46 us
    all_to_all x1, starting transfers between devices, body(): lax.all_to_all(first.reshape(n_seg * n_pair, tiles, 2, rows, TILE), ('seg...  7.3 us
    pallas_call x1, Pallas kernels, pack(): pl.pallas_call(functools.partial(pack_kernel, n_seg, chunk), out_shape=ja...  7.24 us
    ppermute x6, starting transfers between devices, exchange_plane(): lax.ppermute(blocks[k], 'pair', [(i, i ^ 2 * k) for i in range(n_pair)])  6.98 us
  transfers between devices with their start and end apart: 25, of which 8 were waited for; matrix products, arithmetic and copies ran while one was open for 2% of the time, Pallas kernels for 22%

profile of v3, /device:TPU:0, one launch (start us, length us, event | category | flops | bytes accessed | tf_op | source)
XLA Modules:
  0.0 132.8 jit_solution(11772631743058493064)
XLA Ops:
  0.0 7.2 %pack.1 = bf16[4,8,2,2,32,128]{5,4,3,2,1,0:T(8,128)(2,1)} custom-call(bf16[2,2048,256]{2,1,0:T(8,128)(2,1)} %bitcast.10), custom_call_target="tpu_custom_call" | custom-call | flops 1 | bytes 1 | tf_op jit(solution)/shard_map/pack/pallas_call | solution.py:104
  7.2 7.3 %all-to-all-start = ((bf16[32,2,2,32,128]{4,3,2,1,0:T(8,128)(2,1)}), bf16[32,2,2,32,128]{4,3,2,1,0:T(8,128)(2,1)S(1)}, u32[]{:S(2)}, u32[]{:S(2)}) async-start(bf16[32,2,2,32,128]{4,3,2,1,0:T(8,128)(2,1)} %bitcast.12), calls=%async_computation | async-start | bytes 2097152 | tf_op jit(solution)/shard_map/all_to_all | solution.py:457
  15.2 3.7 %pack_near.1 = (bf16[2,4,2,2,32,128]{5,4,3,2,1,0:T(8,128)(2,1)}, bf16[2,4,2,2,32,128]{5,4,3,2,1,0:T(8,128)(2,1)}, bf16[2,4,2,2,32,128]{5,4,3,2,1,0:T(8,128)(2,1)}, bf16[2,4,2,2,32,128]{5,4,3,2,1,0:T(8,128)(2,1)}) custom-call(s32[2]{0:T(128)} %pad_add_fusion.me_ref, bf16[2,2048,256]{2,1,0:T(8,128)(2,1)} %bitcast.11), custom_call_target="tpu_custom_call" | custom-call | flops 1 | bytes 1 | tf_op jit(solution)/shard_map/pack_near/pallas_call | solution.py:142
  19.9 1.8 %collective-permute-start = (bf16[2,4,2,2,32,128]{5,4,3,2,1,0:T(8,128)(2,1)}, bf16[2,4,2,2,32,128]{5,4,3,2,1,0:T(8,128)(2,1)S(1)}, u32[]{:S(2)}, u32[]{:S(2)}) collective-permute-start(bf16[2,4,2,2,32,128]{5,4,3,2,1,0:T(8,128)(2,1)} %get-tuple-element.53), channel_id=1, source_target_pairs={{0,2},{1,3},{2,0},{3,1},{4,6},{5,7},{6,4},{7,5},{8,10},{9,11},{10,... | collective-permute-start | bytes 786440 | tf_op jit(solution)/shard_map/ppermute | solution.py:433
  21.6 1.5 %collective-permute-start.1 = (bf16[2,4,2,2,32,128]{5,4,3,2,1,0:T(8,128)(2,1)}, bf16[2,4,2,2,32,128]{5,4,3,2,1,0:T(8,128)(2,1)S(1)}, u32[]{:S(2)}, u32[]{:S(2)}) collective-permute-start(bf16[2,4,2,2,32,128]{5,4,3,2,1,0:T(8,128)(2,1)} %get-tuple-element.54), channel_id=1, source_target_pairs={{0,4},{1,5},{2,6},{3,7},{4,0},{5,1},{6,2},{7,3},{8,12},{9,13},{10,... | collective-permute-start | bytes 786440 | tf_op jit(solution)/shard_map/ppermute | solution.py:433
  23.4 10.1 %collective-permute-done.refs_1_ = bf16[2,4,2,2,32,128]{5,4,3,2,1,0:T(8,128)(2,1)S(1)} collective-permute-done((bf16[2,4,2,2,32,128]{5,4,3,2,1,0:T(8,128)(2,1)}, bf16[2,4,2,2,32,128]{5,4,3,2,1,0:T(8,128)(2,1)S(1)}, u32[]{:S(2)}, u32[]{:S(2)}) %collective-permute-start) | collective-permute-done | bytes 262176 | tf_op jit(solution)/shard_map/ppermute | solution.py:433
  33.4 8.0 %collective-permute-done.1.refs_2_ = bf16[2,4,2,2,32,128]{5,4,3,2,1,0:T(8,128)(2,1)S(1)} collective-permute-done((bf16[2,4,2,2,32,128]{5,4,3,2,1,0:T(8,128)(2,1)}, bf16[2,4,2,2,32,128]{5,4,3,2,1,0:T(8,128)(2,1)S(1)}, u32[]{:S(2)}, u32[]{:S(2)}) %collective-permute-start.1) | collective-permute-done | bytes 262176 | tf_op jit(solution)/shard_map/ppermute | solution.py:433
  42.0 1.0 collective-permute-done.5.refs_6_
  44.4 2.5 %regroup.1 = (bf16[8,2,2,32,128]{4,3,2,1,0:T(8,128)(2,1)}, bf16[8,2,2,32,128]{4,3,2,1,0:T(8,128)(2,1)}, bf16[8,2,2,32,128]{4,3,2,1,0:T(8,128)(2,1)}, bf16[8,2,2,32,128]{4,3,2,1,0:T(8,128)(2,1)}) custom-call(s32[2]{0:T(128)} %pad_add_fusion.me_ref, bf16[2,4,2,2,32,128]{5,4,3,2,1,0:T(8,128)(2,1)} %get-tuple-element.52.refs_0_, ...), custom_call_target="tpu_custom_call" | custom-call | flops 1 | bytes 1 | tf_op jit(solution)/shard_map/regroup/pallas_call | solution.py:165
  46.9 1.0 collective-permute-start.7
  48.0 2.7 %collective-permute-start.8 = (bf16[8,2,2,32,128]{4,3,2,1,0:T(8,128)(2,1)}, bf16[8,2,2,32,128]{4,3,2,1,0:T(8,128)(2,1)S(1)}, u32[]{:S(2)}, u32[]{:S(2)}) collective-permute-start(bf16[8,2,2,32,128]{4,3,2,1,0:T(8,128)(2,1)} %get-tuple-element.58), channel_id=1, source_target_pairs={{0,16},{8,24},{16,0},{24,8},{1,17},{9,25},{17,1},{25,9},{2,18},{10... | collective-permute-start | bytes 786440 | tf_op jit(solution)/shard_map/ppermute | solution.py:426
  51.3 2.3 %turns.1 = (bf16[1024,256]{1,0:T(8,128)(2,1)}, bf16[1024,256]{1,0:T(8,128)(2,1)}) custom-call(), custom_call_target="tpu_custom_call" | custom-call | flops 1 | bytes 1 | tf_op jit(solution)/shard_map/turns/pallas_call | solution.py:347
  55.1 6.5 %all-reduce = s32[72]{0:T(128)S(1)} all-reduce(s32[72]{0:T(128)S(1)} %dynamic-update-slice), channel_id=2, replica_groups=mesh['seg'=4,'pair'=8] {'pair'}, use_global_device_ids=true, to_apply=%add | all-reduce | flops 72 | bytes 576
  62.3 1.0 copy-done.8
  63.2 3.7 %stack.14 = f32[8,4,2,32,128]{4,3,2,1,0:T(8,128)} custom-call(s32[2]{0:T(128)} %pad_add_fusion.me_ref, s32[8,9]{1,0:T(8,128)} %reshape.32.table_ref, bf16[4,16,2,32,128]{4,3,2,1,0:T(8,128)(2,1)} %bitcast.13), custom_call_target="tpu_custom_call" | custom-call | flops 1 | bytes 1 | tf_op jit(solution)/shard_map/stack/pallas_call | solution.py:223
  66.9 3.7 %all-to-all-start.1 = ((f32[8,4,2,32,128]{4,3,2,1,0:T(8,128)}), f32[8,4,2,32,128]{4,3,2,1,0:T(8,128)S(1)}, u32[]{:S(2)}, u32[]{:S(2)}) async-start(f32[8,4,2,32,128]{4,3,2,1,0:T(8,128)} %stack.14), calls=%async_computation.1 | async-start | bytes 2097152 | tf_op jit(solution)/shard_map/all_to_all | solution.py:469
  71.6 3.8 %stack.15 = (f32[2,4,2,32,128]{4,3,2,1,0:T(8,128)}, f32[2,4,2,32,128]{4,3,2,1,0:T(8,128)}, f32[2,4,2,32,128]{4,3,2,1,0:T(8,128)}, f32[2,4,2,32,128]{4,3,2,1,0:T(8,128)}) custom-call(s32[2]{0:T(128)} %pad_add_fusion.me_ref, s32[8,9]{1,0:T(8,128)} %reshape.32.table_ref, bf16[1,16,2,32,128]{4,3,2,1,0:T(8,128)(2,1)} %bitcast.14, ...), custom_call_target="tpu_custom_call" | custom-call | flops 99999997952 | bytes 1 | tf_op jit(solution)/shard_map/stack/pallas_call | solution.py:223
  75.4 1.7 %collective-permute-start.13 = (f32[2,4,2,32,128]{4,3,2,1,0:T(8,128)}, f32[2,4,2,32,128]{4,3,2,1,0:T(8,128)}, u32[]{:S(2)}, u32[]{:S(2)}) collective-permute-start(f32[2,4,2,32,128]{4,3,2,1,0:T(8,128)} %get-tuple-element.65), channel_id=1, source_target_pairs={{0,2},{1,3},{2,0},{3,1},{4,6},{5,7},{6,4},{7,5},{8,10},{9,11},{10,... | collective-permute-start | bytes 786440 | tf_op jit(solution)/shard_map/ppermute | solution.py:433
  77.1 1.5 %collective-permute-start.14 = (f32[2,4,2,32,128]{4,3,2,1,0:T(8,128)}, f32[2,4,2,32,128]{4,3,2,1,0:T(8,128)}, u32[]{:S(2)}, u32[]{:S(2)}) collective-permute-start(f32[2,4,2,32,128]{4,3,2,1,0:T(8,128)} %get-tuple-element.66), channel_id=1, source_target_pairs={{0,4},{1,5},{2,6},{3,7},{4,0},{5,1},{6,2},{7,3},{8,12},{9,13},{10,... | collective-permute-start | bytes 786440 | tf_op jit(solution)/shard_map/ppermute | solution.py:433
  78.9 12.3 %collective-permute-done.13.refs_7_ = f32[2,4,2,32,128]{4,3,2,1,0:T(8,128)} collective-permute-done((f32[2,4,2,32,128]{4,3,2,1,0:T(8,128)}, f32[2,4,2,32,128]{4,3,2,1,0:T(8,128)}, u32[]{:S(2)}, u32[]{:S(2)}) %collective-permute-start.13) | collective-permute-done | bytes 262176 | tf_op jit(solution)/shard_map/ppermute | solution.py:433
  91.6 5.6 %collective-permute-done.15.refs_9_ = f32[2,4,2,32,128]{4,3,2,1,0:T(8,128)} collective-permute-done((f32[2,4,2,32,128]{4,3,2,1,0:T(8,128)}, f32[2,4,2,32,128]{4,3,2,1,0:T(8,128)}, u32[]{:S(2)}, u32[]{:S(2)}) %collective-permute-start.15) | collective-permute-done | bytes 262176 | tf_op jit(solution)/shard_map/ppermute | solution.py:433
  97.3 0.9 copy-done.5
  98.2 6.0 %dft.2 = (f32[256,128]{1,0:T(8,128)S(1)}, f32[256,128]{1,0:T(8,128)S(1)}, f32[256,128]{1,0:T(8,128)S(1)}, f32[256,128]{1,0:T(8,128)S(1)}) custom-call(s32[2]{0:T(128)S(1)} %copy-done.7, bf16[512,512]{1,0:T(8,128)(2,1)S(1)} %copy-done.1, bf16[512,512]{1,0:T(8,128)(2,1)S(1)} %copy-done, f32[512,128]{1,0:T(8,128)S(1)} %copy-done.5, f32[512,128]{1,0:T(8,128)S(1)} %copy-done.4, ...), custom_call_target="tpu_custom_call" | custom-call | flops 1 | bytes 1 | tf_op jit(solution)/shard_map/dft/pallas_call | solution.py:364
  104.2 1.1 collective-permute-start.10
  105.3 2.5 %collective-permute-start.11 = (f32[256,128]{1,0:T(8,128)S(1)}, f32[256,128]{1,0:T(8,128)S(1)}, u32[]{:S(2)}, u32[]{:S(2)}) collective-permute-start(f32[256,128]{1,0:T(8,128)S(1)} %get-tuple-element.71), channel_id=1, source_target_pairs={{0,16},{8,24},{16,0},{24,8},{1,17},{9,25},{17,1},{25,9},{2,18},{10... | collective-permute-start | bytes 393224 | tf_op jit(solution)/shard_map/ppermute | solution.py:426
  107.8 0.9 collective-permute-start.12
  108.7 7.0 %dft.3 = (f32[256,128]{1,0:T(8,128)S(1)}, f32[256,128]{1,0:T(8,128)S(1)}, f32[256,128]{1,0:T(8,128)S(1)}, f32[256,128]{1,0:T(8,128)S(1)}) custom-call(s32[2]{0:T(128)S(1)} %copy-done.7, bf16[512,512]{1,0:T(8,128)(2,1)S(1)} %copy-done.1, bf16[512,512]{1,0:T(8,128)(2,1)S(1)} %copy-done, f32[512,128]{1,0:T(8,128)S(1)} %copy-done.5, f32[512,128]{1,0:T(8,128)S(1)} %copy-done.4, ...), custom_call_target="tpu_custom_call" | custom-call | flops 1 | bytes 1 | tf_op jit(solution)/shard_map/dft/pallas_call | solution.py:364
  115.8 3.4 %collective-permute-start.21 = (f32[256,128]{1,0:T(8,128)S(1)}, f32[256,128]{1,0:T(8,128)S(1)}, u32[]{:S(2)}, u32[]{:S(2)}) collective-permute-start(f32[256,128]{1,0:T(8,128)S(1)} %get-tuple-element.83), channel_id=1, source_target_pairs={{0,16},{8,24},{16,0},{24,8},{1,17},{9,25},{17,1},{25,9},{2,18},{10... | collective-permute-start | bytes 393224 | tf_op jit(solution)/shard_map/ppermute | solution.py:426
  119.2 0.9 collective-permute-start.22
  120.1 2.1 %collective-permute-done.20.refs_5_ = f32[256,128]{1,0:T(8,128)S(1)} collective-permute-done((f32[256,128]{1,0:T(8,128)S(1)}, f32[256,128]{1,0:T(8,128)S(1)}, u32[]{:S(2)}, u32[]{:S(2)}) %collective-permute-start.20) | collective-permute-done | bytes 131104 | tf_op jit(solution)/shard_map/ppermute | solution.py:426
  122.2 7.2 %collective-permute-done.21.refs_6_ = f32[256,128]{1,0:T(8,128)S(1)} collective-permute-done((f32[256,128]{1,0:T(8,128)S(1)}, f32[256,128]{1,0:T(8,128)S(1)}, u32[]{:S(2)}, u32[]{:S(2)}) %collective-permute-start.21) | collective-permute-done | bytes 131104 | tf_op jit(solution)/shard_map/ppermute | solution.py:426
  129.4 3.4 %unpack.1 = f32[512,4,128]{2,1,0:T(4,128)} custom-call(s32[2]{0:T(128)S(1)} %copy-done.7, f32[256,128]{1,0:T(8,128)S(1)} %get-tuple-element.69.refs_0_, f32[256,128]{1,0:T(8,128)S(1)} %collective-permute-done.10.refs_1_, f32[256,128]{1,0:T(8,128)S(1)} %collective-permute-done.11.refs_2_, f32[256,128]{1,0:T(8,128)S(1)} %collective-permute-done.12.refs_3_, ...), custom_call_target="tpu_custom_call" | custom-call | flops 1 | bytes 1 | tf_op jit(solution)/shard_map/unpack/pallas_call | solution.py:412
  (78 shorter events, 7.1 us)
Async XLA Ops:
  7.2 55.0 %all-to-all-start = ((bf16[32,2,2,32,128]{4,3,2,1,0:T(8,128)(2,1)}), bf16[32,2,2,32,128]{4,3,2,1,0:T(8,128)(2,1)S(1)}, u32[]{:S(2)}, u32[]{:S(2)}) async-start(bf16[32,2,2,32,128]{4,3,2,1,0:T(8,128)(2,1)} %bitcast.12), calls=%async_computation | async-start | bytes 2097152 | tf_op jit(solution)/shard_map/all_to_all | solution.py:457
  15.2 38.4 %copy-start.20 = (u32[32]{0:T(128)S(1)}, u32[32]{0:T(128)}, u32[]{:S(2)}) copy-start(u32[32]{0:T(128)} %constant.25) | copy-start | bytes 388
  19.9 13.5 %collective-permute-start = (bf16[2,4,2,2,32,128]{5,4,3,2,1,0:T(8,128)(2,1)}, bf16[2,4,2,2,32,128]{5,4,3,2,1,0:T(8,128)(2,1)S(1)}, u32[]{:S(2)}, u32[]{:S(2)}) collective-permute-start(bf16[2,4,2,2,32,128]{5,4,3,2,1,0:T(8,128)(2,1)} %get-tuple-element.53), channel_id=1, source_target_pairs={{0,2},{1,3},{2,0},{3,1},{4,6},{5,7},{6,4},{7,5},{8,10},{9,11},{10,... | collective-permute-start | bytes 786440 | tf_op jit(solution)/shard_map/ppermute | solution.py:433
  21.6 19.8 %collective-permute-start.1 = (bf16[2,4,2,2,32,128]{5,4,3,2,1,0:T(8,128)(2,1)}, bf16[2,4,2,2,32,128]{5,4,3,2,1,0:T(8,128)(2,1)S(1)}, u32[]{:S(2)}, u32[]{:S(2)}) collective-permute-start(bf16[2,4,2,2,32,128]{5,4,3,2,1,0:T(8,128)(2,1)} %get-tuple-element.54), channel_id=1, source_target_pairs={{0,4},{1,5},{2,6},{3,7},{4,0},{5,1},{6,2},{7,3},{8,12},{9,13},{10,... | collective-permute-start | bytes 786440 | tf_op jit(solution)/shard_map/ppermute | solution.py:433
  23.1 18.4 %collective-permute-start.2 = (bf16[2,4,2,2,32,128]{5,4,3,2,1,0:T(8,128)(2,1)}, bf16[2,4,2,2,32,128]{5,4,3,2,1,0:T(8,128)(2,1)S(1)}, u32[]{:S(2)}, u32[]{:S(2)}) collective-permute-start(bf16[2,4,2,2,32,128]{5,4,3,2,1,0:T(8,128)(2,1)} %get-tuple-element.55), channel_id=1, source_target_pairs={{0,6},{1,7},{2,4},{3,5},{4,2},{5,3},{6,0},{7,1},{8,14},{9,15},{10,... | collective-permute-start | bytes 786440 | tf_op jit(solution)/shard_map/ppermute | solution.py:433
  23.4 18.6 %collective-permute-start.3 = (bf16[2,4,2,2,32,128]{5,4,3,2,1,0:T(8,128)(2,1)}, bf16[2,4,2,2,32,128]{5,4,3,2,1,0:T(8,128)(2,1)S(1)}, u32[]{:S(2)}, u32[]{:S(2)}) collective-permute-start(bf16[2,4,2,2,32,128]{5,4,3,2,1,0:T(8,128)(2,1)} %get-tuple-element.52.refs_0_), channel_id=1, source_target_pairs={{0,1},{1,0},{2,3},{3,2},{4,5},{5,4},{6,7},{7,6},{8,9},{9,8},{10,11... | collective-permute-start | bytes 786440 | tf_op jit(solution)/shard_map/ppermute | solution.py:437
  33.4 8.6 %collective-permute-start.4 = (bf16[2,4,2,2,32,128]{5,4,3,2,1,0:T(8,128)(2,1)S(1)}, bf16[2,4,2,2,32,128]{5,4,3,2,1,0:T(8,128)(2,1)S(1)}, u32[]{:S(2)}, u32[]{:S(2)}) collective-permute-start(bf16[2,4,2,2,32,128]{5,4,3,2,1,0:T(8,128)(2,1)S(1)} %collective-permute-done.refs_1_), channel_id=1, source_target_pairs={{0,1},{1,0},{2,3},{3,2},{4,5},{5,4},{6,7},{7,6},{8,9},{9,8},{10,11... | collective-permute-start | bytes 786440 | tf_op jit(solution)/shard_map/ppermute | solution.py:437
  41.4 1.5 %collective-permute-start.5 = (bf16[2,4,2,2,32,128]{5,4,3,2,1,0:T(8,128)(2,1)S(1)}, bf16[2,4,2,2,32,128]{5,4,3,2,1,0:T(8,128)(2,1)S(1)}, u32[]{:S(2)}, u32[]{:S(2)}) collective-permute-start(bf16[2,4,2,2,32,128]{5,4,3,2,1,0:T(8,128)(2,1)S(1)} %collective-permute-done.1.refs_2_), channel_id=1, source_target_pairs={{0,1},{1,0},{2,3},{3,2},{4,5},{5,4},{6,7},{7,6},{8,9},{9,8},{10,11... | collective-permute-start | bytes 786440 | tf_op jit(solution)/shard_map/ppermute | solution.py:437
  41.5 1.9 %collective-permute-start.6 = (bf16[2,4,2,2,32,128]{5,4,3,2,1,0:T(8,128)(2,1)S(1)}, bf16[2,4,2,2,32,128]{5,4,3,2,1,0:T(8,128)(2,1)S(1)}, u32[]{:S(2)}, u32[]{:S(2)}) collective-permute-start(bf16[2,4,2,2,32,128]{5,4,3,2,1,0:T(8,128)(2,1)S(1)} %collective-permute-done.2.refs_3_), channel_id=1, source_target_pairs={{0,1},{1,0},{2,3},{3,2},{4,5},{5,4},{6,7},{7,6},{8,9},{9,8},{10,11... | collective-permute-start | bytes 786440 | tf_op jit(solution)/shard_map/ppermute | solution.py:437
  46.9 23.7 %collective-permute-start.7 = (bf16[8,2,2,32,128]{4,3,2,1,0:T(8,128)(2,1)}, bf16[8,2,2,32,128]{4,3,2,1,0:T(8,128)(2,1)S(1)}, u32[]{:S(2)}, u32[]{:S(2)}) collective-permute-start(bf16[8,2,2,32,128]{4,3,2,1,0:T(8,128)(2,1)} %get-tuple-element.57), channel_id=1, source_target_pairs={{0,8},{8,0},{16,24},{24,16},{1,9},{9,1},{17,25},{25,17},{2,10},{10... | collective-permute-start | bytes 786440 | tf_op jit(solution)/shard_map/ppermute | solution.py:426
  48.0 22.7 %collective-permute-start.8 = (bf16[8,2,2,32,128]{4,3,2,1,0:T(8,128)(2,1)}, bf16[8,2,2,32,128]{4,3,2,1,0:T(8,128)(2,1)S(1)}, u32[]{:S(2)}, u32[]{:S(2)}) collective-permute-start(bf16[8,2,2,32,128]{4,3,2,1,0:T(8,128)(2,1)} %get-tuple-element.58), channel_id=1, source_target_pairs={{0,16},{8,24},{16,0},{24,8},{1,17},{9,25},{17,1},{25,9},{2,18},{10... | collective-permute-start | bytes 786440 | tf_op jit(solution)/shard_map/ppermute | solution.py:426
  50.6 20.0 %collective-permute-start.9 = (bf16[8,2,2,32,128]{4,3,2,1,0:T(8,128)(2,1)}, bf16[8,2,2,32,128]{4,3,2,1,0:T(8,128)(2,1)S(1)}, u32[]{:S(2)}, u32[]{:S(2)}) collective-permute-start(bf16[8,2,2,32,128]{4,3,2,1,0:T(8,128)(2,1)} %get-tuple-element.59), channel_id=1, source_target_pairs={{0,24},{8,16},{16,8},{24,0},{1,25},{9,17},{17,9},{25,1},{2,26},{10... | collective-permute-start | bytes 786440 | tf_op jit(solution)/shard_map/ppermute | solution.py:426
  66.9 30.3 %all-to-all-start.1 = ((f32[8,4,2,32,128]{4,3,2,1,0:T(8,128)}), f32[8,4,2,32,128]{4,3,2,1,0:T(8,128)S(1)}, u32[]{:S(2)}, u32[]{:S(2)}) async-start(f32[8,4,2,32,128]{4,3,2,1,0:T(8,128)} %stack.14), calls=%async_computation.1 | async-start | bytes 2097152 | tf_op jit(solution)/shard_map/all_to_all | solution.py:469
  71.5 25.7 %copy-start = (bf16[512,512]{1,0:T(8,128)(2,1)S(1)}, bf16[512,512]{1,0:T(8,128)(2,1)}, u32[]{:S(2)}) copy-start(bf16[512,512]{1,0:T(8,128)(2,1)} %constant.17.clone.refs_1_) | copy-start | bytes 1572868
  71.5 25.7 %copy-start.1 = (bf16[512,512]{1,0:T(8,128)(2,1)S(1)}, bf16[512,512]{1,0:T(8,128)(2,1)}, u32[]{:S(2)}) copy-start(bf16[512,512]{1,0:T(8,128)(2,1)} %constant.16.clone.refs_0_) | copy-start | bytes 1572868
  71.5 25.7 %copy-start.2 = (bf16[1024,256]{1,0:T(8,128)(2,1)S(1)}, bf16[1024,256]{1,0:T(8,128)(2,1)}, u32[]{:S(2)}) copy-start(bf16[1024,256]{1,0:T(8,128)(2,1)} %get-tuple-element.60.refs_4_) | copy-start | bytes 1572868
  71.5 25.7 %copy-start.3 = (bf16[1024,256]{1,0:T(8,128)(2,1)S(1)}, bf16[1024,256]{1,0:T(8,128)(2,1)}, u32[]{:S(2)}) copy-start(bf16[1024,256]{1,0:T(8,128)(2,1)} %get-tuple-element.61.refs_5_) | copy-start | bytes 1572868
  71.5 25.7 %copy-start.4 = (f32[512,128]{1,0:T(8,128)S(1)}, f32[512,128]{1,0:T(8,128)}, u32[]{:S(2)}) copy-start(f32[512,128]{1,0:T(8,128)} %constant.19.clone.refs_3_) | copy-start | bytes 786436
  71.5 25.7 %copy-start.7 = (s32[2]{0:T(128)S(1)}, s32[2]{0:T(128)}, u32[]{:S(2)}) copy-start(s32[2]{0:T(128)} %pad_add_fusion.me_ref) | copy-start | bytes 28
  75.4 15.8 %collective-permute-start.13 = (f32[2,4,2,32,128]{4,3,2,1,0:T(8,128)}, f32[2,4,2,32,128]{4,3,2,1,0:T(8,128)}, u32[]{:S(2)}, u32[]{:S(2)}) collective-permute-start(f32[2,4,2,32,128]{4,3,2,1,0:T(8,128)} %get-tuple-element.65), channel_id=1, source_target_pairs={{0,2},{1,3},{2,0},{3,1},{4,6},{5,7},{6,4},{7,5},{8,10},{9,11},{10,... | collective-permute-start | bytes 786440 | tf_op jit(solution)/shard_map/ppermute | solution.py:433
  77.1 14.0 %collective-permute-start.14 = (f32[2,4,2,32,128]{4,3,2,1,0:T(8,128)}, f32[2,4,2,32,128]{4,3,2,1,0:T(8,128)}, u32[]{:S(2)}, u32[]{:S(2)}) collective-permute-start(f32[2,4,2,32,128]{4,3,2,1,0:T(8,128)} %get-tuple-element.66), channel_id=1, source_target_pairs={{0,4},{1,5},{2,6},{3,7},{4,0},{5,1},{6,2},{7,3},{8,12},{9,13},{10,... | collective-permute-start | bytes 786440 | tf_op jit(solution)/shard_map/ppermute | solution.py:433
  78.6 18.6 %collective-permute-start.15 = (f32[2,4,2,32,128]{4,3,2,1,0:T(8,128)}, f32[2,4,2,32,128]{4,3,2,1,0:T(8,128)}, u32[]{:S(2)}, u32[]{:S(2)}) collective-permute-start(f32[2,4,2,32,128]{4,3,2,1,0:T(8,128)} %get-tuple-element.67), channel_id=1, source_target_pairs={{0,6},{1,7},{2,4},{3,5},{4,2},{5,3},{6,0},{7,1},{8,14},{9,15},{10,... | collective-permute-start | bytes 786440 | tf_op jit(solution)/shard_map/ppermute | solution.py:433
  78.8 26.4 %collective-permute-start.16 = (f32[2,4,2,32,128]{4,3,2,1,0:T(8,128)}, f32[2,4,2,32,128]{4,3,2,1,0:T(8,128)}, u32[]{:S(2)}, u32[]{:S(2)}) collective-permute-start(f32[2,4,2,32,128]{4,3,2,1,0:T(8,128)} %get-tuple-element.73.refs_6_), channel_id=1, source_target_pairs={{0,1},{1,0},{2,3},{3,2},{4,5},{5,4},{6,7},{7,6},{8,9},{9,8},{10,11... | collective-permute-start | bytes 786440 | tf_op jit(solution)/shard_map/ppermute | solution.py:437
  91.1 16.7 %collective-permute-start.17 = (f32[2,4,2,32,128]{4,3,2,1,0:T(8,128)}, f32[2,4,2,32,128]{4,3,2,1,0:T(8,128)}, u32[]{:S(2)}, u32[]{:S(2)}) collective-permute-start(f32[2,4,2,32,128]{4,3,2,1,0:T(8,128)} %collective-permute-done.13.refs_7_), channel_id=1, source_target_pairs={{0,1},{1,0},{2,3},{3,2},{4,5},{5,4},{6,7},{7,6},{8,9},{9,8},{10,11... | collective-permute-start | bytes 786440 | tf_op jit(solution)/shard_map/ppermute | solution.py:437
  91.1 17.6 %collective-permute-start.18 = (f32[2,4,2,32,128]{4,3,2,1,0:T(8,128)}, f32[2,4,2,32,128]{4,3,2,1,0:T(8,128)}, u32[]{:S(2)}, u32[]{:S(2)}) collective-permute-start(f32[2,4,2,32,128]{4,3,2,1,0:T(8,128)} %collective-permute-done.14.refs_8_), channel_id=1, source_target_pairs={{0,1},{1,0},{2,3},{3,2},{4,5},{5,4},{6,7},{7,6},{8,9},{9,8},{10,11... | collective-permute-start | bytes 786440 | tf_op jit(solution)/shard_map/ppermute | solution.py:437
  97.2 11.5 %collective-permute-start.19 = (f32[2,4,2,32,128]{4,3,2,1,0:T(8,128)}, f32[2,4,2,32,128]{4,3,2,1,0:T(8,128)}, u32[]{:S(2)}, u32[]{:S(2)}) collective-permute-start(f32[2,4,2,32,128]{4,3,2,1,0:T(8,128)} %collective-permute-done.15.refs_9_), channel_id=1, source_target_pairs={{0,1},{1,0},{2,3},{3,2},{4,5},{5,4},{6,7},{7,6},{8,9},{9,8},{10,11... | collective-permute-start | bytes 786440 | tf_op jit(solution)/shard_map/ppermute | solution.py:437
  104.2 15.0 %collective-permute-start.10 = (f32[256,128]{1,0:T(8,128)S(1)}, f32[256,128]{1,0:T(8,128)S(1)}, u32[]{:S(2)}, u32[]{:S(2)}) collective-permute-start(f32[256,128]{1,0:T(8,128)S(1)} %get-tuple-element.70), channel_id=1, source_target_pairs={{0,8},{8,0},{16,24},{24,16},{1,9},{9,1},{17,25},{25,17},{2,10},{10... | collective-permute-start | bytes 393224 | tf_op jit(solution)/shard_map/ppermute | solution.py:426
  105.3 14.9 %collective-permute-start.11 = (f32[256,128]{1,0:T(8,128)S(1)}, f32[256,128]{1,0:T(8,128)S(1)}, u32[]{:S(2)}, u32[]{:S(2)}) collective-permute-start(f32[256,128]{1,0:T(8,128)S(1)} %get-tuple-element.71), channel_id=1, source_target_pairs={{0,16},{8,24},{16,0},{24,8},{1,17},{9,25},{17,1},{25,9},{2,18},{10... | collective-permute-start | bytes 393224 | tf_op jit(solution)/shard_map/ppermute | solution.py:426
  107.8 12.4 %collective-permute-start.12 = (f32[256,128]{1,0:T(8,128)S(1)}, f32[256,128]{1,0:T(8,128)S(1)}, u32[]{:S(2)}, u32[]{:S(2)}) collective-permute-start(f32[256,128]{1,0:T(8,128)S(1)} %get-tuple-element.72), channel_id=1, source_target_pairs={{0,24},{8,16},{16,8},{24,0},{1,25},{9,17},{17,9},{25,1},{2,26},{10... | collective-permute-start | bytes 393224 | tf_op jit(solution)/shard_map/ppermute | solution.py:426
  115.7 6.5 %collective-permute-start.20 = (f32[256,128]{1,0:T(8,128)S(1)}, f32[256,128]{1,0:T(8,128)S(1)}, u32[]{:S(2)}, u32[]{:S(2)}) collective-permute-start(f32[256,128]{1,0:T(8,128)S(1)} %get-tuple-element.82), channel_id=1, source_target_pairs={{0,8},{8,0},{16,24},{24,16},{1,9},{9,1},{17,25},{25,17},{2,10},{10... | collective-permute-start | bytes 393224 | tf_op jit(solution)/shard_map/ppermute | solution.py:426
  115.8 13.6 %collective-permute-start.21 = (f32[256,128]{1,0:T(8,128)S(1)}, f32[256,128]{1,0:T(8,128)S(1)}, u32[]{:S(2)}, u32[]{:S(2)}) collective-permute-start(f32[256,128]{1,0:T(8,128)S(1)} %get-tuple-element.83), channel_id=1, source_target_pairs={{0,16},{8,24},{16,0},{24,8},{1,17},{9,25},{17,1},{25,9},{2,18},{10... | collective-permute-start | bytes 393224 | tf_op jit(solution)/shard_map/ppermute | solution.py:426
  119.2 10.2 %collective-permute-start.22 = (f32[256,128]{1,0:T(8,128)S(1)}, f32[256,128]{1,0:T(8,128)S(1)}, u32[]{:S(2)}, u32[]{:S(2)}) collective-permute-start(f32[256,128]{1,0:T(8,128)S(1)} %get-tuple-element.84), channel_id=1, source_target_pairs={{0,24},{8,16},{16,8},{24,0},{1,25},{9,17},{17,9},{25,1},{2,26},{10... | collective-permute-start | bytes 393224 | tf_op jit(solution)/shard_map/ppermute | solution.py:426
  (14 other events, 45.1 us)

commit v4 on v3

v4 whole, which is shorter than its diff:
```python
import functools
import math

import jax
import jax.numpy as jnp
import numpy as np
from jax import lax
from jax.experimental import pallas as pl
from jax.experimental.pallas import tpu as pltpu
from jax.sharding import PartitionSpec as P

TILE = 128
LAG = 2048
GROUPS = 8
SMALL = pl.CostEstimate(flops=1, bytes_accessed=1, transcendentals=0)
CC = TILE // GROUPS


def lane_groups(shape):
    return lax.broadcasted_iota(jnp.int32, shape, len(shape) - 1) // CC


def shift_groups(x, by):
    return pltpu.roll(x, (by * CC) % TILE, x.ndim - 1)


def transpose_groups(vectors):
    v = list(vectors)
    grp = lane_groups(v[0].shape)
    for bit in (4, 2, 1):
        low = (grp & bit) == 0
        for i in range(GROUPS):
            if i & bit:
                continue
            a, b = v[i], v[i | bit]
            v[i] = jnp.where(low, a, shift_groups(b, bit))
            v[i | bit] = jnp.where(low, shift_groups(a, -bit), b)
    return v


def reduce_groups(vectors):
    v = list(vectors)
    grp = lane_groups(v[0].shape)
    low = (grp & 4) == 0
    v = [
        jnp.where(low, v[i], v[i + 4])
        + shift_groups(jnp.where(low, v[i + 4], v[i]), 4)
        for i in range(4)
    ]
    for bit in (2, 1):
        low = (grp & bit) == 0
        v = [
            jnp.where(low, v[i], v[i + bit])
            + jnp.where(low, shift_groups(v[i], -bit), shift_groups(v[i + bit], bit))
            for i in range(bit)
        ]
    return v[0]


def selection(n_seg, chunk, chans):
    wide = chans // TILE * n_seg * CC
    row = lax.broadcasted_iota(jnp.int32, (chans, wide), 0)
    col = lax.broadcasted_iota(jnp.int32, (chans, wide), 1)
    group = col // CC
    want = (
        group // n_seg * TILE
        + group % n_seg * (TILE // n_seg)
        + chunk * CC
        + col % CC
    )
    return (row == want).astype(jnp.bfloat16)


def pack_kernel(n_seg, n_pair, chunk, x_ref, out_ref, x_buf, buf_ref, sems):
    band = x_ref.shape[1] // n_pair
    copies = []
    for p in range(n_pair):
        at = pl.ds(p * band, band)
        copies.append(
            pltpu.make_async_copy(x_ref.at[:, at], x_buf.at[p], sems.at[p])
        )
        copies[-1].start()
    sel = selection(n_seg, chunk, x_ref.shape[2])
    rows = band // GROUPS
    for p in range(n_pair):
        copies[p].wait()
        for ri in range(2):
            for part in range(sel.shape[1] // TILE):
                lanes = slice(part * TILE, (part + 1) * TILE)
                buf = buf_ref.at[p % 2, ri]
                buf[...] = jnp.dot(
                    x_buf[p, ri], sel[:, lanes], preferred_element_type=jnp.float32
                )
                v = [buf[pl.ds(fb, rows, stride=GROUPS), :] for fb in range(GROUPS)]
                v = transpose_groups(v)
                for g in range(GROUPS):
                    t, z = divmod(part * GROUPS + g, n_seg)
                    out_ref[z, p, t, ri] = v[g].astype(jnp.bfloat16)


def pack(x, chunk, n_seg, n_pair):
    _, freq, chans = x.shape
    band = freq // n_pair
    shape = (n_seg, n_pair, chans // TILE, 2, band // GROUPS, TILE)
    return pl.pallas_call(
        functools.partial(pack_kernel, n_seg, n_pair, chunk),
        out_shape=jax.ShapeDtypeStruct(shape, jnp.bfloat16),
        in_specs=[pl.BlockSpec(memory_space=pltpu.HBM)],
        out_specs=pl.BlockSpec(memory_space=pltpu.VMEM),
        scratch_shapes=[
            pltpu.VMEM((n_pair, 2, band, chans), jnp.bfloat16),
            pltpu.VMEM((2, 2, band, TILE), jnp.float32),
            pltpu.SemaphoreType.DMA((n_pair,)),
        ],
        name="pack",
        cost_estimate=SMALL,
    )(x)


def stack_kernel(n_seg, n_pair, most, n_specs, me_ref, table_ref, *refs):
    specs, out_refs = refs[:n_specs], refs[n_specs:]
    parts = [r.at[g] for r in specs for g in range(r.shape[0])]
    inv = 1.0 / float(n_seg * n_seg)
    for k in range(n_pair):
        owner = jnp.bitwise_xor(me_ref[1], k)
        count = table_ref[owner, 2 * most]
        out_ref = out_refs[k // 2].at[k % 2]

        def one(s, _):
            src = table_ref[owner, 2 * s]
            rcv = table_ref[owner, 2 * s + 1]

            @pl.when(s < count)
            def _():
                lr = li = pr = pi = None
                for g in range(n_seg):
                    a0 = parts[g][src, 0].astype(jnp.float32)
                    a1 = parts[g][src, 1].astype(jnp.float32)
                    b0 = parts[g][rcv, 0].astype(jnp.float32)
                    b1 = parts[g][rcv, 1].astype(jnp.float32)
                    cr = a0 * b0 + a1 * b1
                    ci = a1 * b0 - a0 * b1
                    m = lax.rsqrt(cr * cr + ci * ci + 1.0)
                    if g == 0:
                        lr, li, pr, pi = cr, ci, cr * m, ci * m
                    else:
                        lr, li, pr, pi = lr + cr, li + ci, pr + cr * m, pi + ci * m
                w = (pr * pr + pi * pi) * inv
                out_ref[s, 0] = lr * w
                out_ref[s, 1] = li * w

            @pl.when(s >= count)
            def _():
                out_ref[s] = jnp.zeros(out_ref.shape[1:], jnp.float32)

            return 0

        lax.fori_loop(0, most, one, 0)


def stacks(me, table, specs, cost, n_seg, n_pair, most):
    rows = specs[0].shape[3]
    arrays = n_pair // 2
    shape = (n_pair // arrays, most, 2, rows, TILE)
    smem = pl.BlockSpec(memory_space=pltpu.SMEM)
    vmem = pl.BlockSpec(memory_space=pltpu.VMEM)
    return pl.pallas_call(
        functools.partial(stack_kernel, n_seg, n_pair, most, len(specs)),
        out_shape=[jax.ShapeDtypeStruct(shape, jnp.float32)] * arrays,
        in_specs=[smem, smem] + [vmem] * len(specs),
        out_specs=[vmem] * arrays,
        name="stack",
        compiler_params=pltpu.CompilerParams(vmem_limit_bytes=8 << 20),
        cost_estimate=cost,
    )(me, table, *specs)


def dft_kernel(n_seg, n_pair, most, me_ref, tables_ref, *refs):
    ins, outs = refs[:n_pair], refs[n_pair : n_pair + n_seg]
    held, sems = refs[n_pair + n_seg :][:4], refs[n_pair + n_seg + 4]
    s32, shi, slo, y, zhi, zlo, sums, parts = refs[n_pair + n_seg + 5 :]
    whi_ref, wlo_ref, t_ref, phase_ref = held
    copies = []
    row = 0
    for i, to in enumerate(held):
        src = tables_ref.at[pl.ds(row, to.shape[0])]
        copies.append(pltpu.make_async_copy(src, to, sems.at[i]))
        copies[-1].start()
        row += to.shape[0]
    rows = ins[0].shape[3]
    half_h = whi_ref.shape[1] // 2
    wide = most * TILE
    for k in range(n_pair):
        band = jnp.bitwise_xor(me_ref[1], k)
        src = ins[k % 2 * (n_pair // 2) + k // 2].at[k % 2]
        at = pl.ds(pl.multiple_of(band * rows, rows), rows)
        for s in range(most):
            for ri in range(2):
                s32[ri, at, s * TILE : (s + 1) * TILE] = src[s, ri]
    for ri in range(2):
        full = s32[ri]
        hi = full.astype(jnp.bfloat16)
        lo = (full - hi.astype(jnp.float32)).astype(jnp.bfloat16)
        own = slice(ri * wide, (ri + 1) * wide)
        other = slice((1 - ri) * wide, (2 - ri) * wide)
        for to, part in ((shi, hi), (slo, lo)):
            to[:half_h, own] = part
            to[half_h:, other] = part if ri == 0 else -part
    copies[0].wait()
    copies[1].wait()
    for ri in range(2):
        n = slice(ri * wide, (ri + 1) * wide)
        y[ri] = (
            jnp.dot(wlo_ref[...], shi[:, n], preferred_element_type=jnp.float32)
            + jnp.dot(whi_ref[...], slo[:, n], preferred_element_type=jnp.float32)
        ) + jnp.dot(whi_ref[...], shi[:, n], preferred_element_type=jnp.float32)
    copies[3].wait()
    period = y.shape[1]
    step_rows = 64
    for b in range(period // step_rows):
        at = slice(b * step_rows, (b + 1) * step_rows)
        turn = phase_ref[at, :].astype(jnp.float32)
        c = turn[:, :TILE] + turn[:, TILE : 2 * TILE]
        d = turn[:, 2 * TILE : 3 * TILE] + turn[:, 3 * TILE :]
        for s in range(most):
            lanes = slice(s * TILE, (s + 1) * TILE)
            yr = y[0, at, lanes]
            yi = y[1, at, lanes]
            for ri, z in enumerate((c * yr - d * yi, d * yr + c * yi)):
                to = slice((ri * most + s) * TILE, (ri * most + s + 1) * TILE)
                hi = z.astype(jnp.bfloat16)
                zhi[at, to] = hi
                zlo[at, to] = (z - hi.astype(jnp.float32)).astype(jnp.bfloat16)
    copies[2].wait()
    thi, tlo = t_ref[:, : sums.shape[1]], t_ref[:, sums.shape[1] :]
    sums[...] = (
        jnp.dot(zhi[...], tlo, preferred_element_type=jnp.float32)
        + jnp.dot(zlo[...], thi, preferred_element_type=jnp.float32)
    ) + jnp.dot(zhi[...], thi, preferred_element_type=jnp.float32)
    half = outs[0].shape[0]
    first = lax.broadcasted_iota(jnp.int32, (half, TILE), 1) < TILE // 2
    for dest in range(n_seg):
        lag = dest * 2 * half
        r, l0 = lag // period, lag % period
        col = slice(r // 2 * TILE, (r // 2 + 1) * TILE)
        low = sums[l0 : l0 + half, col]
        high = sums[l0 + half : l0 + 2 * half, col]
        if r % 2 == 0:
            high = pltpu.roll(high, TILE // 2, 1)
        else:
            low = pltpu.roll(low, TILE // 2, 1)
        parts[dest] = jnp.where(first, low, high)
    for k in range(n_seg):
        outs[k][...] = parts[jnp.bitwise_xor(me_ref[0], k)]


def tables_kernel(most, turns, shift, whi_ref, wlo_ref, phase_ref, out_ref, t_ref, sems):
    h = whi_ref.shape[0]
    k = t_ref.shape[0]
    copies = [
        pltpu.make_async_copy(whi_ref, out_ref.at[pl.ds(0, h)], sems.at[0]),
        pltpu.make_async_copy(wlo_ref, out_ref.at[pl.ds(h, h)], sems.at[1]),
        pltpu.make_async_copy(phase_ref, out_ref.at[pl.ds(2 * h + k, h)], sems.at[2]),
        pltpu.make_async_copy(t_ref, out_ref.at[pl.ds(2 * h, k)], sems.at[3]),
    ]
    for copy in copies[:3]:
        copy.start()
    shape = (most * TILE, turns * most * CC)
    row = lax.broadcasted_iota(jnp.int32, shape, 0)
    col = lax.broadcasted_iota(jnp.int32, shape, 1)
    same = (row // TILE == col // CC % most) & (row % CC == col % CC)
    eighths = (col // (most * CC) - shift) * (row // CC % GROUPS)
    diagonal = jnp.float32(math.sqrt(0.5))
    for ri in range(2):
        e = jnp.bitwise_and(eighths + 2 * ri, 7)
        size = jnp.where(e % 4 == 2, 0.0, jnp.where(e % 2 == 0, 1.0, diagonal))
        t = jnp.where(same, jnp.where((e > 2) & (e < 6), -size, size), 0.0)
        at = slice(ri * most * TILE, (ri + 1) * most * TILE)
        hi = t.astype(jnp.bfloat16)
        t_ref[at, : shape[1]] = hi
        t_ref[at, shape[1] :] = (t - hi.astype(jnp.float32)).astype(jnp.bfloat16)
    copies[3].start()
    for copy in copies:
        copy.wait()


def split(x):
    hi = x.astype(np.float32).astype(jnp.bfloat16)
    return hi, (x - hi.astype(np.float64)).astype(np.float32).astype(jnp.bfloat16)


def make_tables(freq, most):
    h = freq // GROUPS
    period = 2 * h
    turns = LAG // period
    angle = np.arange(period)[:, None] * np.arange(h)[None, :] % period
    angle = angle * (2.0 * math.pi / period)
    whi, wlo = split(np.concatenate([np.cos(angle), np.sin(angle)], 1))
    fb = np.arange(TILE) // CC
    phase = ((np.arange(period)[:, None] * fb[None, :]) % (2 * freq)) * (math.pi / freq)
    scale = 1.0 / math.sqrt(freq)
    phase = np.concatenate(split(np.cos(phase) * scale) + split(np.sin(phase) * scale), 1)
    hbm = pl.BlockSpec(memory_space=pltpu.HBM)
    width = period
    return pl.pallas_call(
        functools.partial(tables_kernel, most, turns, LAG // 2 // period),
        out_shape=jax.ShapeDtypeStruct((48 << 10, width), jnp.bfloat16),
        in_specs=[hbm] * 3,
        out_specs=hbm,
        scratch_shapes=[
            pltpu.VMEM((2 * most * TILE, width), jnp.bfloat16),
            pltpu.SemaphoreType.DMA((4,)),
        ],
        name="tables",
        cost_estimate=SMALL,
    )(jnp.asarray(whi), jnp.asarray(wlo), jnp.asarray(phase))


def dft(me, tables, blocks, freq, n_seg, n_pair, most):
    period = 2 * (freq // GROUPS)
    smem = pl.BlockSpec(memory_space=pltpu.SMEM)
    vmem = pl.BlockSpec(memory_space=pltpu.VMEM)
    half = LAG // n_seg // 2
    wide = most * TILE
    return pl.pallas_call(
        functools.partial(dft_kernel, n_seg, n_pair, most),
        out_shape=[jax.ShapeDtypeStruct((half, TILE), jnp.float32)] * n_seg,
        in_specs=[smem, pl.BlockSpec(memory_space=pltpu.HBM)] + [vmem] * len(blocks),
        out_specs=[vmem] * n_seg,
        scratch_shapes=[
            pltpu.VMEM((period, period), jnp.bfloat16),
            pltpu.VMEM((period, period), jnp.bfloat16),
            pltpu.VMEM((2 * wide, period), jnp.bfloat16),
            pltpu.VMEM((period, 4 * TILE), jnp.bfloat16),
            pltpu.SemaphoreType.DMA((4,)),
            pltpu.VMEM((2, period // 2, wide), jnp.float32),
            pltpu.VMEM((period, 2 * wide), jnp.bfloat16),
            pltpu.VMEM((period, 2 * wide), jnp.bfloat16),
            pltpu.VMEM((2, period, wide), jnp.float32),
            pltpu.VMEM((period, 2 * wide), jnp.bfloat16),
            pltpu.VMEM((period, 2 * wide), jnp.bfloat16),
            pltpu.VMEM((period, LAG // period * most * CC), jnp.float32),
            pltpu.VMEM((n_seg, half, TILE), jnp.float32),
        ],
        name="dft",
        compiler_params=pltpu.CompilerParams(vmem_limit_bytes=24 << 20),
        cost_estimate=SMALL,
    )(me, tables, *blocks)


def unpack_kernel(n_seg, chunks, most, me_ref, *refs):
    ins = refs[: n_seg * chunks]
    out_ref, buf = refs[n_seg * chunks :]
    half = ins[0].shape[0]
    for k in range(n_seg):
        z = jnp.bitwise_xor(me_ref[0], k)
        for ch in range(chunks):
            buf[z * chunks + ch] = ins[ch * n_seg + k][...]
    step_rows = 16

    def one(b, _):
        at = pl.multiple_of(b * step_rows, step_rows)
        v = transpose_groups([buf[i, pl.ds(at, step_rows), :] for i in range(GROUPS)])
        for h in range(2):
            for s in range(most):
                out_ref[pl.ds(h * half + at, step_rows), s, :] = v[h * most + s]
        return 0

    lax.fori_loop(0, half // step_rows, one, 0, unroll=4)


def unpack(me, parts, n_seg, chunks, most):
    half = parts[0].shape[0]
    smem = pl.BlockSpec(memory_space=pltpu.SMEM)
    vmem = pl.BlockSpec(memory_space=pltpu.VMEM)
    return pl.pallas_call(
        functools.partial(unpack_kernel, n_seg, chunks, most),
        out_shape=jax.ShapeDtypeStruct((2 * half, most, TILE), jnp.float32),
        in_specs=[smem] + [vmem] * len(parts),
        out_specs=vmem,
        scratch_shapes=[pltpu.VMEM((GROUPS, half, TILE), jnp.float32)],
        name="unpack",
        compiler_params=pltpu.CompilerParams(vmem_limit_bytes=12 << 20),
        cost_estimate=SMALL,
    )(me, *parts)


def exchange(blocks, axis, size):
    return [blocks[0]] + [
        lax.ppermute(blocks[k], axis, [(i, i ^ k) for i in range(size)])
        for k in range(1, size)
    ]


def exchange_plane(blocks, n_pair):
    direct = [blocks[0]] + [
        lax.ppermute(blocks[k], "pair", [(i, i ^ (2 * k)) for i in range(n_pair)])
        for k in range(1, n_pair // 2)
    ]
    swap = [(i, i ^ 1) for i in range(n_pair)]
    return direct + [lax.ppermute(d, "pair", swap) for d in direct]


def body(spectra, pair_lists, pair_counts):
    n_pair = lax.axis_size("pair")
    n_seg = lax.axis_size("seg")
    freq = spectra.shape[2]
    most = pair_lists.shape[0]
    tiles = spectra.shape[3] // TILE
    chunks = GROUPS // n_seg
    rows = freq // n_pair // GROUPS
    me = jnp.stack([lax.axis_index("seg"), lax.axis_index("pair")]).astype(jnp.int32)
    x = spectra.reshape(2, freq, spectra.shape[3])
    lists = jnp.concatenate([pair_lists.reshape(-1), pair_counts])
    tables = make_tables(freq, most)
    packed = [pack(x, chunk, n_seg, n_pair) for chunk in range(chunks)]
    lists, packed[-1] = lax.optimization_barrier((lists, packed[-1]))
    table = lax.all_gather(lists, "pair", axis=0)
    if chunks > 1:
        table, packed[1], _ = lax.optimization_barrier((table, packed[1], tables))
    done = []
    lags = None
    for sent in packed:
        got = lax.all_to_all(
            sent.reshape(n_seg * n_pair, tiles, 2, rows, TILE),
            ("seg", "pair"),
            split_axis=0,
            concat_axis=0,
            tiled=True,
        )
        if lags is not None:
            got, _ = lax.optimization_barrier((got, lags))
        spec = got.reshape(n_seg, n_pair * tiles, 2, rows, TILE)
        blocks = stacks(me, table, [spec], SMALL, n_seg, n_pair, most)
        blocks = exchange_plane(blocks, n_pair)
        lags = dft(me, tables, blocks, freq, n_seg, n_pair, most)
        done += exchange(lags, "seg", n_seg)
    return unpack(me, done, n_seg, chunks, most)


def solution(mesh):
    return jax.shard_map(
        body,
        mesh=mesh,
        in_specs=(P("seg", None, None, "pair"), P("pair", None), P("pair")),
        out_specs=P("seg", "pair", None),
        check_vma=False,
    )
```

time: 133 us -> 164 us (1.23)
  Pallas kernels: 39.6 us -> 81.7 us
  local copies, waits for them, and re-layouts: 5.48 us -> 1.17 us
  starting transfers between devices: 32.3 us -> 28.3 us
  waiting for transfers between devices: 46.6 us -> 43 us
  blocking collectives: 6.49 us -> 8.23 us
    pallas_call x6 -> x5, Pallas kernels: 28.8 us -> 74.2 us  [the longest x1 48.8 us: make_tables(): pl.pallas_call(functools.partial(tables_kernel, most, turns, LAG // 2 //...]
    ppermute x6, waiting for transfers between devices: 35.9 us -> 31 us  [exchange_plane(): lax.ppermute(blocks[k], 'pair', [(i, i ^ 2 * k) for i in range(n_pair)])]
    ppermute x9 -> x6, starting transfers between devices: 13.3 us -> 9.17 us  [exchange(): lax.ppermute(blocks[k], axis, [(i, i ^ k) for i in range(size)])]
    unnamed x46 -> x8, local copies, waits for them, and re-layouts: 4.73 us -> 1.01 us
    pallas_call x2, Pallas kernels: 7.46 us -> 4.19 us  [stacks(): pl.pallas_call(functools.partial(stack_kernel, n_seg, n_pair, most, len(s...]
    unnamed x1, blocking collectives: 6.49 us -> 8.23 us
    ppermute x9 -> x6, waiting for transfers between devices: 9.28 us -> 10.4 us  [exchange(): lax.ppermute(blocks[k], axis, [(i, i ^ k) for i in range(size)])]
  transfers between devices with their start and end apart: 25 -> 22, of which waited for: 8 -> 8; matrix products, arithmetic and copies ran while one was open for 2% -> 1% of each run, Pallas kernels for 22% -> 43%
where the time goes in v4:
time: 164 us
  Pallas kernels  81.7 us (50%)
  waiting for transfers between devices  43 us (26%)
  starting transfers between devices  28.3 us (17%)
  blocking collectives  8.23 us (5%)
    pallas_call x1, Pallas kernels, make_tables(): pl.pallas_call(functools.partial(tables_kernel, most, turns, LAG // 2 //...  48.8 us
    ppermute x6, waiting for transfers between devices, exchange_plane(): lax.ppermute(blocks[k], 'pair', [(i, i ^ 2 * k) for i in range(n_pair)])  31 us
    pallas_call x2, Pallas kernels, dft(): pl.pallas_call(functools.partial(dft_kernel, n_seg, n_pair, most), out_sh...  13.8 us
    pallas_call x2, Pallas kernels, pack(): pl.pallas_call(functools.partial(pack_kernel, n_seg, n_pair, chunk), out_...  11.6 us
    all_to_all x2, starting transfers between devices, body(): lax.all_to_all(sent.reshape(n_seg * n_pair, tiles, 2, rows, TILE), ('seg'...  11.5 us
    ppermute x6, waiting for transfers between devices, exchange(): lax.ppermute(blocks[k], axis, [(i, i ^ k) for i in range(size)])  10.4 us
    ppermute x6, starting transfers between devices, exchange(): lax.ppermute(blocks[k], axis, [(i, i ^ k) for i in range(size)])  9.17 us
    unnamed x1, blocking collectives  8.23 us
  transfers between devices with their start and end apart: 22, of which 8 were waited for; matrix products, arithmetic and copies ran while one was open for 1% of the time, Pallas kernels for 43%

profile of v4, /device:TPU:0, one launch (start us, length us, event | category | flops | bytes accessed | tf_op | source)
XLA Modules:
  0.0 164.1 jit_solution(2287549254620986405)
XLA Ops:
  0.0 5.8 %pack.3 = bf16[4,8,2,2,32,128]{5,4,3,2,1,0:T(8,128)(2,1)} custom-call(bf16[2,2048,256]{2,1,0:T(8,128)(2,1)} %bitcast.10), custom_call_target="tpu_custom_call" | custom-call | flops 1 | bytes 1 | tf_op jit(solution)/shard_map/pack/pallas_call | solution.py:105
  5.8 7.3 %all-to-all-start = ((bf16[32,2,2,32,128]{4,3,2,1,0:T(8,128)(2,1)}), bf16[32,2,2,32,128]{4,3,2,1,0:T(8,128)(2,1)S(1)}, u32[]{:S(2)}, u32[]{:S(2)}) async-start(bf16[32,2,2,32,128]{4,3,2,1,0:T(8,128)(2,1)} %bitcast.12), calls=%async_computation | async-start | bytes 2097152 | tf_op jit(solution)/shard_map/all_to_all | solution.py:424
  13.1 5.8 %pack.2 = bf16[4,8,2,2,32,128]{5,4,3,2,1,0:T(8,128)(2,1)} custom-call(bf16[2,2048,256]{2,1,0:T(8,128)(2,1)} %bitcast.11), custom_call_target="tpu_custom_call" | custom-call | flops 1 | bytes 1 | tf_op jit(solution)/shard_map/pack/pallas_call | solution.py:105
  18.9 48.8 %tables.1.tables_ref = bf16[49152,512]{1,0:T(8,128)(2,1)} custom-call(bf16[512,512]{1,0:T(8,128)(2,1)} %constant.14.clone.whi_ref, bf16[512,512]{1,0:T(8,128)(2,1)} %constant.15.clone.wlo_ref, bf16[512,512]{1,0:T(8,128)(2,1)} %constant.16.clone.phase_ref), custom_call_target="tpu_custom_call" | custom-call | flops 1 | bytes 1 | tf_op jit(solution)/shard_map/tables/pallas_call | solution.py:305
  68.7 0.7 dynamic-slice
  70.3 8.2 %all-reduce = s32[72]{0:T(128)S(1)} all-reduce(s32[72]{0:T(128)S(1)} %dynamic-update-slice), channel_id=2, replica_groups=mesh['seg'=4,'pair'=8] {'pair'}, use_global_device_ids=true, to_apply=%add | all-reduce | flops 72 | bytes 576
  78.6 4.2 %all-to-all-start.1 = ((bf16[32,2,2,32,128]{4,3,2,1,0:T(8,128)(2,1)}), bf16[32,2,2,32,128]{4,3,2,1,0:T(8,128)(2,1)S(1)}, u32[]{:S(2)}, u32[]{:S(2)}) async-start(bf16[32,2,2,32,128]{4,3,2,1,0:T(8,128)(2,1)} %bitcast.6), calls=%async_computation.1 | async-start | bytes 2097152 | tf_op jit(solution)/shard_map/all_to_all | solution.py:424
  82.9 2.1 %stack.14 = (f32[2,4,2,32,128]{4,3,2,1,0:T(8,128)S(1)}, f32[2,4,2,32,128]{4,3,2,1,0:T(8,128)S(1)}, f32[2,4,2,32,128]{4,3,2,1,0:T(8,128)S(1)}, f32[2,4,2,32,128]{4,3,2,1,0:T(8,128)S(1)}) custom-call(s32[2]{0:T(128)S(1)} %pad_add_fusion.me_ref, s32[8,9]{1,0:T(8,128)S(1)} %reshape.24.table_ref, bf16[4,16,2,32,128]{4,3,2,1,0:T(8,128)(2,1)S(1)} %bitcast.9), custom_call_target="tpu_custom_call" | custom-call | flops 1 | bytes 1 | tf_op jit(solution)/shard_map/stack/pallas_call | solution.py:167
  85.0 1.7 %collective-permute-start = (f32[2,4,2,32,128]{4,3,2,1,0:T(8,128)S(1)}, f32[2,4,2,32,128]{4,3,2,1,0:T(8,128)S(1)}, u32[]{:S(2)}, u32[]{:S(2)}) collective-permute-start(f32[2,4,2,32,128]{4,3,2,1,0:T(8,128)S(1)} %get-tuple-element.30), channel_id=1, source_target_pairs={{0,2},{1,3},{2,0},{3,1},{4,6},{5,7},{6,4},{7,5},{8,10},{9,11},{10,... | collective-permute-start | bytes 786440 | tf_op jit(solution)/shard_map/ppermute | solution.py:397
  86.7 1.5 collective-permute-start.1
  88.1 0.4 collective-permute-start.2
  88.6 12.9 %collective-permute-done.refs_1_ = f32[2,4,2,32,128]{4,3,2,1,0:T(8,128)S(1)} collective-permute-done((f32[2,4,2,32,128]{4,3,2,1,0:T(8,128)S(1)}, f32[2,4,2,32,128]{4,3,2,1,0:T(8,128)S(1)}, u32[]{:S(2)}, u32[]{:S(2)}) %collective-permute-start) | collective-permute-done | bytes 262176 | tf_op jit(solution)/shard_map/ppermute | solution.py:397
  101.4 0.5 collective-permute-start.5
  101.9 7.2 %collective-permute-done.2.refs_3_ = f32[2,4,2,32,128]{4,3,2,1,0:T(8,128)S(1)} collective-permute-done((f32[2,4,2,32,128]{4,3,2,1,0:T(8,128)S(1)}, f32[2,4,2,32,128]{4,3,2,1,0:T(8,128)S(1)}, u32[]{:S(2)}, u32[]{:S(2)}) %collective-permute-start.2) | collective-permute-done | bytes 262176 | tf_op jit(solution)/shard_map/ppermute | solution.py:397
  109.2 1.5 collective-permute-done.6.refs_7_
  110.7 6.9 %dft.2 = (f32[256,128]{1,0:T(8,128)S(1)}, f32[256,128]{1,0:T(8,128)S(1)}, f32[256,128]{1,0:T(8,128)S(1)}, f32[256,128]{1,0:T(8,128)S(1)}) custom-call(s32[2]{0:T(128)S(1)} %pad_add_fusion.me_ref, bf16[49152,512]{1,0:T(8,128)(2,1)} %tables.1.tables_ref, f32[2,4,2,32,128]{4,3,2,1,0:T(8,128)S(1)} %get-tuple-element.29.refs_0_, ...), custom_call_target="tpu_custom_call" | custom-call | flops 1 | bytes 1 | tf_op jit(solution)/shard_map/dft/pallas_call | solution.py:325
  117.6 2.1 %stack.15 = (f32[2,4,2,32,128]{4,3,2,1,0:T(8,128)S(1)}, f32[2,4,2,32,128]{4,3,2,1,0:T(8,128)S(1)}, f32[2,4,2,32,128]{4,3,2,1,0:T(8,128)S(1)}, f32[2,4,2,32,128]{4,3,2,1,0:T(8,128)S(1)}) custom-call(s32[2]{0:T(128)S(1)} %pad_add_fusion.me_ref, s32[8,9]{1,0:T(8,128)S(1)} %reshape.24.table_ref, bf16[4,16,2,32,128]{4,3,2,1,0:T(8,128)(2,1)S(1)} %bitcast.8), custom_call_target="tpu_custom_call" | custom-call | flops 1 | bytes 1 | tf_op jit(solution)/shard_map/stack/pallas_call | solution.py:167
  119.7 0.8 collective-permute-start.10
  120.9 2.4 %collective-permute-start.12 = (f32[2,4,2,32,128]{4,3,2,1,0:T(8,128)S(1)}, f32[2,4,2,32,128]{4,3,2,1,0:T(8,128)S(1)}, u32[]{:S(2)}, u32[]{:S(2)}) collective-permute-start(f32[2,4,2,32,128]{4,3,2,1,0:T(8,128)S(1)} %get-tuple-element.42), channel_id=1, source_target_pairs={{0,6},{1,7},{2,4},{3,5},{4,2},{5,3},{6,0},{7,1},{8,14},{9,15},{10,... | collective-permute-start | bytes 786440 | tf_op jit(solution)/shard_map/ppermute | solution.py:397
  123.3 5.7 %collective-permute-done.10.refs_1_ = f32[2,4,2,32,128]{4,3,2,1,0:T(8,128)S(1)} collective-permute-done((f32[2,4,2,32,128]{4,3,2,1,0:T(8,128)S(1)}, f32[2,4,2,32,128]{4,3,2,1,0:T(8,128)S(1)}, u32[]{:S(2)}, u32[]{:S(2)}) %collective-permute-start.10) | collective-permute-done | bytes 262176 | tf_op jit(solution)/shard_map/ppermute | solution.py:397
  128.9 0.5 collective-permute-done.11.refs_2_
  129.4 4.8 %collective-permute-done.12.refs_3_ = f32[2,4,2,32,128]{4,3,2,1,0:T(8,128)S(1)} collective-permute-done((f32[2,4,2,32,128]{4,3,2,1,0:T(8,128)S(1)}, f32[2,4,2,32,128]{4,3,2,1,0:T(8,128)S(1)}, u32[]{:S(2)}, u32[]{:S(2)}) %collective-permute-start.12) | collective-permute-done | bytes 262176 | tf_op jit(solution)/shard_map/ppermute | solution.py:397
  134.2 2.3 %collective-permute-start.7 = (f32[256,128]{1,0:T(8,128)S(1)}, f32[256,128]{1,0:T(8,128)S(1)}, u32[]{:S(2)}, u32[]{:S(2)}) collective-permute-start(f32[256,128]{1,0:T(8,128)S(1)} %get-tuple-element.34), channel_id=1, source_target_pairs={{0,8},{8,0},{16,24},{24,16},{1,9},{9,1},{17,25},{25,17},{2,10},{10... | collective-permute-start | bytes 393224 | tf_op jit(solution)/shard_map/ppermute | solution.py:390
  136.6 1.2 collective-permute-start.8
  137.7 1.2 collective-permute-start.9
  139.0 6.9 %dft.3 = (f32[256,128]{1,0:T(8,128)S(1)}, f32[256,128]{1,0:T(8,128)S(1)}, f32[256,128]{1,0:T(8,128)S(1)}, f32[256,128]{1,0:T(8,128)S(1)}) custom-call(s32[2]{0:T(128)S(1)} %pad_add_fusion.me_ref, bf16[49152,512]{1,0:T(8,128)(2,1)} %tables.1.tables_ref, f32[2,4,2,32,128]{4,3,2,1,0:T(8,128)S(1)} %get-tuple-element.39.refs_0_, ...), custom_call_target="tpu_custom_call" | custom-call | flops 1 | bytes 1 | tf_op jit(solution)/shard_map/dft/pallas_call | solution.py:325
  145.8 1.2 collective-permute-start.17
  147.0 2.1 %collective-permute-start.18 = (f32[256,128]{1,0:T(8,128)S(1)}, f32[256,128]{1,0:T(8,128)S(1)}, u32[]{:S(2)}, u32[]{:S(2)}) collective-permute-start(f32[256,128]{1,0:T(8,128)S(1)} %get-tuple-element.45), channel_id=1, source_target_pairs={{0,16},{8,24},{16,0},{24,8},{1,17},{9,25},{17,1},{25,9},{2,18},{10... | collective-permute-start | bytes 393224 | tf_op jit(solution)/shard_map/ppermute | solution.py:390
  149.1 1.2 collective-permute-start.19
  150.3 1.9 %collective-permute-done.17.refs_5_ = f32[256,128]{1,0:T(8,128)S(1)} collective-permute-done((f32[256,128]{1,0:T(8,128)S(1)}, f32[256,128]{1,0:T(8,128)S(1)}, u32[]{:S(2)}, u32[]{:S(2)}) %collective-permute-start.17) | collective-permute-done | bytes 131104 | tf_op jit(solution)/shard_map/ppermute | solution.py:390
  152.2 8.5 %collective-permute-done.18.refs_6_ = f32[256,128]{1,0:T(8,128)S(1)} collective-permute-done((f32[256,128]{1,0:T(8,128)S(1)}, f32[256,128]{1,0:T(8,128)S(1)}, u32[]{:S(2)}, u32[]{:S(2)}) %collective-permute-start.18) | collective-permute-done | bytes 131104 | tf_op jit(solution)/shard_map/ppermute | solution.py:390
  160.7 3.4 %unpack.1 = f32[512,4,128]{2,1,0:T(4,128)} custom-call(s32[2]{0:T(128)S(1)} %pad_add_fusion.me_ref, f32[256,128]{1,0:T(8,128)S(1)} %get-tuple-element.33.refs_0_, f32[256,128]{1,0:T(8,128)S(1)} %collective-permute-done.7.refs_1_, f32[256,128]{1,0:T(8,128)S(1)} %collective-permute-done.8.refs_2_, f32[256,128]{1,0:T(8,128)S(1)} %collective-permute-done.9.refs_3_, ...), custom_call_target="tpu_custom_call" | custom-call | flops 1 | bytes 1 | tf_op jit(solution)/shard_map/unpack/pallas_call | solution.py:376
  (33 shorter events, 1.1 us)
Async XLA Ops:
  0.0 68.7 %copy-start.1 = (u32[32]{0:T(128)S(1)}, u32[32]{0:T(128)}, u32[]{:S(2)}) copy-start(u32[32]{0:T(128)} %constant.22) | copy-start | bytes 388
  0.0 68.4 %copy-start = (s32[4,2]{0,1:T(2,128)S(1)}, s32[4,2]{0,1:T(2,128)}, u32[]{:S(2)}) copy-start(s32[4,2]{0,1:T(2,128)} %param.7) | copy-start | bytes 100
  5.8 72.8 %all-to-all-start = ((bf16[32,2,2,32,128]{4,3,2,1,0:T(8,128)(2,1)}), bf16[32,2,2,32,128]{4,3,2,1,0:T(8,128)(2,1)S(1)}, u32[]{:S(2)}, u32[]{:S(2)}) async-start(bf16[32,2,2,32,128]{4,3,2,1,0:T(8,128)(2,1)} %bitcast.12), calls=%async_computation | async-start | bytes 2097152 | tf_op jit(solution)/shard_map/all_to_all | solution.py:424
  78.6 39.0 %all-to-all-start.1 = ((bf16[32,2,2,32,128]{4,3,2,1,0:T(8,128)(2,1)}), bf16[32,2,2,32,128]{4,3,2,1,0:T(8,128)(2,1)S(1)}, u32[]{:S(2)}, u32[]{:S(2)}) async-start(bf16[32,2,2,32,128]{4,3,2,1,0:T(8,128)(2,1)} %bitcast.6), calls=%async_computation.1 | async-start | bytes 2097152 | tf_op jit(solution)/shard_map/all_to_all | solution.py:424
  85.0 16.4 %collective-permute-start = (f32[2,4,2,32,128]{4,3,2,1,0:T(8,128)S(1)}, f32[2,4,2,32,128]{4,3,2,1,0:T(8,128)S(1)}, u32[]{:S(2)}, u32[]{:S(2)}) collective-permute-start(f32[2,4,2,32,128]{4,3,2,1,0:T(8,128)S(1)} %get-tuple-element.30), channel_id=1, source_target_pairs={{0,2},{1,3},{2,0},{3,1},{4,6},{5,7},{6,4},{7,5},{8,10},{9,11},{10,... | collective-permute-start | bytes 786440 | tf_op jit(solution)/shard_map/ppermute | solution.py:397
  86.7 14.8 %collective-permute-start.1 = (f32[2,4,2,32,128]{4,3,2,1,0:T(8,128)S(1)}, f32[2,4,2,32,128]{4,3,2,1,0:T(8,128)S(1)}, u32[]{:S(2)}, u32[]{:S(2)}) collective-permute-start(f32[2,4,2,32,128]{4,3,2,1,0:T(8,128)S(1)} %get-tuple-element.31), channel_id=1, source_target_pairs={{0,4},{1,5},{2,6},{3,7},{4,0},{5,1},{6,2},{7,3},{8,12},{9,13},{10,... | collective-permute-start | bytes 786440 | tf_op jit(solution)/shard_map/ppermute | solution.py:397
  88.1 21.0 %collective-permute-start.2 = (f32[2,4,2,32,128]{4,3,2,1,0:T(8,128)S(1)}, f32[2,4,2,32,128]{4,3,2,1,0:T(8,128)S(1)}, u32[]{:S(2)}, u32[]{:S(2)}) collective-permute-start(f32[2,4,2,32,128]{4,3,2,1,0:T(8,128)S(1)} %get-tuple-element.32), channel_id=1, source_target_pairs={{0,6},{1,7},{2,4},{3,5},{4,2},{5,3},{6,0},{7,1},{8,14},{9,15},{10,... | collective-permute-start | bytes 786440 | tf_op jit(solution)/shard_map/ppermute | solution.py:397
  88.6 20.6 %collective-permute-start.3 = (f32[2,4,2,32,128]{4,3,2,1,0:T(8,128)S(1)}, f32[2,4,2,32,128]{4,3,2,1,0:T(8,128)S(1)}, u32[]{:S(2)}, u32[]{:S(2)}) collective-permute-start(f32[2,4,2,32,128]{4,3,2,1,0:T(8,128)S(1)} %get-tuple-element.29.refs_0_), channel_id=1, source_target_pairs={{0,1},{1,0},{2,3},{3,2},{4,5},{5,4},{6,7},{7,6},{8,9},{9,8},{10,11... | collective-permute-start | bytes 786440 | tf_op jit(solution)/shard_map/ppermute | solution.py:401
  101.4 7.8 %collective-permute-start.4 = (f32[2,4,2,32,128]{4,3,2,1,0:T(8,128)S(1)}, f32[2,4,2,32,128]{4,3,2,1,0:T(8,128)S(1)}, u32[]{:S(2)}, u32[]{:S(2)}) collective-permute-start(f32[2,4,2,32,128]{4,3,2,1,0:T(8,128)S(1)} %collective-permute-done.refs_1_), channel_id=1, source_target_pairs={{0,1},{1,0},{2,3},{3,2},{4,5},{5,4},{6,7},{7,6},{8,9},{9,8},{10,11... | collective-permute-start | bytes 786440 | tf_op jit(solution)/shard_map/ppermute | solution.py:401
  101.4 7.8 %collective-permute-start.5 = (f32[2,4,2,32,128]{4,3,2,1,0:T(8,128)S(1)}, f32[2,4,2,32,128]{4,3,2,1,0:T(8,128)S(1)}, u32[]{:S(2)}, u32[]{:S(2)}) collective-permute-start(f32[2,4,2,32,128]{4,3,2,1,0:T(8,128)S(1)} %collective-permute-done.1.refs_2_), channel_id=1, source_target_pairs={{0,1},{1,0},{2,3},{3,2},{4,5},{5,4},{6,7},{7,6},{8,9},{9,8},{10,11... | collective-permute-start | bytes 786440 | tf_op jit(solution)/shard_map/ppermute | solution.py:401
  109.2 1.5 collective-permute-start.6
  119.7 9.2 %collective-permute-start.10 = (f32[2,4,2,32,128]{4,3,2,1,0:T(8,128)S(1)}, f32[2,4,2,32,128]{4,3,2,1,0:T(8,128)S(1)}, u32[]{:S(2)}, u32[]{:S(2)}) collective-permute-start(f32[2,4,2,32,128]{4,3,2,1,0:T(8,128)S(1)} %get-tuple-element.40), channel_id=1, source_target_pairs={{0,2},{1,3},{2,0},{3,1},{4,6},{5,7},{6,4},{7,5},{8,10},{9,11},{10,... | collective-permute-start | bytes 786440 | tf_op jit(solution)/shard_map/ppermute | solution.py:397
  120.5 8.9 %collective-permute-start.11 = (f32[2,4,2,32,128]{4,3,2,1,0:T(8,128)S(1)}, f32[2,4,2,32,128]{4,3,2,1,0:T(8,128)S(1)}, u32[]{:S(2)}, u32[]{:S(2)}) collective-permute-start(f32[2,4,2,32,128]{4,3,2,1,0:T(8,128)S(1)} %get-tuple-element.41), channel_id=1, source_target_pairs={{0,4},{1,5},{2,6},{3,7},{4,0},{5,1},{6,2},{7,3},{8,12},{9,13},{10,... | collective-permute-start | bytes 786440 | tf_op jit(solution)/shard_map/ppermute | solution.py:397
  120.9 13.3 %collective-permute-start.12 = (f32[2,4,2,32,128]{4,3,2,1,0:T(8,128)S(1)}, f32[2,4,2,32,128]{4,3,2,1,0:T(8,128)S(1)}, u32[]{:S(2)}, u32[]{:S(2)}) collective-permute-start(f32[2,4,2,32,128]{4,3,2,1,0:T(8,128)S(1)} %get-tuple-element.42), channel_id=1, source_target_pairs={{0,6},{1,7},{2,4},{3,5},{4,2},{5,3},{6,0},{7,1},{8,14},{9,15},{10,... | collective-permute-start | bytes 786440 | tf_op jit(solution)/shard_map/ppermute | solution.py:397
  123.3 13.3 %collective-permute-start.13 = (f32[2,4,2,32,128]{4,3,2,1,0:T(8,128)S(1)}, f32[2,4,2,32,128]{4,3,2,1,0:T(8,128)S(1)}, u32[]{:S(2)}, u32[]{:S(2)}) collective-permute-start(f32[2,4,2,32,128]{4,3,2,1,0:T(8,128)S(1)} %get-tuple-element.39.refs_0_), channel_id=1, source_target_pairs={{0,1},{1,0},{2,3},{3,2},{4,5},{5,4},{6,7},{7,6},{8,9},{9,8},{10,11... | collective-permute-start | bytes 786440 | tf_op jit(solution)/shard_map/ppermute | solution.py:401
  128.9 8.8 %collective-permute-start.14 = (f32[2,4,2,32,128]{4,3,2,1,0:T(8,128)S(1)}, f32[2,4,2,32,128]{4,3,2,1,0:T(8,128)S(1)}, u32[]{:S(2)}, u32[]{:S(2)}) collective-permute-start(f32[2,4,2,32,128]{4,3,2,1,0:T(8,128)S(1)} %collective-permute-done.10.refs_1_), channel_id=1, source_target_pairs={{0,1},{1,0},{2,3},{3,2},{4,5},{5,4},{6,7},{7,6},{8,9},{9,8},{10,11... | collective-permute-start | bytes 786440 | tf_op jit(solution)/shard_map/ppermute | solution.py:401
  129.4 9.5 %collective-permute-start.15 = (f32[2,4,2,32,128]{4,3,2,1,0:T(8,128)S(1)}, f32[2,4,2,32,128]{4,3,2,1,0:T(8,128)S(1)}, u32[]{:S(2)}, u32[]{:S(2)}) collective-permute-start(f32[2,4,2,32,128]{4,3,2,1,0:T(8,128)S(1)} %collective-permute-done.11.refs_2_), channel_id=1, source_target_pairs={{0,1},{1,0},{2,3},{3,2},{4,5},{5,4},{6,7},{7,6},{8,9},{9,8},{10,11... | collective-permute-start | bytes 786440 | tf_op jit(solution)/shard_map/ppermute | solution.py:401
  134.2 4.7 %collective-permute-start.16 = (f32[2,4,2,32,128]{4,3,2,1,0:T(8,128)S(1)}, f32[2,4,2,32,128]{4,3,2,1,0:T(8,128)S(1)}, u32[]{:S(2)}, u32[]{:S(2)}) collective-permute-start(f32[2,4,2,32,128]{4,3,2,1,0:T(8,128)S(1)} %collective-permute-done.12.refs_3_), channel_id=1, source_target_pairs={{0,1},{1,0},{2,3},{3,2},{4,5},{5,4},{6,7},{7,6},{8,9},{9,8},{10,11... | collective-permute-start | bytes 786440 | tf_op jit(solution)/shard_map/ppermute | solution.py:401
  134.2 14.8 %collective-permute-start.7 = (f32[256,128]{1,0:T(8,128)S(1)}, f32[256,128]{1,0:T(8,128)S(1)}, u32[]{:S(2)}, u32[]{:S(2)}) collective-permute-start(f32[256,128]{1,0:T(8,128)S(1)} %get-tuple-element.34), channel_id=1, source_target_pairs={{0,8},{8,0},{16,24},{24,16},{1,9},{9,1},{17,25},{25,17},{2,10},{10... | collective-permute-start | bytes 393224 | tf_op jit(solution)/shard_map/ppermute | solution.py:390
  136.6 13.7 %collective-permute-start.8 = (f32[256,128]{1,0:T(8,128)S(1)}, f32[256,128]{1,0:T(8,128)S(1)}, u32[]{:S(2)}, u32[]{:S(2)}) collective-permute-start(f32[256,128]{1,0:T(8,128)S(1)} %get-tuple-element.35), channel_id=1, source_target_pairs={{0,16},{8,24},{16,0},{24,8},{1,17},{9,25},{17,1},{25,9},{2,18},{10... | collective-permute-start | bytes 393224 | tf_op jit(solution)/shard_map/ppermute | solution.py:390
  137.7 12.6 %collective-permute-start.9 = (f32[256,128]{1,0:T(8,128)S(1)}, f32[256,128]{1,0:T(8,128)S(1)}, u32[]{:S(2)}, u32[]{:S(2)}) collective-permute-start(f32[256,128]{1,0:T(8,128)S(1)} %get-tuple-element.36), channel_id=1, source_target_pairs={{0,24},{8,16},{16,8},{24,0},{1,25},{9,17},{17,9},{25,1},{2,26},{10... | collective-permute-start | bytes 393224 | tf_op jit(solution)/shard_map/ppermute | solution.py:390
  145.8 6.3 %collective-permute-start.17 = (f32[256,128]{1,0:T(8,128)S(1)}, f32[256,128]{1,0:T(8,128)S(1)}, u32[]{:S(2)}, u32[]{:S(2)}) collective-permute-start(f32[256,128]{1,0:T(8,128)S(1)} %get-tuple-element.44), channel_id=1, source_target_pairs={{0,8},{8,0},{16,24},{24,16},{1,9},{9,1},{17,25},{25,17},{2,10},{10... | collective-permute-start | bytes 393224 | tf_op jit(solution)/shard_map/ppermute | solution.py:390
  147.0 13.7 %collective-permute-start.18 = (f32[256,128]{1,0:T(8,128)S(1)}, f32[256,128]{1,0:T(8,128)S(1)}, u32[]{:S(2)}, u32[]{:S(2)}) collective-permute-start(f32[256,128]{1,0:T(8,128)S(1)} %get-tuple-element.45), channel_id=1, source_target_pairs={{0,16},{8,24},{16,0},{24,8},{1,17},{9,25},{17,1},{25,9},{2,18},{10... | collective-permute-start | bytes 393224 | tf_op jit(solution)/shard_map/ppermute | solution.py:390
  149.1 11.7 %collective-permute-start.19 = (f32[256,128]{1,0:T(8,128)S(1)}, f32[256,128]{1,0:T(8,128)S(1)}, u32[]{:S(2)}, u32[]{:S(2)}) collective-permute-start(f32[256,128]{1,0:T(8,128)S(1)} %get-tuple-element.46), channel_id=1, source_target_pairs={{0,24},{8,16},{16,8},{24,0},{1,25},{9,17},{17,9},{25,1},{2,26},{10... | collective-permute-start | bytes 393224 | tf_op jit(solution)/shard_map/ppermute | solution.py:390

commit v5 on v4

--- a/solution.py
+++ b/solution.py
@@ -71,25 +71,19 @@
     return (row == want).astype(jnp.bfloat16)
 
 
-def pack_kernel(n_seg, n_pair, chunk, x_ref, out_ref, x_buf, buf_ref, sems):
+def pack_kernel(n_seg, n_pair, chunk, x_ref, out_ref, buf_ref):
     band = x_ref.shape[1] // n_pair
-    copies = []
-    for p in range(n_pair):
-        at = pl.ds(p * band, band)
-        copies.append(
-            pltpu.make_async_copy(x_ref.at[:, at], x_buf.at[p], sems.at[p])
-        )
-        copies[-1].start()
     sel = selection(n_seg, chunk, x_ref.shape[2])
     rows = band // GROUPS
     for p in range(n_pair):
-        copies[p].wait()
         for ri in range(2):
             for part in range(sel.shape[1] // TILE):
                 lanes = slice(part * TILE, (part + 1) * TILE)
                 buf = buf_ref.at[p % 2, ri]
                 buf[...] = jnp.dot(
-                    x_buf[p, ri], sel[:, lanes], preferred_element_type=jnp.float32
+                    x_ref[ri, p * band : (p + 1) * band, :],
+                    sel[:, lanes],
+                    preferred_element_type=jnp.float32,
                 )
                 v = [buf[pl.ds(fb, rows, stride=GROUPS), :] for fb in range(GROUPS)]
                 v = transpose_groups(v)
@@ -105,13 +99,9 @@
     return pl.pallas_call(
         functools.partial(pack_kernel, n_seg, n_pair, chunk),
         out_shape=jax.ShapeDtypeStruct(shape, jnp.bfloat16),
-        in_specs=[pl.BlockSpec(memory_space=pltpu.HBM)],
+        in_specs=[pl.BlockSpec(memory_space=pltpu.VMEM)],
         out_specs=pl.BlockSpec(memory_space=pltpu.VMEM),
-        scratch_shapes=[
-            pltpu.VMEM((n_pair, 2, band, chans), jnp.bfloat16),
-            pltpu.VMEM((2, 2, band, TILE), jnp.float32),
-            pltpu.SemaphoreType.DMA((n_pair,)),
-        ],
+        scratch_shapes=[pltpu.VMEM((2, 2, band, TILE), jnp.float32)],
         name="pack",
         cost_estimate=SMALL,
     )(x)
@@ -177,12 +167,13 @@
 
 def dft_kernel(n_seg, n_pair, most, me_ref, tables_ref, *refs):
     ins, outs = refs[:n_pair], refs[n_pair : n_pair + n_seg]
-    held, sems = refs[n_pair + n_seg :][:4], refs[n_pair + n_seg + 4]
-    s32, shi, slo, y, zhi, zlo, sums, parts = refs[n_pair + n_seg + 5 :]
-    whi_ref, wlo_ref, t_ref, phase_ref = held
+    w_ref, phase_ref, t_ref, sems = refs[n_pair + n_seg :][:4]
+    whi_ref, wlo_ref, s32, shi, slo, y, zhi, zlo, sums, parts = refs[
+        n_pair + n_seg + 4 :
+    ]
     copies = []
     row = 0
-    for i, to in enumerate(held):
+    for i, to in enumerate((w_ref.at[0], w_ref.at[1], phase_ref, t_ref)):
         src = tables_ref.at[pl.ds(row, to.shape[0])]
         copies.append(pltpu.make_async_copy(src, to, sems.at[i]))
         copies[-1].start()
@@ -209,19 +200,23 @@
     copies[0].wait()
     copies[1].wait()
     for ri in range(2):
+        hi = w_ref[ri].astype(jnp.bfloat16)
+        n = slice(ri * half_h, (ri + 1) * half_h)
+        whi_ref[:, n] = hi
+        wlo_ref[:, n] = (w_ref[ri] - hi.astype(jnp.float32)).astype(jnp.bfloat16)
+    for ri in range(2):
         n = slice(ri * wide, (ri + 1) * wide)
         y[ri] = (
             jnp.dot(wlo_ref[...], shi[:, n], preferred_element_type=jnp.float32)
             + jnp.dot(whi_ref[...], slo[:, n], preferred_element_type=jnp.float32)
         ) + jnp.dot(whi_ref[...], shi[:, n], preferred_element_type=jnp.float32)
-    copies[3].wait()
+    copies[2].wait()
     period = y.shape[1]
     step_rows = 64
     for b in range(period // step_rows):
         at = slice(b * step_rows, (b + 1) * step_rows)
-        turn = phase_ref[at, :].astype(jnp.float32)
-        c = turn[:, :TILE] + turn[:, TILE : 2 * TILE]
-        d = turn[:, 2 * TILE : 3 * TILE] + turn[:, 3 * TILE :]
+        c = phase_ref[at, :TILE]
+        d = phase_ref[at, TILE:]
         for s in range(most):
             lanes = slice(s * TILE, (s + 1) * TILE)
             yr = y[0, at, lanes]
@@ -231,8 +226,9 @@
                 hi = z.astype(jnp.bfloat16)
                 zhi[at, to] = hi
                 zlo[at, to] = (z - hi.astype(jnp.float32)).astype(jnp.bfloat16)
-    copies[2].wait()
-    thi, tlo = t_ref[:, : sums.shape[1]], t_ref[:, sums.shape[1] :]
+    copies[3].wait()
+    thi = t_ref[...].astype(jnp.bfloat16)
+    tlo = (t_ref[...] - thi.astype(jnp.float32)).astype(jnp.bfloat16)
     sums[...] = (
         jnp.dot(zhi[...], tlo, preferred_element_type=jnp.float32)
         + jnp.dot(zlo[...], thi, preferred_element_type=jnp.float32)
@@ -254,17 +250,15 @@
         outs[k][...] = parts[jnp.bitwise_xor(me_ref[0], k)]
 
 
-def tables_kernel(most, turns, shift, whi_ref, wlo_ref, phase_ref, out_ref, t_ref, sems):
-    h = whi_ref.shape[0]
-    k = t_ref.shape[0]
+def tables_kernel(most, turns, shift, fixed_ref, out_ref, t_ref, sems):
+    used = fixed_ref.shape[0]
     copies = [
-        pltpu.make_async_copy(whi_ref, out_ref.at[pl.ds(0, h)], sems.at[0]),
-        pltpu.make_async_copy(wlo_ref, out_ref.at[pl.ds(h, h)], sems.at[1]),
-        pltpu.make_async_copy(phase_ref, out_ref.at[pl.ds(2 * h + k, h)], sems.at[2]),
-        pltpu.make_async_copy(t_ref, out_ref.at[pl.ds(2 * h, k)], sems.at[3]),
+        pltpu.make_async_copy(fixed_ref, out_ref.at[pl.ds(0, used)], sems.at[0]),
+        pltpu.make_async_copy(
+            t_ref, out_ref.at[pl.ds(used, t_ref.shape[0])], sems.at[1]
+        ),
     ]
-    for copy in copies[:3]:
-        copy.start()
+    copies[0].start()
     shape = (most * TILE, turns * most * CC)
     row = lax.broadcasted_iota(jnp.int32, shape, 0)
     col = lax.broadcasted_iota(jnp.int32, shape, 1)
@@ -275,45 +269,36 @@
         e = jnp.bitwise_and(eighths + 2 * ri, 7)
         size = jnp.where(e % 4 == 2, 0.0, jnp.where(e % 2 == 0, 1.0, diagonal))
         t = jnp.where(same, jnp.where((e > 2) & (e < 6), -size, size), 0.0)
-        at = slice(ri * most * TILE, (ri + 1) * most * TILE)
-        hi = t.astype(jnp.bfloat16)
-        t_ref[at, : shape[1]] = hi
-        t_ref[at, shape[1] :] = (t - hi.astype(jnp.float32)).astype(jnp.bfloat16)
-    copies[3].start()
+        t_ref[ri * most * TILE : (ri + 1) * most * TILE, :] = t
+    copies[1].start()
     for copy in copies:
         copy.wait()
-
-
-def split(x):
-    hi = x.astype(np.float32).astype(jnp.bfloat16)
-    return hi, (x - hi.astype(np.float64)).astype(np.float32).astype(jnp.bfloat16)
 
 
 def make_tables(freq, most):
     h = freq // GROUPS
     period = 2 * h
     turns = LAG // period
+    width = turns * most * CC
     angle = np.arange(period)[:, None] * np.arange(h)[None, :] % period
     angle = angle * (2.0 * math.pi / period)
-    whi, wlo = split(np.concatenate([np.cos(angle), np.sin(angle)], 1))
     fb = np.arange(TILE) // CC
     phase = ((np.arange(period)[:, None] * fb[None, :]) % (2 * freq)) * (math.pi / freq)
     scale = 1.0 / math.sqrt(freq)
-    phase = np.concatenate(split(np.cos(phase) * scale) + split(np.sin(phase) * scale), 1)
-    hbm = pl.BlockSpec(memory_space=pltpu.HBM)
-    width = period
+    phase = np.concatenate([np.cos(phase), np.sin(phase)], 1) * scale
+    fixed = np.concatenate([np.cos(angle), np.sin(angle), phase]).astype(np.float32)
     return pl.pallas_call(
         functools.partial(tables_kernel, most, turns, LAG // 2 // period),
-        out_shape=jax.ShapeDtypeStruct((48 << 10, width), jnp.bfloat16),
-        in_specs=[hbm] * 3,
-        out_specs=hbm,
+        out_shape=jax.ShapeDtypeStruct((48 << 10, width), jnp.float32),
+        in_specs=[pl.BlockSpec(memory_space=pltpu.VMEM)],
+        out_specs=pl.BlockSpec(memory_space=pltpu.HBM),
         scratch_shapes=[
-            pltpu.VMEM((2 * most * TILE, width), jnp.bfloat16),
-            pltpu.SemaphoreType.DMA((4,)),
+            pltpu.VMEM((2 * most * TILE, width), jnp.float32),
+            pltpu.SemaphoreType.DMA((2,)),
         ],
         name="tables",
         cost_estimate=SMALL,
-    )(jnp.asarray(whi), jnp.asarray(wlo), jnp.asarray(phase))
+    )(jnp.asarray(fixed))
 
 
 def dft(me, tables, blocks, freq, n_seg, n_pair, most):
@@ -328,11 +313,12 @@
         in_specs=[smem, pl.BlockSpec(memory_space=pltpu.HBM)] + [vmem] * len(blocks),
         out_specs=[vmem] * n_seg,
         scratch_shapes=[
+            pltpu.VMEM((2, period, period // 2), jnp.float32),
+            pltpu.VMEM((period, 2 * TILE), jnp.float32),
+            pltpu.VMEM((2 * wide, LAG // period * most * CC), jnp.float32),
+            pltpu.SemaphoreType.DMA((4,)),
             pltpu.VMEM((period, period), jnp.bfloat16),
             pltpu.VMEM((period, period), jnp.bfloat16),
-            pltpu.VMEM((2 * wide, period), jnp.bfloat16),
-            pltpu.VMEM((period, 4 * TILE), jnp.bfloat16),
-            pltpu.SemaphoreType.DMA((4,)),
             pltpu.VMEM((2, period // 2, wide), jnp.float32),
             pltpu.VMEM((period, 2 * wide), jnp.bfloat16),
             pltpu.VMEM((period, 2 * wide), jnp.bfloat16),

time: 164 us -> 123 us (0.75)
  Pallas kernels: 81.7 us -> 32.7 us
  waiting for transfers between devices: 43 us -> 50.8 us
    pallas_call x1, Pallas kernels: 48.8 us -> 3.65 us  [make_tables(): pl.pallas_call(functools.partial(tables_kernel, most, turns, LAG // 2 //...]
    all_to_all x2, waiting for transfers between devices: 0.01 us -> 7.67 us  [body(): lax.all_to_all(sent.reshape(n_seg * n_pair, tiles, 2, rows, TILE), ('seg'...]
    pallas_call x2, Pallas kernels: 11.6 us -> 7.92 us  [pack(): pl.pallas_call(functools.partial(pack_kernel, n_seg, n_pair, chunk), out_...]
  transfers between devices with their start and end apart: 22 -> 22, of which waited for: 8 -> 9; matrix products, arithmetic and copies ran while one was open for 1% -> 1% of each run, Pallas kernels for 43% -> 19%
where the time goes in v5:
time: 123 us; the launch traced here: 122 us
  waiting for transfers between devices  50.8 us (41%)
  Pallas kernels  32.7 us (27%)
  starting transfers between devices  27.9 us (23%)
  blocking collectives  8.31 us (7%)
  between operations  1.47 us (1%)
    ppermute x6, waiting for transfers between devices, exchange_plane(): lax.ppermute(blocks[k], 'pair', [(i, i ^ 2 * k) for i in range(n_pair)])  31.1 us
    pallas_call x2, Pallas kernels, dft(): pl.pallas_call(functools.partial(dft_kernel, n_seg, n_pair, most), out_sh...  13.7 us
    all_to_all x2, starting transfers between devices, body(): lax.all_to_all(sent.reshape(n_seg * n_pair, tiles, 2, rows, TILE), ('seg'...  11.1 us
    ppermute x6, waiting for transfers between devices, exchange(): lax.ppermute(blocks[k], axis, [(i, i ^ k) for i in range(size)])  10.4 us
    ppermute x6, starting transfers between devices, exchange(): lax.ppermute(blocks[k], axis, [(i, i ^ k) for i in range(size)])  9.17 us
    unnamed x1, blocking collectives  8.31 us
    pallas_call x2, Pallas kernels, pack(): pl.pallas_call(functools.partial(pack_kernel, n_seg, n_pair, chunk), out_...  7.92 us
    all_to_all x2, waiting for transfers between devices, body(): lax.all_to_all(sent.reshape(n_seg * n_pair, tiles, 2, rows, TILE), ('seg'...  7.67 us
  transfers between devices with their start and end apart: 22, of which 9 were waited for; matrix products, arithmetic and copies ran while one was open for 1% of the time, Pallas kernels for 19%

profile of v5, /device:TPU:0, one launch (start us, length us, event | category | flops | bytes accessed | tf_op | source)
XLA Modules:
  0.0 122.5 jit_solution(14622709672797788592)
XLA Ops:
  0.0 3.9 %pack.3 = bf16[4,8,2,2,32,128]{5,4,3,2,1,0:T(8,128)(2,1)} custom-call(bf16[2,2048,256]{2,1,0:T(8,128)(2,1)} %bitcast.10), custom_call_target="tpu_custom_call" | custom-call | flops 1 | bytes 1 | tf_op jit(solution)/shard_map/pack/pallas_call | solution.py:99
  3.9 7.3 %all-to-all-start = ((bf16[32,2,2,32,128]{4,3,2,1,0:T(8,128)(2,1)}), bf16[32,2,2,32,128]{4,3,2,1,0:T(8,128)(2,1)S(1)}, u32[]{:S(2)}, u32[]{:S(2)}) async-start(bf16[32,2,2,32,128]{4,3,2,1,0:T(8,128)(2,1)} %bitcast.12), calls=%async_computation | async-start | bytes 2097152 | tf_op jit(solution)/shard_map/all_to_all | solution.py:410
  11.3 4.0 %pack.2 = bf16[4,8,2,2,32,128]{5,4,3,2,1,0:T(8,128)(2,1)} custom-call(bf16[2,2048,256]{2,1,0:T(8,128)(2,1)} %bitcast.11), custom_call_target="tpu_custom_call" | custom-call | flops 1 | bytes 1 | tf_op jit(solution)/shard_map/pack/pallas_call | solution.py:99
  15.2 3.7 %tables.1.tables_ref = f32[49152,256]{1,0:T(8,128)} custom-call(f32[1536,256]{1,0:T(8,128)} %constant.10.clone.fixed_ref), custom_call_target="tpu_custom_call" | custom-call | flops 1 | bytes 1 | tf_op jit(solution)/shard_map/tables/pallas_call | solution.py:290
  19.8 0.7 dynamic-slice
  21.4 8.3 %all-reduce = s32[72]{0:T(128)S(1)} all-reduce(s32[72]{0:T(128)S(1)} %dynamic-update-slice), channel_id=2, replica_groups=mesh['seg'=4,'pair'=8] {'pair'}, use_global_device_ids=true, to_apply=%add | all-reduce | flops 72 | bytes 576
  29.8 7.7 %all-to-all-done = bf16[32,2,2,32,128]{4,3,2,1,0:T(8,128)(2,1)S(1)} async-done(((bf16[32,2,2,32,128]{4,3,2,1,0:T(8,128)(2,1)}), bf16[32,2,2,32,128]{4,3,2,1,0:T(8,128)(2,1)S(1)}, u32[]{:S(2)}, u32[]{:S(2)}) %all-to-all-start) | async-done | bytes 1048608 | tf_op jit(solution)/shard_map/all_to_all | solution.py:410
  37.5 3.8 %all-to-all-start.1 = ((bf16[32,2,2,32,128]{4,3,2,1,0:T(8,128)(2,1)}), bf16[32,2,2,32,128]{4,3,2,1,0:T(8,128)(2,1)S(1)}, u32[]{:S(2)}, u32[]{:S(2)}) async-start(bf16[32,2,2,32,128]{4,3,2,1,0:T(8,128)(2,1)} %bitcast.6), calls=%async_computation.1 | async-start | bytes 2097152 | tf_op jit(solution)/shard_map/all_to_all | solution.py:410
  41.4 2.0 %stack.14 = (f32[2,4,2,32,128]{4,3,2,1,0:T(8,128)S(1)}, f32[2,4,2,32,128]{4,3,2,1,0:T(8,128)S(1)}, f32[2,4,2,32,128]{4,3,2,1,0:T(8,128)S(1)}, f32[2,4,2,32,128]{4,3,2,1,0:T(8,128)S(1)}) custom-call(s32[2]{0:T(128)S(1)} %pad_add_fusion.me_ref, s32[8,9]{1,0:T(8,128)S(1)} %reshape.24.table_ref, bf16[4,16,2,32,128]{4,3,2,1,0:T(8,128)(2,1)S(1)} %bitcast.9), custom_call_target="tpu_custom_call" | custom-call | flops 1 | bytes 1 | tf_op jit(solution)/shard_map/stack/pallas_call | solution.py:157
  43.4 1.7 %collective-permute-start = (f32[2,4,2,32,128]{4,3,2,1,0:T(8,128)S(1)}, f32[2,4,2,32,128]{4,3,2,1,0:T(8,128)S(1)}, u32[]{:S(2)}, u32[]{:S(2)}) collective-permute-start(f32[2,4,2,32,128]{4,3,2,1,0:T(8,128)S(1)} %get-tuple-element.30), channel_id=1, source_target_pairs={{0,2},{1,3},{2,0},{3,1},{4,6},{5,7},{6,4},{7,5},{8,10},{9,11},{10,... | collective-permute-start | bytes 786440 | tf_op jit(solution)/shard_map/ppermute | solution.py:383
  45.0 1.5 %collective-permute-start.1 = (f32[2,4,2,32,128]{4,3,2,1,0:T(8,128)S(1)}, f32[2,4,2,32,128]{4,3,2,1,0:T(8,128)S(1)}, u32[]{:S(2)}, u32[]{:S(2)}) collective-permute-start(f32[2,4,2,32,128]{4,3,2,1,0:T(8,128)S(1)} %get-tuple-element.31), channel_id=1, source_target_pairs={{0,4},{1,5},{2,6},{3,7},{4,0},{5,1},{6,2},{7,3},{8,12},{9,13},{10,... | collective-permute-start | bytes 786440 | tf_op jit(solution)/shard_map/ppermute | solution.py:383
  46.9 13.0 %collective-permute-done.refs_1_ = f32[2,4,2,32,128]{4,3,2,1,0:T(8,128)S(1)} collective-permute-done((f32[2,4,2,32,128]{4,3,2,1,0:T(8,128)S(1)}, f32[2,4,2,32,128]{4,3,2,1,0:T(8,128)S(1)}, u32[]{:S(2)}, u32[]{:S(2)}) %collective-permute-start) | collective-permute-done | bytes 262176 | tf_op jit(solution)/shard_map/ppermute | solution.py:383
  59.9 0.5 collective-permute-start.5
  60.4 7.2 %collective-permute-done.2.refs_3_ = f32[2,4,2,32,128]{4,3,2,1,0:T(8,128)S(1)} collective-permute-done((f32[2,4,2,32,128]{4,3,2,1,0:T(8,128)S(1)}, f32[2,4,2,32,128]{4,3,2,1,0:T(8,128)S(1)}, u32[]{:S(2)}, u32[]{:S(2)}) %collective-permute-start.2) | collective-permute-done | bytes 262176 | tf_op jit(solution)/shard_map/ppermute | solution.py:383
  67.7 1.5 %collective-permute-done.6.refs_7_ = f32[2,4,2,32,128]{4,3,2,1,0:T(8,128)S(1)} collective-permute-done((f32[2,4,2,32,128]{4,3,2,1,0:T(8,128)S(1)}, f32[2,4,2,32,128]{4,3,2,1,0:T(8,128)S(1)}, u32[]{:S(2)}, u32[]{:S(2)}) %collective-permute-start.6) | collective-permute-done | bytes 262176 | tf_op jit(solution)/shard_map/ppermute | solution.py:387
  69.2 6.9 %dft.2 = (f32[256,128]{1,0:T(8,128)S(1)}, f32[256,128]{1,0:T(8,128)S(1)}, f32[256,128]{1,0:T(8,128)S(1)}, f32[256,128]{1,0:T(8,128)S(1)}) custom-call(s32[2]{0:T(128)S(1)} %pad_add_fusion.me_ref, f32[49152,256]{1,0:T(8,128)} %tables.1.tables_ref, f32[2,4,2,32,128]{4,3,2,1,0:T(8,128)S(1)} %get-tuple-element.29.refs_0_, ...), custom_call_target="tpu_custom_call" | custom-call | flops 1 | bytes 1 | tf_op jit(solution)/shard_map/dft/pallas_call | solution.py:310
  76.1 2.0 %stack.15 = (f32[2,4,2,32,128]{4,3,2,1,0:T(8,128)S(1)}, f32[2,4,2,32,128]{4,3,2,1,0:T(8,128)S(1)}, f32[2,4,2,32,128]{4,3,2,1,0:T(8,128)S(1)}, f32[2,4,2,32,128]{4,3,2,1,0:T(8,128)S(1)}) custom-call(s32[2]{0:T(128)S(1)} %pad_add_fusion.me_ref, s32[8,9]{1,0:T(8,128)S(1)} %reshape.24.table_ref, bf16[4,16,2,32,128]{4,3,2,1,0:T(8,128)(2,1)S(1)} %bitcast.8), custom_call_target="tpu_custom_call" | custom-call | flops 1 | bytes 1 | tf_op jit(solution)/shard_map/stack/pallas_call | solution.py:157
  78.1 0.8 collective-permute-start.10
  79.2 2.4 %collective-permute-start.12 = (f32[2,4,2,32,128]{4,3,2,1,0:T(8,128)S(1)}, f32[2,4,2,32,128]{4,3,2,1,0:T(8,128)S(1)}, u32[]{:S(2)}, u32[]{:S(2)}) collective-permute-start(f32[2,4,2,32,128]{4,3,2,1,0:T(8,128)S(1)} %get-tuple-element.42), channel_id=1, source_target_pairs={{0,6},{1,7},{2,4},{3,5},{4,2},{5,3},{6,0},{7,1},{8,14},{9,15},{10,... | collective-permute-start | bytes 786440 | tf_op jit(solution)/shard_map/ppermute | solution.py:383
  81.6 5.7 %collective-permute-done.10.refs_1_ = f32[2,4,2,32,128]{4,3,2,1,0:T(8,128)S(1)} collective-permute-done((f32[2,4,2,32,128]{4,3,2,1,0:T(8,128)S(1)}, f32[2,4,2,32,128]{4,3,2,1,0:T(8,128)S(1)}, u32[]{:S(2)}, u32[]{:S(2)}) %collective-permute-start.10) | collective-permute-done | bytes 262176 | tf_op jit(solution)/shard_map/ppermute | solution.py:383
  87.3 0.5 collective-permute-done.11.refs_2_
  87.8 4.8 %collective-permute-done.12.refs_3_ = f32[2,4,2,32,128]{4,3,2,1,0:T(8,128)S(1)} collective-permute-done((f32[2,4,2,32,128]{4,3,2,1,0:T(8,128)S(1)}, f32[2,4,2,32,128]{4,3,2,1,0:T(8,128)S(1)}, u32[]{:S(2)}, u32[]{:S(2)}) %collective-permute-start.12) | collective-permute-done | bytes 262176 | tf_op jit(solution)/shard_map/ppermute | solution.py:383
  92.6 2.3 %collective-permute-start.7 = (f32[256,128]{1,0:T(8,128)S(1)}, f32[256,128]{1,0:T(8,128)S(1)}, u32[]{:S(2)}, u32[]{:S(2)}) collective-permute-start(f32[256,128]{1,0:T(8,128)S(1)} %get-tuple-element.34), channel_id=1, source_target_pairs={{0,8},{8,0},{16,24},{24,16},{1,9},{9,1},{17,25},{25,17},{2,10},{10... | collective-permute-start | bytes 393224 | tf_op jit(solution)/shard_map/ppermute | solution.py:376
  94.9 1.2 collective-permute-start.8
  96.1 1.2 %collective-permute-start.9 = (f32[256,128]{1,0:T(8,128)S(1)}, f32[256,128]{1,0:T(8,128)S(1)}, u32[]{:S(2)}, u32[]{:S(2)}) collective-permute-start(f32[256,128]{1,0:T(8,128)S(1)} %get-tuple-element.36), channel_id=1, source_target_pairs={{0,24},{8,16},{16,8},{24,0},{1,25},{9,17},{17,9},{25,1},{2,26},{10... | collective-permute-start | bytes 393224 | tf_op jit(solution)/shard_map/ppermute | solution.py:376
  97.3 6.9 %dft.3 = (f32[256,128]{1,0:T(8,128)S(1)}, f32[256,128]{1,0:T(8,128)S(1)}, f32[256,128]{1,0:T(8,128)S(1)}, f32[256,128]{1,0:T(8,128)S(1)}) custom-call(s32[2]{0:T(128)S(1)} %pad_add_fusion.me_ref, f32[49152,256]{1,0:T(8,128)} %tables.1.tables_ref, f32[2,4,2,32,128]{4,3,2,1,0:T(8,128)S(1)} %get-tuple-element.39.refs_0_, ...), custom_call_target="tpu_custom_call" | custom-call | flops 1 | bytes 1 | tf_op jit(solution)/shard_map/dft/pallas_call | solution.py:310
  104.2 1.2 collective-permute-start.17
  105.4 2.1 %collective-permute-start.18 = (f32[256,128]{1,0:T(8,128)S(1)}, f32[256,128]{1,0:T(8,128)S(1)}, u32[]{:S(2)}, u32[]{:S(2)}) collective-permute-start(f32[256,128]{1,0:T(8,128)S(1)} %get-tuple-element.45), channel_id=1, source_target_pairs={{0,16},{8,24},{16,0},{24,8},{1,17},{9,25},{17,1},{25,9},{2,18},{10... | collective-permute-start | bytes 393224 | tf_op jit(solution)/shard_map/ppermute | solution.py:376
  107.4 1.2 %collective-permute-start.19 = (f32[256,128]{1,0:T(8,128)S(1)}, f32[256,128]{1,0:T(8,128)S(1)}, u32[]{:S(2)}, u32[]{:S(2)}) collective-permute-start(f32[256,128]{1,0:T(8,128)S(1)} %get-tuple-element.46), channel_id=1, source_target_pairs={{0,24},{8,16},{16,8},{24,0},{1,25},{9,17},{17,9},{25,1},{2,26},{10... | collective-permute-start | bytes 393224 | tf_op jit(solution)/shard_map/ppermute | solution.py:376
  108.7 1.9 %collective-permute-done.17.refs_5_ = f32[256,128]{1,0:T(8,128)S(1)} collective-permute-done((f32[256,128]{1,0:T(8,128)S(1)}, f32[256,128]{1,0:T(8,128)S(1)}, u32[]{:S(2)}, u32[]{:S(2)}) %collective-permute-start.17) | collective-permute-done | bytes 131104 | tf_op jit(solution)/shard_map/ppermute | solution.py:376
  110.5 8.6 %collective-permute-done.18.refs_6_ = f32[256,128]{1,0:T(8,128)S(1)} collective-permute-done((f32[256,128]{1,0:T(8,128)S(1)}, f32[256,128]{1,0:T(8,128)S(1)}, u32[]{:S(2)}, u32[]{:S(2)}) %collective-permute-start.18) | collective-permute-done | bytes 131104 | tf_op jit(solution)/shard_map/ppermute | solution.py:376
  119.1 3.4 %unpack.1 = f32[512,4,128]{2,1,0:T(4,128)} custom-call(s32[2]{0:T(128)S(1)} %pad_add_fusion.me_ref, f32[256,128]{1,0:T(8,128)S(1)} %get-tuple-element.33.refs_0_, f32[256,128]{1,0:T(8,128)S(1)} %collective-permute-done.7.refs_1_, f32[256,128]{1,0:T(8,128)S(1)} %collective-permute-done.8.refs_2_, f32[256,128]{1,0:T(8,128)S(1)} %collective-permute-done.9.refs_3_, ...), custom_call_target="tpu_custom_call" | custom-call | flops 1 | bytes 1 | tf_op jit(solution)/shard_map/unpack/pallas_call | solution.py:362
  (33 shorter events, 1.5 us)
Async XLA Ops:
  3.9 33.5 %all-to-all-start = ((bf16[32,2,2,32,128]{4,3,2,1,0:T(8,128)(2,1)}), bf16[32,2,2,32,128]{4,3,2,1,0:T(8,128)(2,1)S(1)}, u32[]{:S(2)}, u32[]{:S(2)}) async-start(bf16[32,2,2,32,128]{4,3,2,1,0:T(8,128)(2,1)} %bitcast.12), calls=%async_computation | async-start | bytes 2097152 | tf_op jit(solution)/shard_map/all_to_all | solution.py:410
  15.2 4.3 %copy-start = (s32[4,2]{0,1:T(2,128)S(1)}, s32[4,2]{0,1:T(2,128)}, u32[]{:S(2)}) copy-start(s32[4,2]{0,1:T(2,128)} %param.5) | copy-start | bytes 100
  15.2 4.6 %copy-start.1 = (u32[32]{0:T(128)S(1)}, u32[32]{0:T(128)}, u32[]{:S(2)}) copy-start(u32[32]{0:T(128)} %constant.16) | copy-start | bytes 388
  37.5 38.6 %all-to-all-start.1 = ((bf16[32,2,2,32,128]{4,3,2,1,0:T(8,128)(2,1)}), bf16[32,2,2,32,128]{4,3,2,1,0:T(8,128)(2,1)S(1)}, u32[]{:S(2)}, u32[]{:S(2)}) async-start(bf16[32,2,2,32,128]{4,3,2,1,0:T(8,128)(2,1)} %bitcast.6), calls=%async_computation.1 | async-start | bytes 2097152 | tf_op jit(solution)/shard_map/all_to_all | solution.py:410
  43.4 16.5 %collective-permute-start = (f32[2,4,2,32,128]{4,3,2,1,0:T(8,128)S(1)}, f32[2,4,2,32,128]{4,3,2,1,0:T(8,128)S(1)}, u32[]{:S(2)}, u32[]{:S(2)}) collective-permute-start(f32[2,4,2,32,128]{4,3,2,1,0:T(8,128)S(1)} %get-tuple-element.30), channel_id=1, source_target_pairs={{0,2},{1,3},{2,0},{3,1},{4,6},{5,7},{6,4},{7,5},{8,10},{9,11},{10,... | collective-permute-start | bytes 786440 | tf_op jit(solution)/shard_map/ppermute | solution.py:383
  45.0 14.9 %collective-permute-start.1 = (f32[2,4,2,32,128]{4,3,2,1,0:T(8,128)S(1)}, f32[2,4,2,32,128]{4,3,2,1,0:T(8,128)S(1)}, u32[]{:S(2)}, u32[]{:S(2)}) collective-permute-start(f32[2,4,2,32,128]{4,3,2,1,0:T(8,128)S(1)} %get-tuple-element.31), channel_id=1, source_target_pairs={{0,4},{1,5},{2,6},{3,7},{4,0},{5,1},{6,2},{7,3},{8,12},{9,13},{10,... | collective-permute-start | bytes 786440 | tf_op jit(solution)/shard_map/ppermute | solution.py:383
  46.5 21.1 %collective-permute-start.2 = (f32[2,4,2,32,128]{4,3,2,1,0:T(8,128)S(1)}, f32[2,4,2,32,128]{4,3,2,1,0:T(8,128)S(1)}, u32[]{:S(2)}, u32[]{:S(2)}) collective-permute-start(f32[2,4,2,32,128]{4,3,2,1,0:T(8,128)S(1)} %get-tuple-element.32), channel_id=1, source_target_pairs={{0,6},{1,7},{2,4},{3,5},{4,2},{5,3},{6,0},{7,1},{8,14},{9,15},{10,... | collective-permute-start | bytes 786440 | tf_op jit(solution)/shard_map/ppermute | solution.py:383
  46.9 20.7 %collective-permute-start.3 = (f32[2,4,2,32,128]{4,3,2,1,0:T(8,128)S(1)}, f32[2,4,2,32,128]{4,3,2,1,0:T(8,128)S(1)}, u32[]{:S(2)}, u32[]{:S(2)}) collective-permute-start(f32[2,4,2,32,128]{4,3,2,1,0:T(8,128)S(1)} %get-tuple-element.29.refs_0_), channel_id=1, source_target_pairs={{0,1},{1,0},{2,3},{3,2},{4,5},{5,4},{6,7},{7,6},{8,9},{9,8},{10,11... | collective-permute-start | bytes 786440 | tf_op jit(solution)/shard_map/ppermute | solution.py:387
  59.9 7.8 %collective-permute-start.4 = (f32[2,4,2,32,128]{4,3,2,1,0:T(8,128)S(1)}, f32[2,4,2,32,128]{4,3,2,1,0:T(8,128)S(1)}, u32[]{:S(2)}, u32[]{:S(2)}) collective-permute-start(f32[2,4,2,32,128]{4,3,2,1,0:T(8,128)S(1)} %collective-permute-done.refs_1_), channel_id=1, source_target_pairs={{0,1},{1,0},{2,3},{3,2},{4,5},{5,4},{6,7},{7,6},{8,9},{9,8},{10,11... | collective-permute-start | bytes 786440 | tf_op jit(solution)/shard_map/ppermute | solution.py:387
  59.9 7.8 %collective-permute-start.5 = (f32[2,4,2,32,128]{4,3,2,1,0:T(8,128)S(1)}, f32[2,4,2,32,128]{4,3,2,1,0:T(8,128)S(1)}, u32[]{:S(2)}, u32[]{:S(2)}) collective-permute-start(f32[2,4,2,32,128]{4,3,2,1,0:T(8,128)S(1)} %collective-permute-done.1.refs_2_), channel_id=1, source_target_pairs={{0,1},{1,0},{2,3},{3,2},{4,5},{5,4},{6,7},{7,6},{8,9},{9,8},{10,11... | collective-permute-start | bytes 786440 | tf_op jit(solution)/shard_map/ppermute | solution.py:387
  67.6 1.5 %collective-permute-start.6 = (f32[2,4,2,32,128]{4,3,2,1,0:T(8,128)S(1)}, f32[2,4,2,32,128]{4,3,2,1,0:T(8,128)S(1)}, u32[]{:S(2)}, u32[]{:S(2)}) collective-permute-start(f32[2,4,2,32,128]{4,3,2,1,0:T(8,128)S(1)} %collective-permute-done.2.refs_3_), channel_id=1, source_target_pairs={{0,1},{1,0},{2,3},{3,2},{4,5},{5,4},{6,7},{7,6},{8,9},{9,8},{10,11... | collective-permute-start | bytes 786440 | tf_op jit(solution)/shard_map/ppermute | solution.py:387
  78.1 9.2 %collective-permute-start.10 = (f32[2,4,2,32,128]{4,3,2,1,0:T(8,128)S(1)}, f32[2,4,2,32,128]{4,3,2,1,0:T(8,128)S(1)}, u32[]{:S(2)}, u32[]{:S(2)}) collective-permute-start(f32[2,4,2,32,128]{4,3,2,1,0:T(8,128)S(1)} %get-tuple-element.40), channel_id=1, source_target_pairs={{0,2},{1,3},{2,0},{3,1},{4,6},{5,7},{6,4},{7,5},{8,10},{9,11},{10,... | collective-permute-start | bytes 786440 | tf_op jit(solution)/shard_map/ppermute | solution.py:383
  78.9 8.9 %collective-permute-start.11 = (f32[2,4,2,32,128]{4,3,2,1,0:T(8,128)S(1)}, f32[2,4,2,32,128]{4,3,2,1,0:T(8,128)S(1)}, u32[]{:S(2)}, u32[]{:S(2)}) collective-permute-start(f32[2,4,2,32,128]{4,3,2,1,0:T(8,128)S(1)} %get-tuple-element.41), channel_id=1, source_target_pairs={{0,4},{1,5},{2,6},{3,7},{4,0},{5,1},{6,2},{7,3},{8,12},{9,13},{10,... | collective-permute-start | bytes 786440 | tf_op jit(solution)/shard_map/ppermute | solution.py:383
  79.2 13.4 %collective-permute-start.12 = (f32[2,4,2,32,128]{4,3,2,1,0:T(8,128)S(1)}, f32[2,4,2,32,128]{4,3,2,1,0:T(8,128)S(1)}, u32[]{:S(2)}, u32[]{:S(2)}) collective-permute-start(f32[2,4,2,32,128]{4,3,2,1,0:T(8,128)S(1)} %get-tuple-element.42), channel_id=1, source_target_pairs={{0,6},{1,7},{2,4},{3,5},{4,2},{5,3},{6,0},{7,1},{8,14},{9,15},{10,... | collective-permute-start | bytes 786440 | tf_op jit(solution)/shard_map/ppermute | solution.py:383
  81.6 13.3 %collective-permute-start.13 = (f32[2,4,2,32,128]{4,3,2,1,0:T(8,128)S(1)}, f32[2,4,2,32,128]{4,3,2,1,0:T(8,128)S(1)}, u32[]{:S(2)}, u32[]{:S(2)}) collective-permute-start(f32[2,4,2,32,128]{4,3,2,1,0:T(8,128)S(1)} %get-tuple-element.39.refs_0_), channel_id=1, source_target_pairs={{0,1},{1,0},{2,3},{3,2},{4,5},{5,4},{6,7},{7,6},{8,9},{9,8},{10,11... | collective-permute-start | bytes 786440 | tf_op jit(solution)/shard_map/ppermute | solution.py:387
  87.3 8.8 %collective-permute-start.14 = (f32[2,4,2,32,128]{4,3,2,1,0:T(8,128)S(1)}, f32[2,4,2,32,128]{4,3,2,1,0:T(8,128)S(1)}, u32[]{:S(2)}, u32[]{:S(2)}) collective-permute-start(f32[2,4,2,32,128]{4,3,2,1,0:T(8,128)S(1)} %collective-permute-done.10.refs_1_), channel_id=1, source_target_pairs={{0,1},{1,0},{2,3},{3,2},{4,5},{5,4},{6,7},{7,6},{8,9},{9,8},{10,11... | collective-permute-start | bytes 786440 | tf_op jit(solution)/shard_map/ppermute | solution.py:387
  87.8 9.5 %collective-permute-start.15 = (f32[2,4,2,32,128]{4,3,2,1,0:T(8,128)S(1)}, f32[2,4,2,32,128]{4,3,2,1,0:T(8,128)S(1)}, u32[]{:S(2)}, u32[]{:S(2)}) collective-permute-start(f32[2,4,2,32,128]{4,3,2,1,0:T(8,128)S(1)} %collective-permute-done.11.refs_2_), channel_id=1, source_target_pairs={{0,1},{1,0},{2,3},{3,2},{4,5},{5,4},{6,7},{7,6},{8,9},{9,8},{10,11... | collective-permute-start | bytes 786440 | tf_op jit(solution)/shard_map/ppermute | solution.py:387
  92.6 4.7 %collective-permute-start.16 = (f32[2,4,2,32,128]{4,3,2,1,0:T(8,128)S(1)}, f32[2,4,2,32,128]{4,3,2,1,0:T(8,128)S(1)}, u32[]{:S(2)}, u32[]{:S(2)}) collective-permute-start(f32[2,4,2,32,128]{4,3,2,1,0:T(8,128)S(1)} %collective-permute-done.12.refs_3_), channel_id=1, source_target_pairs={{0,1},{1,0},{2,3},{3,2},{4,5},{5,4},{6,7},{7,6},{8,9},{9,8},{10,11... | collective-permute-start | bytes 786440 | tf_op jit(solution)/shard_map/ppermute | solution.py:387
  92.6 14.8 %collective-permute-start.7 = (f32[256,128]{1,0:T(8,128)S(1)}, f32[256,128]{1,0:T(8,128)S(1)}, u32[]{:S(2)}, u32[]{:S(2)}) collective-permute-start(f32[256,128]{1,0:T(8,128)S(1)} %get-tuple-element.34), channel_id=1, source_target_pairs={{0,8},{8,0},{16,24},{24,16},{1,9},{9,1},{17,25},{25,17},{2,10},{10... | collective-permute-start | bytes 393224 | tf_op jit(solution)/shard_map/ppermute | solution.py:376
  94.9 13.7 %collective-permute-start.8 = (f32[256,128]{1,0:T(8,128)S(1)}, f32[256,128]{1,0:T(8,128)S(1)}, u32[]{:S(2)}, u32[]{:S(2)}) collective-permute-start(f32[256,128]{1,0:T(8,128)S(1)} %get-tuple-element.35), channel_id=1, source_target_pairs={{0,16},{8,24},{16,0},{24,8},{1,17},{9,25},{17,1},{25,9},{2,18},{10... | collective-permute-start | bytes 393224 | tf_op jit(solution)/shard_map/ppermute | solution.py:376
  96.1 12.6 %collective-permute-start.9 = (f32[256,128]{1,0:T(8,128)S(1)}, f32[256,128]{1,0:T(8,128)S(1)}, u32[]{:S(2)}, u32[]{:S(2)}) collective-permute-start(f32[256,128]{1,0:T(8,128)S(1)} %get-tuple-element.36), channel_id=1, source_target_pairs={{0,24},{8,16},{16,8},{24,0},{1,25},{9,17},{17,9},{25,1},{2,26},{10... | collective-permute-start | bytes 393224 | tf_op jit(solution)/shard_map/ppermute | solution.py:376
  104.2 6.3 %collective-permute-start.17 = (f32[256,128]{1,0:T(8,128)S(1)}, f32[256,128]{1,0:T(8,128)S(1)}, u32[]{:S(2)}, u32[]{:S(2)}) collective-permute-start(f32[256,128]{1,0:T(8,128)S(1)} %get-tuple-element.44), channel_id=1, source_target_pairs={{0,8},{8,0},{16,24},{24,16},{1,9},{9,1},{17,25},{25,17},{2,10},{10... | collective-permute-start | bytes 393224 | tf_op jit(solution)/shard_map/ppermute | solution.py:376
  105.4 13.7 %collective-permute-start.18 = (f32[256,128]{1,0:T(8,128)S(1)}, f32[256,128]{1,0:T(8,128)S(1)}, u32[]{:S(2)}, u32[]{:S(2)}) collective-permute-start(f32[256,128]{1,0:T(8,128)S(1)} %get-tuple-element.45), channel_id=1, source_target_pairs={{0,16},{8,24},{16,0},{24,8},{1,17},{9,25},{17,1},{25,9},{2,18},{10... | collective-permute-start | bytes 393224 | tf_op jit(solution)/shard_map/ppermute | solution.py:376
  107.4 11.7 %collective-permute-start.19 = (f32[256,128]{1,0:T(8,128)S(1)}, f32[256,128]{1,0:T(8,128)S(1)}, u32[]{:S(2)}, u32[]{:S(2)}) collective-permute-start(f32[256,128]{1,0:T(8,128)S(1)} %get-tuple-element.46), channel_id=1, source_target_pairs={{0,24},{8,16},{16,8},{24,0},{1,25},{9,17},{17,9},{25,1},{2,26},{10... | collective-permute-start | bytes 393224 | tf_op jit(solution)/shard_map/ppermute | solution.py:376

commit v6 on v5

--- a/solution.py
+++ b/solution.py
@@ -22,6 +22,33 @@
 
 def shift_groups(x, by):
     return pltpu.roll(x, (by * CC) % TILE, x.ndim - 1)
+
+
+def top_exponent(largest):
+    return jnp.maximum(jnp.floor(jnp.log2(jnp.maximum(largest, 1e-36))), -100.0)
+
+
+def encode(a, b, top):
+    m = jnp.maximum(jnp.maximum(jnp.abs(a), jnp.abs(b)), 1e-36)
+    e = jnp.floor(jnp.log2(m))
+    e = jnp.minimum(jnp.maximum(jnp.maximum(e, top - 63.0), -110.0), top)
+    s = jnp.exp2(11.0 - e)
+    qa, qb = (
+        jnp.clip(jnp.floor(x * s + 0.5), -4095.0, 4095.0).astype(jnp.int32) + 4096
+        for x in (a, b)
+    )
+    field = (e - (top - 63.0)).astype(jnp.int32)
+    return (field << 26) | (qa << 13) | qb
+
+
+ZERO = (4096 << 13) | 4096
+
+
+def decode(code, top):
+    e = ((code >> 26) & 63).astype(jnp.float32) + (top - 63.0)
+    s = jnp.exp2(e - 11.0)
+    a, b = (((q & 8191) - 4096).astype(jnp.float32) * s for q in (code >> 13, code))
+    return a, b
 
 
 def transpose_groups(vectors):
@@ -107,62 +134,79 @@
     )(x)
 
 
-def stack_kernel(n_seg, n_pair, most, n_specs, me_ref, table_ref, *refs):
-    specs, out_refs = refs[:n_specs], refs[n_specs:]
-    parts = [r.at[g] for r in specs for g in range(r.shape[0])]
+def stack_kernel(n_seg, n_pair, most, me_ref, table_ref, spec_ref, *refs):
+    outs, (sum_ref, big_ref) = refs[:-2], refs[-2:]
+    rows = spec_ref.shape[3]
     inv = 1.0 / float(n_seg * n_seg)
+    big_ref[...] = jnp.zeros_like(big_ref)
     for k in range(n_pair):
         owner = jnp.bitwise_xor(me_ref[1], k)
         count = table_ref[owner, 2 * most]
-        out_ref = out_refs[k // 2].at[k % 2]
 
         def one(s, _):
             src = table_ref[owner, 2 * s]
             rcv = table_ref[owner, 2 * s + 1]
-
-            @pl.when(s < count)
-            def _():
-                lr = li = pr = pi = None
-                for g in range(n_seg):
-                    a0 = parts[g][src, 0].astype(jnp.float32)
-                    a1 = parts[g][src, 1].astype(jnp.float32)
-                    b0 = parts[g][rcv, 0].astype(jnp.float32)
-                    b1 = parts[g][rcv, 1].astype(jnp.float32)
-                    cr = a0 * b0 + a1 * b1
-                    ci = a1 * b0 - a0 * b1
-                    m = lax.rsqrt(cr * cr + ci * ci + 1.0)
-                    if g == 0:
-                        lr, li, pr, pi = cr, ci, cr * m, ci * m
-                    else:
-                        lr, li, pr, pi = lr + cr, li + ci, pr + cr * m, pi + ci * m
-                w = (pr * pr + pi * pi) * inv
-                out_ref[s, 0] = lr * w
-                out_ref[s, 1] = li * w
-
-            @pl.when(s >= count)
-            def _():
-                out_ref[s] = jnp.zeros(out_ref.shape[1:], jnp.float32)
-
+            lr = li = pr = pi = None
+            for g in range(n_seg):
+                a0 = spec_ref[g, src, 0].astype(jnp.float32)
+                a1 = spec_ref[g, src, 1].astype(jnp.float32)
+                b0 = spec_ref[g, rcv, 0].astype(jnp.float32)
+                b1 = spec_ref[g, rcv, 1].astype(jnp.float32)
+                cr = a0 * b0 + a1 * b1
+                ci = a1 * b0 - a0 * b1
+                m = lax.rsqrt(cr * cr + ci * ci + 1.0)
+                if g == 0:
+                    lr, li, pr, pi = cr, ci, cr * m, ci * m
+                else:
+                    lr, li, pr, pi = lr + cr, li + ci, pr + cr * m, pi + ci * m
+            w = (pr * pr + pi * pi) * inv
+            re, im = lr * w, li * w
+            sum_ref[k, s, 0] = re
+            sum_ref[k, s, 1] = im
+            big = jnp.maximum(jnp.abs(re), jnp.abs(im))
+            big_ref[...] = jnp.maximum(big_ref[...], big)
             return 0
 
-        lax.fori_loop(0, most, one, 0)
-
-
-def stacks(me, table, specs, cost, n_seg, n_pair, most):
-    rows = specs[0].shape[3]
-    arrays = n_pair // 2
-    shape = (n_pair // arrays, most, 2, rows, TILE)
+        lax.fori_loop(0, count, one, 0)
+    top = top_exponent(jnp.max(big_ref[...], keepdims=True))
+    for k in range(n_pair):
+        owner = jnp.bitwise_xor(me_ref[1], k)
+        count = table_ref[owner, 2 * most]
+        out_ref = outs[k // 2].at[k % 2]
+
+        def code(s, _):
+            at = pl.ds(pl.multiple_of(s * rows, rows), rows)
+            out_ref[at, :] = encode(sum_ref[k, s, 0], sum_ref[k, s, 1], top)
+            return 0
+
+        def dead(s, _):
+            at = pl.ds(pl.multiple_of(s * rows, rows), rows)
+            out_ref[at, :] = jnp.full((rows, TILE), ZERO, jnp.int32)
+            return 0
+
+        lax.fori_loop(0, count, code, 0)
+        lax.fori_loop(count, most, dead, 0)
+        out_ref[most * rows :, :] = jnp.broadcast_to(top, (8, TILE)).astype(jnp.int32)
+
+
+def stacks(me, table, spec, n_seg, n_pair, most):
+    rows = spec.shape[3]
+    shape = (2, most * rows + 8, TILE)
     smem = pl.BlockSpec(memory_space=pltpu.SMEM)
     vmem = pl.BlockSpec(memory_space=pltpu.VMEM)
     return pl.pallas_call(
-        functools.partial(stack_kernel, n_seg, n_pair, most, len(specs)),
-        out_shape=[jax.ShapeDtypeStruct(shape, jnp.float32)] * arrays,
-        in_specs=[smem, smem] + [vmem] * len(specs),
-        out_specs=[vmem] * arrays,
+        functools.partial(stack_kernel, n_seg, n_pair, most),
+        out_shape=[jax.ShapeDtypeStruct(shape, jnp.int32)] * (n_pair // 2),
+        in_specs=[smem, smem, vmem],
+        out_specs=[vmem] * (n_pair // 2),
+        scratch_shapes=[
+            pltpu.VMEM((n_pair, most, 2, rows, TILE), jnp.float32),
+            pltpu.VMEM((rows, TILE), jnp.float32),
+        ],
         name="stack",
-        compiler_params=pltpu.CompilerParams(vmem_limit_bytes=8 << 20),
-        cost_estimate=cost,
-    )(me, table, *specs)
+        compiler_params=pltpu.CompilerParams(vmem_limit_bytes=12 << 20),
+        cost_estimate=SMALL,
+    )(me, table, spec)
 
 
 def dft_kernel(n_seg, n_pair, most, me_ref, tables_ref, *refs):
@@ -178,16 +222,18 @@
         copies.append(pltpu.make_async_copy(src, to, sems.at[i]))
         copies[-1].start()
         row += to.shape[0]
-    rows = ins[0].shape[3]
+    rows = (ins[0].shape[1] - 8) // most
     half_h = whi_ref.shape[1] // 2
     wide = most * TILE
     for k in range(n_pair):
         band = jnp.bitwise_xor(me_ref[1], k)
         src = ins[k % 2 * (n_pair // 2) + k // 2].at[k % 2]
         at = pl.ds(pl.multiple_of(band * rows, rows), rows)
+        top = src[most * rows : most * rows + 1, :].astype(jnp.float32)
         for s in range(most):
+            pair = decode(src[s * rows : (s + 1) * rows, :], top)
             for ri in range(2):
-                s32[ri, at, s * TILE : (s + 1) * TILE] = src[s, ri]
+                s32[ri, at, s * TILE : (s + 1) * TILE] = pair[ri]
     for ri in range(2):
         full = s32[ri]
         hi = full.astype(jnp.bfloat16)
@@ -233,7 +279,8 @@
         jnp.dot(zhi[...], tlo, preferred_element_type=jnp.float32)
         + jnp.dot(zlo[...], thi, preferred_element_type=jnp.float32)
     ) + jnp.dot(zhi[...], thi, preferred_element_type=jnp.float32)
-    half = outs[0].shape[0]
+    half = parts.shape[1]
+    big = None
     first = lax.broadcasted_iota(jnp.int32, (half, TILE), 1) < TILE // 2
     for dest in range(n_seg):
         lag = dest * 2 * half
@@ -245,9 +292,15 @@
             high = pltpu.roll(high, TILE // 2, 1)
         else:
             low = pltpu.roll(low, TILE // 2, 1)
-        parts[dest] = jnp.where(first, low, high)
+        part = jnp.where(first, low, high)
+        parts[dest] = part
+        part = jnp.max(jnp.abs(part), axis=0, keepdims=True)
+        big = part if big is None else jnp.maximum(big, part)
+    top = top_exponent(jnp.max(big, keepdims=True))
     for k in range(n_seg):
-        outs[k][...] = parts[jnp.bitwise_xor(me_ref[0], k)]
+        part = parts[jnp.bitwise_xor(me_ref[0], k)]
+        outs[k][: half // 2, :] = encode(part[: half // 2], part[half // 2 :], top)
+        outs[k][half // 2 :, :] = jnp.broadcast_to(top, (8, TILE)).astype(jnp.int32)
 
 
 def tables_kernel(most, turns, shift, fixed_ref, out_ref, t_ref, sems):
@@ -309,7 +362,7 @@
     wide = most * TILE
     return pl.pallas_call(
         functools.partial(dft_kernel, n_seg, n_pair, most),
-        out_shape=[jax.ShapeDtypeStruct((half, TILE), jnp.float32)] * n_seg,
+        out_shape=[jax.ShapeDtypeStruct((half // 2 + 8, TILE), jnp.int32)] * n_seg,
         in_specs=[smem, pl.BlockSpec(memory_space=pltpu.HBM)] + [vmem] * len(blocks),
         out_specs=[vmem] * n_seg,
         scratch_shapes=[
@@ -337,11 +390,15 @@
 def unpack_kernel(n_seg, chunks, most, me_ref, *refs):
     ins = refs[: n_seg * chunks]
     out_ref, buf = refs[n_seg * chunks :]
-    half = ins[0].shape[0]
+    half = buf.shape[1]
     for k in range(n_seg):
         z = jnp.bitwise_xor(me_ref[0], k)
         for ch in range(chunks):
-            buf[z * chunks + ch] = ins[ch * n_seg + k][...]
+            src = ins[ch * n_seg + k]
+            top = src[half // 2 : half // 2 + 1, :].astype(jnp.float32)
+            low, high = decode(src[: half // 2, :], top)
+            buf[z * chunks + ch, : half // 2] = low
+            buf[z * chunks + ch, half // 2 :] = high
     step_rows = 16
 
     def one(b, _):
@@ -356,7 +413,7 @@
 
 
 def unpack(me, parts, n_seg, chunks, most):
-    half = parts[0].shape[0]
+    half = 2 * (parts[0].shape[0] - 8)
     smem = pl.BlockSpec(memory_space=pltpu.SMEM)
     vmem = pl.BlockSpec(memory_space=pltpu.VMEM)
     return pl.pallas_call(
@@ -417,7 +474,7 @@
         if lags is not None:
             got, _ = lax.optimization_barrier((got, lags))
         spec = got.reshape(n_seg, n_pair * tiles, 2, rows, TILE)
-        blocks = stacks(me, table, [spec], SMALL, n_seg, n_pair, most)
+        blocks = stacks(me, table, spec, n_seg, n_pair, most)
         blocks = exchange_plane(blocks, n_pair)
         lags = dft(me, tables, blocks, freq, n_seg, n_pair, most)
         done += exchange(lags, "seg", n_seg)

time: 123 us -> 108 us (0.88)
  waiting for transfers between devices: 50.8 us -> 33.7 us
  Pallas kernels: 32.7 us -> 34.5 us
    ppermute x6, waiting for transfers between devices: 31.1 us -> 19.3 us  [exchange_plane(): lax.ppermute(blocks[k], 'pair', [(i, i ^ 2 * k) for i in range(n_pair)])]
    ppermute x6, waiting for transfers between devices: 10.4 us -> 5.38 us  [exchange(): lax.ppermute(blocks[k], axis, [(i, i ^ k) for i in range(size)])]
  transfers between devices with their start and end apart: 22 -> 22, of which waited for: 9 -> 9; matrix products, arithmetic and copies ran while one was open for 1% -> 1% of each run, Pallas kernels for 19% -> 23%
where the time goes in v6:
time: 108 us; the launch traced here: 107 us
  Pallas kernels  34.5 us (32%)
  waiting for transfers between devices  33.7 us (31%)
  starting transfers between devices  27.9 us (26%)
  blocking collectives  8.31 us (8%)
  between operations  1.47 us (1%)
  local copies, waits for them, and re-layouts  1.17 us (1%)
    ppermute x6, waiting for transfers between devices, exchange_plane(): lax.ppermute(blocks[k], 'pair', [(i, i ^ 2 * k) for i in range(n_pair)])  19.3 us
    pallas_call x2, Pallas kernels, dft(): pl.pallas_call(functools.partial(dft_kernel, n_seg, n_pair, most), out_sh...  14.4 us
    all_to_all x2, starting transfers between devices, body(): lax.all_to_all(sent.reshape(n_seg * n_pair, tiles, 2, rows, TILE), ('seg'...  10.9 us
    ppermute x6, starting transfers between devices, exchange(): lax.ppermute(blocks[k], axis, [(i, i ^ k) for i in range(size)])  8.84 us
    unnamed x1, blocking collectives  8.31 us
    pallas_call x2, Pallas kernels, pack(): pl.pallas_call(functools.partial(pack_kernel, n_seg, n_pair, chunk), out_...  7.92 us
    all_to_all x2, waiting for transfers between devices, body(): lax.all_to_all(sent.reshape(n_seg * n_pair, tiles, 2, rows, TILE), ('seg'...  7.67 us
    ppermute x6, starting transfers between devices, exchange_plane(): lax.ppermute(blocks[k], 'pair', [(i, i ^ 2 * k) for i in range(n_pair)])  7.11 us
  transfers between devices with their start and end apart: 22, of which 9 were waited for; matrix products, arithmetic and copies ran while one was open for 1% of the time, Pallas kernels for 23%

profile of v6, /device:TPU:0, one launch (start us, length us, event | category | flops | bytes accessed | tf_op | source)
XLA Modules:
  0.0 107.2 jit_solution(2349464961503691484)
XLA Ops:
  0.0 3.9 %pack.3 = bf16[4,8,2,2,32,128]{5,4,3,2,1,0:T(8,128)(2,1)} custom-call(bf16[2,2048,256]{2,1,0:T(8,128)(2,1)} %bitcast.10), custom_call_target="tpu_custom_call" | custom-call | flops 1 | bytes 1 | tf_op jit(solution)/shard_map/pack/pallas_call | solution.py:126
  3.9 7.3 %all-to-all-start = ((bf16[32,2,2,32,128]{4,3,2,1,0:T(8,128)(2,1)}), bf16[32,2,2,32,128]{4,3,2,1,0:T(8,128)(2,1)S(1)}, u32[]{:S(2)}, u32[]{:S(2)}) async-start(bf16[32,2,2,32,128]{4,3,2,1,0:T(8,128)(2,1)} %bitcast.12), calls=%async_computation | async-start | bytes 2097152 | tf_op jit(solution)/shard_map/all_to_all | solution.py:467
  11.3 4.0 %pack.2 = bf16[4,8,2,2,32,128]{5,4,3,2,1,0:T(8,128)(2,1)} custom-call(bf16[2,2048,256]{2,1,0:T(8,128)(2,1)} %bitcast.11), custom_call_target="tpu_custom_call" | custom-call | flops 1 | bytes 1 | tf_op jit(solution)/shard_map/pack/pallas_call | solution.py:126
  15.2 3.7 %tables.1.tables_ref = f32[49152,256]{1,0:T(8,128)} custom-call(f32[1536,256]{1,0:T(8,128)} %constant.10.clone.fixed_ref), custom_call_target="tpu_custom_call" | custom-call | flops 1 | bytes 1 | tf_op jit(solution)/shard_map/tables/pallas_call | solution.py:343
  19.8 0.7 dynamic-slice
  21.4 8.3 %all-reduce = s32[72]{0:T(128)S(1)} all-reduce(s32[72]{0:T(128)S(1)} %dynamic-update-slice), channel_id=2, replica_groups=mesh['seg'=4,'pair'=8] {'pair'}, use_global_device_ids=true, to_apply=%add | all-reduce | flops 72 | bytes 576
  29.8 7.7 %all-to-all-done = bf16[32,2,2,32,128]{4,3,2,1,0:T(8,128)(2,1)S(1)} async-done(((bf16[32,2,2,32,128]{4,3,2,1,0:T(8,128)(2,1)}), bf16[32,2,2,32,128]{4,3,2,1,0:T(8,128)(2,1)S(1)}, u32[]{:S(2)}, u32[]{:S(2)}) %all-to-all-start) | async-done | bytes 1048608 | tf_op jit(solution)/shard_map/all_to_all | solution.py:467
  37.5 3.6 %all-to-all-start.1 = ((bf16[32,2,2,32,128]{4,3,2,1,0:T(8,128)(2,1)}), bf16[32,2,2,32,128]{4,3,2,1,0:T(8,128)(2,1)S(1)}, u32[]{:S(2)}, u32[]{:S(2)}) async-start(bf16[32,2,2,32,128]{4,3,2,1,0:T(8,128)(2,1)} %bitcast.6), calls=%async_computation.1 | async-start | bytes 2097152 | tf_op jit(solution)/shard_map/all_to_all | solution.py:467
  41.2 2.4 %stack.14 = (s32[2,136,128]{2,1,0:T(8,128)S(1)}, s32[2,136,128]{2,1,0:T(8,128)S(1)}, s32[2,136,128]{2,1,0:T(8,128)S(1)}, s32[2,136,128]{2,1,0:T(8,128)S(1)}) custom-call(s32[2]{0:T(128)S(1)} %pad_add_fusion.me_ref, s32[8,9]{1,0:T(8,128)S(1)} %reshape.24.table_ref, bf16[4,16,2,32,128]{4,3,2,1,0:T(8,128)(2,1)S(1)} %bitcast.9), custom_call_target="tpu_custom_call" | custom-call | flops 1 | bytes 1 | tf_op jit(solution)/shard_map/stack/pallas_call | solution.py:197
  43.6 1.8 %collective-permute-start = (s32[2,136,128]{2,1,0:T(8,128)S(1)}, s32[2,136,128]{2,1,0:T(8,128)S(1)}, u32[]{:S(2)}, u32[]{:S(2)}) collective-permute-start(s32[2,136,128]{2,1,0:T(8,128)S(1)} %get-tuple-element.30), channel_id=1, source_target_pairs={{0,2},{1,3},{2,0},{3,1},{4,6},{5,7},{6,4},{7,5},{8,10},{9,11},{10,... | collective-permute-start | bytes 417800 | tf_op jit(solution)/shard_map/ppermute | solution.py:440
  45.4 1.5 %collective-permute-start.1 = (s32[2,136,128]{2,1,0:T(8,128)S(1)}, s32[2,136,128]{2,1,0:T(8,128)S(1)}, u32[]{:S(2)}, u32[]{:S(2)}) collective-permute-start(s32[2,136,128]{2,1,0:T(8,128)S(1)} %get-tuple-element.31), channel_id=1, source_target_pairs={{0,4},{1,5},{2,6},{3,7},{4,0},{5,1},{6,2},{7,3},{8,12},{9,13},{10,... | collective-permute-start | bytes 417800 | tf_op jit(solution)/shard_map/ppermute | solution.py:440
  47.2 8.9 %collective-permute-done.refs_1_ = s32[2,136,128]{2,1,0:T(8,128)S(1)} collective-permute-done((s32[2,136,128]{2,1,0:T(8,128)S(1)}, s32[2,136,128]{2,1,0:T(8,128)S(1)}, u32[]{:S(2)}, u32[]{:S(2)}) %collective-permute-start) | collective-permute-done | bytes 139296 | tf_op jit(solution)/shard_map/ppermute | solution.py:440
  56.1 0.5 collective-permute-start.5
  56.6 4.1 %collective-permute-done.2.refs_3_ = s32[2,136,128]{2,1,0:T(8,128)S(1)} collective-permute-done((s32[2,136,128]{2,1,0:T(8,128)S(1)}, s32[2,136,128]{2,1,0:T(8,128)S(1)}, u32[]{:S(2)}, u32[]{:S(2)}) %collective-permute-start.2) | collective-permute-done | bytes 139296 | tf_op jit(solution)/shard_map/ppermute | solution.py:440
  60.7 1.3 %collective-permute-done.6.refs_7_ = s32[2,136,128]{2,1,0:T(8,128)S(1)} collective-permute-done((s32[2,136,128]{2,1,0:T(8,128)S(1)}, s32[2,136,128]{2,1,0:T(8,128)S(1)}, u32[]{:S(2)}, u32[]{:S(2)}) %collective-permute-start.6) | collective-permute-done | bytes 139296 | tf_op jit(solution)/shard_map/ppermute | solution.py:444
  62.1 7.2 %dft.2 = (s32[136,128]{1,0:T(8,128)S(1)}, s32[136,128]{1,0:T(8,128)S(1)}, s32[136,128]{1,0:T(8,128)S(1)}, s32[136,128]{1,0:T(8,128)S(1)}) custom-call(s32[2]{0:T(128)S(1)} %pad_add_fusion.me_ref, f32[49152,256]{1,0:T(8,128)} %tables.1.tables_ref, s32[2,136,128]{2,1,0:T(8,128)S(1)} %get-tuple-element.29.refs_0_, ...), custom_call_target="tpu_custom_call" | custom-call | flops 1 | bytes 1 | tf_op jit(solution)/shard_map/dft/pallas_call | solution.py:363
  69.3 2.6 %stack.15 = (s32[2,136,128]{2,1,0:T(8,128)S(1)}, s32[2,136,128]{2,1,0:T(8,128)S(1)}, s32[2,136,128]{2,1,0:T(8,128)S(1)}, s32[2,136,128]{2,1,0:T(8,128)S(1)}) custom-call(s32[2]{0:T(128)S(1)} %pad_add_fusion.me_ref, s32[8,9]{1,0:T(8,128)S(1)} %reshape.24.table_ref, bf16[4,16,2,32,128]{4,3,2,1,0:T(8,128)(2,1)S(1)} %bitcast.8), custom_call_target="tpu_custom_call" | custom-call | flops 1 | bytes 1 | tf_op jit(solution)/shard_map/stack/pallas_call | solution.py:197
  71.9 1.4 %collective-permute-start.10 = (s32[2,136,128]{2,1,0:T(8,128)S(1)}, s32[2,136,128]{2,1,0:T(8,128)S(1)}, u32[]{:S(2)}, u32[]{:S(2)}) collective-permute-start(s32[2,136,128]{2,1,0:T(8,128)S(1)} %get-tuple-element.40), channel_id=1, source_target_pairs={{0,2},{1,3},{2,0},{3,1},{4,6},{5,7},{6,4},{7,5},{8,10},{9,11},{10,... | collective-permute-start | bytes 417800 | tf_op jit(solution)/shard_map/ppermute | solution.py:440
  73.3 2.2 %collective-permute-start.12 = (s32[2,136,128]{2,1,0:T(8,128)S(1)}, s32[2,136,128]{2,1,0:T(8,128)S(1)}, u32[]{:S(2)}, u32[]{:S(2)}) collective-permute-start(s32[2,136,128]{2,1,0:T(8,128)S(1)} %get-tuple-element.42), channel_id=1, source_target_pairs={{0,6},{1,7},{2,4},{3,5},{4,2},{5,3},{6,0},{7,1},{8,14},{9,15},{10,... | collective-permute-start | bytes 417800 | tf_op jit(solution)/shard_map/ppermute | solution.py:440
  75.5 2.9 %collective-permute-done.10.refs_1_ = s32[2,136,128]{2,1,0:T(8,128)S(1)} collective-permute-done((s32[2,136,128]{2,1,0:T(8,128)S(1)}, s32[2,136,128]{2,1,0:T(8,128)S(1)}, u32[]{:S(2)}, u32[]{:S(2)}) %collective-permute-start.10) | collective-permute-done | bytes 139296 | tf_op jit(solution)/shard_map/ppermute | solution.py:440
  78.4 3.3 %collective-permute-done.11.refs_2_ = s32[2,136,128]{2,1,0:T(8,128)S(1)} collective-permute-done((s32[2,136,128]{2,1,0:T(8,128)S(1)}, s32[2,136,128]{2,1,0:T(8,128)S(1)}, u32[]{:S(2)}, u32[]{:S(2)}) %collective-permute-start.11) | collective-permute-done | bytes 139296 | tf_op jit(solution)/shard_map/ppermute | solution.py:440
  81.7 0.5 collective-permute-start.16
  82.2 1.1 collective-permute-start.7
  83.3 2.6 %collective-permute-start.8 = (s32[136,128]{1,0:T(8,128)S(1)}, s32[136,128]{1,0:T(8,128)S(1)}, u32[]{:S(2)}, u32[]{:S(2)}) collective-permute-start(s32[136,128]{1,0:T(8,128)S(1)} %get-tuple-element.35), channel_id=1, source_target_pairs={{0,16},{8,24},{16,0},{24,8},{1,17},{9,25},{17,1},{25,9},{2,18},{10... | collective-permute-start | bytes 208904 | tf_op jit(solution)/shard_map/ppermute | solution.py:433
  85.9 0.7 collective-permute-start.9
  86.6 7.2 %dft.3 = (s32[136,128]{1,0:T(8,128)S(1)}, s32[136,128]{1,0:T(8,128)S(1)}, s32[136,128]{1,0:T(8,128)S(1)}, s32[136,128]{1,0:T(8,128)S(1)}) custom-call(s32[2]{0:T(128)S(1)} %pad_add_fusion.me_ref, f32[49152,256]{1,0:T(8,128)} %tables.1.tables_ref, s32[2,136,128]{2,1,0:T(8,128)S(1)} %get-tuple-element.39.refs_0_, ...), custom_call_target="tpu_custom_call" | custom-call | flops 1 | bytes 1 | tf_op jit(solution)/shard_map/dft/pallas_call | solution.py:363
  94.1 3.5 %collective-permute-start.18 = (s32[136,128]{1,0:T(8,128)S(1)}, s32[136,128]{1,0:T(8,128)S(1)}, u32[]{:S(2)}, u32[]{:S(2)}) collective-permute-start(s32[136,128]{1,0:T(8,128)S(1)} %get-tuple-element.45), channel_id=1, source_target_pairs={{0,16},{8,24},{16,0},{24,8},{1,17},{9,25},{17,1},{25,9},{2,18},{10... | collective-permute-start | bytes 208904 | tf_op jit(solution)/shard_map/ppermute | solution.py:433
  97.6 0.7 collective-permute-start.19
  98.3 0.3 collective-permute-done.17.refs_5_
  98.6 3.2 %collective-permute-done.18.refs_6_ = s32[136,128]{1,0:T(8,128)S(1)} collective-permute-done((s32[136,128]{1,0:T(8,128)S(1)}, s32[136,128]{1,0:T(8,128)S(1)}, u32[]{:S(2)}, u32[]{:S(2)}) %collective-permute-start.18) | collective-permute-done | bytes 69664 | tf_op jit(solution)/shard_map/ppermute | solution.py:433
  101.8 1.9 %collective-permute-done.19.refs_7_ = s32[136,128]{1,0:T(8,128)S(1)} collective-permute-done((s32[136,128]{1,0:T(8,128)S(1)}, s32[136,128]{1,0:T(8,128)S(1)}, u32[]{:S(2)}, u32[]{:S(2)}) %collective-permute-start.19) | collective-permute-done | bytes 69664 | tf_op jit(solution)/shard_map/ppermute | solution.py:433
  103.7 3.6 %unpack.1 = f32[512,4,128]{2,1,0:T(4,128)} custom-call(s32[2]{0:T(128)S(1)} %pad_add_fusion.me_ref, s32[136,128]{1,0:T(8,128)S(1)} %get-tuple-element.33.refs_0_, s32[136,128]{1,0:T(8,128)S(1)} %collective-permute-done.7.refs_1_, s32[136,128]{1,0:T(8,128)S(1)} %collective-permute-done.8.refs_2_, s32[136,128]{1,0:T(8,128)S(1)} %collective-permute-done.9.refs_3_, ...), custom_call_target="tpu_custom_call" | custom-call | flops 1 | bytes 1 | tf_op jit(solution)/shard_map/unpack/pallas_call | solution.py:419
  (33 shorter events, 1.2 us)
Async XLA Ops:
  3.9 33.5 %all-to-all-start = ((bf16[32,2,2,32,128]{4,3,2,1,0:T(8,128)(2,1)}), bf16[32,2,2,32,128]{4,3,2,1,0:T(8,128)(2,1)S(1)}, u32[]{:S(2)}, u32[]{:S(2)}) async-start(bf16[32,2,2,32,128]{4,3,2,1,0:T(8,128)(2,1)} %bitcast.12), calls=%async_computation | async-start | bytes 2097152 | tf_op jit(solution)/shard_map/all_to_all | solution.py:467
  15.2 4.3 %copy-start = (s32[4,2]{0,1:T(2,128)S(1)}, s32[4,2]{0,1:T(2,128)}, u32[]{:S(2)}) copy-start(s32[4,2]{0,1:T(2,128)} %param.5) | copy-start | bytes 100
  15.2 4.6 %copy-start.1 = (u32[32]{0:T(128)S(1)}, u32[32]{0:T(128)}, u32[]{:S(2)}) copy-start(u32[32]{0:T(128)} %constant.16) | copy-start | bytes 388
  37.5 31.8 %all-to-all-start.1 = ((bf16[32,2,2,32,128]{4,3,2,1,0:T(8,128)(2,1)}), bf16[32,2,2,32,128]{4,3,2,1,0:T(8,128)(2,1)S(1)}, u32[]{:S(2)}, u32[]{:S(2)}) async-start(bf16[32,2,2,32,128]{4,3,2,1,0:T(8,128)(2,1)} %bitcast.6), calls=%async_computation.1 | async-start | bytes 2097152 | tf_op jit(solution)/shard_map/all_to_all | solution.py:467
  43.6 12.5 %collective-permute-start = (s32[2,136,128]{2,1,0:T(8,128)S(1)}, s32[2,136,128]{2,1,0:T(8,128)S(1)}, u32[]{:S(2)}, u32[]{:S(2)}) collective-permute-start(s32[2,136,128]{2,1,0:T(8,128)S(1)} %get-tuple-element.30), channel_id=1, source_target_pairs={{0,2},{1,3},{2,0},{3,1},{4,6},{5,7},{6,4},{7,5},{8,10},{9,11},{10,... | collective-permute-start | bytes 417800 | tf_op jit(solution)/shard_map/ppermute | solution.py:440
  45.4 10.6 %collective-permute-start.1 = (s32[2,136,128]{2,1,0:T(8,128)S(1)}, s32[2,136,128]{2,1,0:T(8,128)S(1)}, u32[]{:S(2)}, u32[]{:S(2)}) collective-permute-start(s32[2,136,128]{2,1,0:T(8,128)S(1)} %get-tuple-element.31), channel_id=1, source_target_pairs={{0,4},{1,5},{2,6},{3,7},{4,0},{5,1},{6,2},{7,3},{8,12},{9,13},{10,... | collective-permute-start | bytes 417800 | tf_op jit(solution)/shard_map/ppermute | solution.py:440
  46.9 13.8 %collective-permute-start.2 = (s32[2,136,128]{2,1,0:T(8,128)S(1)}, s32[2,136,128]{2,1,0:T(8,128)S(1)}, u32[]{:S(2)}, u32[]{:S(2)}) collective-permute-start(s32[2,136,128]{2,1,0:T(8,128)S(1)} %get-tuple-element.32), channel_id=1, source_target_pairs={{0,6},{1,7},{2,4},{3,5},{4,2},{5,3},{6,0},{7,1},{8,14},{9,15},{10,... | collective-permute-start | bytes 417800 | tf_op jit(solution)/shard_map/ppermute | solution.py:440
  47.2 13.5 %collective-permute-start.3 = (s32[2,136,128]{2,1,0:T(8,128)S(1)}, s32[2,136,128]{2,1,0:T(8,128)S(1)}, u32[]{:S(2)}, u32[]{:S(2)}) collective-permute-start(s32[2,136,128]{2,1,0:T(8,128)S(1)} %get-tuple-element.29.refs_0_), channel_id=1, source_target_pairs={{0,1},{1,0},{2,3},{3,2},{4,5},{5,4},{6,7},{7,6},{8,9},{9,8},{10,11... | collective-permute-start | bytes 417800 | tf_op jit(solution)/shard_map/ppermute | solution.py:444
  56.1 4.6 %collective-permute-start.4 = (s32[2,136,128]{2,1,0:T(8,128)S(1)}, s32[2,136,128]{2,1,0:T(8,128)S(1)}, u32[]{:S(2)}, u32[]{:S(2)}) collective-permute-start(s32[2,136,128]{2,1,0:T(8,128)S(1)} %collective-permute-done.refs_1_), channel_id=1, source_target_pairs={{0,1},{1,0},{2,3},{3,2},{4,5},{5,4},{6,7},{7,6},{8,9},{9,8},{10,11... | collective-permute-start | bytes 417800 | tf_op jit(solution)/shard_map/ppermute | solution.py:444
  56.1 4.6 %collective-permute-start.5 = (s32[2,136,128]{2,1,0:T(8,128)S(1)}, s32[2,136,128]{2,1,0:T(8,128)S(1)}, u32[]{:S(2)}, u32[]{:S(2)}) collective-permute-start(s32[2,136,128]{2,1,0:T(8,128)S(1)} %collective-permute-done.1.refs_2_), channel_id=1, source_target_pairs={{0,1},{1,0},{2,3},{3,2},{4,5},{5,4},{6,7},{7,6},{8,9},{9,8},{10,11... | collective-permute-start | bytes 417800 | tf_op jit(solution)/shard_map/ppermute | solution.py:444
  60.7 1.4 %collective-permute-start.6 = (s32[2,136,128]{2,1,0:T(8,128)S(1)}, s32[2,136,128]{2,1,0:T(8,128)S(1)}, u32[]{:S(2)}, u32[]{:S(2)}) collective-permute-start(s32[2,136,128]{2,1,0:T(8,128)S(1)} %collective-permute-done.2.refs_3_), channel_id=1, source_target_pairs={{0,1},{1,0},{2,3},{3,2},{4,5},{5,4},{6,7},{7,6},{8,9},{9,8},{10,11... | collective-permute-start | bytes 417800 | tf_op jit(solution)/shard_map/ppermute | solution.py:444
  71.9 6.5 %collective-permute-start.10 = (s32[2,136,128]{2,1,0:T(8,128)S(1)}, s32[2,136,128]{2,1,0:T(8,128)S(1)}, u32[]{:S(2)}, u32[]{:S(2)}) collective-permute-start(s32[2,136,128]{2,1,0:T(8,128)S(1)} %get-tuple-element.40), channel_id=1, source_target_pairs={{0,2},{1,3},{2,0},{3,1},{4,6},{5,7},{6,4},{7,5},{8,10},{9,11},{10,... | collective-permute-start | bytes 417800 | tf_op jit(solution)/shard_map/ppermute | solution.py:440
  73.3 8.4 %collective-permute-start.11 = (s32[2,136,128]{2,1,0:T(8,128)S(1)}, s32[2,136,128]{2,1,0:T(8,128)S(1)}, u32[]{:S(2)}, u32[]{:S(2)}) collective-permute-start(s32[2,136,128]{2,1,0:T(8,128)S(1)} %get-tuple-element.41), channel_id=1, source_target_pairs={{0,4},{1,5},{2,6},{3,7},{4,0},{5,1},{6,2},{7,3},{8,12},{9,13},{10,... | collective-permute-start | bytes 417800 | tf_op jit(solution)/shard_map/ppermute | solution.py:440
  73.3 8.4 %collective-permute-start.12 = (s32[2,136,128]{2,1,0:T(8,128)S(1)}, s32[2,136,128]{2,1,0:T(8,128)S(1)}, u32[]{:S(2)}, u32[]{:S(2)}) collective-permute-start(s32[2,136,128]{2,1,0:T(8,128)S(1)} %get-tuple-element.42), channel_id=1, source_target_pairs={{0,6},{1,7},{2,4},{3,5},{4,2},{5,3},{6,0},{7,1},{8,14},{9,15},{10,... | collective-permute-start | bytes 417800 | tf_op jit(solution)/shard_map/ppermute | solution.py:440
  75.4 7.8 %collective-permute-start.13 = (s32[2,136,128]{2,1,0:T(8,128)S(1)}, s32[2,136,128]{2,1,0:T(8,128)S(1)}, u32[]{:S(2)}, u32[]{:S(2)}) collective-permute-start(s32[2,136,128]{2,1,0:T(8,128)S(1)} %get-tuple-element.39.refs_0_), channel_id=1, source_target_pairs={{0,1},{1,0},{2,3},{3,2},{4,5},{5,4},{6,7},{7,6},{8,9},{9,8},{10,11... | collective-permute-start | bytes 417800 | tf_op jit(solution)/shard_map/ppermute | solution.py:444
  78.4 7.5 %collective-permute-start.14 = (s32[2,136,128]{2,1,0:T(8,128)S(1)}, s32[2,136,128]{2,1,0:T(8,128)S(1)}, u32[]{:S(2)}, u32[]{:S(2)}) collective-permute-start(s32[2,136,128]{2,1,0:T(8,128)S(1)} %collective-permute-done.10.refs_1_), channel_id=1, source_target_pairs={{0,1},{1,0},{2,3},{3,2},{4,5},{5,4},{6,7},{7,6},{8,9},{9,8},{10,11... | collective-permute-start | bytes 417800 | tf_op jit(solution)/shard_map/ppermute | solution.py:444
  81.7 4.9 %collective-permute-start.15 = (s32[2,136,128]{2,1,0:T(8,128)S(1)}, s32[2,136,128]{2,1,0:T(8,128)S(1)}, u32[]{:S(2)}, u32[]{:S(2)}) collective-permute-start(s32[2,136,128]{2,1,0:T(8,128)S(1)} %collective-permute-done.11.refs_2_), channel_id=1, source_target_pairs={{0,1},{1,0},{2,3},{3,2},{4,5},{5,4},{6,7},{7,6},{8,9},{9,8},{10,11... | collective-permute-start | bytes 417800 | tf_op jit(solution)/shard_map/ppermute | solution.py:444
  81.7 4.9 %collective-permute-start.16 = (s32[2,136,128]{2,1,0:T(8,128)S(1)}, s32[2,136,128]{2,1,0:T(8,128)S(1)}, u32[]{:S(2)}, u32[]{:S(2)}) collective-permute-start(s32[2,136,128]{2,1,0:T(8,128)S(1)} %collective-permute-done.12.refs_3_), channel_id=1, source_target_pairs={{0,1},{1,0},{2,3},{3,2},{4,5},{5,4},{6,7},{7,6},{8,9},{9,8},{10,11... | collective-permute-start | bytes 417800 | tf_op jit(solution)/shard_map/ppermute | solution.py:444
  82.2 15.3 %collective-permute-start.7 = (s32[136,128]{1,0:T(8,128)S(1)}, s32[136,128]{1,0:T(8,128)S(1)}, u32[]{:S(2)}, u32[]{:S(2)}) collective-permute-start(s32[136,128]{1,0:T(8,128)S(1)} %get-tuple-element.34), channel_id=1, source_target_pairs={{0,8},{8,0},{16,24},{24,16},{1,9},{9,1},{17,25},{25,17},{2,10},{10... | collective-permute-start | bytes 208904 | tf_op jit(solution)/shard_map/ppermute | solution.py:433
  83.3 15.0 %collective-permute-start.8 = (s32[136,128]{1,0:T(8,128)S(1)}, s32[136,128]{1,0:T(8,128)S(1)}, u32[]{:S(2)}, u32[]{:S(2)}) collective-permute-start(s32[136,128]{1,0:T(8,128)S(1)} %get-tuple-element.35), channel_id=1, source_target_pairs={{0,16},{8,24},{16,0},{24,8},{1,17},{9,25},{17,1},{25,9},{2,18},{10... | collective-permute-start | bytes 208904 | tf_op jit(solution)/shard_map/ppermute | solution.py:433
  85.9 12.4 %collective-permute-start.9 = (s32[136,128]{1,0:T(8,128)S(1)}, s32[136,128]{1,0:T(8,128)S(1)}, u32[]{:S(2)}, u32[]{:S(2)}) collective-permute-start(s32[136,128]{1,0:T(8,128)S(1)} %get-tuple-element.36), channel_id=1, source_target_pairs={{0,24},{8,16},{16,8},{24,0},{1,25},{9,17},{17,9},{25,1},{2,26},{10... | collective-permute-start | bytes 208904 | tf_op jit(solution)/shard_map/ppermute | solution.py:433
  93.8 4.8 %collective-permute-start.17 = (s32[136,128]{1,0:T(8,128)S(1)}, s32[136,128]{1,0:T(8,128)S(1)}, u32[]{:S(2)}, u32[]{:S(2)}) collective-permute-start(s32[136,128]{1,0:T(8,128)S(1)} %get-tuple-element.44), channel_id=1, source_target_pairs={{0,8},{8,0},{16,24},{24,16},{1,9},{9,1},{17,25},{25,17},{2,10},{10... | collective-permute-start | bytes 208904 | tf_op jit(solution)/shard_map/ppermute | solution.py:433
  94.1 7.7 %collective-permute-start.18 = (s32[136,128]{1,0:T(8,128)S(1)}, s32[136,128]{1,0:T(8,128)S(1)}, u32[]{:S(2)}, u32[]{:S(2)}) collective-permute-start(s32[136,128]{1,0:T(8,128)S(1)} %get-tuple-element.45), channel_id=1, source_target_pairs={{0,16},{8,24},{16,0},{24,8},{1,17},{9,25},{17,1},{25,9},{2,18},{10... | collective-permute-start | bytes 208904 | tf_op jit(solution)/shard_map/ppermute | solution.py:433
  97.6 6.1 %collective-permute-start.19 = (s32[136,128]{1,0:T(8,128)S(1)}, s32[136,128]{1,0:T(8,128)S(1)}, u32[]{:S(2)}, u32[]{:S(2)}) collective-permute-start(s32[136,128]{1,0:T(8,128)S(1)} %get-tuple-element.46), channel_id=1, source_target_pairs={{0,24},{8,16},{16,8},{24,0},{1,25},{9,17},{17,9},{25,1},{2,26},{10... | collective-permute-start | bytes 208904 | tf_op jit(solution)/shard_map/ppermute | solution.py:433

commit v7 on v6

--- a/solution.py
+++ b/solution.py
@@ -25,29 +25,28 @@
 
 
 def top_exponent(largest):
-    return jnp.maximum(jnp.floor(jnp.log2(jnp.maximum(largest, 1e-36))), -100.0)
+    return jnp.maximum(jnp.floor(jnp.log2(jnp.maximum(largest, 1e-36))), -90.0)
 
 
 def encode(a, b, top):
     m = jnp.maximum(jnp.maximum(jnp.abs(a), jnp.abs(b)), 1e-36)
-    e = jnp.floor(jnp.log2(m))
-    e = jnp.minimum(jnp.maximum(jnp.maximum(e, top - 63.0), -110.0), top)
-    s = jnp.exp2(11.0 - e)
+    e = jnp.minimum(jnp.maximum(jnp.floor(jnp.log2(m)), top - 15.0), top)
+    s = jnp.exp2(12.0 - e)
     qa, qb = (
-        jnp.clip(jnp.floor(x * s + 0.5), -4095.0, 4095.0).astype(jnp.int32) + 4096
+        jnp.clip(jnp.floor(x * s + 0.5), -8191.0, 8191.0).astype(jnp.int32) + 8192
         for x in (a, b)
     )
-    field = (e - (top - 63.0)).astype(jnp.int32)
-    return (field << 26) | (qa << 13) | qb
-
-
-ZERO = (4096 << 13) | 4096
+    return ((e - (top - 15.0)).astype(jnp.int32) << 28) | (qa << 14) | qb
+
+
+ZERO = (8192 << 14) | 8192
 
 
 def decode(code, top):
-    e = ((code >> 26) & 63).astype(jnp.float32) + (top - 63.0)
-    s = jnp.exp2(e - 11.0)
-    a, b = (((q & 8191) - 4096).astype(jnp.float32) * s for q in (code >> 13, code))
+    s = jnp.exp2(((code >> 28) & 15).astype(jnp.float32) + (top - 27.0))
+    a, b = (
+        ((q & 16383) - 8192).astype(jnp.float32) * s for q in (code >> 14, code)
+    )
     return a, b
 
 
@@ -209,19 +208,15 @@
     )(me, table, spec)
 
 
-def dft_kernel(n_seg, n_pair, most, me_ref, tables_ref, *refs):
+def dft_kernel(
+    n_seg, n_pair, most, me_ref, whi_ref, wlo_ref, phase_ref, tables_ref, *refs
+):
     ins, outs = refs[:n_pair], refs[n_pair : n_pair + n_seg]
-    w_ref, phase_ref, t_ref, sems = refs[n_pair + n_seg :][:4]
-    whi_ref, wlo_ref, s32, shi, slo, y, zhi, zlo, sums, parts = refs[
-        n_pair + n_seg + 4 :
-    ]
-    copies = []
-    row = 0
-    for i, to in enumerate((w_ref.at[0], w_ref.at[1], phase_ref, t_ref)):
-        src = tables_ref.at[pl.ds(row, to.shape[0])]
-        copies.append(pltpu.make_async_copy(src, to, sems.at[i]))
-        copies[-1].start()
-        row += to.shape[0]
+    t_ref, sem, s32, shi, slo, y, zhi, zlo, sums, parts = refs[n_pair + n_seg :]
+    copy = pltpu.make_async_copy(
+        tables_ref.at[pl.ds(0, t_ref.shape[0])], t_ref, sem.at[0]
+    )
+    copy.start()
     rows = (ins[0].shape[1] - 8) // most
     half_h = whi_ref.shape[1] // 2
     wide = most * TILE
@@ -243,20 +238,12 @@
         for to, part in ((shi, hi), (slo, lo)):
             to[:half_h, own] = part
             to[half_h:, other] = part if ri == 0 else -part
-    copies[0].wait()
-    copies[1].wait()
-    for ri in range(2):
-        hi = w_ref[ri].astype(jnp.bfloat16)
-        n = slice(ri * half_h, (ri + 1) * half_h)
-        whi_ref[:, n] = hi
-        wlo_ref[:, n] = (w_ref[ri] - hi.astype(jnp.float32)).astype(jnp.bfloat16)
     for ri in range(2):
         n = slice(ri * wide, (ri + 1) * wide)
         y[ri] = (
             jnp.dot(wlo_ref[...], shi[:, n], preferred_element_type=jnp.float32)
             + jnp.dot(whi_ref[...], slo[:, n], preferred_element_type=jnp.float32)
         ) + jnp.dot(whi_ref[...], shi[:, n], preferred_element_type=jnp.float32)
-    copies[2].wait()
     period = y.shape[1]
     step_rows = 64
     for b in range(period // step_rows):
@@ -272,7 +259,7 @@
                 hi = z.astype(jnp.bfloat16)
                 zhi[at, to] = hi
                 zlo[at, to] = (z - hi.astype(jnp.float32)).astype(jnp.bfloat16)
-    copies[3].wait()
+    copy.wait()
     thi = t_ref[...].astype(jnp.bfloat16)
     tlo = (t_ref[...] - thi.astype(jnp.float32)).astype(jnp.bfloat16)
     sums[...] = (
@@ -303,15 +290,7 @@
         outs[k][half // 2 :, :] = jnp.broadcast_to(top, (8, TILE)).astype(jnp.int32)
 
 
-def tables_kernel(most, turns, shift, fixed_ref, out_ref, t_ref, sems):
-    used = fixed_ref.shape[0]
-    copies = [
-        pltpu.make_async_copy(fixed_ref, out_ref.at[pl.ds(0, used)], sems.at[0]),
-        pltpu.make_async_copy(
-            t_ref, out_ref.at[pl.ds(used, t_ref.shape[0])], sems.at[1]
-        ),
-    ]
-    copies[0].start()
+def sums_kernel(most, turns, shift, out_ref, t_ref, sem):
     shape = (most * TILE, turns * most * CC)
     row = lax.broadcasted_iota(jnp.int32, shape, 0)
     col = lax.broadcasted_iota(jnp.int32, shape, 1)
@@ -323,35 +302,43 @@
         size = jnp.where(e % 4 == 2, 0.0, jnp.where(e % 2 == 0, 1.0, diagonal))
         t = jnp.where(same, jnp.where((e > 2) & (e < 6), -size, size), 0.0)
         t_ref[ri * most * TILE : (ri + 1) * most * TILE, :] = t
-    copies[1].start()
-    for copy in copies:
-        copy.wait()
-
-
-def make_tables(freq, most):
+    copy = pltpu.make_async_copy(
+        t_ref, out_ref.at[pl.ds(0, t_ref.shape[0])], sem.at[0]
+    )
+    copy.start()
+    copy.wait()
+
+
+def make_sums(freq, most):
+    period = 2 * (freq // GROUPS)
+    turns = LAG // period
+    width = turns * most * CC
+    return pl.pallas_call(
+        functools.partial(sums_kernel, most, turns, LAG // 2 // period),
+        out_shape=jax.ShapeDtypeStruct((48 << 10, width), jnp.float32),
+        out_specs=pl.BlockSpec(memory_space=pltpu.HBM),
+        scratch_shapes=[
+            pltpu.VMEM((2 * most * TILE, width), jnp.float32),
+            pltpu.SemaphoreType.DMA((1,)),
+        ],
+        name="sums",
+        cost_estimate=SMALL,
+    )()
+
+
+def make_tables(freq):
     h = freq // GROUPS
     period = 2 * h
-    turns = LAG // period
-    width = turns * most * CC
     angle = np.arange(period)[:, None] * np.arange(h)[None, :] % period
     angle = angle * (2.0 * math.pi / period)
+    w = np.concatenate([np.cos(angle), np.sin(angle)], 1).astype(np.float32)
+    whi = w.astype(jnp.bfloat16)
+    wlo = (w - whi.astype(np.float32)).astype(jnp.bfloat16)
     fb = np.arange(TILE) // CC
     phase = ((np.arange(period)[:, None] * fb[None, :]) % (2 * freq)) * (math.pi / freq)
     scale = 1.0 / math.sqrt(freq)
-    phase = np.concatenate([np.cos(phase), np.sin(phase)], 1) * scale
-    fixed = np.concatenate([np.cos(angle), np.sin(angle), phase]).astype(np.float32)
-    return pl.pallas_call(
-        functools.partial(tables_kernel, most, turns, LAG // 2 // period),
-        out_shape=jax.ShapeDtypeStruct((48 << 10, width), jnp.float32),
-        in_specs=[pl.BlockSpec(memory_space=pltpu.VMEM)],
-        out_specs=pl.BlockSpec(memory_space=pltpu.HBM),
-        scratch_shapes=[
-            pltpu.VMEM((2 * most * TILE, width), jnp.float32),
-            pltpu.SemaphoreType.DMA((2,)),
-        ],
-        name="tables",
-        cost_estimate=SMALL,
-    )(jnp.asarray(fixed))
+    phase = (np.concatenate([np.cos(phase), np.sin(phase)], 1) * scale).astype(np.float32)
+    return [jnp.asarray(c) for c in (whi, wlo, phase)]
 
 
 def dft(me, tables, blocks, freq, n_seg, n_pair, most):
@@ -363,15 +350,12 @@
     return pl.pallas_call(
         functools.partial(dft_kernel, n_seg, n_pair, most),
         out_shape=[jax.ShapeDtypeStruct((half // 2 + 8, TILE), jnp.int32)] * n_seg,
-        in_specs=[smem, pl.BlockSpec(memory_space=pltpu.HBM)] + [vmem] * len(blocks),
+        in_specs=[smem, vmem, vmem, vmem, pl.BlockSpec(memory_space=pltpu.HBM)]
+        + [vmem] * len(blocks),
         out_specs=[vmem] * n_seg,
         scratch_shapes=[
-            pltpu.VMEM((2, period, period // 2), jnp.float32),
-            pltpu.VMEM((period, 2 * TILE), jnp.float32),
             pltpu.VMEM((2 * wide, LAG // period * most * CC), jnp.float32),
-            pltpu.SemaphoreType.DMA((4,)),
-            pltpu.VMEM((period, period), jnp.bfloat16),
-            pltpu.VMEM((period, period), jnp.bfloat16),
+            pltpu.SemaphoreType.DMA((1,)),
             pltpu.VMEM((2, period // 2, wide), jnp.float32),
             pltpu.VMEM((period, 2 * wide), jnp.bfloat16),
             pltpu.VMEM((period, 2 * wide), jnp.bfloat16),
@@ -384,48 +368,52 @@
         name="dft",
         compiler_params=pltpu.CompilerParams(vmem_limit_bytes=24 << 20),
         cost_estimate=SMALL,
-    )(me, tables, *blocks)
+    )(me, *tables, *blocks)
 
 
 def unpack_kernel(n_seg, chunks, most, me_ref, *refs):
     ins = refs[: n_seg * chunks]
     out_ref, buf = refs[n_seg * chunks :]
     half = buf.shape[1]
-    for k in range(n_seg):
-        z = jnp.bitwise_xor(me_ref[0], k)
-        for ch in range(chunks):
-            src = ins[ch * n_seg + k]
-            top = src[half // 2 : half // 2 + 1, :].astype(jnp.float32)
-            low, high = decode(src[: half // 2, :], top)
-            buf[z * chunks + ch, : half // 2] = low
-            buf[z * chunks + ch, half // 2 :] = high
+
+    @pl.when(pl.program_id(0) == 0)
+    def _():
+        for k in range(n_seg):
+            z = jnp.bitwise_xor(me_ref[0], k)
+            for ch in range(chunks):
+                src = ins[ch * n_seg + k]
+                top = src[half // 2 : half // 2 + 1, :].astype(jnp.float32)
+                low, high = decode(src[: half // 2, :], top)
+                buf[z * chunks + ch, : half // 2] = low
+                buf[z * chunks + ch, half // 2 :] = high
+
     step_rows = 16
-
-    def one(b, _):
-        at = pl.multiple_of(b * step_rows, step_rows)
+    block = out_ref.shape[1]
+    for b in range(block // step_rows):
+        at = pl.multiple_of(pl.program_id(0) * block + b * step_rows, step_rows)
         v = transpose_groups([buf[i, pl.ds(at, step_rows), :] for i in range(GROUPS)])
         for h in range(2):
             for s in range(most):
-                out_ref[pl.ds(h * half + at, step_rows), s, :] = v[h * most + s]
-        return 0
-
-    lax.fori_loop(0, half // step_rows, one, 0, unroll=4)
+                out_ref[h, b * step_rows : (b + 1) * step_rows, s, :] = v[h * most + s]
 
 
 def unpack(me, parts, n_seg, chunks, most):
     half = 2 * (parts[0].shape[0] - 8)
+    steps = 4
     smem = pl.BlockSpec(memory_space=pltpu.SMEM)
-    vmem = pl.BlockSpec(memory_space=pltpu.VMEM)
-    return pl.pallas_call(
+    whole = pl.BlockSpec(parts[0].shape, lambda b: (0, 0))
+    out = pl.pallas_call(
         functools.partial(unpack_kernel, n_seg, chunks, most),
-        out_shape=jax.ShapeDtypeStruct((2 * half, most, TILE), jnp.float32),
-        in_specs=[smem] + [vmem] * len(parts),
-        out_specs=vmem,
+        out_shape=jax.ShapeDtypeStruct((2, half, most, TILE), jnp.float32),
+        grid=(steps,),
+        in_specs=[smem] + [whole] * len(parts),
+        out_specs=pl.BlockSpec((2, half // steps, most, TILE), lambda b: (0, b, 0, 0)),
         scratch_shapes=[pltpu.VMEM((GROUPS, half, TILE), jnp.float32)],
         name="unpack",
         compiler_params=pltpu.CompilerParams(vmem_limit_bytes=12 << 20),
         cost_estimate=SMALL,
     )(me, *parts)
+    return out.reshape(2 * half, most, TILE)
 
 
 def exchange(blocks, axis, size):
@@ -455,12 +443,13 @@
     me = jnp.stack([lax.axis_index("seg"), lax.axis_index("pair")]).astype(jnp.int32)
     x = spectra.reshape(2, freq, spectra.shape[3])
     lists = jnp.concatenate([pair_lists.reshape(-1), pair_counts])
-    tables = make_tables(freq, most)
+    sums = make_sums(freq, most)
+    tables = make_tables(freq) + [sums]
     packed = [pack(x, chunk, n_seg, n_pair) for chunk in range(chunks)]
     lists, packed[-1] = lax.optimization_barrier((lists, packed[-1]))
     table = lax.all_gather(lists, "pair", axis=0)
     if chunks > 1:
-        table, packed[1], _ = lax.optimization_barrier((table, packed[1], tables))
+        table, packed[1], _ = lax.optimization_barrier((table, packed[1], sums))
     done = []
     lags = None
     for sent in packed:
@@ -476,6 +465,8 @@
         spec = got.reshape(n_seg, n_pair * tiles, 2, rows, TILE)
         blocks = stacks(me, table, spec, n_seg, n_pair, most)
         blocks = exchange_plane(blocks, n_pair)
+        if done:
+            blocks, _ = lax.optimization_barrier((blocks, done[2:]))
         lags = dft(me, tables, blocks, freq, n_seg, n_pair, most)
         done += exchange(lags, "seg", n_seg)
     return unpack(me, done, n_seg, chunks, most)

time: 108 us -> 109 us (level)
  Pallas kernels: 34.5 us -> 31.1 us
  waiting for transfers between devices: 33.7 us -> 36.2 us
  starting transfers between devices: 27.9 us -> 29.1 us
    ppermute x6, waiting for transfers between devices: 5.38 us -> 7.83 us  [exchange(): lax.ppermute(blocks[k], axis, [(i, i ^ k) for i in range(size)])]
    pallas_call x2, Pallas kernels: 14.4 us -> 12.7 us  [dft(): pl.pallas_call(functools.partial(dft_kernel, n_seg, n_pair, most), out_sh...]
    all_to_all x2, waiting for transfers between devices: 7.67 us -> 9.3 us  [body(): lax.all_to_all(sent.reshape(n_seg * n_pair, tiles, 2, rows, TILE), ('seg'...]
    ppermute x6, waiting for transfers between devices: 19.3 us -> 17.7 us  [exchange_plane(): lax.ppermute(blocks[k], 'pair', [(i, i ^ 2 * k) for i in range(n_pair)])]
    pallas_call x1, Pallas kernels: 3.65 us -> 2.21 us  [make_sums(): pl.pallas_call(functools.partial(sums_kernel, most, turns, LAG // 2 // pe...]
    ppermute x6, starting transfers between devices: 8.84 us -> 10 us  [exchange(): lax.ppermute(blocks[k], axis, [(i, i ^ k) for i in range(size)])]
  transfers between devices with their start and end apart: 22 -> 22, of which waited for: 9 -> 10; matrix products, arithmetic and copies ran while one was open for 1% -> 1% of each run, Pallas kernels for 23% -> 19%
where the time goes in v7:
time: 109 us; the launch traced here: 108 us
  waiting for transfers between devices  36.2 us (33%)
  Pallas kernels  31.1 us (29%)
  starting transfers between devices  29.1 us (27%)
  blocking collectives  8.28 us (8%)
  local copies, waits for them, and re-layouts  2.15 us (2%)
  between operations  1.42 us (1%)
    ppermute x6, waiting for transfers between devices, exchange_plane(): lax.ppermute(blocks[k], 'pair', [(i, i ^ 2 * k) for i in range(n_pair)])  17.7 us
    pallas_call x2, Pallas kernels, dft(): pl.pallas_call(functools.partial(dft_kernel, n_seg, n_pair, most), out_sh...  12.7 us
    all_to_all x2, starting transfers between devices, body(): lax.all_to_all(sent.reshape(n_seg * n_pair, tiles, 2, rows, TILE), ('seg'...  10.9 us
    ppermute x6, starting transfers between devices, exchange(): lax.ppermute(blocks[k], axis, [(i, i ^ k) for i in range(size)])  10 us
    all_to_all x2, waiting for transfers between devices, body(): lax.all_to_all(sent.reshape(n_seg * n_pair, tiles, 2, rows, TILE), ('seg'...  9.3 us
    unnamed x1, blocking collectives  8.28 us
    pallas_call x2, Pallas kernels, pack(): pl.pallas_call(functools.partial(pack_kernel, n_seg, n_pair, chunk), out_...  8.01 us
    ppermute x6, waiting for transfers between devices, exchange(): lax.ppermute(blocks[k], axis, [(i, i ^ k) for i in range(size)])  7.83 us
  transfers between devices with their start and end apart: 22, of which 10 were waited for; matrix products, arithmetic and copies ran while one was open for 1% of the time, Pallas kernels for 19%

profile of v7, /device:TPU:0, one launch (start us, length us, event | category | flops | bytes accessed | tf_op | source)
XLA Modules:
  0.0 108.4 jit_solution(8952451995394473079)
XLA Ops:
  0.0 4.0 %pack.3 = bf16[4,8,2,2,32,128]{5,4,3,2,1,0:T(8,128)(2,1)} custom-call(bf16[2,2048,256]{2,1,0:T(8,128)(2,1)} %bitcast.11), custom_call_target="tpu_custom_call" | custom-call | flops 1 | bytes 1 | tf_op jit(solution)/shard_map/pack/pallas_call | solution.py:125
  4.1 7.3 %all-to-all-start = ((bf16[32,2,2,32,128]{4,3,2,1,0:T(8,128)(2,1)}), bf16[32,2,2,32,128]{4,3,2,1,0:T(8,128)(2,1)S(1)}, u32[]{:S(2)}, u32[]{:S(2)}) async-start(bf16[32,2,2,32,128]{4,3,2,1,0:T(8,128)(2,1)} %bitcast.14), calls=%async_computation | async-start | bytes 2097152 | tf_op jit(solution)/shard_map/all_to_all | solution.py:456
  11.4 4.0 %pack.2 = bf16[4,8,2,2,32,128]{5,4,3,2,1,0:T(8,128)(2,1)} custom-call(bf16[2,2048,256]{2,1,0:T(8,128)(2,1)} %bitcast.12), custom_call_target="tpu_custom_call" | custom-call | flops 1 | bytes 1 | tf_op jit(solution)/shard_map/pack/pallas_call | solution.py:125
  15.3 2.2 %sums.1.tables_ref = f32[49152,256]{1,0:T(8,128)} custom-call(), custom_call_target="tpu_custom_call" | custom-call | flops 1 | bytes 1 | tf_op jit(solution)/shard_map/sums/pallas_call | solution.py:316
  18.5 0.6 dynamic-slice
  19.9 8.3 %all-reduce = s32[72]{0:T(128)S(1)} all-reduce(s32[72]{0:T(128)S(1)} %dynamic-update-slice), channel_id=2, replica_groups=mesh['seg'=4,'pair'=8] {'pair'}, use_global_device_ids=true, to_apply=%add | all-reduce | flops 72 | bytes 576
  28.3 9.3 %all-to-all-done = bf16[32,2,2,32,128]{4,3,2,1,0:T(8,128)(2,1)S(1)} async-done(((bf16[32,2,2,32,128]{4,3,2,1,0:T(8,128)(2,1)}), bf16[32,2,2,32,128]{4,3,2,1,0:T(8,128)(2,1)S(1)}, u32[]{:S(2)}, u32[]{:S(2)}) %all-to-all-start) | async-done | bytes 1048608 | tf_op jit(solution)/shard_map/all_to_all | solution.py:456
  37.6 3.6 %all-to-all-start.1 = ((bf16[32,2,2,32,128]{4,3,2,1,0:T(8,128)(2,1)}), bf16[32,2,2,32,128]{4,3,2,1,0:T(8,128)(2,1)S(1)}, u32[]{:S(2)}, u32[]{:S(2)}) async-start(bf16[32,2,2,32,128]{4,3,2,1,0:T(8,128)(2,1)} %bitcast.13), calls=%async_computation.1 | async-start | bytes 2097152 | tf_op jit(solution)/shard_map/all_to_all | solution.py:456
  41.3 2.2 %stack.14 = (s32[2,136,128]{2,1,0:T(8,128)S(1)}, s32[2,136,128]{2,1,0:T(8,128)S(1)}, s32[2,136,128]{2,1,0:T(8,128)S(1)}, s32[2,136,128]{2,1,0:T(8,128)S(1)}) custom-call(s32[2]{0:T(128)S(1)} %pad_add_fusion.me_ref, s32[8,9]{1,0:T(8,128)S(1)} %reshape.28.table_ref, bf16[4,16,2,32,128]{4,3,2,1,0:T(8,128)(2,1)S(1)} %bitcast.10), custom_call_target="tpu_custom_call" | custom-call | flops 1 | bytes 1 | tf_op jit(solution)/shard_map/stack/pallas_call | solution.py:196
  43.5 1.8 %collective-permute-start = (s32[2,136,128]{2,1,0:T(8,128)S(1)}, s32[2,136,128]{2,1,0:T(8,128)S(1)}, u32[]{:S(2)}, u32[]{:S(2)}) collective-permute-start(s32[2,136,128]{2,1,0:T(8,128)S(1)} %get-tuple-element.38), channel_id=1, source_target_pairs={{0,2},{1,3},{2,0},{3,1},{4,6},{5,7},{6,4},{7,5},{8,10},{9,11},{10,... | collective-permute-start | bytes 417800 | tf_op jit(solution)/shard_map/ppermute | solution.py:428
  45.4 1.5 %collective-permute-start.1 = (s32[2,136,128]{2,1,0:T(8,128)S(1)}, s32[2,136,128]{2,1,0:T(8,128)S(1)}, u32[]{:S(2)}, u32[]{:S(2)}) collective-permute-start(s32[2,136,128]{2,1,0:T(8,128)S(1)} %get-tuple-element.39), channel_id=1, source_target_pairs={{0,4},{1,5},{2,6},{3,7},{4,0},{5,1},{6,2},{7,3},{8,12},{9,13},{10,... | collective-permute-start | bytes 417800 | tf_op jit(solution)/shard_map/ppermute | solution.py:428
  47.1 9.1 %collective-permute-done.refs_1_ = s32[2,136,128]{2,1,0:T(8,128)S(1)} collective-permute-done((s32[2,136,128]{2,1,0:T(8,128)S(1)}, s32[2,136,128]{2,1,0:T(8,128)S(1)}, u32[]{:S(2)}, u32[]{:S(2)}) %collective-permute-start) | collective-permute-done | bytes 139296 | tf_op jit(solution)/shard_map/ppermute | solution.py:428
  56.7 4.1 %collective-permute-done.2.refs_3_ = s32[2,136,128]{2,1,0:T(8,128)S(1)} collective-permute-done((s32[2,136,128]{2,1,0:T(8,128)S(1)}, s32[2,136,128]{2,1,0:T(8,128)S(1)}, u32[]{:S(2)}, u32[]{:S(2)}) %collective-permute-start.2) | collective-permute-done | bytes 139296 | tf_op jit(solution)/shard_map/ppermute | solution.py:428
  60.8 1.3 %collective-permute-done.6.refs_7_ = s32[2,136,128]{2,1,0:T(8,128)S(1)} collective-permute-done((s32[2,136,128]{2,1,0:T(8,128)S(1)}, s32[2,136,128]{2,1,0:T(8,128)S(1)}, u32[]{:S(2)}, u32[]{:S(2)}) %collective-permute-start.6) | collective-permute-done | bytes 139296 | tf_op jit(solution)/shard_map/ppermute | solution.py:432
  62.2 1.0 copy-done.2
  63.2 6.4 %dft.2 = (s32[136,128]{1,0:T(8,128)S(1)}, s32[136,128]{1,0:T(8,128)S(1)}, s32[136,128]{1,0:T(8,128)S(1)}, s32[136,128]{1,0:T(8,128)S(1)}) custom-call(s32[2]{0:T(128)S(1)} %pad_add_fusion.me_ref, bf16[512,512]{1,0:T(8,128)(2,1)S(1)} %copy-done.2, bf16[512,512]{1,0:T(8,128)(2,1)S(1)} %copy-done.1, f32[512,256]{1,0:T(8,128)S(1)} %copy-done, ...), custom_call_target="tpu_custom_call" | custom-call | flops 1 | bytes 1 | tf_op jit(solution)/shard_map/dft/pallas_call | solution.py:350
  69.6 2.4 %stack.15 = (s32[2,136,128]{2,1,0:T(8,128)S(1)}, s32[2,136,128]{2,1,0:T(8,128)S(1)}, s32[2,136,128]{2,1,0:T(8,128)S(1)}, s32[2,136,128]{2,1,0:T(8,128)S(1)}) custom-call(s32[2]{0:T(128)S(1)} %pad_add_fusion.me_ref, s32[8,9]{1,0:T(8,128)S(1)} %reshape.28.table_ref, bf16[4,16,2,32,128]{4,3,2,1,0:T(8,128)(2,1)S(1)} %bitcast.9), custom_call_target="tpu_custom_call" | custom-call | flops 1 | bytes 1 | tf_op jit(solution)/shard_map/stack/pallas_call | solution.py:196
  72.0 1.4 %collective-permute-start.10 = (s32[2,136,128]{2,1,0:T(8,128)S(1)}, s32[2,136,128]{2,1,0:T(8,128)S(1)}, u32[]{:S(2)}, u32[]{:S(2)}) collective-permute-start(s32[2,136,128]{2,1,0:T(8,128)S(1)} %get-tuple-element.48), channel_id=1, source_target_pairs={{0,2},{1,3},{2,0},{3,1},{4,6},{5,7},{6,4},{7,5},{8,10},{9,11},{10,... | collective-permute-start | bytes 417800 | tf_op jit(solution)/shard_map/ppermute | solution.py:428
  73.4 2.2 %collective-permute-start.12 = (s32[2,136,128]{2,1,0:T(8,128)S(1)}, s32[2,136,128]{2,1,0:T(8,128)S(1)}, u32[]{:S(2)}, u32[]{:S(2)}) collective-permute-start(s32[2,136,128]{2,1,0:T(8,128)S(1)} %get-tuple-element.50), channel_id=1, source_target_pairs={{0,6},{1,7},{2,4},{3,5},{4,2},{5,3},{6,0},{7,1},{8,14},{9,15},{10,... | collective-permute-start | bytes 417800 | tf_op jit(solution)/shard_map/ppermute | solution.py:428
  75.6 1.8 %collective-permute-start.8 = (s32[136,128]{1,0:T(8,128)S(1)}, s32[136,128]{1,0:T(8,128)S(1)}, u32[]{:S(2)}, u32[]{:S(2)}) collective-permute-start(s32[136,128]{1,0:T(8,128)S(1)} %get-tuple-element.43), channel_id=1, source_target_pairs={{0,16},{8,24},{16,0},{24,8},{1,17},{9,25},{17,1},{25,9},{2,18},{10... | collective-permute-start | bytes 208904 | tf_op jit(solution)/shard_map/ppermute | solution.py:421
  77.3 1.2 %collective-permute-done.10.refs_1_ = s32[2,136,128]{2,1,0:T(8,128)S(1)} collective-permute-done((s32[2,136,128]{2,1,0:T(8,128)S(1)}, s32[2,136,128]{2,1,0:T(8,128)S(1)}, u32[]{:S(2)}, u32[]{:S(2)}) %collective-permute-start.10) | collective-permute-done | bytes 139296 | tf_op jit(solution)/shard_map/ppermute | solution.py:428
  78.5 3.3 %collective-permute-done.11.refs_2_ = s32[2,136,128]{2,1,0:T(8,128)S(1)} collective-permute-done((s32[2,136,128]{2,1,0:T(8,128)S(1)}, s32[2,136,128]{2,1,0:T(8,128)S(1)}, u32[]{:S(2)}, u32[]{:S(2)}) %collective-permute-start.11) | collective-permute-done | bytes 139296 | tf_op jit(solution)/shard_map/ppermute | solution.py:428
  82.3 3.1 %collective-permute-start.9 = (s32[136,128]{1,0:T(8,128)S(1)}, s32[136,128]{1,0:T(8,128)S(1)}, u32[]{:S(2)}, u32[]{:S(2)}) collective-permute-start(s32[136,128]{1,0:T(8,128)S(1)} %get-tuple-element.44), channel_id=1, source_target_pairs={{0,24},{8,16},{16,8},{24,0},{1,25},{9,17},{17,9},{25,1},{2,26},{10... | collective-permute-start | bytes 208904 | tf_op jit(solution)/shard_map/ppermute | solution.py:421
  85.4 3.1 %collective-permute-done.9.refs_3_ = s32[136,128]{1,0:T(8,128)S(1)} collective-permute-done((s32[136,128]{1,0:T(8,128)S(1)}, s32[136,128]{1,0:T(8,128)S(1)}, u32[]{:S(2)}, u32[]{:S(2)}) %collective-permute-start.9) | collective-permute-done | bytes 69664 | tf_op jit(solution)/shard_map/ppermute | solution.py:421
  88.5 0.7 collective-permute-start.7
  89.2 6.4 %dft.3 = (s32[136,128]{1,0:T(8,128)S(1)}, s32[136,128]{1,0:T(8,128)S(1)}, s32[136,128]{1,0:T(8,128)S(1)}, s32[136,128]{1,0:T(8,128)S(1)}) custom-call(s32[2]{0:T(128)S(1)} %pad_add_fusion.me_ref, bf16[512,512]{1,0:T(8,128)(2,1)S(1)} %copy-done.2, bf16[512,512]{1,0:T(8,128)(2,1)S(1)} %copy-done.1, f32[512,256]{1,0:T(8,128)S(1)} %copy-done, ...), custom_call_target="tpu_custom_call" | custom-call | flops 1 | bytes 1 | tf_op jit(solution)/shard_map/dft/pallas_call | solution.py:350
  95.6 1.4 %collective-permute-start.17 = (s32[136,128]{1,0:T(8,128)S(1)}, s32[136,128]{1,0:T(8,128)S(1)}, u32[]{:S(2)}, u32[]{:S(2)}) collective-permute-start(s32[136,128]{1,0:T(8,128)S(1)} %get-tuple-element.60), channel_id=1, source_target_pairs={{0,8},{8,0},{16,24},{24,16},{1,9},{9,1},{17,25},{25,17},{2,10},{10... | collective-permute-start | bytes 208904 | tf_op jit(solution)/shard_map/ppermute | solution.py:421
  97.0 1.7 %collective-permute-start.18 = (s32[136,128]{1,0:T(8,128)S(1)}, s32[136,128]{1,0:T(8,128)S(1)}, u32[]{:S(2)}, u32[]{:S(2)}) collective-permute-start(s32[136,128]{1,0:T(8,128)S(1)} %get-tuple-element.61), channel_id=1, source_target_pairs={{0,16},{8,24},{16,0},{24,8},{1,17},{9,25},{17,1},{25,9},{2,18},{10... | collective-permute-start | bytes 208904 | tf_op jit(solution)/shard_map/ppermute | solution.py:421
  98.6 1.4 %collective-permute-start.19 = (s32[136,128]{1,0:T(8,128)S(1)}, s32[136,128]{1,0:T(8,128)S(1)}, u32[]{:S(2)}, u32[]{:S(2)}) collective-permute-start(s32[136,128]{1,0:T(8,128)S(1)} %get-tuple-element.62), channel_id=1, source_target_pairs={{0,24},{8,16},{16,8},{24,0},{1,25},{9,17},{17,9},{25,1},{2,26},{10... | collective-permute-start | bytes 208904 | tf_op jit(solution)/shard_map/ppermute | solution.py:421
  100.4 3.3 %collective-permute-done.18.refs_6_ = s32[136,128]{1,0:T(8,128)S(1)} collective-permute-done((s32[136,128]{1,0:T(8,128)S(1)}, s32[136,128]{1,0:T(8,128)S(1)}, u32[]{:S(2)}, u32[]{:S(2)}) %collective-permute-start.18) | collective-permute-done | bytes 69664 | tf_op jit(solution)/shard_map/ppermute | solution.py:421
  103.7 1.1 %collective-permute-done.19.refs_7_ = s32[136,128]{1,0:T(8,128)S(1)} collective-permute-done((s32[136,128]{1,0:T(8,128)S(1)}, s32[136,128]{1,0:T(8,128)S(1)}, u32[]{:S(2)}, u32[]{:S(2)}) %collective-permute-start.19) | collective-permute-done | bytes 69664 | tf_op jit(solution)/shard_map/ppermute | solution.py:421
  104.8 3.6 %unpack.1 = f32[2,256,4,128]{3,2,1,0:T(4,128)} custom-call(s32[2]{0:T(128)S(1)} %pad_add_fusion.me_ref, s32[136,128]{1,0:T(8,128)S(1)} %get-tuple-element.41.refs_0_, s32[136,128]{1,0:T(8,128)S(1)} %collective-permute-done.7.refs_1_, s32[136,128]{1,0:T(8,128)S(1)} %collective-permute-done.8.refs_2_, s32[136,128]{1,0:T(8,128)S(1)} %collective-permute-done.9.refs_3_, ...), custom_call_target="tpu_custom_call" | custom-call | flops 1 | bytes 1 | tf_op jit(solution)/shard_map/unpack/pallas_call | solution.py:405
  (39 shorter events, 2.3 us)
Async XLA Ops:
  0.0 18.5 %copy-start.4 = (u32[32]{0:T(128)S(1)}, u32[32]{0:T(128)}, u32[]{:S(2)}) copy-start(u32[32]{0:T(128)} %constant.22) | copy-start | bytes 388
  0.0 62.2 %copy-start = (f32[512,256]{1,0:T(8,128)S(1)}, f32[512,256]{1,0:T(8,128)}, u32[]{:S(2)}) copy-start(f32[512,256]{1,0:T(8,128)} %constant.16.clone.phase_ref) | copy-start | bytes 1572868
  0.0 62.2 %copy-start.1 = (bf16[512,512]{1,0:T(8,128)(2,1)S(1)}, bf16[512,512]{1,0:T(8,128)(2,1)}, u32[]{:S(2)}) copy-start(bf16[512,512]{1,0:T(8,128)(2,1)} %constant.15.clone.wlo_ref) | copy-start | bytes 1572868
  0.0 18.2 %copy-start.3 = (s32[4,2]{0,1:T(2,128)S(1)}, s32[4,2]{0,1:T(2,128)}, u32[]{:S(2)}) copy-start(s32[4,2]{0,1:T(2,128)} %param.7) | copy-start | bytes 100
  4.1 33.5 %all-to-all-start = ((bf16[32,2,2,32,128]{4,3,2,1,0:T(8,128)(2,1)}), bf16[32,2,2,32,128]{4,3,2,1,0:T(8,128)(2,1)S(1)}, u32[]{:S(2)}, u32[]{:S(2)}) async-start(bf16[32,2,2,32,128]{4,3,2,1,0:T(8,128)(2,1)} %bitcast.14), calls=%async_computation | async-start | bytes 2097152 | tf_op jit(solution)/shard_map/all_to_all | solution.py:456
  37.6 32.0 %all-to-all-start.1 = ((bf16[32,2,2,32,128]{4,3,2,1,0:T(8,128)(2,1)}), bf16[32,2,2,32,128]{4,3,2,1,0:T(8,128)(2,1)S(1)}, u32[]{:S(2)}, u32[]{:S(2)}) async-start(bf16[32,2,2,32,128]{4,3,2,1,0:T(8,128)(2,1)} %bitcast.13), calls=%async_computation.1 | async-start | bytes 2097152 | tf_op jit(solution)/shard_map/all_to_all | solution.py:456
  43.5 12.6 %collective-permute-start = (s32[2,136,128]{2,1,0:T(8,128)S(1)}, s32[2,136,128]{2,1,0:T(8,128)S(1)}, u32[]{:S(2)}, u32[]{:S(2)}) collective-permute-start(s32[2,136,128]{2,1,0:T(8,128)S(1)} %get-tuple-element.38), channel_id=1, source_target_pairs={{0,2},{1,3},{2,0},{3,1},{4,6},{5,7},{6,4},{7,5},{8,10},{9,11},{10,... | collective-permute-start | bytes 417800 | tf_op jit(solution)/shard_map/ppermute | solution.py:428
  45.4 10.8 %collective-permute-start.1 = (s32[2,136,128]{2,1,0:T(8,128)S(1)}, s32[2,136,128]{2,1,0:T(8,128)S(1)}, u32[]{:S(2)}, u32[]{:S(2)}) collective-permute-start(s32[2,136,128]{2,1,0:T(8,128)S(1)} %get-tuple-element.39), channel_id=1, source_target_pairs={{0,4},{1,5},{2,6},{3,7},{4,0},{5,1},{6,2},{7,3},{8,12},{9,13},{10,... | collective-permute-start | bytes 417800 | tf_op jit(solution)/shard_map/ppermute | solution.py:428
  46.8 14.0 %collective-permute-start.2 = (s32[2,136,128]{2,1,0:T(8,128)S(1)}, s32[2,136,128]{2,1,0:T(8,128)S(1)}, u32[]{:S(2)}, u32[]{:S(2)}) collective-permute-start(s32[2,136,128]{2,1,0:T(8,128)S(1)} %get-tuple-element.40), channel_id=1, source_target_pairs={{0,6},{1,7},{2,4},{3,5},{4,2},{5,3},{6,0},{7,1},{8,14},{9,15},{10,... | collective-permute-start | bytes 417800 | tf_op jit(solution)/shard_map/ppermute | solution.py:428
  47.1 13.7 %collective-permute-start.3 = (s32[2,136,128]{2,1,0:T(8,128)S(1)}, s32[2,136,128]{2,1,0:T(8,128)S(1)}, u32[]{:S(2)}, u32[]{:S(2)}) collective-permute-start(s32[2,136,128]{2,1,0:T(8,128)S(1)} %get-tuple-element.37.refs_0_), channel_id=1, source_target_pairs={{0,1},{1,0},{2,3},{3,2},{4,5},{5,4},{6,7},{7,6},{8,9},{9,8},{10,11... | collective-permute-start | bytes 417800 | tf_op jit(solution)/shard_map/ppermute | solution.py:432
  56.2 4.6 %collective-permute-start.4 = (s32[2,136,128]{2,1,0:T(8,128)S(1)}, s32[2,136,128]{2,1,0:T(8,128)S(1)}, u32[]{:S(2)}, u32[]{:S(2)}) collective-permute-start(s32[2,136,128]{2,1,0:T(8,128)S(1)} %collective-permute-done.refs_1_), channel_id=1, source_target_pairs={{0,1},{1,0},{2,3},{3,2},{4,5},{5,4},{6,7},{7,6},{8,9},{9,8},{10,11... | collective-permute-start | bytes 417800 | tf_op jit(solution)/shard_map/ppermute | solution.py:432
  56.2 4.6 %collective-permute-start.5 = (s32[2,136,128]{2,1,0:T(8,128)S(1)}, s32[2,136,128]{2,1,0:T(8,128)S(1)}, u32[]{:S(2)}, u32[]{:S(2)}) collective-permute-start(s32[2,136,128]{2,1,0:T(8,128)S(1)} %collective-permute-done.1.refs_2_), channel_id=1, source_target_pairs={{0,1},{1,0},{2,3},{3,2},{4,5},{5,4},{6,7},{7,6},{8,9},{9,8},{10,11... | collective-permute-start | bytes 417800 | tf_op jit(solution)/shard_map/ppermute | solution.py:432
  60.8 1.4 %collective-permute-start.6 = (s32[2,136,128]{2,1,0:T(8,128)S(1)}, s32[2,136,128]{2,1,0:T(8,128)S(1)}, u32[]{:S(2)}, u32[]{:S(2)}) collective-permute-start(s32[2,136,128]{2,1,0:T(8,128)S(1)} %collective-permute-done.2.refs_3_), channel_id=1, source_target_pairs={{0,1},{1,0},{2,3},{3,2},{4,5},{5,4},{6,7},{7,6},{8,9},{9,8},{10,11... | collective-permute-start | bytes 417800 | tf_op jit(solution)/shard_map/ppermute | solution.py:432
  62.2 1.0 copy-start.2
  72.0 6.5 %collective-permute-start.10 = (s32[2,136,128]{2,1,0:T(8,128)S(1)}, s32[2,136,128]{2,1,0:T(8,128)S(1)}, u32[]{:S(2)}, u32[]{:S(2)}) collective-permute-start(s32[2,136,128]{2,1,0:T(8,128)S(1)} %get-tuple-element.48), channel_id=1, source_target_pairs={{0,2},{1,3},{2,0},{3,1},{4,6},{5,7},{6,4},{7,5},{8,10},{9,11},{10,... | collective-permute-start | bytes 417800 | tf_op jit(solution)/shard_map/ppermute | solution.py:428
  73.4 8.4 %collective-permute-start.11 = (s32[2,136,128]{2,1,0:T(8,128)S(1)}, s32[2,136,128]{2,1,0:T(8,128)S(1)}, u32[]{:S(2)}, u32[]{:S(2)}) collective-permute-start(s32[2,136,128]{2,1,0:T(8,128)S(1)} %get-tuple-element.49), channel_id=1, source_target_pairs={{0,4},{1,5},{2,6},{3,7},{4,0},{5,1},{6,2},{7,3},{8,12},{9,13},{10,... | collective-permute-start | bytes 417800 | tf_op jit(solution)/shard_map/ppermute | solution.py:428
  73.4 8.4 %collective-permute-start.12 = (s32[2,136,128]{2,1,0:T(8,128)S(1)}, s32[2,136,128]{2,1,0:T(8,128)S(1)}, u32[]{:S(2)}, u32[]{:S(2)}) collective-permute-start(s32[2,136,128]{2,1,0:T(8,128)S(1)} %get-tuple-element.50), channel_id=1, source_target_pairs={{0,6},{1,7},{2,4},{3,5},{4,2},{5,3},{6,0},{7,1},{8,14},{9,15},{10,... | collective-permute-start | bytes 417800 | tf_op jit(solution)/shard_map/ppermute | solution.py:428
  75.6 6.8 %collective-permute-start.8 = (s32[136,128]{1,0:T(8,128)S(1)}, s32[136,128]{1,0:T(8,128)S(1)}, u32[]{:S(2)}, u32[]{:S(2)}) collective-permute-start(s32[136,128]{1,0:T(8,128)S(1)} %get-tuple-element.43), channel_id=1, source_target_pairs={{0,16},{8,24},{16,0},{24,8},{1,17},{9,25},{17,1},{25,9},{2,18},{10... | collective-permute-start | bytes 208904 | tf_op jit(solution)/shard_map/ppermute | solution.py:421
  77.3 11.9 %collective-permute-start.13 = (s32[2,136,128]{2,1,0:T(8,128)S(1)}, s32[2,136,128]{2,1,0:T(8,128)S(1)}, u32[]{:S(2)}, u32[]{:S(2)}) collective-permute-start(s32[2,136,128]{2,1,0:T(8,128)S(1)} %get-tuple-element.51.refs_0_), channel_id=1, source_target_pairs={{0,1},{1,0},{2,3},{3,2},{4,5},{5,4},{6,7},{7,6},{8,9},{9,8},{10,11... | collective-permute-start | bytes 417800 | tf_op jit(solution)/shard_map/ppermute | solution.py:432
  78.5 10.7 %collective-permute-start.14 = (s32[2,136,128]{2,1,0:T(8,128)S(1)}, s32[2,136,128]{2,1,0:T(8,128)S(1)}, u32[]{:S(2)}, u32[]{:S(2)}) collective-permute-start(s32[2,136,128]{2,1,0:T(8,128)S(1)} %collective-permute-done.10.refs_1_), channel_id=1, source_target_pairs={{0,1},{1,0},{2,3},{3,2},{4,5},{5,4},{6,7},{7,6},{8,9},{9,8},{10,11... | collective-permute-start | bytes 417800 | tf_op jit(solution)/shard_map/ppermute | solution.py:432
  81.8 7.4 %collective-permute-start.15 = (s32[2,136,128]{2,1,0:T(8,128)S(1)}, s32[2,136,128]{2,1,0:T(8,128)S(1)}, u32[]{:S(2)}, u32[]{:S(2)}) collective-permute-start(s32[2,136,128]{2,1,0:T(8,128)S(1)} %collective-permute-done.11.refs_2_), channel_id=1, source_target_pairs={{0,1},{1,0},{2,3},{3,2},{4,5},{5,4},{6,7},{7,6},{8,9},{9,8},{10,11... | collective-permute-start | bytes 417800 | tf_op jit(solution)/shard_map/ppermute | solution.py:432
  81.8 7.4 %collective-permute-start.16 = (s32[2,136,128]{2,1,0:T(8,128)S(1)}, s32[2,136,128]{2,1,0:T(8,128)S(1)}, u32[]{:S(2)}, u32[]{:S(2)}) collective-permute-start(s32[2,136,128]{2,1,0:T(8,128)S(1)} %collective-permute-done.12.refs_3_), channel_id=1, source_target_pairs={{0,1},{1,0},{2,3},{3,2},{4,5},{5,4},{6,7},{7,6},{8,9},{9,8},{10,11... | collective-permute-start | bytes 417800 | tf_op jit(solution)/shard_map/ppermute | solution.py:432
  82.3 6.2 %collective-permute-start.9 = (s32[136,128]{1,0:T(8,128)S(1)}, s32[136,128]{1,0:T(8,128)S(1)}, u32[]{:S(2)}, u32[]{:S(2)}) collective-permute-start(s32[136,128]{1,0:T(8,128)S(1)} %get-tuple-element.44), channel_id=1, source_target_pairs={{0,24},{8,16},{16,8},{24,0},{1,25},{9,17},{17,9},{25,1},{2,26},{10... | collective-permute-start | bytes 208904 | tf_op jit(solution)/shard_map/ppermute | solution.py:421
  88.5 11.5 %collective-permute-start.7 = (s32[136,128]{1,0:T(8,128)S(1)}, s32[136,128]{1,0:T(8,128)S(1)}, u32[]{:S(2)}, u32[]{:S(2)}) collective-permute-start(s32[136,128]{1,0:T(8,128)S(1)} %get-tuple-element.42), channel_id=1, source_target_pairs={{0,8},{8,0},{16,24},{24,16},{1,9},{9,1},{17,25},{25,17},{2,10},{10... | collective-permute-start | bytes 208904 | tf_op jit(solution)/shard_map/ppermute | solution.py:421
  95.6 4.8 %collective-permute-start.17 = (s32[136,128]{1,0:T(8,128)S(1)}, s32[136,128]{1,0:T(8,128)S(1)}, u32[]{:S(2)}, u32[]{:S(2)}) collective-permute-start(s32[136,128]{1,0:T(8,128)S(1)} %get-tuple-element.60), channel_id=1, source_target_pairs={{0,8},{8,0},{16,24},{24,16},{1,9},{9,1},{17,25},{25,17},{2,10},{10... | collective-permute-start | bytes 208904 | tf_op jit(solution)/shard_map/ppermute | solution.py:421
  97.0 6.7 %collective-permute-start.18 = (s32[136,128]{1,0:T(8,128)S(1)}, s32[136,128]{1,0:T(8,128)S(1)}, u32[]{:S(2)}, u32[]{:S(2)}) collective-permute-start(s32[136,128]{1,0:T(8,128)S(1)} %get-tuple-element.61), channel_id=1, source_target_pairs={{0,16},{8,24},{16,0},{24,8},{1,17},{9,25},{17,1},{25,9},{2,18},{10... | collective-permute-start | bytes 208904 | tf_op jit(solution)/shard_map/ppermute | solution.py:421
  98.6 6.2 %collective-permute-start.19 = (s32[136,128]{1,0:T(8,128)S(1)}, s32[136,128]{1,0:T(8,128)S(1)}, u32[]{:S(2)}, u32[]{:S(2)}) collective-permute-start(s32[136,128]{1,0:T(8,128)S(1)} %get-tuple-element.62), channel_id=1, source_target_pairs={{0,24},{8,16},{16,8},{24,0},{1,25},{9,17},{17,9},{25,1},{2,26},{10... | collective-permute-start | bytes 208904 | tf_op jit(solution)/shard_map/ppermute | solution.py:421

commit v8 on v7

--- a/solution.py
+++ b/solution.py
@@ -97,7 +97,8 @@
     return (row == want).astype(jnp.bfloat16)
 
 
-def pack_kernel(n_seg, n_pair, chunk, x_ref, out_ref, buf_ref):
+def pack_kernel(n_seg, chunk, x_ref, out_ref, buf_ref):
+    n_pair = out_ref.shape[1]
     band = x_ref.shape[1] // n_pair
     sel = selection(n_seg, chunk, x_ref.shape[2])
     rows = band // GROUPS
@@ -123,10 +124,13 @@
     band = freq // n_pair
     shape = (n_seg, n_pair, chans // TILE, 2, band // GROUPS, TILE)
     return pl.pallas_call(
-        functools.partial(pack_kernel, n_seg, n_pair, chunk),
+        functools.partial(pack_kernel, n_seg, chunk),
         out_shape=jax.ShapeDtypeStruct(shape, jnp.bfloat16),
-        in_specs=[pl.BlockSpec(memory_space=pltpu.VMEM)],
-        out_specs=pl.BlockSpec(memory_space=pltpu.VMEM),
+        grid=(2,),
+        in_specs=[pl.BlockSpec((2, freq // 2, chans), lambda i: (0, i, 0))],
+        out_specs=pl.BlockSpec(
+            (n_seg, n_pair // 2) + shape[2:], lambda i: (0, i, 0, 0, 0, 0)
+        ),
         scratch_shapes=[pltpu.VMEM((2, 2, band, TILE), jnp.float32)],
         name="pack",
         cost_estimate=SMALL,
@@ -423,11 +427,13 @@
     ]
 
 
-def exchange_plane(blocks, n_pair):
+def exchange_plane(blocks, n_pair, between=None):
     direct = [blocks[0]] + [
         lax.ppermute(blocks[k], "pair", [(i, i ^ (2 * k)) for i in range(n_pair)])
         for k in range(1, n_pair // 2)
     ]
+    if between is not None:
+        direct, _ = lax.optimization_barrier((direct, between))
     swap = [(i, i ^ 1) for i in range(n_pair)]
     return direct + [lax.ppermute(d, "pair", swap) for d in direct]
 
@@ -451,7 +457,7 @@
     if chunks > 1:
         table, packed[1], _ = lax.optimization_barrier((table, packed[1], sums))
     done = []
-    lags = None
+    blocks = lags = None
     for sent in packed:
         got = lax.all_to_all(
             sent.reshape(n_seg * n_pair, tiles, 2, rows, TILE),
@@ -460,15 +466,17 @@
             concat_axis=0,
             tiled=True,
         )
-        if lags is not None:
-            got, _ = lax.optimization_barrier((got, lags))
+        if blocks is not None:
+            got, _ = lax.optimization_barrier((got, blocks))
         spec = got.reshape(n_seg, n_pair * tiles, 2, rows, TILE)
-        blocks = stacks(me, table, spec, n_seg, n_pair, most)
-        blocks = exchange_plane(blocks, n_pair)
-        if done:
-            blocks, _ = lax.optimization_barrier((blocks, done[2:]))
-        lags = dft(me, tables, blocks, freq, n_seg, n_pair, most)
-        done += exchange(lags, "seg", n_seg)
+        stack = stacks(me, table, spec, n_seg, n_pair, most)
+        if blocks is not None:
+            blocks, _ = lax.optimization_barrier((blocks, stack))
+            lags = dft(me, tables, blocks, freq, n_seg, n_pair, most)
+            done += exchange(lags, "seg", n_seg)
+        blocks = exchange_plane(stack, n_pair, lags)
+    lags = dft(me, tables, blocks, freq, n_seg, n_pair, most)
+    done += exchange(lags, "seg", n_seg)
     return unpack(me, done, n_seg, chunks, most)
 
 

time: 109 us -> 105 us (0.963)
  waiting for transfers between devices: 36.2 us -> 33.3 us
    all_to_all x2, waiting for transfers between devices: 9.3 us -> 16.3 us  [body(): lax.all_to_all(sent.reshape(n_seg * n_pair, tiles, 2, rows, TILE), ('seg'...]
    ppermute x6, waiting for transfers between devices: 17.7 us -> 13.3 us  [exchange_plane(): lax.ppermute(blocks[k], 'pair', [(i, i ^ 2 * k) for i in range(n_pair)])]
    ppermute x6, waiting for transfers between devices: 7.83 us -> 3.68 us  [exchange(): lax.ppermute(blocks[k], axis, [(i, i ^ k) for i in range(size)])]
    ppermute x8, waiting for transfers between devices: 1.36 us -> 0.02 us  [exchange_plane(): return direct + [lax.ppermute(d, 'pair', swap) for d in direct]]
    ppermute x6, starting transfers between devices: 10 us -> 8.83 us  [exchange(): lax.ppermute(blocks[k], axis, [(i, i ^ k) for i in range(size)])]
  transfers between devices with their start and end apart: 22 -> 22, of which waited for: 10 -> 6; matrix products, arithmetic and copies ran while one was open for 1% -> 1% of each run, Pallas kernels for 19% -> 20%
where the time goes in v8:
time: 105 us; the launch traced here: 104 us
  waiting for transfers between devices  33.3 us (32%)
  Pallas kernels  30.3 us (29%)
  starting transfers between devices  28.5 us (27%)
  blocking collectives  8.28 us (8%)
  local copies, waits for them, and re-layouts  2.15 us (2%)
  between operations  1.44 us (1%)
    all_to_all x2, waiting for transfers between devices, body(): lax.all_to_all(sent.reshape(n_seg * n_pair, tiles, 2, rows, TILE), ('seg'...  16.3 us
    ppermute x6, waiting for transfers between devices, exchange_plane(): lax.ppermute(blocks[k], 'pair', [(i, i ^ 2 * k) for i in range(n_pair)])  13.3 us
    pallas_call x2, Pallas kernels, dft(): pl.pallas_call(functools.partial(dft_kernel, n_seg, n_pair, most), out_sh...  12.7 us
    all_to_all x2, starting transfers between devices, body(): lax.all_to_all(sent.reshape(n_seg * n_pair, tiles, 2, rows, TILE), ('seg'...  10.9 us
    ppermute x6, starting transfers between devices, exchange(): lax.ppermute(blocks[k], axis, [(i, i ^ k) for i in range(size)])  8.83 us
    unnamed x1, blocking collectives  8.28 us
    pallas_call x2, Pallas kernels, pack(): pl.pallas_call(functools.partial(pack_kernel, n_seg, chunk), out_shape=ja...  7.35 us
    ppermute x6, starting transfers between devices, exchange_plane(): lax.ppermute(blocks[k], 'pair', [(i, i ^ 2 * k) for i in range(n_pair)])  7.11 us
  transfers between devices with their start and end apart: 22, of which 6 were waited for; matrix products, arithmetic and copies ran while one was open for 1% of the time, Pallas kernels for 20%

profile of v8, /device:TPU:0, one launch (start us, length us, event | category | flops | bytes accessed | tf_op | source)
XLA Modules:
  0.0 104.1 jit_solution(5531120712162121445)
XLA Ops:
  0.0 3.7 %pack.3 = bf16[4,8,2,2,32,128]{5,4,3,2,1,0:T(8,128)(2,1)} custom-call(bf16[2,2048,256]{2,1,0:T(8,128)(2,1)} %bitcast.11), custom_call_target="tpu_custom_call" | custom-call | flops 1 | bytes 1 | tf_op jit(solution)/shard_map/pack/pallas_call | solution.py:126
  3.7 7.3 %all-to-all-start = ((bf16[32,2,2,32,128]{4,3,2,1,0:T(8,128)(2,1)}), bf16[32,2,2,32,128]{4,3,2,1,0:T(8,128)(2,1)S(1)}, u32[]{:S(2)}, u32[]{:S(2)}) async-start(bf16[32,2,2,32,128]{4,3,2,1,0:T(8,128)(2,1)} %bitcast.14), calls=%async_computation | async-start | bytes 2097152 | tf_op jit(solution)/shard_map/all_to_all | solution.py:462
  11.0 3.6 %pack.2 = bf16[4,8,2,2,32,128]{5,4,3,2,1,0:T(8,128)(2,1)} custom-call(bf16[2,2048,256]{2,1,0:T(8,128)(2,1)} %bitcast.12), custom_call_target="tpu_custom_call" | custom-call | flops 1 | bytes 1 | tf_op jit(solution)/shard_map/pack/pallas_call | solution.py:126
  14.7 2.2 %sums.1.tables_ref = f32[49152,256]{1,0:T(8,128)} custom-call(), custom_call_target="tpu_custom_call" | custom-call | flops 1 | bytes 1 | tf_op jit(solution)/shard_map/sums/pallas_call | solution.py:320
  17.8 0.6 dynamic-slice
  19.3 8.3 %all-reduce = s32[72]{0:T(128)S(1)} all-reduce(s32[72]{0:T(128)S(1)} %dynamic-update-slice), channel_id=2, replica_groups=mesh['seg'=4,'pair'=8] {'pair'}, use_global_device_ids=true, to_apply=%add | all-reduce | flops 72 | bytes 576
  27.7 9.6 %all-to-all-done = bf16[32,2,2,32,128]{4,3,2,1,0:T(8,128)(2,1)S(1)} async-done(((bf16[32,2,2,32,128]{4,3,2,1,0:T(8,128)(2,1)}), bf16[32,2,2,32,128]{4,3,2,1,0:T(8,128)(2,1)S(1)}, u32[]{:S(2)}, u32[]{:S(2)}) %all-to-all-start) | async-done | bytes 1048608 | tf_op jit(solution)/shard_map/all_to_all | solution.py:462
  37.3 3.6 %all-to-all-start.1 = ((bf16[32,2,2,32,128]{4,3,2,1,0:T(8,128)(2,1)}), bf16[32,2,2,32,128]{4,3,2,1,0:T(8,128)(2,1)S(1)}, u32[]{:S(2)}, u32[]{:S(2)}) async-start(bf16[32,2,2,32,128]{4,3,2,1,0:T(8,128)(2,1)} %bitcast.13), calls=%async_computation.1 | async-start | bytes 2097152 | tf_op jit(solution)/shard_map/all_to_all | solution.py:462
  41.0 2.1 %stack.14 = (s32[2,136,128]{2,1,0:T(8,128)S(1)}, s32[2,136,128]{2,1,0:T(8,128)S(1)}, s32[2,136,128]{2,1,0:T(8,128)S(1)}, s32[2,136,128]{2,1,0:T(8,128)S(1)}) custom-call(s32[2]{0:T(128)S(1)} %pad_add_fusion.me_ref, s32[8,9]{1,0:T(8,128)S(1)} %reshape.28.table_ref, bf16[4,16,2,32,128]{4,3,2,1,0:T(8,128)(2,1)S(1)} %bitcast.10), custom_call_target="tpu_custom_call" | custom-call | flops 1 | bytes 1 | tf_op jit(solution)/shard_map/stack/pallas_call | solution.py:200
  43.1 1.8 %collective-permute-start = (s32[2,136,128]{2,1,0:T(8,128)S(1)}, s32[2,136,128]{2,1,0:T(8,128)S(1)}, u32[]{:S(2)}, u32[]{:S(2)}) collective-permute-start(s32[2,136,128]{2,1,0:T(8,128)S(1)} %get-tuple-element.42), channel_id=1, source_target_pairs={{0,2},{1,3},{2,0},{3,1},{4,6},{5,7},{6,4},{7,5},{8,10},{9,11},{10,... | collective-permute-start | bytes 417800 | tf_op jit(solution)/shard_map/ppermute | solution.py:432
  45.0 1.5 %collective-permute-start.1 = (s32[2,136,128]{2,1,0:T(8,128)S(1)}, s32[2,136,128]{2,1,0:T(8,128)S(1)}, u32[]{:S(2)}, u32[]{:S(2)}) collective-permute-start(s32[2,136,128]{2,1,0:T(8,128)S(1)} %get-tuple-element.43), channel_id=1, source_target_pairs={{0,4},{1,5},{2,6},{3,7},{4,0},{5,1},{6,2},{7,3},{8,12},{9,13},{10,... | collective-permute-start | bytes 417800 | tf_op jit(solution)/shard_map/ppermute | solution.py:432
  46.7 9.2 %collective-permute-done.refs_1_ = s32[2,136,128]{2,1,0:T(8,128)S(1)} collective-permute-done((s32[2,136,128]{2,1,0:T(8,128)S(1)}, s32[2,136,128]{2,1,0:T(8,128)S(1)}, u32[]{:S(2)}, u32[]{:S(2)}) %collective-permute-start) | collective-permute-done | bytes 139296 | tf_op jit(solution)/shard_map/ppermute | solution.py:432
  55.9 0.5 collective-permute-start.5
  56.4 4.1 %collective-permute-done.2.refs_3_ = s32[2,136,128]{2,1,0:T(8,128)S(1)} collective-permute-done((s32[2,136,128]{2,1,0:T(8,128)S(1)}, s32[2,136,128]{2,1,0:T(8,128)S(1)}, u32[]{:S(2)}, u32[]{:S(2)}) %collective-permute-start.2) | collective-permute-done | bytes 139296 | tf_op jit(solution)/shard_map/ppermute | solution.py:432
  60.5 6.6 %all-to-all-done.1 = bf16[32,2,2,32,128]{4,3,2,1,0:T(8,128)(2,1)S(1)} async-done(((bf16[32,2,2,32,128]{4,3,2,1,0:T(8,128)(2,1)}), bf16[32,2,2,32,128]{4,3,2,1,0:T(8,128)(2,1)S(1)}, u32[]{:S(2)}, u32[]{:S(2)}) %all-to-all-start.1) | async-done | bytes 1048608 | tf_op jit(solution)/shard_map/all_to_all | solution.py:462
  67.2 2.3 %stack.15 = (s32[2,136,128]{2,1,0:T(8,128)S(1)}, s32[2,136,128]{2,1,0:T(8,128)S(1)}, s32[2,136,128]{2,1,0:T(8,128)S(1)}, s32[2,136,128]{2,1,0:T(8,128)S(1)}) custom-call(s32[2]{0:T(128)S(1)} %pad_add_fusion.me_ref, s32[8,9]{1,0:T(8,128)S(1)} %reshape.28.table_ref, bf16[4,16,2,32,128]{4,3,2,1,0:T(8,128)(2,1)S(1)} %bitcast.9), custom_call_target="tpu_custom_call" | custom-call | flops 1 | bytes 1 | tf_op jit(solution)/shard_map/stack/pallas_call | solution.py:200
  69.5 1.5 %collective-permute-start.10 = (s32[2,136,128]{2,1,0:T(8,128)S(1)}, s32[2,136,128]{2,1,0:T(8,128)S(1)}, u32[]{:S(2)}, u32[]{:S(2)}) collective-permute-start(s32[2,136,128]{2,1,0:T(8,128)S(1)} %get-tuple-element.48), channel_id=1, source_target_pairs={{0,2},{1,3},{2,0},{3,1},{4,6},{5,7},{6,4},{7,5},{8,10},{9,11},{10,... | collective-permute-start | bytes 417800 | tf_op jit(solution)/shard_map/ppermute | solution.py:432
  71.0 1.5 %collective-permute-start.11 = (s32[2,136,128]{2,1,0:T(8,128)S(1)}, s32[2,136,128]{2,1,0:T(8,128)S(1)}, u32[]{:S(2)}, u32[]{:S(2)}) collective-permute-start(s32[2,136,128]{2,1,0:T(8,128)S(1)} %get-tuple-element.49), channel_id=1, source_target_pairs={{0,4},{1,5},{2,6},{3,7},{4,0},{5,1},{6,2},{7,3},{8,12},{9,13},{10,... | collective-permute-start | bytes 417800 | tf_op jit(solution)/shard_map/ppermute | solution.py:432
  72.5 0.5 collective-permute-start.12
  73.1 1.0 copy-done.2
  74.1 6.4 %dft.2 = (s32[136,128]{1,0:T(8,128)S(1)}, s32[136,128]{1,0:T(8,128)S(1)}, s32[136,128]{1,0:T(8,128)S(1)}, s32[136,128]{1,0:T(8,128)S(1)}) custom-call(s32[2]{0:T(128)S(1)} %pad_add_fusion.me_ref, bf16[512,512]{1,0:T(8,128)(2,1)S(1)} %copy-done.2, bf16[512,512]{1,0:T(8,128)(2,1)S(1)} %copy-done.1, f32[512,256]{1,0:T(8,128)S(1)} %copy-done, ...), custom_call_target="tpu_custom_call" | custom-call | flops 1 | bytes 1 | tf_op jit(solution)/shard_map/dft/pallas_call | solution.py:354
  80.6 0.5 collective-permute-start.14
  81.2 0.4 collective-permute-start.16
  81.6 0.8 collective-permute-start.7
  82.4 1.1 %collective-permute-start.8 = (s32[136,128]{1,0:T(8,128)S(1)}, s32[136,128]{1,0:T(8,128)S(1)}, u32[]{:S(2)}, u32[]{:S(2)}) collective-permute-start(s32[136,128]{1,0:T(8,128)S(1)} %get-tuple-element.61), channel_id=1, source_target_pairs={{0,16},{8,24},{16,0},{24,8},{1,17},{9,25},{17,1},{25,9},{2,18},{10... | collective-permute-start | bytes 208904 | tf_op jit(solution)/shard_map/ppermute | solution.py:425
  83.5 2.5 %collective-permute-start.9 = (s32[136,128]{1,0:T(8,128)S(1)}, s32[136,128]{1,0:T(8,128)S(1)}, u32[]{:S(2)}, u32[]{:S(2)}) collective-permute-start(s32[136,128]{1,0:T(8,128)S(1)} %get-tuple-element.62), channel_id=1, source_target_pairs={{0,24},{8,16},{16,8},{24,0},{1,25},{9,17},{17,9},{25,1},{2,26},{10... | collective-permute-start | bytes 208904 | tf_op jit(solution)/shard_map/ppermute | solution.py:425
  86.0 6.4 %dft.3 = (s32[136,128]{1,0:T(8,128)S(1)}, s32[136,128]{1,0:T(8,128)S(1)}, s32[136,128]{1,0:T(8,128)S(1)}, s32[136,128]{1,0:T(8,128)S(1)}) custom-call(s32[2]{0:T(128)S(1)} %pad_add_fusion.me_ref, bf16[512,512]{1,0:T(8,128)(2,1)S(1)} %copy-done.2, bf16[512,512]{1,0:T(8,128)(2,1)S(1)} %copy-done.1, f32[512,256]{1,0:T(8,128)S(1)} %copy-done, ...), custom_call_target="tpu_custom_call" | custom-call | flops 1 | bytes 1 | tf_op jit(solution)/shard_map/dft/pallas_call | solution.py:354
  92.5 1.8 %collective-permute-start.18 = (s32[136,128]{1,0:T(8,128)S(1)}, s32[136,128]{1,0:T(8,128)S(1)}, u32[]{:S(2)}, u32[]{:S(2)}) collective-permute-start(s32[136,128]{1,0:T(8,128)S(1)} %get-tuple-element.69), channel_id=1, source_target_pairs={{0,16},{8,24},{16,0},{24,8},{1,17},{9,25},{17,1},{25,9},{2,18},{10... | collective-permute-start | bytes 208904 | tf_op jit(solution)/shard_map/ppermute | solution.py:425
  94.3 2.5 %collective-permute-start.19 = (s32[136,128]{1,0:T(8,128)S(1)}, s32[136,128]{1,0:T(8,128)S(1)}, u32[]{:S(2)}, u32[]{:S(2)}) collective-permute-start(s32[136,128]{1,0:T(8,128)S(1)} %get-tuple-element.70), channel_id=1, source_target_pairs={{0,24},{8,16},{16,8},{24,0},{1,25},{9,17},{17,9},{25,1},{2,26},{10... | collective-permute-start | bytes 208904 | tf_op jit(solution)/shard_map/ppermute | solution.py:425
  96.8 2.9 %collective-permute-done.18.refs_6_ = s32[136,128]{1,0:T(8,128)S(1)} collective-permute-done((s32[136,128]{1,0:T(8,128)S(1)}, s32[136,128]{1,0:T(8,128)S(1)}, u32[]{:S(2)}, u32[]{:S(2)}) %collective-permute-start.18) | collective-permute-done | bytes 69664 | tf_op jit(solution)/shard_map/ppermute | solution.py:425
  99.7 0.8 collective-permute-done.19.refs_7_
  100.5 3.6 %unpack.1 = f32[2,256,4,128]{3,2,1,0:T(4,128)} custom-call(s32[2]{0:T(128)S(1)} %pad_add_fusion.me_ref, s32[136,128]{1,0:T(8,128)S(1)} %get-tuple-element.59.refs_0_, s32[136,128]{1,0:T(8,128)S(1)} %collective-permute-done.7.refs_1_, s32[136,128]{1,0:T(8,128)S(1)} %collective-permute-done.8.refs_2_, s32[136,128]{1,0:T(8,128)S(1)} %collective-permute-done.9.refs_3_, ...), custom_call_target="tpu_custom_call" | custom-call | flops 1 | bytes 1 | tf_op jit(solution)/shard_map/unpack/pallas_call | solution.py:409
  (39 shorter events, 1.2 us)
Async XLA Ops:
  0.0 17.8 %copy-start.4 = (u32[32]{0:T(128)S(1)}, u32[32]{0:T(128)}, u32[]{:S(2)}) copy-start(u32[32]{0:T(128)} %constant.22) | copy-start | bytes 388
  0.0 73.0 %copy-start = (f32[512,256]{1,0:T(8,128)S(1)}, f32[512,256]{1,0:T(8,128)}, u32[]{:S(2)}) copy-start(f32[512,256]{1,0:T(8,128)} %constant.16.clone.phase_ref) | copy-start | bytes 1572868
  0.0 73.0 %copy-start.1 = (bf16[512,512]{1,0:T(8,128)(2,1)S(1)}, bf16[512,512]{1,0:T(8,128)(2,1)}, u32[]{:S(2)}) copy-start(bf16[512,512]{1,0:T(8,128)(2,1)} %constant.15.clone.wlo_ref) | copy-start | bytes 1572868
  0.0 17.5 %copy-start.3 = (s32[4,2]{0,1:T(2,128)S(1)}, s32[4,2]{0,1:T(2,128)}, u32[]{:S(2)}) copy-start(s32[4,2]{0,1:T(2,128)} %param.7) | copy-start | bytes 100
  3.7 33.6 %all-to-all-start = ((bf16[32,2,2,32,128]{4,3,2,1,0:T(8,128)(2,1)}), bf16[32,2,2,32,128]{4,3,2,1,0:T(8,128)(2,1)S(1)}, u32[]{:S(2)}, u32[]{:S(2)}) async-start(bf16[32,2,2,32,128]{4,3,2,1,0:T(8,128)(2,1)} %bitcast.14), calls=%async_computation | async-start | bytes 2097152 | tf_op jit(solution)/shard_map/all_to_all | solution.py:462
  37.3 29.9 %all-to-all-start.1 = ((bf16[32,2,2,32,128]{4,3,2,1,0:T(8,128)(2,1)}), bf16[32,2,2,32,128]{4,3,2,1,0:T(8,128)(2,1)S(1)}, u32[]{:S(2)}, u32[]{:S(2)}) async-start(bf16[32,2,2,32,128]{4,3,2,1,0:T(8,128)(2,1)} %bitcast.13), calls=%async_computation.1 | async-start | bytes 2097152 | tf_op jit(solution)/shard_map/all_to_all | solution.py:462
  43.1 12.7 %collective-permute-start = (s32[2,136,128]{2,1,0:T(8,128)S(1)}, s32[2,136,128]{2,1,0:T(8,128)S(1)}, u32[]{:S(2)}, u32[]{:S(2)}) collective-permute-start(s32[2,136,128]{2,1,0:T(8,128)S(1)} %get-tuple-element.42), channel_id=1, source_target_pairs={{0,2},{1,3},{2,0},{3,1},{4,6},{5,7},{6,4},{7,5},{8,10},{9,11},{10,... | collective-permute-start | bytes 417800 | tf_op jit(solution)/shard_map/ppermute | solution.py:432
  45.0 10.9 %collective-permute-start.1 = (s32[2,136,128]{2,1,0:T(8,128)S(1)}, s32[2,136,128]{2,1,0:T(8,128)S(1)}, u32[]{:S(2)}, u32[]{:S(2)}) collective-permute-start(s32[2,136,128]{2,1,0:T(8,128)S(1)} %get-tuple-element.43), channel_id=1, source_target_pairs={{0,4},{1,5},{2,6},{3,7},{4,0},{5,1},{6,2},{7,3},{8,12},{9,13},{10,... | collective-permute-start | bytes 417800 | tf_op jit(solution)/shard_map/ppermute | solution.py:432
  46.4 14.1 %collective-permute-start.2 = (s32[2,136,128]{2,1,0:T(8,128)S(1)}, s32[2,136,128]{2,1,0:T(8,128)S(1)}, u32[]{:S(2)}, u32[]{:S(2)}) collective-permute-start(s32[2,136,128]{2,1,0:T(8,128)S(1)} %get-tuple-element.44), channel_id=1, source_target_pairs={{0,6},{1,7},{2,4},{3,5},{4,2},{5,3},{6,0},{7,1},{8,14},{9,15},{10,... | collective-permute-start | bytes 417800 | tf_op jit(solution)/shard_map/ppermute | solution.py:432
  46.7 20.5 %collective-permute-start.3 = (s32[2,136,128]{2,1,0:T(8,128)S(1)}, s32[2,136,128]{2,1,0:T(8,128)S(1)}, u32[]{:S(2)}, u32[]{:S(2)}) collective-permute-start(s32[2,136,128]{2,1,0:T(8,128)S(1)} %get-tuple-element.51.refs_0_), channel_id=1, source_target_pairs={{0,1},{1,0},{2,3},{3,2},{4,5},{5,4},{6,7},{7,6},{8,9},{9,8},{10,11... | collective-permute-start | bytes 417800 | tf_op jit(solution)/shard_map/ppermute | solution.py:438
  55.9 11.3 %collective-permute-start.4 = (s32[2,136,128]{2,1,0:T(8,128)S(1)}, s32[2,136,128]{2,1,0:T(8,128)S(1)}, u32[]{:S(2)}, u32[]{:S(2)}) collective-permute-start(s32[2,136,128]{2,1,0:T(8,128)S(1)} %collective-permute-done.refs_1_), channel_id=1, source_target_pairs={{0,1},{1,0},{2,3},{3,2},{4,5},{5,4},{6,7},{7,6},{8,9},{9,8},{10,11... | collective-permute-start | bytes 417800 | tf_op jit(solution)/shard_map/ppermute | solution.py:438
  55.9 11.3 %collective-permute-start.5 = (s32[2,136,128]{2,1,0:T(8,128)S(1)}, s32[2,136,128]{2,1,0:T(8,128)S(1)}, u32[]{:S(2)}, u32[]{:S(2)}) collective-permute-start(s32[2,136,128]{2,1,0:T(8,128)S(1)} %collective-permute-done.1.refs_2_), channel_id=1, source_target_pairs={{0,1},{1,0},{2,3},{3,2},{4,5},{5,4},{6,7},{7,6},{8,9},{9,8},{10,11... | collective-permute-start | bytes 417800 | tf_op jit(solution)/shard_map/ppermute | solution.py:438
  60.5 6.7 %collective-permute-start.6 = (s32[2,136,128]{2,1,0:T(8,128)S(1)}, s32[2,136,128]{2,1,0:T(8,128)S(1)}, u32[]{:S(2)}, u32[]{:S(2)}) collective-permute-start(s32[2,136,128]{2,1,0:T(8,128)S(1)} %collective-permute-done.2.refs_3_), channel_id=1, source_target_pairs={{0,1},{1,0},{2,3},{3,2},{4,5},{5,4},{6,7},{7,6},{8,9},{9,8},{10,11... | collective-permute-start | bytes 417800 | tf_op jit(solution)/shard_map/ppermute | solution.py:438
  69.5 11.0 %collective-permute-start.10 = (s32[2,136,128]{2,1,0:T(8,128)S(1)}, s32[2,136,128]{2,1,0:T(8,128)S(1)}, u32[]{:S(2)}, u32[]{:S(2)}) collective-permute-start(s32[2,136,128]{2,1,0:T(8,128)S(1)} %get-tuple-element.48), channel_id=1, source_target_pairs={{0,2},{1,3},{2,0},{3,1},{4,6},{5,7},{6,4},{7,5},{8,10},{9,11},{10,... | collective-permute-start | bytes 417800 | tf_op jit(solution)/shard_map/ppermute | solution.py:432
  71.0 9.5 %collective-permute-start.11 = (s32[2,136,128]{2,1,0:T(8,128)S(1)}, s32[2,136,128]{2,1,0:T(8,128)S(1)}, u32[]{:S(2)}, u32[]{:S(2)}) collective-permute-start(s32[2,136,128]{2,1,0:T(8,128)S(1)} %get-tuple-element.49), channel_id=1, source_target_pairs={{0,4},{1,5},{2,6},{3,7},{4,0},{5,1},{6,2},{7,3},{8,12},{9,13},{10,... | collective-permute-start | bytes 417800 | tf_op jit(solution)/shard_map/ppermute | solution.py:432
  72.5 8.0 %collective-permute-start.12 = (s32[2,136,128]{2,1,0:T(8,128)S(1)}, s32[2,136,128]{2,1,0:T(8,128)S(1)}, u32[]{:S(2)}, u32[]{:S(2)}) collective-permute-start(s32[2,136,128]{2,1,0:T(8,128)S(1)} %get-tuple-element.50), channel_id=1, source_target_pairs={{0,6},{1,7},{2,4},{3,5},{4,2},{5,3},{6,0},{7,1},{8,14},{9,15},{10,... | collective-permute-start | bytes 417800 | tf_op jit(solution)/shard_map/ppermute | solution.py:432
  73.1 1.0 %copy-start.2 = (bf16[512,512]{1,0:T(8,128)(2,1)S(1)}, bf16[512,512]{1,0:T(8,128)(2,1)}, u32[]{:S(2)}) copy-start(bf16[512,512]{1,0:T(8,128)(2,1)} %constant.14.clone.whi_ref) | copy-start | bytes 1572868
  80.5 1.8 %collective-permute-start.13 = (s32[2,136,128]{2,1,0:T(8,128)S(1)}, s32[2,136,128]{2,1,0:T(8,128)S(1)}, u32[]{:S(2)}, u32[]{:S(2)}) collective-permute-start(s32[2,136,128]{2,1,0:T(8,128)S(1)} %get-tuple-element.63.refs_0_), channel_id=1, source_target_pairs={{0,1},{1,0},{2,3},{3,2},{4,5},{5,4},{6,7},{7,6},{8,9},{9,8},{10,11... | collective-permute-start | bytes 417800 | tf_op jit(solution)/shard_map/ppermute | solution.py:438
  80.6 2.9 %collective-permute-start.14 = (s32[2,136,128]{2,1,0:T(8,128)S(1)}, s32[2,136,128]{2,1,0:T(8,128)S(1)}, u32[]{:S(2)}, u32[]{:S(2)}) collective-permute-start(s32[2,136,128]{2,1,0:T(8,128)S(1)} %collective-permute-done.10.refs_1_), channel_id=1, source_target_pairs={{0,1},{1,0},{2,3},{3,2},{4,5},{5,4},{6,7},{7,6},{8,9},{9,8},{10,11... | collective-permute-start | bytes 417800 | tf_op jit(solution)/shard_map/ppermute | solution.py:438
  81.1 4.9 %collective-permute-start.15 = (s32[2,136,128]{2,1,0:T(8,128)S(1)}, s32[2,136,128]{2,1,0:T(8,128)S(1)}, u32[]{:S(2)}, u32[]{:S(2)}) collective-permute-start(s32[2,136,128]{2,1,0:T(8,128)S(1)} %collective-permute-done.11.refs_2_), channel_id=1, source_target_pairs={{0,1},{1,0},{2,3},{3,2},{4,5},{5,4},{6,7},{7,6},{8,9},{9,8},{10,11... | collective-permute-start | bytes 417800 | tf_op jit(solution)/shard_map/ppermute | solution.py:438
  81.2 4.8 %collective-permute-start.16 = (s32[2,136,128]{2,1,0:T(8,128)S(1)}, s32[2,136,128]{2,1,0:T(8,128)S(1)}, u32[]{:S(2)}, u32[]{:S(2)}) collective-permute-start(s32[2,136,128]{2,1,0:T(8,128)S(1)} %collective-permute-done.12.refs_3_), channel_id=1, source_target_pairs={{0,1},{1,0},{2,3},{3,2},{4,5},{5,4},{6,7},{7,6},{8,9},{9,8},{10,11... | collective-permute-start | bytes 417800 | tf_op jit(solution)/shard_map/ppermute | solution.py:438
  81.6 12.7 %collective-permute-start.7 = (s32[136,128]{1,0:T(8,128)S(1)}, s32[136,128]{1,0:T(8,128)S(1)}, u32[]{:S(2)}, u32[]{:S(2)}) collective-permute-start(s32[136,128]{1,0:T(8,128)S(1)} %get-tuple-element.60), channel_id=1, source_target_pairs={{0,8},{8,0},{16,24},{24,16},{1,9},{9,1},{17,25},{25,17},{2,10},{10... | collective-permute-start | bytes 208904 | tf_op jit(solution)/shard_map/ppermute | solution.py:425
  82.4 14.5 %collective-permute-start.8 = (s32[136,128]{1,0:T(8,128)S(1)}, s32[136,128]{1,0:T(8,128)S(1)}, u32[]{:S(2)}, u32[]{:S(2)}) collective-permute-start(s32[136,128]{1,0:T(8,128)S(1)} %get-tuple-element.61), channel_id=1, source_target_pairs={{0,16},{8,24},{16,0},{24,8},{1,17},{9,25},{17,1},{25,9},{2,18},{10... | collective-permute-start | bytes 208904 | tf_op jit(solution)/shard_map/ppermute | solution.py:425
  83.5 13.4 %collective-permute-start.9 = (s32[136,128]{1,0:T(8,128)S(1)}, s32[136,128]{1,0:T(8,128)S(1)}, u32[]{:S(2)}, u32[]{:S(2)}) collective-permute-start(s32[136,128]{1,0:T(8,128)S(1)} %get-tuple-element.62), channel_id=1, source_target_pairs={{0,24},{8,16},{16,8},{24,0},{1,25},{9,17},{17,9},{25,1},{2,26},{10... | collective-permute-start | bytes 208904 | tf_op jit(solution)/shard_map/ppermute | solution.py:425
  92.4 4.5 %collective-permute-start.17 = (s32[136,128]{1,0:T(8,128)S(1)}, s32[136,128]{1,0:T(8,128)S(1)}, u32[]{:S(2)}, u32[]{:S(2)}) collective-permute-start(s32[136,128]{1,0:T(8,128)S(1)} %get-tuple-element.68), channel_id=1, source_target_pairs={{0,8},{8,0},{16,24},{24,16},{1,9},{9,1},{17,25},{25,17},{2,10},{10... | collective-permute-start | bytes 208904 | tf_op jit(solution)/shard_map/ppermute | solution.py:425
  92.5 7.3 %collective-permute-start.18 = (s32[136,128]{1,0:T(8,128)S(1)}, s32[136,128]{1,0:T(8,128)S(1)}, u32[]{:S(2)}, u32[]{:S(2)}) collective-permute-start(s32[136,128]{1,0:T(8,128)S(1)} %get-tuple-element.69), channel_id=1, source_target_pairs={{0,16},{8,24},{16,0},{24,8},{1,17},{9,25},{17,1},{25,9},{2,18},{10... | collective-permute-start | bytes 208904 | tf_op jit(solution)/shard_map/ppermute | solution.py:425
  94.3 6.2 %collective-permute-start.19 = (s32[136,128]{1,0:T(8,128)S(1)}, s32[136,128]{1,0:T(8,128)S(1)}, u32[]{:S(2)}, u32[]{:S(2)}) collective-permute-start(s32[136,128]{1,0:T(8,128)S(1)} %get-tuple-element.70), channel_id=1, source_target_pairs={{0,24},{8,16},{16,8},{24,0},{1,25},{9,17},{17,9},{25,1},{2,26},{10... | collective-permute-start | bytes 208904 | tf_op jit(solution)/shard_map/ppermute | solution.py:425

commit v9 on v8

--- a/solution.py
+++ b/solution.py
@@ -213,16 +213,25 @@
 
 
 def dft_kernel(
-    n_seg, n_pair, most, me_ref, whi_ref, wlo_ref, phase_ref, tables_ref, *refs
+    n_seg, n_pair, most, me_ref, w_ref, tables_ref, *refs
 ):
     ins, outs = refs[:n_pair], refs[n_pair : n_pair + n_seg]
-    t_ref, sem, s32, shi, slo, y, zhi, zlo, sums, parts = refs[n_pair + n_seg :]
-    copy = pltpu.make_async_copy(
-        tables_ref.at[pl.ds(0, t_ref.shape[0])], t_ref, sem.at[0]
-    )
-    copy.start()
+    t_ref, phase_ref, sem, s32, shi, slo, y, zhi, zlo, sums, parts = refs[n_pair + n_seg :]
+    copies = [
+        pltpu.make_async_copy(
+            tables_ref.at[pl.ds(t_ref.shape[0], phase_ref.shape[0])],
+            phase_ref,
+            sem.at[0],
+        ),
+        pltpu.make_async_copy(
+            tables_ref.at[pl.ds(0, t_ref.shape[0])], t_ref, sem.at[1]
+        ),
+    ]
+    for copy in copies:
+        copy.start()
     rows = (ins[0].shape[1] - 8) // most
-    half_h = whi_ref.shape[1] // 2
+    half_h = w_ref.shape[1] // 2
+    whi_ref, wlo_ref = w_ref.at[: 2 * half_h], w_ref.at[2 * half_h :]
     wide = most * TILE
     for k in range(n_pair):
         band = jnp.bitwise_xor(me_ref[1], k)
@@ -248,6 +257,7 @@
             jnp.dot(wlo_ref[...], shi[:, n], preferred_element_type=jnp.float32)
             + jnp.dot(whi_ref[...], slo[:, n], preferred_element_type=jnp.float32)
         ) + jnp.dot(whi_ref[...], shi[:, n], preferred_element_type=jnp.float32)
+    copies[0].wait()
     period = y.shape[1]
     step_rows = 64
     for b in range(period // step_rows):
@@ -263,7 +273,7 @@
                 hi = z.astype(jnp.bfloat16)
                 zhi[at, to] = hi
                 zlo[at, to] = (z - hi.astype(jnp.float32)).astype(jnp.bfloat16)
-    copy.wait()
+    copies[1].wait()
     thi = t_ref[...].astype(jnp.bfloat16)
     tlo = (t_ref[...] - thi.astype(jnp.float32)).astype(jnp.bfloat16)
     sums[...] = (
@@ -294,7 +304,7 @@
         outs[k][half // 2 :, :] = jnp.broadcast_to(top, (8, TILE)).astype(jnp.int32)
 
 
-def sums_kernel(most, turns, shift, out_ref, t_ref, sem):
+def sums_kernel(most, turns, shift, phase_ref, out_ref, t_ref, sem):
     shape = (most * TILE, turns * most * CC)
     row = lax.broadcasted_iota(jnp.int32, shape, 0)
     col = lax.broadcasted_iota(jnp.int32, shape, 1)
@@ -306,28 +316,38 @@
         size = jnp.where(e % 4 == 2, 0.0, jnp.where(e % 2 == 0, 1.0, diagonal))
         t = jnp.where(same, jnp.where((e > 2) & (e < 6), -size, size), 0.0)
         t_ref[ri * most * TILE : (ri + 1) * most * TILE, :] = t
-    copy = pltpu.make_async_copy(
-        t_ref, out_ref.at[pl.ds(0, t_ref.shape[0])], sem.at[0]
-    )
-    copy.start()
-    copy.wait()
-
-
-def make_sums(freq, most):
+    copies = [
+        pltpu.make_async_copy(
+            t_ref, out_ref.at[pl.ds(0, t_ref.shape[0])], sem.at[0]
+        ),
+        pltpu.make_async_copy(
+            phase_ref,
+            out_ref.at[pl.ds(t_ref.shape[0], phase_ref.shape[0])],
+            sem.at[1],
+        ),
+    ]
+    for copy in copies:
+        copy.start()
+    for copy in copies:
+        copy.wait()
+
+
+def make_sums(phase, freq, most):
     period = 2 * (freq // GROUPS)
     turns = LAG // period
     width = turns * most * CC
     return pl.pallas_call(
         functools.partial(sums_kernel, most, turns, LAG // 2 // period),
         out_shape=jax.ShapeDtypeStruct((48 << 10, width), jnp.float32),
+        in_specs=[pl.BlockSpec(memory_space=pltpu.VMEM)],
         out_specs=pl.BlockSpec(memory_space=pltpu.HBM),
         scratch_shapes=[
             pltpu.VMEM((2 * most * TILE, width), jnp.float32),
-            pltpu.SemaphoreType.DMA((1,)),
+            pltpu.SemaphoreType.DMA((2,)),
         ],
         name="sums",
         cost_estimate=SMALL,
-    )()
+    )(phase)
 
 
 def make_tables(freq):
@@ -342,7 +362,7 @@
     phase = ((np.arange(period)[:, None] * fb[None, :]) % (2 * freq)) * (math.pi / freq)
     scale = 1.0 / math.sqrt(freq)
     phase = (np.concatenate([np.cos(phase), np.sin(phase)], 1) * scale).astype(np.float32)
-    return [jnp.asarray(c) for c in (whi, wlo, phase)]
+    return [jnp.asarray(c) for c in (np.concatenate([whi, wlo]), phase)]
 
 
 def dft(me, tables, blocks, freq, n_seg, n_pair, most):
@@ -354,12 +374,13 @@
     return pl.pallas_call(
         functools.partial(dft_kernel, n_seg, n_pair, most),
         out_shape=[jax.ShapeDtypeStruct((half // 2 + 8, TILE), jnp.int32)] * n_seg,
-        in_specs=[smem, vmem, vmem, vmem, pl.BlockSpec(memory_space=pltpu.HBM)]
+        in_specs=[smem, vmem, pl.BlockSpec(memory_space=pltpu.HBM)]
         + [vmem] * len(blocks),
         out_specs=[vmem] * n_seg,
         scratch_shapes=[
             pltpu.VMEM((2 * wide, LAG // period * most * CC), jnp.float32),
-            pltpu.SemaphoreType.DMA((1,)),
+            pltpu.VMEM((period, 2 * TILE), jnp.float32),
+            pltpu.SemaphoreType.DMA((2,)),
             pltpu.VMEM((2, period // 2, wide), jnp.float32),
             pltpu.VMEM((period, 2 * wide), jnp.bfloat16),
             pltpu.VMEM((period, 2 * wide), jnp.bfloat16),
@@ -449,15 +470,16 @@
     me = jnp.stack([lax.axis_index("seg"), lax.axis_index("pair")]).astype(jnp.int32)
     x = spectra.reshape(2, freq, spectra.shape[3])
     lists = jnp.concatenate([pair_lists.reshape(-1), pair_counts])
-    sums = make_sums(freq, most)
-    tables = make_tables(freq) + [sums]
+    tables, phase = make_tables(freq)
+    sums = make_sums(phase, freq, most)
+    tables = [tables, sums]
     packed = [pack(x, chunk, n_seg, n_pair) for chunk in range(chunks)]
     lists, packed[-1] = lax.optimization_barrier((lists, packed[-1]))
     table = lax.all_gather(lists, "pair", axis=0)
     if chunks > 1:
         table, packed[1], _ = lax.optimization_barrier((table, packed[1], sums))
     done = []
-    blocks = lags = None
+    lags = None
     for sent in packed:
         got = lax.all_to_all(
             sent.reshape(n_seg * n_pair, tiles, 2, rows, TILE),
@@ -466,17 +488,13 @@
             concat_axis=0,
             tiled=True,
         )
-        if blocks is not None:
-            got, _ = lax.optimization_barrier((got, blocks))
+        if lags is not None:
+            got, _ = lax.optimization_barrier((got, lags))
         spec = got.reshape(n_seg, n_pair * tiles, 2, rows, TILE)
         stack = stacks(me, table, spec, n_seg, n_pair, most)
-        if blocks is not None:
-            blocks, _ = lax.optimization_barrier((blocks, stack))
-            lags = dft(me, tables, blocks, freq, n_seg, n_pair, most)
-            done += exchange(lags, "seg", n_seg)
-        blocks = exchange_plane(stack, n_pair, lags)
-    lags = dft(me, tables, blocks, freq, n_seg, n_pair, most)
-    done += exchange(lags, "seg", n_seg)
+        blocks = exchange_plane(stack, n_pair, done[1:3] or None)
+        lags = dft(me, tables, blocks, freq, n_seg, n_pair, most)
+        done += exchange(lags, "seg", n_seg)
     return unpack(me, done, n_seg, chunks, most)
 
 

time: 105 us -> 106 us (level)
  Pallas kernels: 30.3 us -> 33.2 us
  waiting for transfers between devices: 33.3 us -> 30.9 us
  starting transfers between devices: 28.5 us -> 30.1 us
    all_to_all x2, waiting for transfers between devices: 16.3 us -> 8.29 us  [body(): lax.all_to_all(sent.reshape(n_seg * n_pair, tiles, 2, rows, TILE), ('seg'...]
    ppermute x6, waiting for transfers between devices: 3.68 us -> 8.14 us  [exchange(): lax.ppermute(blocks[k], axis, [(i, i ^ k) for i in range(size)])]
    ppermute x6, starting transfers between devices: 8.83 us -> 10.5 us  [exchange(): lax.ppermute(blocks[k], axis, [(i, i ^ k) for i in range(size)])]
    ppermute x8, waiting for transfers between devices: 0.02 us -> 1.36 us  [exchange_plane(): return direct + [lax.ppermute(d, 'pair', swap) for d in direct]]
    pallas_call x2, Pallas kernels: 12.7 us -> 14 us  [dft(): pl.pallas_call(functools.partial(dft_kernel, n_seg, n_pair, most), out_sh...]
    pallas_call x1, Pallas kernels: 2.21 us -> 3.45 us  [make_sums(): pl.pallas_call(functools.partial(sums_kernel, most, turns, LAG // 2 // pe...]
  transfers between devices with their start and end apart: 22 -> 22, of which waited for: 6 -> 7; matrix products, arithmetic and copies ran while one was open for 1% -> 1% of each run, Pallas kernels for 20% -> 22%
where the time goes in v9:
time: 106 us; the launch traced here: 105 us
  Pallas kernels  33.2 us (31%)
  waiting for transfers between devices  30.9 us (29%)
  starting transfers between devices  30.1 us (28%)
  blocking collectives  8.3 us (8%)
  between operations  1.43 us (1%)
  local copies, waits for them, and re-layouts  1.15 us (1%)
    pallas_call x2, Pallas kernels, dft(): pl.pallas_call(functools.partial(dft_kernel, n_seg, n_pair, most), out_sh...  14 us
    ppermute x6, waiting for transfers between devices, exchange_plane(): lax.ppermute(blocks[k], 'pair', [(i, i ^ 2 * k) for i in range(n_pair)])  13.1 us
    all_to_all x2, starting transfers between devices, body(): lax.all_to_all(sent.reshape(n_seg * n_pair, tiles, 2, rows, TILE), ('seg'...  10.9 us
    ppermute x6, starting transfers between devices, exchange(): lax.ppermute(blocks[k], axis, [(i, i ^ k) for i in range(size)])  10.5 us
    unnamed x1, blocking collectives  8.3 us
    all_to_all x2, waiting for transfers between devices, body(): lax.all_to_all(sent.reshape(n_seg * n_pair, tiles, 2, rows, TILE), ('seg'...  8.29 us
    ppermute x6, waiting for transfers between devices, exchange(): lax.ppermute(blocks[k], axis, [(i, i ^ k) for i in range(size)])  8.14 us
    pallas_call x2, Pallas kernels, pack(): pl.pallas_call(functools.partial(pack_kernel, n_seg, chunk), out_shape=ja...  7.39 us
  transfers between devices with their start and end apart: 22, of which 7 were waited for; matrix products, arithmetic and copies ran while one was open for 1% of the time, Pallas kernels for 22%

profile of v9, /device:TPU:0, one launch (start us, length us, event | category | flops | bytes accessed | tf_op | source)
XLA Modules:
  0.0 105.3 jit_solution(5449513393458985492)
XLA Ops:
  0.0 3.7 %pack.3 = bf16[4,8,2,2,32,128]{5,4,3,2,1,0:T(8,128)(2,1)} custom-call(bf16[2,2048,256]{2,1,0:T(8,128)(2,1)} %bitcast.11), custom_call_target="tpu_custom_call" | custom-call | flops 1 | bytes 1 | tf_op jit(solution)/shard_map/pack/pallas_call | solution.py:126
  3.7 7.3 %all-to-all-start = ((bf16[32,2,2,32,128]{4,3,2,1,0:T(8,128)(2,1)}), bf16[32,2,2,32,128]{4,3,2,1,0:T(8,128)(2,1)S(1)}, u32[]{:S(2)}, u32[]{:S(2)}) async-start(bf16[32,2,2,32,128]{4,3,2,1,0:T(8,128)(2,1)} %bitcast.14), calls=%async_computation | async-start | bytes 2097152 | tf_op jit(solution)/shard_map/all_to_all | solution.py:484
  11.0 3.7 %pack.2 = bf16[4,8,2,2,32,128]{5,4,3,2,1,0:T(8,128)(2,1)} custom-call(bf16[2,2048,256]{2,1,0:T(8,128)(2,1)} %bitcast.12), custom_call_target="tpu_custom_call" | custom-call | flops 1 | bytes 1 | tf_op jit(solution)/shard_map/pack/pallas_call | solution.py:126
  14.7 3.5 %sums.1.tables_ref = f32[49152,256]{1,0:T(8,128)} custom-call(f32[512,256]{1,0:T(8,128)} %constant.13.clone.phase_ref), custom_call_target="tpu_custom_call" | custom-call | flops 1 | bytes 1 | tf_op jit(solution)/shard_map/sums/pallas_call | solution.py:339
  19.1 0.6 dynamic-slice
  20.6 8.3 %all-reduce = s32[72]{0:T(128)S(1)} all-reduce(s32[72]{0:T(128)S(1)} %dynamic-update-slice), channel_id=2, replica_groups=mesh['seg'=4,'pair'=8] {'pair'}, use_global_device_ids=true, to_apply=%add | all-reduce | flops 72 | bytes 576
  29.0 8.3 %all-to-all-done = bf16[32,2,2,32,128]{4,3,2,1,0:T(8,128)(2,1)S(1)} async-done(((bf16[32,2,2,32,128]{4,3,2,1,0:T(8,128)(2,1)}), bf16[32,2,2,32,128]{4,3,2,1,0:T(8,128)(2,1)S(1)}, u32[]{:S(2)}, u32[]{:S(2)}) %all-to-all-start) | async-done | bytes 1048608 | tf_op jit(solution)/shard_map/all_to_all | solution.py:484
  37.3 3.6 %all-to-all-start.1 = ((bf16[32,2,2,32,128]{4,3,2,1,0:T(8,128)(2,1)}), bf16[32,2,2,32,128]{4,3,2,1,0:T(8,128)(2,1)S(1)}, u32[]{:S(2)}, u32[]{:S(2)}) async-start(bf16[32,2,2,32,128]{4,3,2,1,0:T(8,128)(2,1)} %bitcast.13), calls=%async_computation.1 | async-start | bytes 2097152 | tf_op jit(solution)/shard_map/all_to_all | solution.py:484
  41.0 2.3 %stack.14 = (s32[2,136,128]{2,1,0:T(8,128)S(1)}, s32[2,136,128]{2,1,0:T(8,128)S(1)}, s32[2,136,128]{2,1,0:T(8,128)S(1)}, s32[2,136,128]{2,1,0:T(8,128)S(1)}) custom-call(s32[2]{0:T(128)S(1)} %pad_add_fusion.me_ref, s32[8,9]{1,0:T(8,128)S(1)} %reshape.28.table_ref, bf16[4,16,2,32,128]{4,3,2,1,0:T(8,128)(2,1)S(1)} %bitcast.10), custom_call_target="tpu_custom_call" | custom-call | flops 1 | bytes 1 | tf_op jit(solution)/shard_map/stack/pallas_call | solution.py:200
  43.3 1.8 %collective-permute-start = (s32[2,136,128]{2,1,0:T(8,128)S(1)}, s32[2,136,128]{2,1,0:T(8,128)S(1)}, u32[]{:S(2)}, u32[]{:S(2)}) collective-permute-start(s32[2,136,128]{2,1,0:T(8,128)S(1)} %get-tuple-element.34), channel_id=1, source_target_pairs={{0,2},{1,3},{2,0},{3,1},{4,6},{5,7},{6,4},{7,5},{8,10},{9,11},{10,... | collective-permute-start | bytes 417800 | tf_op jit(solution)/shard_map/ppermute | solution.py:453
  45.1 1.5 %collective-permute-start.1 = (s32[2,136,128]{2,1,0:T(8,128)S(1)}, s32[2,136,128]{2,1,0:T(8,128)S(1)}, u32[]{:S(2)}, u32[]{:S(2)}) collective-permute-start(s32[2,136,128]{2,1,0:T(8,128)S(1)} %get-tuple-element.35), channel_id=1, source_target_pairs={{0,4},{1,5},{2,6},{3,7},{4,0},{5,1},{6,2},{7,3},{8,12},{9,13},{10,... | collective-permute-start | bytes 417800 | tf_op jit(solution)/shard_map/ppermute | solution.py:453
  46.8 9.0 %collective-permute-done.refs_1_ = s32[2,136,128]{2,1,0:T(8,128)S(1)} collective-permute-done((s32[2,136,128]{2,1,0:T(8,128)S(1)}, s32[2,136,128]{2,1,0:T(8,128)S(1)}, u32[]{:S(2)}, u32[]{:S(2)}) %collective-permute-start) | collective-permute-done | bytes 139296 | tf_op jit(solution)/shard_map/ppermute | solution.py:453
  55.9 0.5 collective-permute-start.5
  56.4 4.1 %collective-permute-done.2.refs_3_ = s32[2,136,128]{2,1,0:T(8,128)S(1)} collective-permute-done((s32[2,136,128]{2,1,0:T(8,128)S(1)}, s32[2,136,128]{2,1,0:T(8,128)S(1)}, u32[]{:S(2)}, u32[]{:S(2)}) %collective-permute-start.2) | collective-permute-done | bytes 139296 | tf_op jit(solution)/shard_map/ppermute | solution.py:453
  60.5 1.3 %collective-permute-done.6.refs_7_ = s32[2,136,128]{2,1,0:T(8,128)S(1)} collective-permute-done((s32[2,136,128]{2,1,0:T(8,128)S(1)}, s32[2,136,128]{2,1,0:T(8,128)S(1)}, u32[]{:S(2)}, u32[]{:S(2)}) %collective-permute-start.6) | collective-permute-done | bytes 139296 | tf_op jit(solution)/shard_map/ppermute | solution.py:459
  61.9 7.0 %dft.2 = (s32[136,128]{1,0:T(8,128)S(1)}, s32[136,128]{1,0:T(8,128)S(1)}, s32[136,128]{1,0:T(8,128)S(1)}, s32[136,128]{1,0:T(8,128)S(1)}) custom-call(s32[2]{0:T(128)S(1)} %pad_add_fusion.me_ref, bf16[1024,512]{1,0:T(8,128)(2,1)S(1)} %copy-done, f32[49152,256]{1,0:T(8,128)} %sums.1.tables_ref, s32[2,136,128]{2,1,0:T(8,128)S(1)} %get-tuple-element.33.refs_0_, ...), custom_call_target="tpu_custom_call" | custom-call | flops 1 | bytes 1 | tf_op jit(solution)/shard_map/dft/pallas_call | solution.py:374
  68.9 2.5 %stack.15 = (s32[2,136,128]{2,1,0:T(8,128)S(1)}, s32[2,136,128]{2,1,0:T(8,128)S(1)}, s32[2,136,128]{2,1,0:T(8,128)S(1)}, s32[2,136,128]{2,1,0:T(8,128)S(1)}) custom-call(s32[2]{0:T(128)S(1)} %pad_add_fusion.me_ref, s32[8,9]{1,0:T(8,128)S(1)} %reshape.28.table_ref, bf16[4,16,2,32,128]{4,3,2,1,0:T(8,128)(2,1)S(1)} %bitcast.9), custom_call_target="tpu_custom_call" | custom-call | flops 1 | bytes 1 | tf_op jit(solution)/shard_map/stack/pallas_call | solution.py:200
  71.4 1.4 %collective-permute-start.10 = (s32[2,136,128]{2,1,0:T(8,128)S(1)}, s32[2,136,128]{2,1,0:T(8,128)S(1)}, u32[]{:S(2)}, u32[]{:S(2)}) collective-permute-start(s32[2,136,128]{2,1,0:T(8,128)S(1)} %get-tuple-element.44), channel_id=1, source_target_pairs={{0,2},{1,3},{2,0},{3,1},{4,6},{5,7},{6,4},{7,5},{8,10},{9,11},{10,... | collective-permute-start | bytes 417800 | tf_op jit(solution)/shard_map/ppermute | solution.py:453
  72.8 2.2 %collective-permute-start.12 = (s32[2,136,128]{2,1,0:T(8,128)S(1)}, s32[2,136,128]{2,1,0:T(8,128)S(1)}, u32[]{:S(2)}, u32[]{:S(2)}) collective-permute-start(s32[2,136,128]{2,1,0:T(8,128)S(1)} %get-tuple-element.46), channel_id=1, source_target_pairs={{0,6},{1,7},{2,4},{3,5},{4,2},{5,3},{6,0},{7,1},{8,14},{9,15},{10,... | collective-permute-start | bytes 417800 | tf_op jit(solution)/shard_map/ppermute | solution.py:453
  74.9 1.6 %collective-permute-start.7 = (s32[136,128]{1,0:T(8,128)S(1)}, s32[136,128]{1,0:T(8,128)S(1)}, u32[]{:S(2)}, u32[]{:S(2)}) collective-permute-start(s32[136,128]{1,0:T(8,128)S(1)} %get-tuple-element.38), channel_id=1, source_target_pairs={{0,8},{8,0},{16,24},{24,16},{1,9},{9,1},{17,25},{25,17},{2,10},{10... | collective-permute-start | bytes 208904 | tf_op jit(solution)/shard_map/ppermute | solution.py:446
  76.6 2.7 %collective-permute-start.8 = (s32[136,128]{1,0:T(8,128)S(1)}, s32[136,128]{1,0:T(8,128)S(1)}, u32[]{:S(2)}, u32[]{:S(2)}) collective-permute-start(s32[136,128]{1,0:T(8,128)S(1)} %get-tuple-element.39), channel_id=1, source_target_pairs={{0,16},{8,24},{16,0},{24,8},{1,17},{9,25},{17,1},{25,9},{2,18},{10... | collective-permute-start | bytes 208904 | tf_op jit(solution)/shard_map/ppermute | solution.py:446
  79.3 3.2 %collective-permute-done.8.refs_2_ = s32[136,128]{1,0:T(8,128)S(1)} collective-permute-done((s32[136,128]{1,0:T(8,128)S(1)}, s32[136,128]{1,0:T(8,128)S(1)}, u32[]{:S(2)}, u32[]{:S(2)}) %collective-permute-start.8) | collective-permute-done | bytes 69664 | tf_op jit(solution)/shard_map/ppermute | solution.py:446
  82.6 0.5 collective-permute-start.14
  83.2 0.4 collective-permute-start.16
  83.6 1.7 %collective-permute-start.9 = (s32[136,128]{1,0:T(8,128)S(1)}, s32[136,128]{1,0:T(8,128)S(1)}, u32[]{:S(2)}, u32[]{:S(2)}) collective-permute-start(s32[136,128]{1,0:T(8,128)S(1)} %get-tuple-element.40), channel_id=1, source_target_pairs={{0,24},{8,16},{16,8},{24,0},{1,25},{9,17},{17,9},{25,1},{2,26},{10... | collective-permute-start | bytes 208904 | tf_op jit(solution)/shard_map/ppermute | solution.py:446
  85.3 7.0 %dft.3 = (s32[136,128]{1,0:T(8,128)S(1)}, s32[136,128]{1,0:T(8,128)S(1)}, s32[136,128]{1,0:T(8,128)S(1)}, s32[136,128]{1,0:T(8,128)S(1)}) custom-call(s32[2]{0:T(128)S(1)} %pad_add_fusion.me_ref, bf16[1024,512]{1,0:T(8,128)(2,1)S(1)} %copy-done, f32[49152,256]{1,0:T(8,128)} %sums.1.tables_ref, s32[2,136,128]{2,1,0:T(8,128)S(1)} %get-tuple-element.47.refs_0_, ...), custom_call_target="tpu_custom_call" | custom-call | flops 1 | bytes 1 | tf_op jit(solution)/shard_map/dft/pallas_call | solution.py:374
  92.4 0.9 collective-permute-start.17
  93.3 1.8 %collective-permute-start.18 = (s32[136,128]{1,0:T(8,128)S(1)}, s32[136,128]{1,0:T(8,128)S(1)}, u32[]{:S(2)}, u32[]{:S(2)}) collective-permute-start(s32[136,128]{1,0:T(8,128)S(1)} %get-tuple-element.53), channel_id=1, source_target_pairs={{0,16},{8,24},{16,0},{24,8},{1,17},{9,25},{17,1},{25,9},{2,18},{10... | collective-permute-start | bytes 208904 | tf_op jit(solution)/shard_map/ppermute | solution.py:446
  95.1 1.7 %collective-permute-start.19 = (s32[136,128]{1,0:T(8,128)S(1)}, s32[136,128]{1,0:T(8,128)S(1)}, u32[]{:S(2)}, u32[]{:S(2)}) collective-permute-start(s32[136,128]{1,0:T(8,128)S(1)} %get-tuple-element.54), channel_id=1, source_target_pairs={{0,24},{8,16},{16,8},{24,0},{1,25},{9,17},{17,9},{25,1},{2,26},{10... | collective-permute-start | bytes 208904 | tf_op jit(solution)/shard_map/ppermute | solution.py:446
  96.8 0.7 collective-permute-done.17.refs_5_
  97.5 4.3 %collective-permute-done.18.refs_6_ = s32[136,128]{1,0:T(8,128)S(1)} collective-permute-done((s32[136,128]{1,0:T(8,128)S(1)}, s32[136,128]{1,0:T(8,128)S(1)}, u32[]{:S(2)}, u32[]{:S(2)}) %collective-permute-start.18) | collective-permute-done | bytes 69664 | tf_op jit(solution)/shard_map/ppermute | solution.py:446
  101.7 3.6 %unpack.1 = f32[2,256,4,128]{3,2,1,0:T(4,128)} custom-call(s32[2]{0:T(128)S(1)} %pad_add_fusion.me_ref, s32[136,128]{1,0:T(8,128)S(1)} %get-tuple-element.37.refs_0_, s32[136,128]{1,0:T(8,128)S(1)} %collective-permute-done.7.refs_1_, s32[136,128]{1,0:T(8,128)S(1)} %collective-permute-done.8.refs_2_, s32[136,128]{1,0:T(8,128)S(1)} %collective-permute-done.9.refs_3_, ...), custom_call_target="tpu_custom_call" | custom-call | flops 1 | bytes 1 | tf_op jit(solution)/shard_map/unpack/pallas_call | solution.py:430
  (35 shorter events, 1.1 us)
Async XLA Ops:
  0.0 19.1 %copy-start.2 = (u32[32]{0:T(128)S(1)}, u32[32]{0:T(128)}, u32[]{:S(2)}) copy-start(u32[32]{0:T(128)} %constant.19) | copy-start | bytes 388
  0.0 61.9 %copy-start = (bf16[1024,512]{1,0:T(8,128)(2,1)S(1)}, bf16[1024,512]{1,0:T(8,128)(2,1)}, u32[]{:S(2)}) copy-start(bf16[1024,512]{1,0:T(8,128)(2,1)} %constant.12.clone.w_ref) | copy-start | bytes 3145732
  0.0 18.8 %copy-start.1 = (s32[4,2]{0,1:T(2,128)S(1)}, s32[4,2]{0,1:T(2,128)}, u32[]{:S(2)}) copy-start(s32[4,2]{0,1:T(2,128)} %param.6) | copy-start | bytes 100
  3.7 33.5 %all-to-all-start = ((bf16[32,2,2,32,128]{4,3,2,1,0:T(8,128)(2,1)}), bf16[32,2,2,32,128]{4,3,2,1,0:T(8,128)(2,1)S(1)}, u32[]{:S(2)}, u32[]{:S(2)}) async-start(bf16[32,2,2,32,128]{4,3,2,1,0:T(8,128)(2,1)} %bitcast.14), calls=%async_computation | async-start | bytes 2097152 | tf_op jit(solution)/shard_map/all_to_all | solution.py:484
  37.3 31.6 %all-to-all-start.1 = ((bf16[32,2,2,32,128]{4,3,2,1,0:T(8,128)(2,1)}), bf16[32,2,2,32,128]{4,3,2,1,0:T(8,128)(2,1)S(1)}, u32[]{:S(2)}, u32[]{:S(2)}) async-start(bf16[32,2,2,32,128]{4,3,2,1,0:T(8,128)(2,1)} %bitcast.13), calls=%async_computation.1 | async-start | bytes 2097152 | tf_op jit(solution)/shard_map/all_to_all | solution.py:484
  43.3 12.6 %collective-permute-start = (s32[2,136,128]{2,1,0:T(8,128)S(1)}, s32[2,136,128]{2,1,0:T(8,128)S(1)}, u32[]{:S(2)}, u32[]{:S(2)}) collective-permute-start(s32[2,136,128]{2,1,0:T(8,128)S(1)} %get-tuple-element.34), channel_id=1, source_target_pairs={{0,2},{1,3},{2,0},{3,1},{4,6},{5,7},{6,4},{7,5},{8,10},{9,11},{10,... | collective-permute-start | bytes 417800 | tf_op jit(solution)/shard_map/ppermute | solution.py:453
  45.1 10.7 %collective-permute-start.1 = (s32[2,136,128]{2,1,0:T(8,128)S(1)}, s32[2,136,128]{2,1,0:T(8,128)S(1)}, u32[]{:S(2)}, u32[]{:S(2)}) collective-permute-start(s32[2,136,128]{2,1,0:T(8,128)S(1)} %get-tuple-element.35), channel_id=1, source_target_pairs={{0,4},{1,5},{2,6},{3,7},{4,0},{5,1},{6,2},{7,3},{8,12},{9,13},{10,... | collective-permute-start | bytes 417800 | tf_op jit(solution)/shard_map/ppermute | solution.py:453
  46.6 13.9 %collective-permute-start.2 = (s32[2,136,128]{2,1,0:T(8,128)S(1)}, s32[2,136,128]{2,1,0:T(8,128)S(1)}, u32[]{:S(2)}, u32[]{:S(2)}) collective-permute-start(s32[2,136,128]{2,1,0:T(8,128)S(1)} %get-tuple-element.36), channel_id=1, source_target_pairs={{0,6},{1,7},{2,4},{3,5},{4,2},{5,3},{6,0},{7,1},{8,14},{9,15},{10,... | collective-permute-start | bytes 417800 | tf_op jit(solution)/shard_map/ppermute | solution.py:453
  46.8 13.7 %collective-permute-start.3 = (s32[2,136,128]{2,1,0:T(8,128)S(1)}, s32[2,136,128]{2,1,0:T(8,128)S(1)}, u32[]{:S(2)}, u32[]{:S(2)}) collective-permute-start(s32[2,136,128]{2,1,0:T(8,128)S(1)} %get-tuple-element.33.refs_0_), channel_id=1, source_target_pairs={{0,1},{1,0},{2,3},{3,2},{4,5},{5,4},{6,7},{7,6},{8,9},{9,8},{10,11... | collective-permute-start | bytes 417800 | tf_op jit(solution)/shard_map/ppermute | solution.py:459
  55.9 4.6 %collective-permute-start.4 = (s32[2,136,128]{2,1,0:T(8,128)S(1)}, s32[2,136,128]{2,1,0:T(8,128)S(1)}, u32[]{:S(2)}, u32[]{:S(2)}) collective-permute-start(s32[2,136,128]{2,1,0:T(8,128)S(1)} %collective-permute-done.refs_1_), channel_id=1, source_target_pairs={{0,1},{1,0},{2,3},{3,2},{4,5},{5,4},{6,7},{7,6},{8,9},{9,8},{10,11... | collective-permute-start | bytes 417800 | tf_op jit(solution)/shard_map/ppermute | solution.py:459
  55.9 4.6 %collective-permute-start.5 = (s32[2,136,128]{2,1,0:T(8,128)S(1)}, s32[2,136,128]{2,1,0:T(8,128)S(1)}, u32[]{:S(2)}, u32[]{:S(2)}) collective-permute-start(s32[2,136,128]{2,1,0:T(8,128)S(1)} %collective-permute-done.1.refs_2_), channel_id=1, source_target_pairs={{0,1},{1,0},{2,3},{3,2},{4,5},{5,4},{6,7},{7,6},{8,9},{9,8},{10,11... | collective-permute-start | bytes 417800 | tf_op jit(solution)/shard_map/ppermute | solution.py:459
  60.5 1.4 %collective-permute-start.6 = (s32[2,136,128]{2,1,0:T(8,128)S(1)}, s32[2,136,128]{2,1,0:T(8,128)S(1)}, u32[]{:S(2)}, u32[]{:S(2)}) collective-permute-start(s32[2,136,128]{2,1,0:T(8,128)S(1)} %collective-permute-done.2.refs_3_), channel_id=1, source_target_pairs={{0,1},{1,0},{2,3},{3,2},{4,5},{5,4},{6,7},{7,6},{8,9},{9,8},{10,11... | collective-permute-start | bytes 417800 | tf_op jit(solution)/shard_map/ppermute | solution.py:459
  71.4 11.1 %collective-permute-start.10 = (s32[2,136,128]{2,1,0:T(8,128)S(1)}, s32[2,136,128]{2,1,0:T(8,128)S(1)}, u32[]{:S(2)}, u32[]{:S(2)}) collective-permute-start(s32[2,136,128]{2,1,0:T(8,128)S(1)} %get-tuple-element.44), channel_id=1, source_target_pairs={{0,2},{1,3},{2,0},{3,1},{4,6},{5,7},{6,4},{7,5},{8,10},{9,11},{10,... | collective-permute-start | bytes 417800 | tf_op jit(solution)/shard_map/ppermute | solution.py:453
  72.8 9.8 %collective-permute-start.11 = (s32[2,136,128]{2,1,0:T(8,128)S(1)}, s32[2,136,128]{2,1,0:T(8,128)S(1)}, u32[]{:S(2)}, u32[]{:S(2)}) collective-permute-start(s32[2,136,128]{2,1,0:T(8,128)S(1)} %get-tuple-element.45), channel_id=1, source_target_pairs={{0,4},{1,5},{2,6},{3,7},{4,0},{5,1},{6,2},{7,3},{8,12},{9,13},{10,... | collective-permute-start | bytes 417800 | tf_op jit(solution)/shard_map/ppermute | solution.py:453
  72.8 9.8 %collective-permute-start.12 = (s32[2,136,128]{2,1,0:T(8,128)S(1)}, s32[2,136,128]{2,1,0:T(8,128)S(1)}, u32[]{:S(2)}, u32[]{:S(2)}) collective-permute-start(s32[2,136,128]{2,1,0:T(8,128)S(1)} %get-tuple-element.46), channel_id=1, source_target_pairs={{0,6},{1,7},{2,4},{3,5},{4,2},{5,3},{6,0},{7,1},{8,14},{9,15},{10,... | collective-permute-start | bytes 417800 | tf_op jit(solution)/shard_map/ppermute | solution.py:453
  74.9 4.4 %collective-permute-start.7 = (s32[136,128]{1,0:T(8,128)S(1)}, s32[136,128]{1,0:T(8,128)S(1)}, u32[]{:S(2)}, u32[]{:S(2)}) collective-permute-start(s32[136,128]{1,0:T(8,128)S(1)} %get-tuple-element.38), channel_id=1, source_target_pairs={{0,8},{8,0},{16,24},{24,16},{1,9},{9,1},{17,25},{25,17},{2,10},{10... | collective-permute-start | bytes 208904 | tf_op jit(solution)/shard_map/ppermute | solution.py:446
  76.6 6.0 %collective-permute-start.8 = (s32[136,128]{1,0:T(8,128)S(1)}, s32[136,128]{1,0:T(8,128)S(1)}, u32[]{:S(2)}, u32[]{:S(2)}) collective-permute-start(s32[136,128]{1,0:T(8,128)S(1)} %get-tuple-element.39), channel_id=1, source_target_pairs={{0,16},{8,24},{16,0},{24,8},{1,17},{9,25},{17,1},{25,9},{2,18},{10... | collective-permute-start | bytes 208904 | tf_op jit(solution)/shard_map/ppermute | solution.py:446
  82.5 2.8 %collective-permute-start.13 = (s32[2,136,128]{2,1,0:T(8,128)S(1)}, s32[2,136,128]{2,1,0:T(8,128)S(1)}, u32[]{:S(2)}, u32[]{:S(2)}) collective-permute-start(s32[2,136,128]{2,1,0:T(8,128)S(1)} %get-tuple-element.47.refs_0_), channel_id=1, source_target_pairs={{0,1},{1,0},{2,3},{3,2},{4,5},{5,4},{6,7},{7,6},{8,9},{9,8},{10,11... | collective-permute-start | bytes 417800 | tf_op jit(solution)/shard_map/ppermute | solution.py:459
  82.6 2.7 %collective-permute-start.14 = (s32[2,136,128]{2,1,0:T(8,128)S(1)}, s32[2,136,128]{2,1,0:T(8,128)S(1)}, u32[]{:S(2)}, u32[]{:S(2)}) collective-permute-start(s32[2,136,128]{2,1,0:T(8,128)S(1)} %collective-permute-done.10.refs_1_), channel_id=1, source_target_pairs={{0,1},{1,0},{2,3},{3,2},{4,5},{5,4},{6,7},{7,6},{8,9},{9,8},{10,11... | collective-permute-start | bytes 417800 | tf_op jit(solution)/shard_map/ppermute | solution.py:459
  83.1 2.2 %collective-permute-start.15 = (s32[2,136,128]{2,1,0:T(8,128)S(1)}, s32[2,136,128]{2,1,0:T(8,128)S(1)}, u32[]{:S(2)}, u32[]{:S(2)}) collective-permute-start(s32[2,136,128]{2,1,0:T(8,128)S(1)} %collective-permute-done.11.refs_2_), channel_id=1, source_target_pairs={{0,1},{1,0},{2,3},{3,2},{4,5},{5,4},{6,7},{7,6},{8,9},{9,8},{10,11... | collective-permute-start | bytes 417800 | tf_op jit(solution)/shard_map/ppermute | solution.py:459
  83.2 2.1 %collective-permute-start.16 = (s32[2,136,128]{2,1,0:T(8,128)S(1)}, s32[2,136,128]{2,1,0:T(8,128)S(1)}, u32[]{:S(2)}, u32[]{:S(2)}) collective-permute-start(s32[2,136,128]{2,1,0:T(8,128)S(1)} %collective-permute-done.12.refs_3_), channel_id=1, source_target_pairs={{0,1},{1,0},{2,3},{3,2},{4,5},{5,4},{6,7},{7,6},{8,9},{9,8},{10,11... | collective-permute-start | bytes 417800 | tf_op jit(solution)/shard_map/ppermute | solution.py:459
  83.6 13.2 %collective-permute-start.9 = (s32[136,128]{1,0:T(8,128)S(1)}, s32[136,128]{1,0:T(8,128)S(1)}, u32[]{:S(2)}, u32[]{:S(2)}) collective-permute-start(s32[136,128]{1,0:T(8,128)S(1)} %get-tuple-element.40), channel_id=1, source_target_pairs={{0,24},{8,16},{16,8},{24,0},{1,25},{9,17},{17,9},{25,1},{2,26},{10... | collective-permute-start | bytes 208904 | tf_op jit(solution)/shard_map/ppermute | solution.py:446
  92.4 5.1 %collective-permute-start.17 = (s32[136,128]{1,0:T(8,128)S(1)}, s32[136,128]{1,0:T(8,128)S(1)}, u32[]{:S(2)}, u32[]{:S(2)}) collective-permute-start(s32[136,128]{1,0:T(8,128)S(1)} %get-tuple-element.52), channel_id=1, source_target_pairs={{0,8},{8,0},{16,24},{24,16},{1,9},{9,1},{17,25},{25,17},{2,10},{10... | collective-permute-start | bytes 208904 | tf_op jit(solution)/shard_map/ppermute | solution.py:446
  93.3 8.4 %collective-permute-start.18 = (s32[136,128]{1,0:T(8,128)S(1)}, s32[136,128]{1,0:T(8,128)S(1)}, u32[]{:S(2)}, u32[]{:S(2)}) collective-permute-start(s32[136,128]{1,0:T(8,128)S(1)} %get-tuple-element.53), channel_id=1, source_target_pairs={{0,16},{8,24},{16,0},{24,8},{1,17},{9,25},{17,1},{25,9},{2,18},{10... | collective-permute-start | bytes 208904 | tf_op jit(solution)/shard_map/ppermute | solution.py:446
  95.1 6.6 %collective-permute-start.19 = (s32[136,128]{1,0:T(8,128)S(1)}, s32[136,128]{1,0:T(8,128)S(1)}, u32[]{:S(2)}, u32[]{:S(2)}) collective-permute-start(s32[136,128]{1,0:T(8,128)S(1)} %get-tuple-element.54), channel_id=1, source_target_pairs={{0,24},{8,16},{16,8},{24,0},{1,25},{9,17},{17,9},{25,1},{2,26},{10... | collective-permute-start | bytes 208904 | tf_op jit(solution)/shard_map/ppermute | solution.py:446

commit v10 on v8

--- a/solution.py
+++ b/solution.py
@@ -48,6 +48,10 @@
         ((q & 16383) - 8192).astype(jnp.float32) * s for q in (code >> 14, code)
     )
     return a, b
+
+
+ODD = 239.0 / 256.0
+ODD_DIAGONAL = 169.0 / 256.0
 
 
 def transpose_groups(vectors):
@@ -264,12 +268,10 @@
                 zhi[at, to] = hi
                 zlo[at, to] = (z - hi.astype(jnp.float32)).astype(jnp.bfloat16)
     copy.wait()
-    thi = t_ref[...].astype(jnp.bfloat16)
-    tlo = (t_ref[...] - thi.astype(jnp.float32)).astype(jnp.bfloat16)
-    sums[...] = (
-        jnp.dot(zhi[...], tlo, preferred_element_type=jnp.float32)
-        + jnp.dot(zlo[...], thi, preferred_element_type=jnp.float32)
-    ) + jnp.dot(zhi[...], thi, preferred_element_type=jnp.float32)
+    t = t_ref[...]
+    sums[...] = jnp.dot(zlo[...], t, preferred_element_type=jnp.float32) + jnp.dot(
+        zhi[...], t, preferred_element_type=jnp.float32
+    )
     half = parts.shape[1]
     big = None
     first = lax.broadcasted_iota(jnp.int32, (half, TILE), 1) < TILE // 2
@@ -299,13 +301,14 @@
     row = lax.broadcasted_iota(jnp.int32, shape, 0)
     col = lax.broadcasted_iota(jnp.int32, shape, 1)
     same = (row // TILE == col // CC % most) & (row % CC == col % CC)
-    eighths = (col // (most * CC) - shift) * (row // CC % GROUPS)
-    diagonal = jnp.float32(math.sqrt(0.5))
+    fb = row // CC % GROUPS
+    eighths = (col // (most * CC) - shift) * fb
+    one = jnp.where(fb % 2 == 0, 1.0, ODD)
     for ri in range(2):
         e = jnp.bitwise_and(eighths + 2 * ri, 7)
-        size = jnp.where(e % 4 == 2, 0.0, jnp.where(e % 2 == 0, 1.0, diagonal))
+        size = jnp.where(e % 4 == 2, 0.0, jnp.where(e % 2 == 0, one, ODD_DIAGONAL))
         t = jnp.where(same, jnp.where((e > 2) & (e < 6), -size, size), 0.0)
-        t_ref[ri * most * TILE : (ri + 1) * most * TILE, :] = t
+        t_ref[ri * most * TILE : (ri + 1) * most * TILE, :] = t.astype(jnp.bfloat16)
     copy = pltpu.make_async_copy(
         t_ref, out_ref.at[pl.ds(0, t_ref.shape[0])], sem.at[0]
     )
@@ -319,10 +322,10 @@
     width = turns * most * CC
     return pl.pallas_call(
         functools.partial(sums_kernel, most, turns, LAG // 2 // period),
-        out_shape=jax.ShapeDtypeStruct((48 << 10, width), jnp.float32),
+        out_shape=jax.ShapeDtypeStruct((96 << 10, width), jnp.bfloat16),
         out_specs=pl.BlockSpec(memory_space=pltpu.HBM),
         scratch_shapes=[
-            pltpu.VMEM((2 * most * TILE, width), jnp.float32),
+            pltpu.VMEM((2 * most * TILE, width), jnp.bfloat16),
             pltpu.SemaphoreType.DMA((1,)),
         ],
         name="sums",
@@ -340,7 +343,8 @@
     wlo = (w - whi.astype(np.float32)).astype(jnp.bfloat16)
     fb = np.arange(TILE) // CC
     phase = ((np.arange(period)[:, None] * fb[None, :]) % (2 * freq)) * (math.pi / freq)
-    scale = 1.0 / math.sqrt(freq)
+    scale = np.where(fb % 2 == 0, 1.0, 1.0 / ODD) / math.sqrt(freq)
+    scale = np.concatenate([scale, scale])[None, :]
     phase = (np.concatenate([np.cos(phase), np.sin(phase)], 1) * scale).astype(np.float32)
     return [jnp.asarray(c) for c in (whi, wlo, phase)]
 
@@ -358,7 +362,7 @@
         + [vmem] * len(blocks),
         out_specs=[vmem] * n_seg,
         scratch_shapes=[
-            pltpu.VMEM((2 * wide, LAG // period * most * CC), jnp.float32),
+            pltpu.VMEM((2 * wide, LAG // period * most * CC), jnp.bfloat16),
             pltpu.SemaphoreType.DMA((1,)),
             pltpu.VMEM((2, period // 2, wide), jnp.float32),
             pltpu.VMEM((period, 2 * wide), jnp.bfloat16),
@@ -457,7 +461,7 @@
     if chunks > 1:
         table, packed[1], _ = lax.optimization_barrier((table, packed[1], sums))
     done = []
-    blocks = lags = None
+    lags = None
     for sent in packed:
         got = lax.all_to_all(
             sent.reshape(n_seg * n_pair, tiles, 2, rows, TILE),
@@ -466,17 +470,13 @@
             concat_axis=0,
             tiled=True,
         )
-        if blocks is not None:
-            got, _ = lax.optimization_barrier((got, blocks))
+        if lags is not None:
+            got, _ = lax.optimization_barrier((got, lags))
         spec = got.reshape(n_seg, n_pair * tiles, 2, rows, TILE)
         stack = stacks(me, table, spec, n_seg, n_pair, most)
-        if blocks is not None:
-            blocks, _ = lax.optimization_barrier((blocks, stack))
-            lags = dft(me, tables, blocks, freq, n_seg, n_pair, most)
-            done += exchange(lags, "seg", n_seg)
-        blocks = exchange_plane(stack, n_pair, lags)
-    lags = dft(me, tables, blocks, freq, n_seg, n_pair, most)
-    done += exchange(lags, "seg", n_seg)
+        blocks = exchange_plane(stack, n_pair, done[1:3] or None)
+        lags = dft(me, tables, blocks, freq, n_seg, n_pair, most)
+        done += exchange(lags, "seg", n_seg)
     return unpack(me, done, n_seg, chunks, most)
 
 

time: 105 us -> 104 us (level)
  Pallas kernels: 30.3 us -> 28.5 us
  starting transfers between devices: 28.5 us -> 30.1 us
    all_to_all x2, waiting for transfers between devices: 16.3 us -> 9.73 us  [body(): lax.all_to_all(sent.reshape(n_seg * n_pair, tiles, 2, rows, TILE), ('seg'...]
    ppermute x6, waiting for transfers between devices: 3.68 us -> 8.14 us  [exchange(): lax.ppermute(blocks[k], axis, [(i, i ^ k) for i in range(size)])]
    pallas_call x2, Pallas kernels: 12.7 us -> 10.9 us  [dft(): pl.pallas_call(functools.partial(dft_kernel, n_seg, n_pair, most), out_sh...]
    ppermute x6, starting transfers between devices: 8.83 us -> 10.5 us  [exchange(): lax.ppermute(blocks[k], axis, [(i, i ^ k) for i in range(size)])]
    ppermute x8, waiting for transfers between devices: 0.02 us -> 1.36 us  [exchange_plane(): return direct + [lax.ppermute(d, 'pair', swap) for d in direct]]
  transfers between devices with their start and end apart: 22 -> 22, of which waited for: 6 -> 7; matrix products, arithmetic and copies ran while one was open for 1% -> 1% of each run, Pallas kernels for 20% -> 18%
where the time goes in v10:
time: 104 us; the launch traced here: 103 us
  waiting for transfers between devices  32.4 us (31%)
  starting transfers between devices  30.1 us (29%)
  Pallas kernels  28.5 us (27%)
  blocking collectives  8.26 us (8%)
  local copies, waits for them, and re-layouts  2.15 us (2%)
  between operations  1.43 us (1%)
    ppermute x6, waiting for transfers between devices, exchange_plane(): lax.ppermute(blocks[k], 'pair', [(i, i ^ 2 * k) for i in range(n_pair)])  13.2 us
    all_to_all x2, starting transfers between devices, body(): lax.all_to_all(sent.reshape(n_seg * n_pair, tiles, 2, rows, TILE), ('seg'...  10.9 us
    pallas_call x2, Pallas kernels, dft(): pl.pallas_call(functools.partial(dft_kernel, n_seg, n_pair, most), out_sh...  10.9 us
    ppermute x6, starting transfers between devices, exchange(): lax.ppermute(blocks[k], axis, [(i, i ^ k) for i in range(size)])  10.5 us
    all_to_all x2, waiting for transfers between devices, body(): lax.all_to_all(sent.reshape(n_seg * n_pair, tiles, 2, rows, TILE), ('seg'...  9.73 us
    unnamed x1, blocking collectives  8.26 us
    ppermute x6, waiting for transfers between devices, exchange(): lax.ppermute(blocks[k], axis, [(i, i ^ k) for i in range(size)])  8.14 us
    pallas_call x2, Pallas kernels, pack(): pl.pallas_call(functools.partial(pack_kernel, n_seg, chunk), out_shape=ja...  7.35 us
  transfers between devices with their start and end apart: 22, of which 7 were waited for; matrix products, arithmetic and copies ran while one was open for 1% of the time, Pallas kernels for 18%

profile of v10, /device:TPU:0, one launch (start us, length us, event | category | flops | bytes accessed | tf_op | source)
XLA Modules:
  0.0 103.1 jit_solution(14028094777118487695)
XLA Ops:
  0.0 3.7 %pack.3 = bf16[4,8,2,2,32,128]{5,4,3,2,1,0:T(8,128)(2,1)} custom-call(bf16[2,2048,256]{2,1,0:T(8,128)(2,1)} %bitcast.11), custom_call_target="tpu_custom_call" | custom-call | flops 1 | bytes 1 | tf_op jit(solution)/shard_map/pack/pallas_call | solution.py:130
  3.7 7.3 %all-to-all-start = ((bf16[32,2,2,32,128]{4,3,2,1,0:T(8,128)(2,1)}), bf16[32,2,2,32,128]{4,3,2,1,0:T(8,128)(2,1)S(1)}, u32[]{:S(2)}, u32[]{:S(2)}) async-start(bf16[32,2,2,32,128]{4,3,2,1,0:T(8,128)(2,1)} %bitcast.14), calls=%async_computation | async-start | bytes 2097152 | tf_op jit(solution)/shard_map/all_to_all | solution.py:466
  11.0 3.6 %pack.2 = bf16[4,8,2,2,32,128]{5,4,3,2,1,0:T(8,128)(2,1)} custom-call(bf16[2,2048,256]{2,1,0:T(8,128)(2,1)} %bitcast.12), custom_call_target="tpu_custom_call" | custom-call | flops 1 | bytes 1 | tf_op jit(solution)/shard_map/pack/pallas_call | solution.py:130
  14.7 2.1 %sums.1.tables_ref = bf16[98304,256]{1,0:T(8,128)(2,1)} custom-call(), custom_call_target="tpu_custom_call" | custom-call | flops 1 | bytes 1 | tf_op jit(solution)/shard_map/sums/pallas_call | solution.py:323
  17.7 0.6 dynamic-slice
  19.2 8.3 %all-reduce = s32[72]{0:T(128)S(1)} all-reduce(s32[72]{0:T(128)S(1)} %dynamic-update-slice), channel_id=2, replica_groups=mesh['seg'=4,'pair'=8] {'pair'}, use_global_device_ids=true, to_apply=%add | all-reduce | flops 72 | bytes 576
  27.5 9.7 %all-to-all-done = bf16[32,2,2,32,128]{4,3,2,1,0:T(8,128)(2,1)S(1)} async-done(((bf16[32,2,2,32,128]{4,3,2,1,0:T(8,128)(2,1)}), bf16[32,2,2,32,128]{4,3,2,1,0:T(8,128)(2,1)S(1)}, u32[]{:S(2)}, u32[]{:S(2)}) %all-to-all-start) | async-done | bytes 1048608 | tf_op jit(solution)/shard_map/all_to_all | solution.py:466
  37.3 3.6 %all-to-all-start.1 = ((bf16[32,2,2,32,128]{4,3,2,1,0:T(8,128)(2,1)}), bf16[32,2,2,32,128]{4,3,2,1,0:T(8,128)(2,1)S(1)}, u32[]{:S(2)}, u32[]{:S(2)}) async-start(bf16[32,2,2,32,128]{4,3,2,1,0:T(8,128)(2,1)} %bitcast.13), calls=%async_computation.1 | async-start | bytes 2097152 | tf_op jit(solution)/shard_map/all_to_all | solution.py:466
  41.0 2.2 %stack.14 = (s32[2,136,128]{2,1,0:T(8,128)S(1)}, s32[2,136,128]{2,1,0:T(8,128)S(1)}, s32[2,136,128]{2,1,0:T(8,128)S(1)}, s32[2,136,128]{2,1,0:T(8,128)S(1)}) custom-call(s32[2]{0:T(128)S(1)} %pad_add_fusion.me_ref, s32[8,9]{1,0:T(8,128)S(1)} %reshape.28.table_ref, bf16[4,16,2,32,128]{4,3,2,1,0:T(8,128)(2,1)S(1)} %bitcast.10), custom_call_target="tpu_custom_call" | custom-call | flops 1 | bytes 1 | tf_op jit(solution)/shard_map/stack/pallas_call | solution.py:204
  43.2 1.8 %collective-permute-start = (s32[2,136,128]{2,1,0:T(8,128)S(1)}, s32[2,136,128]{2,1,0:T(8,128)S(1)}, u32[]{:S(2)}, u32[]{:S(2)}) collective-permute-start(s32[2,136,128]{2,1,0:T(8,128)S(1)} %get-tuple-element.34), channel_id=1, source_target_pairs={{0,2},{1,3},{2,0},{3,1},{4,6},{5,7},{6,4},{7,5},{8,10},{9,11},{10,... | collective-permute-start | bytes 417800 | tf_op jit(solution)/shard_map/ppermute | solution.py:436
  45.0 1.5 %collective-permute-start.1 = (s32[2,136,128]{2,1,0:T(8,128)S(1)}, s32[2,136,128]{2,1,0:T(8,128)S(1)}, u32[]{:S(2)}, u32[]{:S(2)}) collective-permute-start(s32[2,136,128]{2,1,0:T(8,128)S(1)} %get-tuple-element.35), channel_id=1, source_target_pairs={{0,4},{1,5},{2,6},{3,7},{4,0},{5,1},{6,2},{7,3},{8,12},{9,13},{10,... | collective-permute-start | bytes 417800 | tf_op jit(solution)/shard_map/ppermute | solution.py:436
  46.8 9.1 %collective-permute-done.refs_1_ = s32[2,136,128]{2,1,0:T(8,128)S(1)} collective-permute-done((s32[2,136,128]{2,1,0:T(8,128)S(1)}, s32[2,136,128]{2,1,0:T(8,128)S(1)}, u32[]{:S(2)}, u32[]{:S(2)}) %collective-permute-start) | collective-permute-done | bytes 139296 | tf_op jit(solution)/shard_map/ppermute | solution.py:436
  55.9 0.5 collective-permute-start.5
  56.4 4.1 %collective-permute-done.2.refs_3_ = s32[2,136,128]{2,1,0:T(8,128)S(1)} collective-permute-done((s32[2,136,128]{2,1,0:T(8,128)S(1)}, s32[2,136,128]{2,1,0:T(8,128)S(1)}, u32[]{:S(2)}, u32[]{:S(2)}) %collective-permute-start.2) | collective-permute-done | bytes 139296 | tf_op jit(solution)/shard_map/ppermute | solution.py:436
  60.5 1.3 %collective-permute-done.6.refs_7_ = s32[2,136,128]{2,1,0:T(8,128)S(1)} collective-permute-done((s32[2,136,128]{2,1,0:T(8,128)S(1)}, s32[2,136,128]{2,1,0:T(8,128)S(1)}, u32[]{:S(2)}, u32[]{:S(2)}) %collective-permute-start.6) | collective-permute-done | bytes 139296 | tf_op jit(solution)/shard_map/ppermute | solution.py:442
  61.9 1.0 %copy-done.2 = bf16[512,512]{1,0:T(8,128)(2,1)S(1)} copy-done((bf16[512,512]{1,0:T(8,128)(2,1)S(1)}, bf16[512,512]{1,0:T(8,128)(2,1)}, u32[]{:S(2)}) %copy-start.2) | copy-done | bytes 524312
  62.9 5.4 %dft.2 = (s32[136,128]{1,0:T(8,128)S(1)}, s32[136,128]{1,0:T(8,128)S(1)}, s32[136,128]{1,0:T(8,128)S(1)}, s32[136,128]{1,0:T(8,128)S(1)}) custom-call(s32[2]{0:T(128)S(1)} %pad_add_fusion.me_ref, bf16[512,512]{1,0:T(8,128)(2,1)S(1)} %copy-done.2, bf16[512,512]{1,0:T(8,128)(2,1)S(1)} %copy-done.1, f32[512,256]{1,0:T(8,128)S(1)} %copy-done, ...), custom_call_target="tpu_custom_call" | custom-call | flops 1 | bytes 1 | tf_op jit(solution)/shard_map/dft/pallas_call | solution.py:358
  68.4 2.4 %stack.15 = (s32[2,136,128]{2,1,0:T(8,128)S(1)}, s32[2,136,128]{2,1,0:T(8,128)S(1)}, s32[2,136,128]{2,1,0:T(8,128)S(1)}, s32[2,136,128]{2,1,0:T(8,128)S(1)}) custom-call(s32[2]{0:T(128)S(1)} %pad_add_fusion.me_ref, s32[8,9]{1,0:T(8,128)S(1)} %reshape.28.table_ref, bf16[4,16,2,32,128]{4,3,2,1,0:T(8,128)(2,1)S(1)} %bitcast.9), custom_call_target="tpu_custom_call" | custom-call | flops 1 | bytes 1 | tf_op jit(solution)/shard_map/stack/pallas_call | solution.py:204
  70.8 1.4 %collective-permute-start.10 = (s32[2,136,128]{2,1,0:T(8,128)S(1)}, s32[2,136,128]{2,1,0:T(8,128)S(1)}, u32[]{:S(2)}, u32[]{:S(2)}) collective-permute-start(s32[2,136,128]{2,1,0:T(8,128)S(1)} %get-tuple-element.44), channel_id=1, source_target_pairs={{0,2},{1,3},{2,0},{3,1},{4,6},{5,7},{6,4},{7,5},{8,10},{9,11},{10,... | collective-permute-start | bytes 417800 | tf_op jit(solution)/shard_map/ppermute | solution.py:436
  72.6 1.7 %collective-permute-start.12 = (s32[2,136,128]{2,1,0:T(8,128)S(1)}, s32[2,136,128]{2,1,0:T(8,128)S(1)}, u32[]{:S(2)}, u32[]{:S(2)}) collective-permute-start(s32[2,136,128]{2,1,0:T(8,128)S(1)} %get-tuple-element.46), channel_id=1, source_target_pairs={{0,6},{1,7},{2,4},{3,5},{4,2},{5,3},{6,0},{7,1},{8,14},{9,15},{10,... | collective-permute-start | bytes 417800 | tf_op jit(solution)/shard_map/ppermute | solution.py:436
  74.3 1.6 %collective-permute-start.7 = (s32[136,128]{1,0:T(8,128)S(1)}, s32[136,128]{1,0:T(8,128)S(1)}, u32[]{:S(2)}, u32[]{:S(2)}) collective-permute-start(s32[136,128]{1,0:T(8,128)S(1)} %get-tuple-element.38), channel_id=1, source_target_pairs={{0,8},{8,0},{16,24},{24,16},{1,9},{9,1},{17,25},{25,17},{2,10},{10... | collective-permute-start | bytes 208904 | tf_op jit(solution)/shard_map/ppermute | solution.py:429
  75.9 2.7 %collective-permute-start.8 = (s32[136,128]{1,0:T(8,128)S(1)}, s32[136,128]{1,0:T(8,128)S(1)}, u32[]{:S(2)}, u32[]{:S(2)}) collective-permute-start(s32[136,128]{1,0:T(8,128)S(1)} %get-tuple-element.39), channel_id=1, source_target_pairs={{0,16},{8,24},{16,0},{24,8},{1,17},{9,25},{17,1},{25,9},{2,18},{10... | collective-permute-start | bytes 208904 | tf_op jit(solution)/shard_map/ppermute | solution.py:429
  78.7 3.2 %collective-permute-done.8.refs_2_ = s32[136,128]{1,0:T(8,128)S(1)} collective-permute-done((s32[136,128]{1,0:T(8,128)S(1)}, s32[136,128]{1,0:T(8,128)S(1)}, u32[]{:S(2)}, u32[]{:S(2)}) %collective-permute-start.8) | collective-permute-done | bytes 69664 | tf_op jit(solution)/shard_map/ppermute | solution.py:429
  82.0 0.5 collective-permute-start.14
  83.0 1.7 %collective-permute-start.9 = (s32[136,128]{1,0:T(8,128)S(1)}, s32[136,128]{1,0:T(8,128)S(1)}, u32[]{:S(2)}, u32[]{:S(2)}) collective-permute-start(s32[136,128]{1,0:T(8,128)S(1)} %get-tuple-element.40), channel_id=1, source_target_pairs={{0,24},{8,16},{16,8},{24,0},{1,25},{9,17},{17,9},{25,1},{2,26},{10... | collective-permute-start | bytes 208904 | tf_op jit(solution)/shard_map/ppermute | solution.py:429
  84.7 5.4 %dft.3 = (s32[136,128]{1,0:T(8,128)S(1)}, s32[136,128]{1,0:T(8,128)S(1)}, s32[136,128]{1,0:T(8,128)S(1)}, s32[136,128]{1,0:T(8,128)S(1)}) custom-call(s32[2]{0:T(128)S(1)} %pad_add_fusion.me_ref, bf16[512,512]{1,0:T(8,128)(2,1)S(1)} %copy-done.2, bf16[512,512]{1,0:T(8,128)(2,1)S(1)} %copy-done.1, f32[512,256]{1,0:T(8,128)S(1)} %copy-done, ...), custom_call_target="tpu_custom_call" | custom-call | flops 1 | bytes 1 | tf_op jit(solution)/shard_map/dft/pallas_call | solution.py:358
  90.2 0.9 collective-permute-start.17
  91.1 1.8 %collective-permute-start.18 = (s32[136,128]{1,0:T(8,128)S(1)}, s32[136,128]{1,0:T(8,128)S(1)}, u32[]{:S(2)}, u32[]{:S(2)}) collective-permute-start(s32[136,128]{1,0:T(8,128)S(1)} %get-tuple-element.53), channel_id=1, source_target_pairs={{0,16},{8,24},{16,0},{24,8},{1,17},{9,25},{17,1},{25,9},{2,18},{10... | collective-permute-start | bytes 208904 | tf_op jit(solution)/shard_map/ppermute | solution.py:429
  92.9 1.7 %collective-permute-start.19 = (s32[136,128]{1,0:T(8,128)S(1)}, s32[136,128]{1,0:T(8,128)S(1)}, u32[]{:S(2)}, u32[]{:S(2)}) collective-permute-start(s32[136,128]{1,0:T(8,128)S(1)} %get-tuple-element.54), channel_id=1, source_target_pairs={{0,24},{8,16},{16,8},{24,0},{1,25},{9,17},{17,9},{25,1},{2,26},{10... | collective-permute-start | bytes 208904 | tf_op jit(solution)/shard_map/ppermute | solution.py:429
  94.6 0.7 collective-permute-done.17.refs_5_
  95.3 4.3 %collective-permute-done.18.refs_6_ = s32[136,128]{1,0:T(8,128)S(1)} collective-permute-done((s32[136,128]{1,0:T(8,128)S(1)}, s32[136,128]{1,0:T(8,128)S(1)}, u32[]{:S(2)}, u32[]{:S(2)}) %collective-permute-start.18) | collective-permute-done | bytes 69664 | tf_op jit(solution)/shard_map/ppermute | solution.py:429
  99.5 3.6 %unpack.1 = f32[2,256,4,128]{3,2,1,0:T(4,128)} custom-call(s32[2]{0:T(128)S(1)} %pad_add_fusion.me_ref, s32[136,128]{1,0:T(8,128)S(1)} %get-tuple-element.37.refs_0_, s32[136,128]{1,0:T(8,128)S(1)} %collective-permute-done.7.refs_1_, s32[136,128]{1,0:T(8,128)S(1)} %collective-permute-done.8.refs_2_, s32[136,128]{1,0:T(8,128)S(1)} %collective-permute-done.9.refs_3_, ...), custom_call_target="tpu_custom_call" | custom-call | flops 1 | bytes 1 | tf_op jit(solution)/shard_map/unpack/pallas_call | solution.py:413
  (39 shorter events, 2.0 us)
Async XLA Ops:
  0.0 17.7 %copy-start.4 = (u32[32]{0:T(128)S(1)}, u32[32]{0:T(128)}, u32[]{:S(2)}) copy-start(u32[32]{0:T(128)} %constant.22) | copy-start | bytes 388
  0.0 61.9 %copy-start = (f32[512,256]{1,0:T(8,128)S(1)}, f32[512,256]{1,0:T(8,128)}, u32[]{:S(2)}) copy-start(f32[512,256]{1,0:T(8,128)} %constant.16.clone.phase_ref) | copy-start | bytes 1572868
  0.0 61.9 %copy-start.1 = (bf16[512,512]{1,0:T(8,128)(2,1)S(1)}, bf16[512,512]{1,0:T(8,128)(2,1)}, u32[]{:S(2)}) copy-start(bf16[512,512]{1,0:T(8,128)(2,1)} %constant.15.clone.wlo_ref) | copy-start | bytes 1572868
  0.0 17.5 %copy-start.3 = (s32[4,2]{0,1:T(2,128)S(1)}, s32[4,2]{0,1:T(2,128)}, u32[]{:S(2)}) copy-start(s32[4,2]{0,1:T(2,128)} %param.7) | copy-start | bytes 100
  3.7 33.6 %all-to-all-start = ((bf16[32,2,2,32,128]{4,3,2,1,0:T(8,128)(2,1)}), bf16[32,2,2,32,128]{4,3,2,1,0:T(8,128)(2,1)S(1)}, u32[]{:S(2)}, u32[]{:S(2)}) async-start(bf16[32,2,2,32,128]{4,3,2,1,0:T(8,128)(2,1)} %bitcast.14), calls=%async_computation | async-start | bytes 2097152 | tf_op jit(solution)/shard_map/all_to_all | solution.py:466
  37.3 31.1 %all-to-all-start.1 = ((bf16[32,2,2,32,128]{4,3,2,1,0:T(8,128)(2,1)}), bf16[32,2,2,32,128]{4,3,2,1,0:T(8,128)(2,1)S(1)}, u32[]{:S(2)}, u32[]{:S(2)}) async-start(bf16[32,2,2,32,128]{4,3,2,1,0:T(8,128)(2,1)} %bitcast.13), calls=%async_computation.1 | async-start | bytes 2097152 | tf_op jit(solution)/shard_map/all_to_all | solution.py:466
  43.2 12.6 %collective-permute-start = (s32[2,136,128]{2,1,0:T(8,128)S(1)}, s32[2,136,128]{2,1,0:T(8,128)S(1)}, u32[]{:S(2)}, u32[]{:S(2)}) collective-permute-start(s32[2,136,128]{2,1,0:T(8,128)S(1)} %get-tuple-element.34), channel_id=1, source_target_pairs={{0,2},{1,3},{2,0},{3,1},{4,6},{5,7},{6,4},{7,5},{8,10},{9,11},{10,... | collective-permute-start | bytes 417800 | tf_op jit(solution)/shard_map/ppermute | solution.py:436
  45.0 10.8 %collective-permute-start.1 = (s32[2,136,128]{2,1,0:T(8,128)S(1)}, s32[2,136,128]{2,1,0:T(8,128)S(1)}, u32[]{:S(2)}, u32[]{:S(2)}) collective-permute-start(s32[2,136,128]{2,1,0:T(8,128)S(1)} %get-tuple-element.35), channel_id=1, source_target_pairs={{0,4},{1,5},{2,6},{3,7},{4,0},{5,1},{6,2},{7,3},{8,12},{9,13},{10,... | collective-permute-start | bytes 417800 | tf_op jit(solution)/shard_map/ppermute | solution.py:436
  46.5 14.0 %collective-permute-start.2 = (s32[2,136,128]{2,1,0:T(8,128)S(1)}, s32[2,136,128]{2,1,0:T(8,128)S(1)}, u32[]{:S(2)}, u32[]{:S(2)}) collective-permute-start(s32[2,136,128]{2,1,0:T(8,128)S(1)} %get-tuple-element.36), channel_id=1, source_target_pairs={{0,6},{1,7},{2,4},{3,5},{4,2},{5,3},{6,0},{7,1},{8,14},{9,15},{10,... | collective-permute-start | bytes 417800 | tf_op jit(solution)/shard_map/ppermute | solution.py:436
  46.8 13.7 %collective-permute-start.3 = (s32[2,136,128]{2,1,0:T(8,128)S(1)}, s32[2,136,128]{2,1,0:T(8,128)S(1)}, u32[]{:S(2)}, u32[]{:S(2)}) collective-permute-start(s32[2,136,128]{2,1,0:T(8,128)S(1)} %get-tuple-element.33.refs_0_), channel_id=1, source_target_pairs={{0,1},{1,0},{2,3},{3,2},{4,5},{5,4},{6,7},{7,6},{8,9},{9,8},{10,11... | collective-permute-start | bytes 417800 | tf_op jit(solution)/shard_map/ppermute | solution.py:442
  55.9 4.6 %collective-permute-start.4 = (s32[2,136,128]{2,1,0:T(8,128)S(1)}, s32[2,136,128]{2,1,0:T(8,128)S(1)}, u32[]{:S(2)}, u32[]{:S(2)}) collective-permute-start(s32[2,136,128]{2,1,0:T(8,128)S(1)} %collective-permute-done.refs_1_), channel_id=1, source_target_pairs={{0,1},{1,0},{2,3},{3,2},{4,5},{5,4},{6,7},{7,6},{8,9},{9,8},{10,11... | collective-permute-start | bytes 417800 | tf_op jit(solution)/shard_map/ppermute | solution.py:442
  55.9 4.6 %collective-permute-start.5 = (s32[2,136,128]{2,1,0:T(8,128)S(1)}, s32[2,136,128]{2,1,0:T(8,128)S(1)}, u32[]{:S(2)}, u32[]{:S(2)}) collective-permute-start(s32[2,136,128]{2,1,0:T(8,128)S(1)} %collective-permute-done.1.refs_2_), channel_id=1, source_target_pairs={{0,1},{1,0},{2,3},{3,2},{4,5},{5,4},{6,7},{7,6},{8,9},{9,8},{10,11... | collective-permute-start | bytes 417800 | tf_op jit(solution)/shard_map/ppermute | solution.py:442
  60.5 1.4 %collective-permute-start.6 = (s32[2,136,128]{2,1,0:T(8,128)S(1)}, s32[2,136,128]{2,1,0:T(8,128)S(1)}, u32[]{:S(2)}, u32[]{:S(2)}) collective-permute-start(s32[2,136,128]{2,1,0:T(8,128)S(1)} %collective-permute-done.2.refs_3_), channel_id=1, source_target_pairs={{0,1},{1,0},{2,3},{3,2},{4,5},{5,4},{6,7},{7,6},{8,9},{9,8},{10,11... | collective-permute-start | bytes 417800 | tf_op jit(solution)/shard_map/ppermute | solution.py:442
  61.9 1.0 %copy-start.2 = (bf16[512,512]{1,0:T(8,128)(2,1)S(1)}, bf16[512,512]{1,0:T(8,128)(2,1)}, u32[]{:S(2)}) copy-start(bf16[512,512]{1,0:T(8,128)(2,1)} %constant.14.clone.whi_ref) | copy-start | bytes 1572868
  70.8 11.1 %collective-permute-start.10 = (s32[2,136,128]{2,1,0:T(8,128)S(1)}, s32[2,136,128]{2,1,0:T(8,128)S(1)}, u32[]{:S(2)}, u32[]{:S(2)}) collective-permute-start(s32[2,136,128]{2,1,0:T(8,128)S(1)} %get-tuple-element.44), channel_id=1, source_target_pairs={{0,2},{1,3},{2,0},{3,1},{4,6},{5,7},{6,4},{7,5},{8,10},{9,11},{10,... | collective-permute-start | bytes 417800 | tf_op jit(solution)/shard_map/ppermute | solution.py:436
  72.1 9.8 %collective-permute-start.11 = (s32[2,136,128]{2,1,0:T(8,128)S(1)}, s32[2,136,128]{2,1,0:T(8,128)S(1)}, u32[]{:S(2)}, u32[]{:S(2)}) collective-permute-start(s32[2,136,128]{2,1,0:T(8,128)S(1)} %get-tuple-element.45), channel_id=1, source_target_pairs={{0,4},{1,5},{2,6},{3,7},{4,0},{5,1},{6,2},{7,3},{8,12},{9,13},{10,... | collective-permute-start | bytes 417800 | tf_op jit(solution)/shard_map/ppermute | solution.py:436
  72.6 9.3 %collective-permute-start.12 = (s32[2,136,128]{2,1,0:T(8,128)S(1)}, s32[2,136,128]{2,1,0:T(8,128)S(1)}, u32[]{:S(2)}, u32[]{:S(2)}) collective-permute-start(s32[2,136,128]{2,1,0:T(8,128)S(1)} %get-tuple-element.46), channel_id=1, source_target_pairs={{0,6},{1,7},{2,4},{3,5},{4,2},{5,3},{6,0},{7,1},{8,14},{9,15},{10,... | collective-permute-start | bytes 417800 | tf_op jit(solution)/shard_map/ppermute | solution.py:436
  74.3 4.4 %collective-permute-start.7 = (s32[136,128]{1,0:T(8,128)S(1)}, s32[136,128]{1,0:T(8,128)S(1)}, u32[]{:S(2)}, u32[]{:S(2)}) collective-permute-start(s32[136,128]{1,0:T(8,128)S(1)} %get-tuple-element.38), channel_id=1, source_target_pairs={{0,8},{8,0},{16,24},{24,16},{1,9},{9,1},{17,25},{25,17},{2,10},{10... | collective-permute-start | bytes 208904 | tf_op jit(solution)/shard_map/ppermute | solution.py:429
  75.9 6.0 %collective-permute-start.8 = (s32[136,128]{1,0:T(8,128)S(1)}, s32[136,128]{1,0:T(8,128)S(1)}, u32[]{:S(2)}, u32[]{:S(2)}) collective-permute-start(s32[136,128]{1,0:T(8,128)S(1)} %get-tuple-element.39), channel_id=1, source_target_pairs={{0,16},{8,24},{16,0},{24,8},{1,17},{9,25},{17,1},{25,9},{2,18},{10... | collective-permute-start | bytes 208904 | tf_op jit(solution)/shard_map/ppermute | solution.py:429
  81.9 2.8 %collective-permute-start.13 = (s32[2,136,128]{2,1,0:T(8,128)S(1)}, s32[2,136,128]{2,1,0:T(8,128)S(1)}, u32[]{:S(2)}, u32[]{:S(2)}) collective-permute-start(s32[2,136,128]{2,1,0:T(8,128)S(1)} %get-tuple-element.47.refs_0_), channel_id=1, source_target_pairs={{0,1},{1,0},{2,3},{3,2},{4,5},{5,4},{6,7},{7,6},{8,9},{9,8},{10,11... | collective-permute-start | bytes 417800 | tf_op jit(solution)/shard_map/ppermute | solution.py:442
  82.0 2.7 %collective-permute-start.14 = (s32[2,136,128]{2,1,0:T(8,128)S(1)}, s32[2,136,128]{2,1,0:T(8,128)S(1)}, u32[]{:S(2)}, u32[]{:S(2)}) collective-permute-start(s32[2,136,128]{2,1,0:T(8,128)S(1)} %collective-permute-done.10.refs_1_), channel_id=1, source_target_pairs={{0,1},{1,0},{2,3},{3,2},{4,5},{5,4},{6,7},{7,6},{8,9},{9,8},{10,11... | collective-permute-start | bytes 417800 | tf_op jit(solution)/shard_map/ppermute | solution.py:442
  82.5 2.2 %collective-permute-start.15 = (s32[2,136,128]{2,1,0:T(8,128)S(1)}, s32[2,136,128]{2,1,0:T(8,128)S(1)}, u32[]{:S(2)}, u32[]{:S(2)}) collective-permute-start(s32[2,136,128]{2,1,0:T(8,128)S(1)} %collective-permute-done.11.refs_2_), channel_id=1, source_target_pairs={{0,1},{1,0},{2,3},{3,2},{4,5},{5,4},{6,7},{7,6},{8,9},{9,8},{10,11... | collective-permute-start | bytes 417800 | tf_op jit(solution)/shard_map/ppermute | solution.py:442
  82.6 2.1 %collective-permute-start.16 = (s32[2,136,128]{2,1,0:T(8,128)S(1)}, s32[2,136,128]{2,1,0:T(8,128)S(1)}, u32[]{:S(2)}, u32[]{:S(2)}) collective-permute-start(s32[2,136,128]{2,1,0:T(8,128)S(1)} %collective-permute-done.12.refs_3_), channel_id=1, source_target_pairs={{0,1},{1,0},{2,3},{3,2},{4,5},{5,4},{6,7},{7,6},{8,9},{9,8},{10,11... | collective-permute-start | bytes 417800 | tf_op jit(solution)/shard_map/ppermute | solution.py:442
  83.0 11.6 %collective-permute-start.9 = (s32[136,128]{1,0:T(8,128)S(1)}, s32[136,128]{1,0:T(8,128)S(1)}, u32[]{:S(2)}, u32[]{:S(2)}) collective-permute-start(s32[136,128]{1,0:T(8,128)S(1)} %get-tuple-element.40), channel_id=1, source_target_pairs={{0,24},{8,16},{16,8},{24,0},{1,25},{9,17},{17,9},{25,1},{2,26},{10... | collective-permute-start | bytes 208904 | tf_op jit(solution)/shard_map/ppermute | solution.py:429
  90.2 5.1 %collective-permute-start.17 = (s32[136,128]{1,0:T(8,128)S(1)}, s32[136,128]{1,0:T(8,128)S(1)}, u32[]{:S(2)}, u32[]{:S(2)}) collective-permute-start(s32[136,128]{1,0:T(8,128)S(1)} %get-tuple-element.52), channel_id=1, source_target_pairs={{0,8},{8,0},{16,24},{24,16},{1,9},{9,1},{17,25},{25,17},{2,10},{10... | collective-permute-start | bytes 208904 | tf_op jit(solution)/shard_map/ppermute | solution.py:429
  91.1 8.4 %collective-permute-start.18 = (s32[136,128]{1,0:T(8,128)S(1)}, s32[136,128]{1,0:T(8,128)S(1)}, u32[]{:S(2)}, u32[]{:S(2)}) collective-permute-start(s32[136,128]{1,0:T(8,128)S(1)} %get-tuple-element.53), channel_id=1, source_target_pairs={{0,16},{8,24},{16,0},{24,8},{1,17},{9,25},{17,1},{25,9},{2,18},{10... | collective-permute-start | bytes 208904 | tf_op jit(solution)/shard_map/ppermute | solution.py:429
  92.9 6.6 %collective-permute-start.19 = (s32[136,128]{1,0:T(8,128)S(1)}, s32[136,128]{1,0:T(8,128)S(1)}, u32[]{:S(2)}, u32[]{:S(2)}) collective-permute-start(s32[136,128]{1,0:T(8,128)S(1)} %get-tuple-element.54), channel_id=1, source_target_pairs={{0,24},{8,16},{16,8},{24,0},{1,25},{9,17},{17,9},{25,1},{2,26},{10... | collective-permute-start | bytes 208904 | tf_op jit(solution)/shard_map/ppermute | solution.py:429

commit v11 on v10

--- a/solution.py
+++ b/solution.py
@@ -50,6 +50,7 @@
     return a, b
 
 
+FINE = 64
 ODD = 239.0 / 256.0
 ODD_DIAGONAL = 169.0 / 256.0
 
@@ -217,7 +218,7 @@
 
 
 def dft_kernel(
-    n_seg, n_pair, most, me_ref, whi_ref, wlo_ref, phase_ref, tables_ref, *refs
+    n_seg, n_pair, most, me_ref, w_ref, phase_ref, tables_ref, *refs
 ):
     ins, outs = refs[:n_pair], refs[n_pair : n_pair + n_seg]
     t_ref, sem, s32, shi, slo, y, zhi, zlo, sums, parts = refs[n_pair + n_seg :]
@@ -226,7 +227,8 @@
     )
     copy.start()
     rows = (ins[0].shape[1] - 8) // most
-    half_h = whi_ref.shape[1] // 2
+    half_h = w_ref.shape[1] // 2
+    whi_ref, wlo_ref = w_ref.at[: 2 * half_h], w_ref.at[2 * half_h :]
     wide = most * TILE
     for k in range(n_pair):
         band = jnp.bitwise_xor(me_ref[1], k)
@@ -253,11 +255,14 @@
             + jnp.dot(whi_ref[...], slo[:, n], preferred_element_type=jnp.float32)
         ) + jnp.dot(whi_ref[...], shi[:, n], preferred_element_type=jnp.float32)
     period = y.shape[1]
-    step_rows = 64
+    step_rows = FINE
+    fine_c, fine_d = phase_ref[:FINE, :TILE], phase_ref[:FINE, TILE:]
     for b in range(period // step_rows):
         at = slice(b * step_rows, (b + 1) * step_rows)
-        c = phase_ref[at, :TILE]
-        d = phase_ref[at, TILE:]
+        big_c = phase_ref[FINE + b : FINE + b + 1, :TILE]
+        big_d = phase_ref[FINE + b : FINE + b + 1, TILE:]
+        c = big_c * fine_c - big_d * fine_d
+        d = big_d * fine_c + big_c * fine_d
         for s in range(most):
             lanes = slice(s * TILE, (s + 1) * TILE)
             yr = y[0, at, lanes]
@@ -342,11 +347,13 @@
     whi = w.astype(jnp.bfloat16)
     wlo = (w - whi.astype(np.float32)).astype(jnp.bfloat16)
     fb = np.arange(TILE) // CC
-    phase = ((np.arange(period)[:, None] * fb[None, :]) % (2 * freq)) * (math.pi / freq)
     scale = np.where(fb % 2 == 0, 1.0, 1.0 / ODD) / math.sqrt(freq)
-    scale = np.concatenate([scale, scale])[None, :]
-    phase = (np.concatenate([np.cos(phase), np.sin(phase)], 1) * scale).astype(np.float32)
-    return [jnp.asarray(c) for c in (whi, wlo, phase)]
+    parts = []
+    for at, gain in ((np.arange(FINE), scale), (np.arange(0, period, FINE), 1.0)):
+        angle = (at[:, None] * fb[None, :] % (2 * freq)) * (math.pi / freq)
+        parts.append(np.concatenate([np.cos(angle) * gain, np.sin(angle) * gain], 1))
+    phase = np.concatenate(parts).astype(np.float32)
+    return [jnp.asarray(c) for c in (np.concatenate([whi, wlo]), phase)]
 
 
 def dft(me, tables, blocks, freq, n_seg, n_pair, most):
@@ -358,7 +365,7 @@
     return pl.pallas_call(
         functools.partial(dft_kernel, n_seg, n_pair, most),
         out_shape=[jax.ShapeDtypeStruct((half // 2 + 8, TILE), jnp.int32)] * n_seg,
-        in_specs=[smem, vmem, vmem, vmem, pl.BlockSpec(memory_space=pltpu.HBM)]
+        in_specs=[smem, vmem, vmem, pl.BlockSpec(memory_space=pltpu.HBM)]
         + [vmem] * len(blocks),
         out_specs=[vmem] * n_seg,
         scratch_shapes=[
@@ -425,10 +432,11 @@
 
 
 def exchange(blocks, axis, size):
-    return [blocks[0]] + [
-        lax.ppermute(blocks[k], axis, [(i, i ^ k) for i in range(size)])
-        for k in range(1, size)
-    ]
+    got = {
+        k: lax.ppermute(blocks[k], axis, [(i, i ^ k) for i in range(size)])
+        for k in reversed(range(1, size))
+    }
+    return [blocks[0]] + [got[k] for k in range(1, size)]
 
 
 def exchange_plane(blocks, n_pair, between=None):

time: 104 us -> 103 us (level)
  local copies, waits for them, and re-layouts: 2.15 us -> 1.09 us
    unnamed x14 -> x12, local copies, waits for them, and re-layouts: 1.99 us -> 0.93 us
  transfers between devices with their start and end apart: 22 -> 22, of which waited for: 7 -> 7; matrix products, arithmetic and copies ran while one was open for 1% -> 1% of each run, Pallas kernels for 18% -> 19%
where the time goes in v11:
time: 103 us
  waiting for transfers between devices  32.5 us (32%)
  starting transfers between devices  30.1 us (29%)
  Pallas kernels  29.3 us (28%)
  blocking collectives  8.35 us (8%)
  between operations  1.37 us (1%)
  local copies, waits for them, and re-layouts  1.09 us (1%)
    ppermute x6, waiting for transfers between devices, exchange_plane(): lax.ppermute(blocks[k], 'pair', [(i, i ^ 2 * k) for i in range(n_pair)])  13.2 us
    pallas_call x2, Pallas kernels, dft(): pl.pallas_call(functools.partial(dft_kernel, n_seg, n_pair, most), out_sh...  11.6 us
    all_to_all x2, starting transfers between devices, body(): lax.all_to_all(sent.reshape(n_seg * n_pair, tiles, 2, rows, TILE), ('seg'...  10.9 us
    ppermute x6, starting transfers between devices, exchange(): lax.ppermute(blocks[k], axis, [(i, i ^ k) for i in range(size)])  10.5 us
    all_to_all x2, waiting for transfers between devices, body(): lax.all_to_all(sent.reshape(n_seg * n_pair, tiles, 2, rows, TILE), ('seg'...  9.73 us
    unnamed x1, blocking collectives  8.35 us
    ppermute x6, waiting for transfers between devices, exchange(): lax.ppermute(blocks[k], axis, [(i, i ^ k) for i in range(size)])  8.15 us
    pallas_call x2, Pallas kernels, pack(): pl.pallas_call(functools.partial(pack_kernel, n_seg, chunk), out_shape=ja...  7.36 us
  transfers between devices with their start and end apart: 22, of which 7 were waited for; matrix products, arithmetic and copies ran while one was open for 1% of the time, Pallas kernels for 19%

profile of v11, /device:TPU:0, one launch (start us, length us, event | category | flops | bytes accessed | tf_op | source)
XLA Modules:
  0.0 102.8 jit_solution(9430604144705478438)
XLA Ops:
  0.0 3.7 %pack.3 = bf16[4,8,2,2,32,128]{5,4,3,2,1,0:T(8,128)(2,1)} custom-call(bf16[2,2048,256]{2,1,0:T(8,128)(2,1)} %bitcast.11), custom_call_target="tpu_custom_call" | custom-call | flops 1 | bytes 1 | tf_op jit(solution)/shard_map/pack/pallas_call | solution.py:131
  3.7 7.3 %all-to-all-start = ((bf16[32,2,2,32,128]{4,3,2,1,0:T(8,128)(2,1)}), bf16[32,2,2,32,128]{4,3,2,1,0:T(8,128)(2,1)S(1)}, u32[]{:S(2)}, u32[]{:S(2)}) async-start(bf16[32,2,2,32,128]{4,3,2,1,0:T(8,128)(2,1)} %bitcast.14), calls=%async_computation | async-start | bytes 2097152 | tf_op jit(solution)/shard_map/all_to_all | solution.py:474
  11.1 3.6 %pack.2 = bf16[4,8,2,2,32,128]{5,4,3,2,1,0:T(8,128)(2,1)} custom-call(bf16[2,2048,256]{2,1,0:T(8,128)(2,1)} %bitcast.12), custom_call_target="tpu_custom_call" | custom-call | flops 1 | bytes 1 | tf_op jit(solution)/shard_map/pack/pallas_call | solution.py:131
  14.7 2.1 %sums.1.tables_ref = bf16[98304,256]{1,0:T(8,128)(2,1)} custom-call(), custom_call_target="tpu_custom_call" | custom-call | flops 1 | bytes 1 | tf_op jit(solution)/shard_map/sums/pallas_call | solution.py:328
  17.7 0.6 dynamic-slice
  19.1 8.4 %all-reduce = s32[72]{0:T(128)S(1)} all-reduce(s32[72]{0:T(128)S(1)} %dynamic-update-slice), channel_id=2, replica_groups=mesh['seg'=4,'pair'=8] {'pair'}, use_global_device_ids=true, to_apply=%add | all-reduce | flops 72 | bytes 576
  27.6 9.7 %all-to-all-done = bf16[32,2,2,32,128]{4,3,2,1,0:T(8,128)(2,1)S(1)} async-done(((bf16[32,2,2,32,128]{4,3,2,1,0:T(8,128)(2,1)}), bf16[32,2,2,32,128]{4,3,2,1,0:T(8,128)(2,1)S(1)}, u32[]{:S(2)}, u32[]{:S(2)}) %all-to-all-start) | async-done | bytes 1048608 | tf_op jit(solution)/shard_map/all_to_all | solution.py:474
  37.3 3.6 %all-to-all-start.1 = ((bf16[32,2,2,32,128]{4,3,2,1,0:T(8,128)(2,1)}), bf16[32,2,2,32,128]{4,3,2,1,0:T(8,128)(2,1)S(1)}, u32[]{:S(2)}, u32[]{:S(2)}) async-start(bf16[32,2,2,32,128]{4,3,2,1,0:T(8,128)(2,1)} %bitcast.13), calls=%async_computation.1 | async-start | bytes 2097152 | tf_op jit(solution)/shard_map/all_to_all | solution.py:474
  41.0 2.2 %stack.14 = (s32[2,136,128]{2,1,0:T(8,128)S(1)}, s32[2,136,128]{2,1,0:T(8,128)S(1)}, s32[2,136,128]{2,1,0:T(8,128)S(1)}, s32[2,136,128]{2,1,0:T(8,128)S(1)}) custom-call(s32[2]{0:T(128)S(1)} %pad_add_fusion.me_ref, s32[8,9]{1,0:T(8,128)S(1)} %reshape.28.table_ref, bf16[4,16,2,32,128]{4,3,2,1,0:T(8,128)(2,1)S(1)} %bitcast.10), custom_call_target="tpu_custom_call" | custom-call | flops 1 | bytes 1 | tf_op jit(solution)/shard_map/stack/pallas_call | solution.py:205
  43.2 1.8 %collective-permute-start = (s32[2,136,128]{2,1,0:T(8,128)S(1)}, s32[2,136,128]{2,1,0:T(8,128)S(1)}, u32[]{:S(2)}, u32[]{:S(2)}) collective-permute-start(s32[2,136,128]{2,1,0:T(8,128)S(1)} %get-tuple-element.34), channel_id=1, source_target_pairs={{0,2},{1,3},{2,0},{3,1},{4,6},{5,7},{6,4},{7,5},{8,10},{9,11},{10,... | collective-permute-start | bytes 417800 | tf_op jit(solution)/shard_map/ppermute | solution.py:444
  45.1 1.5 %collective-permute-start.1 = (s32[2,136,128]{2,1,0:T(8,128)S(1)}, s32[2,136,128]{2,1,0:T(8,128)S(1)}, u32[]{:S(2)}, u32[]{:S(2)}) collective-permute-start(s32[2,136,128]{2,1,0:T(8,128)S(1)} %get-tuple-element.35), channel_id=1, source_target_pairs={{0,4},{1,5},{2,6},{3,7},{4,0},{5,1},{6,2},{7,3},{8,12},{9,13},{10,... | collective-permute-start | bytes 417800 | tf_op jit(solution)/shard_map/ppermute | solution.py:444
  46.8 9.1 %collective-permute-done.refs_1_ = s32[2,136,128]{2,1,0:T(8,128)S(1)} collective-permute-done((s32[2,136,128]{2,1,0:T(8,128)S(1)}, s32[2,136,128]{2,1,0:T(8,128)S(1)}, u32[]{:S(2)}, u32[]{:S(2)}) %collective-permute-start) | collective-permute-done | bytes 139296 | tf_op jit(solution)/shard_map/ppermute | solution.py:444
  55.9 0.5 collective-permute-start.5
  56.4 4.1 %collective-permute-done.2.refs_3_ = s32[2,136,128]{2,1,0:T(8,128)S(1)} collective-permute-done((s32[2,136,128]{2,1,0:T(8,128)S(1)}, s32[2,136,128]{2,1,0:T(8,128)S(1)}, u32[]{:S(2)}, u32[]{:S(2)}) %collective-permute-start.2) | collective-permute-done | bytes 139296 | tf_op jit(solution)/shard_map/ppermute | solution.py:444
  60.5 1.3 %collective-permute-done.6.refs_7_ = s32[2,136,128]{2,1,0:T(8,128)S(1)} collective-permute-done((s32[2,136,128]{2,1,0:T(8,128)S(1)}, s32[2,136,128]{2,1,0:T(8,128)S(1)}, u32[]{:S(2)}, u32[]{:S(2)}) %collective-permute-start.6) | collective-permute-done | bytes 139296 | tf_op jit(solution)/shard_map/ppermute | solution.py:450
  61.9 5.8 %dft.2 = (s32[136,128]{1,0:T(8,128)S(1)}, s32[136,128]{1,0:T(8,128)S(1)}, s32[136,128]{1,0:T(8,128)S(1)}, s32[136,128]{1,0:T(8,128)S(1)}) custom-call(s32[2]{0:T(128)S(1)} %pad_add_fusion.me_ref, bf16[1024,512]{1,0:T(8,128)(2,1)S(1)} %copy-done, f32[72,256]{1,0:T(8,128)S(1)} %copy-done.1, bf16[98304,256]{1,0:T(8,128)(2,1)} %sums.1.tables_ref, ...), custom_call_target="tpu_custom_call" | custom-call | flops 1 | bytes 1 | tf_op jit(solution)/shard_map/dft/pallas_call | solution.py:365
  67.7 2.4 %stack.15 = (s32[2,136,128]{2,1,0:T(8,128)S(1)}, s32[2,136,128]{2,1,0:T(8,128)S(1)}, s32[2,136,128]{2,1,0:T(8,128)S(1)}, s32[2,136,128]{2,1,0:T(8,128)S(1)}) custom-call(s32[2]{0:T(128)S(1)} %pad_add_fusion.me_ref, s32[8,9]{1,0:T(8,128)S(1)} %reshape.28.table_ref, bf16[4,16,2,32,128]{4,3,2,1,0:T(8,128)(2,1)S(1)} %bitcast.9), custom_call_target="tpu_custom_call" | custom-call | flops 1 | bytes 1 | tf_op jit(solution)/shard_map/stack/pallas_call | solution.py:205
  70.1 1.4 %collective-permute-start.10 = (s32[2,136,128]{2,1,0:T(8,128)S(1)}, s32[2,136,128]{2,1,0:T(8,128)S(1)}, u32[]{:S(2)}, u32[]{:S(2)}) collective-permute-start(s32[2,136,128]{2,1,0:T(8,128)S(1)} %get-tuple-element.44), channel_id=1, source_target_pairs={{0,2},{1,3},{2,0},{3,1},{4,6},{5,7},{6,4},{7,5},{8,10},{9,11},{10,... | collective-permute-start | bytes 417800 | tf_op jit(solution)/shard_map/ppermute | solution.py:444
  71.5 1.1 %collective-permute-start.11 = (s32[2,136,128]{2,1,0:T(8,128)S(1)}, s32[2,136,128]{2,1,0:T(8,128)S(1)}, u32[]{:S(2)}, u32[]{:S(2)}) collective-permute-start(s32[2,136,128]{2,1,0:T(8,128)S(1)} %get-tuple-element.45), channel_id=1, source_target_pairs={{0,4},{1,5},{2,6},{3,7},{4,0},{5,1},{6,2},{7,3},{8,12},{9,13},{10,... | collective-permute-start | bytes 417800 | tf_op jit(solution)/shard_map/ppermute | solution.py:444
  72.6 1.1 %collective-permute-start.12 = (s32[2,136,128]{2,1,0:T(8,128)S(1)}, s32[2,136,128]{2,1,0:T(8,128)S(1)}, u32[]{:S(2)}, u32[]{:S(2)}) collective-permute-start(s32[2,136,128]{2,1,0:T(8,128)S(1)} %get-tuple-element.46), channel_id=1, source_target_pairs={{0,6},{1,7},{2,4},{3,5},{4,2},{5,3},{6,0},{7,1},{8,14},{9,15},{10,... | collective-permute-start | bytes 417800 | tf_op jit(solution)/shard_map/ppermute | solution.py:444
  73.7 1.6 %collective-permute-start.7 = (s32[136,128]{1,0:T(8,128)S(1)}, s32[136,128]{1,0:T(8,128)S(1)}, u32[]{:S(2)}, u32[]{:S(2)}) collective-permute-start(s32[136,128]{1,0:T(8,128)S(1)} %get-tuple-element.38), channel_id=1, source_target_pairs={{0,8},{8,0},{16,24},{24,16},{1,9},{9,1},{17,25},{25,17},{2,10},{10... | collective-permute-start | bytes 208904 | tf_op jit(solution)/shard_map/ppermute | solution.py:436
  75.3 2.7 %collective-permute-start.8 = (s32[136,128]{1,0:T(8,128)S(1)}, s32[136,128]{1,0:T(8,128)S(1)}, u32[]{:S(2)}, u32[]{:S(2)}) collective-permute-start(s32[136,128]{1,0:T(8,128)S(1)} %get-tuple-element.39), channel_id=1, source_target_pairs={{0,16},{8,24},{16,0},{24,8},{1,17},{9,25},{17,1},{25,9},{2,18},{10... | collective-permute-start | bytes 208904 | tf_op jit(solution)/shard_map/ppermute | solution.py:436
  78.0 3.2 %collective-permute-done.8.refs_2_ = s32[136,128]{1,0:T(8,128)S(1)} collective-permute-done((s32[136,128]{1,0:T(8,128)S(1)}, s32[136,128]{1,0:T(8,128)S(1)}, u32[]{:S(2)}, u32[]{:S(2)}) %collective-permute-start.8) | collective-permute-done | bytes 69664 | tf_op jit(solution)/shard_map/ppermute | solution.py:436
  81.4 0.5 collective-permute-start.14
  82.4 1.7 %collective-permute-start.9 = (s32[136,128]{1,0:T(8,128)S(1)}, s32[136,128]{1,0:T(8,128)S(1)}, u32[]{:S(2)}, u32[]{:S(2)}) collective-permute-start(s32[136,128]{1,0:T(8,128)S(1)} %get-tuple-element.40), channel_id=1, source_target_pairs={{0,24},{8,16},{16,8},{24,0},{1,25},{9,17},{17,9},{25,1},{2,26},{10... | collective-permute-start | bytes 208904 | tf_op jit(solution)/shard_map/ppermute | solution.py:436
  84.1 5.8 %dft.3 = (s32[136,128]{1,0:T(8,128)S(1)}, s32[136,128]{1,0:T(8,128)S(1)}, s32[136,128]{1,0:T(8,128)S(1)}, s32[136,128]{1,0:T(8,128)S(1)}) custom-call(s32[2]{0:T(128)S(1)} %pad_add_fusion.me_ref, bf16[1024,512]{1,0:T(8,128)(2,1)S(1)} %copy-done, f32[72,256]{1,0:T(8,128)S(1)} %copy-done.1, bf16[98304,256]{1,0:T(8,128)(2,1)} %sums.1.tables_ref, ...), custom_call_target="tpu_custom_call" | custom-call | flops 1 | bytes 1 | tf_op jit(solution)/shard_map/dft/pallas_call | solution.py:365
  89.9 0.9 collective-permute-start.17
  90.8 1.8 %collective-permute-start.18 = (s32[136,128]{1,0:T(8,128)S(1)}, s32[136,128]{1,0:T(8,128)S(1)}, u32[]{:S(2)}, u32[]{:S(2)}) collective-permute-start(s32[136,128]{1,0:T(8,128)S(1)} %get-tuple-element.53), channel_id=1, source_target_pairs={{0,16},{8,24},{16,0},{24,8},{1,17},{9,25},{17,1},{25,9},{2,18},{10... | collective-permute-start | bytes 208904 | tf_op jit(solution)/shard_map/ppermute | solution.py:436
  92.7 1.7 %collective-permute-start.19 = (s32[136,128]{1,0:T(8,128)S(1)}, s32[136,128]{1,0:T(8,128)S(1)}, u32[]{:S(2)}, u32[]{:S(2)}) collective-permute-start(s32[136,128]{1,0:T(8,128)S(1)} %get-tuple-element.54), channel_id=1, source_target_pairs={{0,24},{8,16},{16,8},{24,0},{1,25},{9,17},{17,9},{25,1},{2,26},{10... | collective-permute-start | bytes 208904 | tf_op jit(solution)/shard_map/ppermute | solution.py:436
  94.3 0.7 collective-permute-done.17.refs_5_
  95.0 4.3 %collective-permute-done.18.refs_6_ = s32[136,128]{1,0:T(8,128)S(1)} collective-permute-done((s32[136,128]{1,0:T(8,128)S(1)}, s32[136,128]{1,0:T(8,128)S(1)}, u32[]{:S(2)}, u32[]{:S(2)}) %collective-permute-start.18) | collective-permute-done | bytes 69664 | tf_op jit(solution)/shard_map/ppermute | solution.py:436
  99.3 3.6 %unpack.1 = f32[2,256,4,128]{3,2,1,0:T(4,128)} custom-call(s32[2]{0:T(128)S(1)} %pad_add_fusion.me_ref, s32[136,128]{1,0:T(8,128)S(1)} %get-tuple-element.37.refs_0_, s32[136,128]{1,0:T(8,128)S(1)} %collective-permute-done.7.refs_1_, s32[136,128]{1,0:T(8,128)S(1)} %collective-permute-done.8.refs_2_, s32[136,128]{1,0:T(8,128)S(1)} %collective-permute-done.9.refs_3_, ...), custom_call_target="tpu_custom_call" | custom-call | flops 1 | bytes 1 | tf_op jit(solution)/shard_map/unpack/pallas_call | solution.py:420
  (37 shorter events, 1.6 us)
Async XLA Ops:
  0.0 17.7 %copy-start.3 = (u32[32]{0:T(128)S(1)}, u32[32]{0:T(128)}, u32[]{:S(2)}) copy-start(u32[32]{0:T(128)} %constant.19) | copy-start | bytes 388
  0.0 61.9 %copy-start.1 = (f32[72,256]{1,0:T(8,128)S(1)}, f32[72,256]{1,0:T(8,128)}, u32[]{:S(2)}) copy-start(f32[72,256]{1,0:T(8,128)} %constant.13.clone.phase_ref) | copy-start | bytes 221188
  0.0 61.9 %copy-start = (bf16[1024,512]{1,0:T(8,128)(2,1)S(1)}, bf16[1024,512]{1,0:T(8,128)(2,1)}, u32[]{:S(2)}) copy-start(bf16[1024,512]{1,0:T(8,128)(2,1)} %constant.12.clone.w_ref) | copy-start | bytes 3145732
  0.0 17.5 %copy-start.2 = (s32[4,2]{0,1:T(2,128)S(1)}, s32[4,2]{0,1:T(2,128)}, u32[]{:S(2)}) copy-start(s32[4,2]{0,1:T(2,128)} %param.6) | copy-start | bytes 100
  3.7 33.6 %all-to-all-start = ((bf16[32,2,2,32,128]{4,3,2,1,0:T(8,128)(2,1)}), bf16[32,2,2,32,128]{4,3,2,1,0:T(8,128)(2,1)S(1)}, u32[]{:S(2)}, u32[]{:S(2)}) async-start(bf16[32,2,2,32,128]{4,3,2,1,0:T(8,128)(2,1)} %bitcast.14), calls=%async_computation | async-start | bytes 2097152 | tf_op jit(solution)/shard_map/all_to_all | solution.py:474
  37.3 30.4 %all-to-all-start.1 = ((bf16[32,2,2,32,128]{4,3,2,1,0:T(8,128)(2,1)}), bf16[32,2,2,32,128]{4,3,2,1,0:T(8,128)(2,1)S(1)}, u32[]{:S(2)}, u32[]{:S(2)}) async-start(bf16[32,2,2,32,128]{4,3,2,1,0:T(8,128)(2,1)} %bitcast.13), calls=%async_computation.1 | async-start | bytes 2097152 | tf_op jit(solution)/shard_map/all_to_all | solution.py:474
  43.2 12.6 %collective-permute-start = (s32[2,136,128]{2,1,0:T(8,128)S(1)}, s32[2,136,128]{2,1,0:T(8,128)S(1)}, u32[]{:S(2)}, u32[]{:S(2)}) collective-permute-start(s32[2,136,128]{2,1,0:T(8,128)S(1)} %get-tuple-element.34), channel_id=1, source_target_pairs={{0,2},{1,3},{2,0},{3,1},{4,6},{5,7},{6,4},{7,5},{8,10},{9,11},{10,... | collective-permute-start | bytes 417800 | tf_op jit(solution)/shard_map/ppermute | solution.py:444
  45.1 10.8 %collective-permute-start.1 = (s32[2,136,128]{2,1,0:T(8,128)S(1)}, s32[2,136,128]{2,1,0:T(8,128)S(1)}, u32[]{:S(2)}, u32[]{:S(2)}) collective-permute-start(s32[2,136,128]{2,1,0:T(8,128)S(1)} %get-tuple-element.35), channel_id=1, source_target_pairs={{0,4},{1,5},{2,6},{3,7},{4,0},{5,1},{6,2},{7,3},{8,12},{9,13},{10,... | collective-permute-start | bytes 417800 | tf_op jit(solution)/shard_map/ppermute | solution.py:444
  46.5 14.0 %collective-permute-start.2 = (s32[2,136,128]{2,1,0:T(8,128)S(1)}, s32[2,136,128]{2,1,0:T(8,128)S(1)}, u32[]{:S(2)}, u32[]{:S(2)}) collective-permute-start(s32[2,136,128]{2,1,0:T(8,128)S(1)} %get-tuple-element.36), channel_id=1, source_target_pairs={{0,6},{1,7},{2,4},{3,5},{4,2},{5,3},{6,0},{7,1},{8,14},{9,15},{10,... | collective-permute-start | bytes 417800 | tf_op jit(solution)/shard_map/ppermute | solution.py:444
  46.8 13.7 %collective-permute-start.3 = (s32[2,136,128]{2,1,0:T(8,128)S(1)}, s32[2,136,128]{2,1,0:T(8,128)S(1)}, u32[]{:S(2)}, u32[]{:S(2)}) collective-permute-start(s32[2,136,128]{2,1,0:T(8,128)S(1)} %get-tuple-element.33.refs_0_), channel_id=1, source_target_pairs={{0,1},{1,0},{2,3},{3,2},{4,5},{5,4},{6,7},{7,6},{8,9},{9,8},{10,11... | collective-permute-start | bytes 417800 | tf_op jit(solution)/shard_map/ppermute | solution.py:450
  55.9 4.6 %collective-permute-start.4 = (s32[2,136,128]{2,1,0:T(8,128)S(1)}, s32[2,136,128]{2,1,0:T(8,128)S(1)}, u32[]{:S(2)}, u32[]{:S(2)}) collective-permute-start(s32[2,136,128]{2,1,0:T(8,128)S(1)} %collective-permute-done.refs_1_), channel_id=1, source_target_pairs={{0,1},{1,0},{2,3},{3,2},{4,5},{5,4},{6,7},{7,6},{8,9},{9,8},{10,11... | collective-permute-start | bytes 417800 | tf_op jit(solution)/shard_map/ppermute | solution.py:450
  55.9 4.6 %collective-permute-start.5 = (s32[2,136,128]{2,1,0:T(8,128)S(1)}, s32[2,136,128]{2,1,0:T(8,128)S(1)}, u32[]{:S(2)}, u32[]{:S(2)}) collective-permute-start(s32[2,136,128]{2,1,0:T(8,128)S(1)} %collective-permute-done.1.refs_2_), channel_id=1, source_target_pairs={{0,1},{1,0},{2,3},{3,2},{4,5},{5,4},{6,7},{7,6},{8,9},{9,8},{10,11... | collective-permute-start | bytes 417800 | tf_op jit(solution)/shard_map/ppermute | solution.py:450
  60.5 1.4 %collective-permute-start.6 = (s32[2,136,128]{2,1,0:T(8,128)S(1)}, s32[2,136,128]{2,1,0:T(8,128)S(1)}, u32[]{:S(2)}, u32[]{:S(2)}) collective-permute-start(s32[2,136,128]{2,1,0:T(8,128)S(1)} %collective-permute-done.2.refs_3_), channel_id=1, source_target_pairs={{0,1},{1,0},{2,3},{3,2},{4,5},{5,4},{6,7},{7,6},{8,9},{9,8},{10,11... | collective-permute-start | bytes 417800 | tf_op jit(solution)/shard_map/ppermute | solution.py:450
  70.1 11.1 %collective-permute-start.10 = (s32[2,136,128]{2,1,0:T(8,128)S(1)}, s32[2,136,128]{2,1,0:T(8,128)S(1)}, u32[]{:S(2)}, u32[]{:S(2)}) collective-permute-start(s32[2,136,128]{2,1,0:T(8,128)S(1)} %get-tuple-element.44), channel_id=1, source_target_pairs={{0,2},{1,3},{2,0},{3,1},{4,6},{5,7},{6,4},{7,5},{8,10},{9,11},{10,... | collective-permute-start | bytes 417800 | tf_op jit(solution)/shard_map/ppermute | solution.py:444
  71.5 9.8 %collective-permute-start.11 = (s32[2,136,128]{2,1,0:T(8,128)S(1)}, s32[2,136,128]{2,1,0:T(8,128)S(1)}, u32[]{:S(2)}, u32[]{:S(2)}) collective-permute-start(s32[2,136,128]{2,1,0:T(8,128)S(1)} %get-tuple-element.45), channel_id=1, source_target_pairs={{0,4},{1,5},{2,6},{3,7},{4,0},{5,1},{6,2},{7,3},{8,12},{9,13},{10,... | collective-permute-start | bytes 417800 | tf_op jit(solution)/shard_map/ppermute | solution.py:444
  72.6 8.7 %collective-permute-start.12 = (s32[2,136,128]{2,1,0:T(8,128)S(1)}, s32[2,136,128]{2,1,0:T(8,128)S(1)}, u32[]{:S(2)}, u32[]{:S(2)}) collective-permute-start(s32[2,136,128]{2,1,0:T(8,128)S(1)} %get-tuple-element.46), channel_id=1, source_target_pairs={{0,6},{1,7},{2,4},{3,5},{4,2},{5,3},{6,0},{7,1},{8,14},{9,15},{10,... | collective-permute-start | bytes 417800 | tf_op jit(solution)/shard_map/ppermute | solution.py:444
  73.7 4.4 %collective-permute-start.7 = (s32[136,128]{1,0:T(8,128)S(1)}, s32[136,128]{1,0:T(8,128)S(1)}, u32[]{:S(2)}, u32[]{:S(2)}) collective-permute-start(s32[136,128]{1,0:T(8,128)S(1)} %get-tuple-element.38), channel_id=1, source_target_pairs={{0,8},{8,0},{16,24},{24,16},{1,9},{9,1},{17,25},{25,17},{2,10},{10... | collective-permute-start | bytes 208904 | tf_op jit(solution)/shard_map/ppermute | solution.py:436
  75.3 6.0 %collective-permute-start.8 = (s32[136,128]{1,0:T(8,128)S(1)}, s32[136,128]{1,0:T(8,128)S(1)}, u32[]{:S(2)}, u32[]{:S(2)}) collective-permute-start(s32[136,128]{1,0:T(8,128)S(1)} %get-tuple-element.39), channel_id=1, source_target_pairs={{0,16},{8,24},{16,0},{24,8},{1,17},{9,25},{17,1},{25,9},{2,18},{10... | collective-permute-start | bytes 208904 | tf_op jit(solution)/shard_map/ppermute | solution.py:436
  81.3 2.8 %collective-permute-start.13 = (s32[2,136,128]{2,1,0:T(8,128)S(1)}, s32[2,136,128]{2,1,0:T(8,128)S(1)}, u32[]{:S(2)}, u32[]{:S(2)}) collective-permute-start(s32[2,136,128]{2,1,0:T(8,128)S(1)} %get-tuple-element.47.refs_0_), channel_id=1, source_target_pairs={{0,1},{1,0},{2,3},{3,2},{4,5},{5,4},{6,7},{7,6},{8,9},{9,8},{10,11... | collective-permute-start | bytes 417800 | tf_op jit(solution)/shard_map/ppermute | solution.py:450
  81.4 2.7 %collective-permute-start.14 = (s32[2,136,128]{2,1,0:T(8,128)S(1)}, s32[2,136,128]{2,1,0:T(8,128)S(1)}, u32[]{:S(2)}, u32[]{:S(2)}) collective-permute-start(s32[2,136,128]{2,1,0:T(8,128)S(1)} %collective-permute-done.10.refs_1_), channel_id=1, source_target_pairs={{0,1},{1,0},{2,3},{3,2},{4,5},{5,4},{6,7},{7,6},{8,9},{9,8},{10,11... | collective-permute-start | bytes 417800 | tf_op jit(solution)/shard_map/ppermute | solution.py:450
  81.8 2.2 %collective-permute-start.15 = (s32[2,136,128]{2,1,0:T(8,128)S(1)}, s32[2,136,128]{2,1,0:T(8,128)S(1)}, u32[]{:S(2)}, u32[]{:S(2)}) collective-permute-start(s32[2,136,128]{2,1,0:T(8,128)S(1)} %collective-permute-done.11.refs_2_), channel_id=1, source_target_pairs={{0,1},{1,0},{2,3},{3,2},{4,5},{5,4},{6,7},{7,6},{8,9},{9,8},{10,11... | collective-permute-start | bytes 417800 | tf_op jit(solution)/shard_map/ppermute | solution.py:450
  81.9 2.1 %collective-permute-start.16 = (s32[2,136,128]{2,1,0:T(8,128)S(1)}, s32[2,136,128]{2,1,0:T(8,128)S(1)}, u32[]{:S(2)}, u32[]{:S(2)}) collective-permute-start(s32[2,136,128]{2,1,0:T(8,128)S(1)} %collective-permute-done.12.refs_3_), channel_id=1, source_target_pairs={{0,1},{1,0},{2,3},{3,2},{4,5},{5,4},{6,7},{7,6},{8,9},{9,8},{10,11... | collective-permute-start | bytes 417800 | tf_op jit(solution)/shard_map/ppermute | solution.py:450
  82.4 12.0 %collective-permute-start.9 = (s32[136,128]{1,0:T(8,128)S(1)}, s32[136,128]{1,0:T(8,128)S(1)}, u32[]{:S(2)}, u32[]{:S(2)}) collective-permute-start(s32[136,128]{1,0:T(8,128)S(1)} %get-tuple-element.40), channel_id=1, source_target_pairs={{0,24},{8,16},{16,8},{24,0},{1,25},{9,17},{17,9},{25,1},{2,26},{10... | collective-permute-start | bytes 208904 | tf_op jit(solution)/shard_map/ppermute | solution.py:436
  89.9 5.1 %collective-permute-start.17 = (s32[136,128]{1,0:T(8,128)S(1)}, s32[136,128]{1,0:T(8,128)S(1)}, u32[]{:S(2)}, u32[]{:S(2)}) collective-permute-start(s32[136,128]{1,0:T(8,128)S(1)} %get-tuple-element.52), channel_id=1, source_target_pairs={{0,8},{8,0},{16,24},{24,16},{1,9},{9,1},{17,25},{25,17},{2,10},{10... | collective-permute-start | bytes 208904 | tf_op jit(solution)/shard_map/ppermute | solution.py:436
  90.8 8.5 %collective-permute-start.18 = (s32[136,128]{1,0:T(8,128)S(1)}, s32[136,128]{1,0:T(8,128)S(1)}, u32[]{:S(2)}, u32[]{:S(2)}) collective-permute-start(s32[136,128]{1,0:T(8,128)S(1)} %get-tuple-element.53), channel_id=1, source_target_pairs={{0,16},{8,24},{16,0},{24,8},{1,17},{9,25},{17,1},{25,9},{2,18},{10... | collective-permute-start | bytes 208904 | tf_op jit(solution)/shard_map/ppermute | solution.py:436
  92.7 6.6 %collective-permute-start.19 = (s32[136,128]{1,0:T(8,128)S(1)}, s32[136,128]{1,0:T(8,128)S(1)}, u32[]{:S(2)}, u32[]{:S(2)}) collective-permute-start(s32[136,128]{1,0:T(8,128)S(1)} %get-tuple-element.54), channel_id=1, source_target_pairs={{0,24},{8,16},{16,8},{24,0},{1,25},{9,17},{17,9},{25,1},{2,26},{10... | collective-permute-start | bytes 208904 | tf_op jit(solution)/shard_map/ppermute | solution.py:436

commit v12 on v11

--- a/solution.py
+++ b/solution.py
@@ -396,7 +396,7 @@
         for k in range(n_seg):
             z = jnp.bitwise_xor(me_ref[0], k)
             for ch in range(chunks):
-                src = ins[ch * n_seg + k]
+                src = ins[ch * n_seg + n_seg - 1 - k]
                 top = src[half // 2 : half // 2 + 1, :].astype(jnp.float32)
                 low, high = decode(src[: half // 2, :], top)
                 buf[z * chunks + ch, : half // 2] = low
@@ -468,7 +468,7 @@
     table = lax.all_gather(lists, "pair", axis=0)
     if chunks > 1:
         table, packed[1], _ = lax.optimization_barrier((table, packed[1], sums))
-    done = []
+    done, parts = [], []
     lags = None
     for sent in packed:
         got = lax.all_to_all(
@@ -482,10 +482,11 @@
             got, _ = lax.optimization_barrier((got, lags))
         spec = got.reshape(n_seg, n_pair * tiles, 2, rows, TILE)
         stack = stacks(me, table, spec, n_seg, n_pair, most)
-        blocks = exchange_plane(stack, n_pair, done[1:3] or None)
+        blocks = exchange_plane(stack, n_pair, done[2:0:-1] or None)
         lags = dft(me, tables, blocks, freq, n_seg, n_pair, most)
-        done += exchange(lags, "seg", n_seg)
-    return unpack(me, done, n_seg, chunks, most)
+        done = exchange(lags, "seg", n_seg)
+        parts += done[::-1]
+    return unpack(me, parts, n_seg, chunks, most)
 
 
 def solution(mesh):

time: 103 us -> 103 us (level)
  waiting for transfers between devices: 32.5 us -> 30.9 us
    ppermute x6, waiting for transfers between devices: 8.15 us -> 6.63 us  [exchange(): lax.ppermute(blocks[k], axis, [(i, i ^ k) for i in range(size)])]
  transfers between devices with their start and end apart: 22 -> 22, of which waited for: 7 -> 8; matrix products, arithmetic and copies ran while one was open for 1% -> 1% of each run, Pallas kernels for 19% -> 19%
where the time goes in v12:
time: 103 us; the launch traced here: 102 us
  starting transfers between devices  31.1 us (30%)
  waiting for transfers between devices  30.9 us (30%)
  Pallas kernels  29.3 us (28%)
  blocking collectives  8.35 us (8%)
  between operations  1.37 us (1%)
  local copies, waits for them, and re-layouts  1.09 us (1%)
    ppermute x6, waiting for transfers between devices, exchange_plane(): lax.ppermute(blocks[k], 'pair', [(i, i ^ 2 * k) for i in range(n_pair)])  13.2 us
    pallas_call x2, Pallas kernels, dft(): pl.pallas_call(functools.partial(dft_kernel, n_seg, n_pair, most), out_sh...  11.6 us
    ppermute x6, starting transfers between devices, exchange(): lax.ppermute(blocks[k], axis, [(i, i ^ k) for i in range(size)])  11.4 us
    all_to_all x2, starting transfers between devices, body(): lax.all_to_all(sent.reshape(n_seg * n_pair, tiles, 2, rows, TILE), ('seg'...  10.9 us
    all_to_all x2, waiting for transfers between devices, body(): lax.all_to_all(sent.reshape(n_seg * n_pair, tiles, 2, rows, TILE), ('seg'...  9.73 us
    unnamed x1, blocking collectives  8.35 us
    pallas_call x2, Pallas kernels, pack(): pl.pallas_call(functools.partial(pack_kernel, n_seg, chunk), out_shape=ja...  7.36 us
    ppermute x6, starting transfers between devices, exchange_plane(): lax.ppermute(blocks[k], 'pair', [(i, i ^ 2 * k) for i in range(n_pair)])  7.11 us
  transfers between devices with their start and end apart: 22, of which 8 were waited for; matrix products, arithmetic and copies ran while one was open for 1% of the time, Pallas kernels for 19%

profile of v12, /device:TPU:0, one launch (start us, length us, event | category | flops | bytes accessed | tf_op | source)
XLA Modules:
  0.0 102.3 jit_solution(13372410095379418696)
XLA Ops:
  0.0 3.7 %pack.3 = bf16[4,8,2,2,32,128]{5,4,3,2,1,0:T(8,128)(2,1)} custom-call(bf16[2,2048,256]{2,1,0:T(8,128)(2,1)} %bitcast.11), custom_call_target="tpu_custom_call" | custom-call | flops 1 | bytes 1 | tf_op jit(solution)/shard_map/pack/pallas_call | solution.py:131
  3.7 7.3 %all-to-all-start = ((bf16[32,2,2,32,128]{4,3,2,1,0:T(8,128)(2,1)}), bf16[32,2,2,32,128]{4,3,2,1,0:T(8,128)(2,1)S(1)}, u32[]{:S(2)}, u32[]{:S(2)}) async-start(bf16[32,2,2,32,128]{4,3,2,1,0:T(8,128)(2,1)} %bitcast.14), calls=%async_computation | async-start | bytes 2097152 | tf_op jit(solution)/shard_map/all_to_all | solution.py:474
  11.1 3.6 %pack.2 = bf16[4,8,2,2,32,128]{5,4,3,2,1,0:T(8,128)(2,1)} custom-call(bf16[2,2048,256]{2,1,0:T(8,128)(2,1)} %bitcast.12), custom_call_target="tpu_custom_call" | custom-call | flops 1 | bytes 1 | tf_op jit(solution)/shard_map/pack/pallas_call | solution.py:131
  14.7 2.1 %sums.1.tables_ref = bf16[98304,256]{1,0:T(8,128)(2,1)} custom-call(), custom_call_target="tpu_custom_call" | custom-call | flops 1 | bytes 1 | tf_op jit(solution)/shard_map/sums/pallas_call | solution.py:328
  17.7 0.6 dynamic-slice
  19.1 8.4 %all-reduce = s32[72]{0:T(128)S(1)} all-reduce(s32[72]{0:T(128)S(1)} %dynamic-update-slice), channel_id=2, replica_groups=mesh['seg'=4,'pair'=8] {'pair'}, use_global_device_ids=true, to_apply=%add | all-reduce | flops 72 | bytes 576
  27.6 9.7 %all-to-all-done = bf16[32,2,2,32,128]{4,3,2,1,0:T(8,128)(2,1)S(1)} async-done(((bf16[32,2,2,32,128]{4,3,2,1,0:T(8,128)(2,1)}), bf16[32,2,2,32,128]{4,3,2,1,0:T(8,128)(2,1)S(1)}, u32[]{:S(2)}, u32[]{:S(2)}) %all-to-all-start) | async-done | bytes 1048608 | tf_op jit(solution)/shard_map/all_to_all | solution.py:474
  37.3 3.6 %all-to-all-start.1 = ((bf16[32,2,2,32,128]{4,3,2,1,0:T(8,128)(2,1)}), bf16[32,2,2,32,128]{4,3,2,1,0:T(8,128)(2,1)S(1)}, u32[]{:S(2)}, u32[]{:S(2)}) async-start(bf16[32,2,2,32,128]{4,3,2,1,0:T(8,128)(2,1)} %bitcast.13), calls=%async_computation.1 | async-start | bytes 2097152 | tf_op jit(solution)/shard_map/all_to_all | solution.py:474
  41.0 2.2 %stack.14 = (s32[2,136,128]{2,1,0:T(8,128)S(1)}, s32[2,136,128]{2,1,0:T(8,128)S(1)}, s32[2,136,128]{2,1,0:T(8,128)S(1)}, s32[2,136,128]{2,1,0:T(8,128)S(1)}) custom-call(s32[2]{0:T(128)S(1)} %pad_add_fusion.me_ref, s32[8,9]{1,0:T(8,128)S(1)} %reshape.28.table_ref, bf16[4,16,2,32,128]{4,3,2,1,0:T(8,128)(2,1)S(1)} %bitcast.10), custom_call_target="tpu_custom_call" | custom-call | flops 1 | bytes 1 | tf_op jit(solution)/shard_map/stack/pallas_call | solution.py:205
  43.2 1.8 %collective-permute-start = (s32[2,136,128]{2,1,0:T(8,128)S(1)}, s32[2,136,128]{2,1,0:T(8,128)S(1)}, u32[]{:S(2)}, u32[]{:S(2)}) collective-permute-start(s32[2,136,128]{2,1,0:T(8,128)S(1)} %get-tuple-element.34), channel_id=1, source_target_pairs={{0,2},{1,3},{2,0},{3,1},{4,6},{5,7},{6,4},{7,5},{8,10},{9,11},{10,... | collective-permute-start | bytes 417800 | tf_op jit(solution)/shard_map/ppermute | solution.py:444
  45.1 1.5 %collective-permute-start.1 = (s32[2,136,128]{2,1,0:T(8,128)S(1)}, s32[2,136,128]{2,1,0:T(8,128)S(1)}, u32[]{:S(2)}, u32[]{:S(2)}) collective-permute-start(s32[2,136,128]{2,1,0:T(8,128)S(1)} %get-tuple-element.35), channel_id=1, source_target_pairs={{0,4},{1,5},{2,6},{3,7},{4,0},{5,1},{6,2},{7,3},{8,12},{9,13},{10,... | collective-permute-start | bytes 417800 | tf_op jit(solution)/shard_map/ppermute | solution.py:444
  46.8 9.1 %collective-permute-done.refs_1_ = s32[2,136,128]{2,1,0:T(8,128)S(1)} collective-permute-done((s32[2,136,128]{2,1,0:T(8,128)S(1)}, s32[2,136,128]{2,1,0:T(8,128)S(1)}, u32[]{:S(2)}, u32[]{:S(2)}) %collective-permute-start) | collective-permute-done | bytes 139296 | tf_op jit(solution)/shard_map/ppermute | solution.py:444
  55.9 0.5 collective-permute-start.5
  56.4 4.1 %collective-permute-done.2.refs_3_ = s32[2,136,128]{2,1,0:T(8,128)S(1)} collective-permute-done((s32[2,136,128]{2,1,0:T(8,128)S(1)}, s32[2,136,128]{2,1,0:T(8,128)S(1)}, u32[]{:S(2)}, u32[]{:S(2)}) %collective-permute-start.2) | collective-permute-done | bytes 139296 | tf_op jit(solution)/shard_map/ppermute | solution.py:444
  60.5 1.3 %collective-permute-done.6.refs_7_ = s32[2,136,128]{2,1,0:T(8,128)S(1)} collective-permute-done((s32[2,136,128]{2,1,0:T(8,128)S(1)}, s32[2,136,128]{2,1,0:T(8,128)S(1)}, u32[]{:S(2)}, u32[]{:S(2)}) %collective-permute-start.6) | collective-permute-done | bytes 139296 | tf_op jit(solution)/shard_map/ppermute | solution.py:450
  61.9 5.8 %dft.2 = (s32[136,128]{1,0:T(8,128)S(1)}, s32[136,128]{1,0:T(8,128)S(1)}, s32[136,128]{1,0:T(8,128)S(1)}, s32[136,128]{1,0:T(8,128)S(1)}) custom-call(s32[2]{0:T(128)S(1)} %pad_add_fusion.me_ref, bf16[1024,512]{1,0:T(8,128)(2,1)S(1)} %copy-done, f32[72,256]{1,0:T(8,128)S(1)} %copy-done.1, bf16[98304,256]{1,0:T(8,128)(2,1)} %sums.1.tables_ref, ...), custom_call_target="tpu_custom_call" | custom-call | flops 1 | bytes 1 | tf_op jit(solution)/shard_map/dft/pallas_call | solution.py:365
  67.7 2.4 %stack.15 = (s32[2,136,128]{2,1,0:T(8,128)S(1)}, s32[2,136,128]{2,1,0:T(8,128)S(1)}, s32[2,136,128]{2,1,0:T(8,128)S(1)}, s32[2,136,128]{2,1,0:T(8,128)S(1)}) custom-call(s32[2]{0:T(128)S(1)} %pad_add_fusion.me_ref, s32[8,9]{1,0:T(8,128)S(1)} %reshape.28.table_ref, bf16[4,16,2,32,128]{4,3,2,1,0:T(8,128)(2,1)S(1)} %bitcast.9), custom_call_target="tpu_custom_call" | custom-call | flops 1 | bytes 1 | tf_op jit(solution)/shard_map/stack/pallas_call | solution.py:205
  70.1 1.4 %collective-permute-start.10 = (s32[2,136,128]{2,1,0:T(8,128)S(1)}, s32[2,136,128]{2,1,0:T(8,128)S(1)}, u32[]{:S(2)}, u32[]{:S(2)}) collective-permute-start(s32[2,136,128]{2,1,0:T(8,128)S(1)} %get-tuple-element.44), channel_id=1, source_target_pairs={{0,2},{1,3},{2,0},{3,1},{4,6},{5,7},{6,4},{7,5},{8,10},{9,11},{10,... | collective-permute-start | bytes 417800 | tf_op jit(solution)/shard_map/ppermute | solution.py:444
  71.5 1.1 %collective-permute-start.11 = (s32[2,136,128]{2,1,0:T(8,128)S(1)}, s32[2,136,128]{2,1,0:T(8,128)S(1)}, u32[]{:S(2)}, u32[]{:S(2)}) collective-permute-start(s32[2,136,128]{2,1,0:T(8,128)S(1)} %get-tuple-element.45), channel_id=1, source_target_pairs={{0,4},{1,5},{2,6},{3,7},{4,0},{5,1},{6,2},{7,3},{8,12},{9,13},{10,... | collective-permute-start | bytes 417800 | tf_op jit(solution)/shard_map/ppermute | solution.py:444
  72.6 1.1 %collective-permute-start.12 = (s32[2,136,128]{2,1,0:T(8,128)S(1)}, s32[2,136,128]{2,1,0:T(8,128)S(1)}, u32[]{:S(2)}, u32[]{:S(2)}) collective-permute-start(s32[2,136,128]{2,1,0:T(8,128)S(1)} %get-tuple-element.46), channel_id=1, source_target_pairs={{0,6},{1,7},{2,4},{3,5},{4,2},{5,3},{6,0},{7,1},{8,14},{9,15},{10,... | collective-permute-start | bytes 417800 | tf_op jit(solution)/shard_map/ppermute | solution.py:444
  73.7 1.8 %collective-permute-start.8 = (s32[136,128]{1,0:T(8,128)S(1)}, s32[136,128]{1,0:T(8,128)S(1)}, u32[]{:S(2)}, u32[]{:S(2)}) collective-permute-start(s32[136,128]{1,0:T(8,128)S(1)} %get-tuple-element.38), channel_id=1, source_target_pairs={{0,16},{8,24},{16,0},{24,8},{1,17},{9,25},{17,1},{25,9},{2,18},{10... | collective-permute-start | bytes 208904 | tf_op jit(solution)/shard_map/ppermute | solution.py:436
  75.4 2.6 %collective-permute-start.9 = (s32[136,128]{1,0:T(8,128)S(1)}, s32[136,128]{1,0:T(8,128)S(1)}, u32[]{:S(2)}, u32[]{:S(2)}) collective-permute-start(s32[136,128]{1,0:T(8,128)S(1)} %get-tuple-element.39), channel_id=1, source_target_pairs={{0,8},{8,0},{16,24},{24,16},{1,9},{9,1},{17,25},{25,17},{2,10},{10... | collective-permute-start | bytes 208904 | tf_op jit(solution)/shard_map/ppermute | solution.py:436
  78.0 1.2 %collective-permute-done.8.refs_1_ = s32[136,128]{1,0:T(8,128)S(1)} collective-permute-done((s32[136,128]{1,0:T(8,128)S(1)}, s32[136,128]{1,0:T(8,128)S(1)}, u32[]{:S(2)}, u32[]{:S(2)}) %collective-permute-start.8) | collective-permute-done | bytes 69664 | tf_op jit(solution)/shard_map/ppermute | solution.py:436
  79.2 1.1 %collective-permute-done.9.refs_2_ = s32[136,128]{1,0:T(8,128)S(1)} collective-permute-done((s32[136,128]{1,0:T(8,128)S(1)}, s32[136,128]{1,0:T(8,128)S(1)}, u32[]{:S(2)}, u32[]{:S(2)}) %collective-permute-start.9) | collective-permute-done | bytes 69664 | tf_op jit(solution)/shard_map/ppermute | solution.py:436
  81.4 2.6 %collective-permute-start.7 = (s32[136,128]{1,0:T(8,128)S(1)}, s32[136,128]{1,0:T(8,128)S(1)}, u32[]{:S(2)}, u32[]{:S(2)}) collective-permute-start(s32[136,128]{1,0:T(8,128)S(1)} %get-tuple-element.37), channel_id=1, source_target_pairs={{0,24},{8,16},{16,8},{24,0},{1,25},{9,17},{17,9},{25,1},{2,26},{10... | collective-permute-start | bytes 208904 | tf_op jit(solution)/shard_map/ppermute | solution.py:436
  84.1 5.8 %dft.3 = (s32[136,128]{1,0:T(8,128)S(1)}, s32[136,128]{1,0:T(8,128)S(1)}, s32[136,128]{1,0:T(8,128)S(1)}, s32[136,128]{1,0:T(8,128)S(1)}) custom-call(s32[2]{0:T(128)S(1)} %pad_add_fusion.me_ref, bf16[1024,512]{1,0:T(8,128)(2,1)S(1)} %copy-done, f32[72,256]{1,0:T(8,128)S(1)} %copy-done.1, bf16[98304,256]{1,0:T(8,128)(2,1)} %sums.1.tables_ref, ...), custom_call_target="tpu_custom_call" | custom-call | flops 1 | bytes 1 | tf_op jit(solution)/shard_map/dft/pallas_call | solution.py:365
  89.9 1.3 %collective-permute-start.17 = (s32[136,128]{1,0:T(8,128)S(1)}, s32[136,128]{1,0:T(8,128)S(1)}, u32[]{:S(2)}, u32[]{:S(2)}) collective-permute-start(s32[136,128]{1,0:T(8,128)S(1)} %get-tuple-element.51), channel_id=1, source_target_pairs={{0,24},{8,16},{16,8},{24,0},{1,25},{9,17},{17,9},{25,1},{2,26},{10... | collective-permute-start | bytes 208904 | tf_op jit(solution)/shard_map/ppermute | solution.py:436
  91.2 0.7 collective-permute-start.18
  91.8 2.5 %collective-permute-start.19 = (s32[136,128]{1,0:T(8,128)S(1)}, s32[136,128]{1,0:T(8,128)S(1)}, u32[]{:S(2)}, u32[]{:S(2)}) collective-permute-start(s32[136,128]{1,0:T(8,128)S(1)} %get-tuple-element.53), channel_id=1, source_target_pairs={{0,8},{8,0},{16,24},{24,16},{1,9},{9,1},{17,25},{25,17},{2,10},{10... | collective-permute-start | bytes 208904 | tf_op jit(solution)/shard_map/ppermute | solution.py:436
  94.3 2.5 %collective-permute-done.17.refs_4_ = s32[136,128]{1,0:T(8,128)S(1)} collective-permute-done((s32[136,128]{1,0:T(8,128)S(1)}, s32[136,128]{1,0:T(8,128)S(1)}, u32[]{:S(2)}, u32[]{:S(2)}) %collective-permute-start.17) | collective-permute-done | bytes 69664 | tf_op jit(solution)/shard_map/ppermute | solution.py:436
  96.9 1.8 %collective-permute-done.18.refs_5_ = s32[136,128]{1,0:T(8,128)S(1)} collective-permute-done((s32[136,128]{1,0:T(8,128)S(1)}, s32[136,128]{1,0:T(8,128)S(1)}, u32[]{:S(2)}, u32[]{:S(2)}) %collective-permute-start.18) | collective-permute-done | bytes 69664 | tf_op jit(solution)/shard_map/ppermute | solution.py:436
  98.7 3.6 %unpack.1 = f32[2,256,4,128]{3,2,1,0:T(4,128)} custom-call(s32[2]{0:T(128)S(1)} %pad_add_fusion.me_ref, s32[136,128]{1,0:T(8,128)S(1)} %collective-permute-done.7.refs_0_, s32[136,128]{1,0:T(8,128)S(1)} %collective-permute-done.8.refs_1_, s32[136,128]{1,0:T(8,128)S(1)} %collective-permute-done.9.refs_2_, s32[136,128]{1,0:T(8,128)S(1)} %get-tuple-element.40.refs_3_, ...), custom_call_target="tpu_custom_call" | custom-call | flops 1 | bytes 1 | tf_op jit(solution)/shard_map/unpack/pallas_call | solution.py:420
  (37 shorter events, 2.0 us)
Async XLA Ops:
  0.0 17.7 %copy-start.3 = (u32[32]{0:T(128)S(1)}, u32[32]{0:T(128)}, u32[]{:S(2)}) copy-start(u32[32]{0:T(128)} %constant.19) | copy-start | bytes 388
  0.0 61.9 %copy-start.1 = (f32[72,256]{1,0:T(8,128)S(1)}, f32[72,256]{1,0:T(8,128)}, u32[]{:S(2)}) copy-start(f32[72,256]{1,0:T(8,128)} %constant.13.clone.phase_ref) | copy-start | bytes 221188
  0.0 61.9 %copy-start = (bf16[1024,512]{1,0:T(8,128)(2,1)S(1)}, bf16[1024,512]{1,0:T(8,128)(2,1)}, u32[]{:S(2)}) copy-start(bf16[1024,512]{1,0:T(8,128)(2,1)} %constant.12.clone.w_ref) | copy-start | bytes 3145732
  0.0 17.5 %copy-start.2 = (s32[4,2]{0,1:T(2,128)S(1)}, s32[4,2]{0,1:T(2,128)}, u32[]{:S(2)}) copy-start(s32[4,2]{0,1:T(2,128)} %param.6) | copy-start | bytes 100
  3.7 33.6 %all-to-all-start = ((bf16[32,2,2,32,128]{4,3,2,1,0:T(8,128)(2,1)}), bf16[32,2,2,32,128]{4,3,2,1,0:T(8,128)(2,1)S(1)}, u32[]{:S(2)}, u32[]{:S(2)}) async-start(bf16[32,2,2,32,128]{4,3,2,1,0:T(8,128)(2,1)} %bitcast.14), calls=%async_computation | async-start | bytes 2097152 | tf_op jit(solution)/shard_map/all_to_all | solution.py:474
  37.3 30.4 %all-to-all-start.1 = ((bf16[32,2,2,32,128]{4,3,2,1,0:T(8,128)(2,1)}), bf16[32,2,2,32,128]{4,3,2,1,0:T(8,128)(2,1)S(1)}, u32[]{:S(2)}, u32[]{:S(2)}) async-start(bf16[32,2,2,32,128]{4,3,2,1,0:T(8,128)(2,1)} %bitcast.13), calls=%async_computation.1 | async-start | bytes 2097152 | tf_op jit(solution)/shard_map/all_to_all | solution.py:474
  43.2 12.6 %collective-permute-start = (s32[2,136,128]{2,1,0:T(8,128)S(1)}, s32[2,136,128]{2,1,0:T(8,128)S(1)}, u32[]{:S(2)}, u32[]{:S(2)}) collective-permute-start(s32[2,136,128]{2,1,0:T(8,128)S(1)} %get-tuple-element.34), channel_id=1, source_target_pairs={{0,2},{1,3},{2,0},{3,1},{4,6},{5,7},{6,4},{7,5},{8,10},{9,11},{10,... | collective-permute-start | bytes 417800 | tf_op jit(solution)/shard_map/ppermute | solution.py:444
  45.1 10.8 %collective-permute-start.1 = (s32[2,136,128]{2,1,0:T(8,128)S(1)}, s32[2,136,128]{2,1,0:T(8,128)S(1)}, u32[]{:S(2)}, u32[]{:S(2)}) collective-permute-start(s32[2,136,128]{2,1,0:T(8,128)S(1)} %get-tuple-element.35), channel_id=1, source_target_pairs={{0,4},{1,5},{2,6},{3,7},{4,0},{5,1},{6,2},{7,3},{8,12},{9,13},{10,... | collective-permute-start | bytes 417800 | tf_op jit(solution)/shard_map/ppermute | solution.py:444
  46.5 14.0 %collective-permute-start.2 = (s32[2,136,128]{2,1,0:T(8,128)S(1)}, s32[2,136,128]{2,1,0:T(8,128)S(1)}, u32[]{:S(2)}, u32[]{:S(2)}) collective-permute-start(s32[2,136,128]{2,1,0:T(8,128)S(1)} %get-tuple-element.36), channel_id=1, source_target_pairs={{0,6},{1,7},{2,4},{3,5},{4,2},{5,3},{6,0},{7,1},{8,14},{9,15},{10,... | collective-permute-start | bytes 417800 | tf_op jit(solution)/shard_map/ppermute | solution.py:444
  46.8 13.7 %collective-permute-start.3 = (s32[2,136,128]{2,1,0:T(8,128)S(1)}, s32[2,136,128]{2,1,0:T(8,128)S(1)}, u32[]{:S(2)}, u32[]{:S(2)}) collective-permute-start(s32[2,136,128]{2,1,0:T(8,128)S(1)} %get-tuple-element.33.refs_0_), channel_id=1, source_target_pairs={{0,1},{1,0},{2,3},{3,2},{4,5},{5,4},{6,7},{7,6},{8,9},{9,8},{10,11... | collective-permute-start | bytes 417800 | tf_op jit(solution)/shard_map/ppermute | solution.py:450
  55.9 4.6 %collective-permute-start.4 = (s32[2,136,128]{2,1,0:T(8,128)S(1)}, s32[2,136,128]{2,1,0:T(8,128)S(1)}, u32[]{:S(2)}, u32[]{:S(2)}) collective-permute-start(s32[2,136,128]{2,1,0:T(8,128)S(1)} %collective-permute-done.refs_1_), channel_id=1, source_target_pairs={{0,1},{1,0},{2,3},{3,2},{4,5},{5,4},{6,7},{7,6},{8,9},{9,8},{10,11... | collective-permute-start | bytes 417800 | tf_op jit(solution)/shard_map/ppermute | solution.py:450
  55.9 4.6 %collective-permute-start.5 = (s32[2,136,128]{2,1,0:T(8,128)S(1)}, s32[2,136,128]{2,1,0:T(8,128)S(1)}, u32[]{:S(2)}, u32[]{:S(2)}) collective-permute-start(s32[2,136,128]{2,1,0:T(8,128)S(1)} %collective-permute-done.1.refs_2_), channel_id=1, source_target_pairs={{0,1},{1,0},{2,3},{3,2},{4,5},{5,4},{6,7},{7,6},{8,9},{9,8},{10,11... | collective-permute-start | bytes 417800 | tf_op jit(solution)/shard_map/ppermute | solution.py:450
  60.5 1.4 %collective-permute-start.6 = (s32[2,136,128]{2,1,0:T(8,128)S(1)}, s32[2,136,128]{2,1,0:T(8,128)S(1)}, u32[]{:S(2)}, u32[]{:S(2)}) collective-permute-start(s32[2,136,128]{2,1,0:T(8,128)S(1)} %collective-permute-done.2.refs_3_), channel_id=1, source_target_pairs={{0,1},{1,0},{2,3},{3,2},{4,5},{5,4},{6,7},{7,6},{8,9},{9,8},{10,11... | collective-permute-start | bytes 417800 | tf_op jit(solution)/shard_map/ppermute | solution.py:450
  70.1 10.2 %collective-permute-start.10 = (s32[2,136,128]{2,1,0:T(8,128)S(1)}, s32[2,136,128]{2,1,0:T(8,128)S(1)}, u32[]{:S(2)}, u32[]{:S(2)}) collective-permute-start(s32[2,136,128]{2,1,0:T(8,128)S(1)} %get-tuple-element.44), channel_id=1, source_target_pairs={{0,2},{1,3},{2,0},{3,1},{4,6},{5,7},{6,4},{7,5},{8,10},{9,11},{10,... | collective-permute-start | bytes 417800 | tf_op jit(solution)/shard_map/ppermute | solution.py:444
  71.5 8.8 %collective-permute-start.11 = (s32[2,136,128]{2,1,0:T(8,128)S(1)}, s32[2,136,128]{2,1,0:T(8,128)S(1)}, u32[]{:S(2)}, u32[]{:S(2)}) collective-permute-start(s32[2,136,128]{2,1,0:T(8,128)S(1)} %get-tuple-element.45), channel_id=1, source_target_pairs={{0,4},{1,5},{2,6},{3,7},{4,0},{5,1},{6,2},{7,3},{8,12},{9,13},{10,... | collective-permute-start | bytes 417800 | tf_op jit(solution)/shard_map/ppermute | solution.py:444
  72.6 7.7 %collective-permute-start.12 = (s32[2,136,128]{2,1,0:T(8,128)S(1)}, s32[2,136,128]{2,1,0:T(8,128)S(1)}, u32[]{:S(2)}, u32[]{:S(2)}) collective-permute-start(s32[2,136,128]{2,1,0:T(8,128)S(1)} %get-tuple-element.46), channel_id=1, source_target_pairs={{0,6},{1,7},{2,4},{3,5},{4,2},{5,3},{6,0},{7,1},{8,14},{9,15},{10,... | collective-permute-start | bytes 417800 | tf_op jit(solution)/shard_map/ppermute | solution.py:444
  73.7 5.6 %collective-permute-start.8 = (s32[136,128]{1,0:T(8,128)S(1)}, s32[136,128]{1,0:T(8,128)S(1)}, u32[]{:S(2)}, u32[]{:S(2)}) collective-permute-start(s32[136,128]{1,0:T(8,128)S(1)} %get-tuple-element.38), channel_id=1, source_target_pairs={{0,16},{8,24},{16,0},{24,8},{1,17},{9,25},{17,1},{25,9},{2,18},{10... | collective-permute-start | bytes 208904 | tf_op jit(solution)/shard_map/ppermute | solution.py:436
  75.4 4.9 %collective-permute-start.9 = (s32[136,128]{1,0:T(8,128)S(1)}, s32[136,128]{1,0:T(8,128)S(1)}, u32[]{:S(2)}, u32[]{:S(2)}) collective-permute-start(s32[136,128]{1,0:T(8,128)S(1)} %get-tuple-element.39), channel_id=1, source_target_pairs={{0,8},{8,0},{16,24},{24,16},{1,9},{9,1},{17,25},{25,17},{2,10},{10... | collective-permute-start | bytes 208904 | tf_op jit(solution)/shard_map/ppermute | solution.py:436
  80.3 3.7 %collective-permute-start.13 = (s32[2,136,128]{2,1,0:T(8,128)S(1)}, s32[2,136,128]{2,1,0:T(8,128)S(1)}, u32[]{:S(2)}, u32[]{:S(2)}) collective-permute-start(s32[2,136,128]{2,1,0:T(8,128)S(1)} %get-tuple-element.47.refs_0_), channel_id=1, source_target_pairs={{0,1},{1,0},{2,3},{3,2},{4,5},{5,4},{6,7},{7,6},{8,9},{9,8},{10,11... | collective-permute-start | bytes 417800 | tf_op jit(solution)/shard_map/ppermute | solution.py:450
  80.4 3.6 %collective-permute-start.14 = (s32[2,136,128]{2,1,0:T(8,128)S(1)}, s32[2,136,128]{2,1,0:T(8,128)S(1)}, u32[]{:S(2)}, u32[]{:S(2)}) collective-permute-start(s32[2,136,128]{2,1,0:T(8,128)S(1)} %collective-permute-done.10.refs_1_), channel_id=1, source_target_pairs={{0,1},{1,0},{2,3},{3,2},{4,5},{5,4},{6,7},{7,6},{8,9},{9,8},{10,11... | collective-permute-start | bytes 417800 | tf_op jit(solution)/shard_map/ppermute | solution.py:450
  80.9 3.1 %collective-permute-start.15 = (s32[2,136,128]{2,1,0:T(8,128)S(1)}, s32[2,136,128]{2,1,0:T(8,128)S(1)}, u32[]{:S(2)}, u32[]{:S(2)}) collective-permute-start(s32[2,136,128]{2,1,0:T(8,128)S(1)} %collective-permute-done.11.refs_2_), channel_id=1, source_target_pairs={{0,1},{1,0},{2,3},{3,2},{4,5},{5,4},{6,7},{7,6},{8,9},{9,8},{10,11... | collective-permute-start | bytes 417800 | tf_op jit(solution)/shard_map/ppermute | solution.py:450
  81.0 3.1 %collective-permute-start.16 = (s32[2,136,128]{2,1,0:T(8,128)S(1)}, s32[2,136,128]{2,1,0:T(8,128)S(1)}, u32[]{:S(2)}, u32[]{:S(2)}) collective-permute-start(s32[2,136,128]{2,1,0:T(8,128)S(1)} %collective-permute-done.12.refs_3_), channel_id=1, source_target_pairs={{0,1},{1,0},{2,3},{3,2},{4,5},{5,4},{6,7},{7,6},{8,9},{9,8},{10,11... | collective-permute-start | bytes 417800 | tf_op jit(solution)/shard_map/ppermute | solution.py:450
  81.4 12.9 %collective-permute-start.7 = (s32[136,128]{1,0:T(8,128)S(1)}, s32[136,128]{1,0:T(8,128)S(1)}, u32[]{:S(2)}, u32[]{:S(2)}) collective-permute-start(s32[136,128]{1,0:T(8,128)S(1)} %get-tuple-element.37), channel_id=1, source_target_pairs={{0,24},{8,16},{16,8},{24,0},{1,25},{9,17},{17,9},{25,1},{2,26},{10... | collective-permute-start | bytes 208904 | tf_op jit(solution)/shard_map/ppermute | solution.py:436
  89.9 7.0 %collective-permute-start.17 = (s32[136,128]{1,0:T(8,128)S(1)}, s32[136,128]{1,0:T(8,128)S(1)}, u32[]{:S(2)}, u32[]{:S(2)}) collective-permute-start(s32[136,128]{1,0:T(8,128)S(1)} %get-tuple-element.51), channel_id=1, source_target_pairs={{0,24},{8,16},{16,8},{24,0},{1,25},{9,17},{17,9},{25,1},{2,26},{10... | collective-permute-start | bytes 208904 | tf_op jit(solution)/shard_map/ppermute | solution.py:436
  91.2 7.5 %collective-permute-start.18 = (s32[136,128]{1,0:T(8,128)S(1)}, s32[136,128]{1,0:T(8,128)S(1)}, u32[]{:S(2)}, u32[]{:S(2)}) collective-permute-start(s32[136,128]{1,0:T(8,128)S(1)} %get-tuple-element.52), channel_id=1, source_target_pairs={{0,16},{8,24},{16,0},{24,8},{1,17},{9,25},{17,1},{25,9},{2,18},{10... | collective-permute-start | bytes 208904 | tf_op jit(solution)/shard_map/ppermute | solution.py:436
  91.8 6.9 %collective-permute-start.19 = (s32[136,128]{1,0:T(8,128)S(1)}, s32[136,128]{1,0:T(8,128)S(1)}, u32[]{:S(2)}, u32[]{:S(2)}) collective-permute-start(s32[136,128]{1,0:T(8,128)S(1)} %get-tuple-element.53), channel_id=1, source_target_pairs={{0,8},{8,0},{16,24},{24,16},{1,9},{9,1},{17,25},{25,17},{2,10},{10... | collective-permute-start | bytes 208904 | tf_op jit(solution)/shard_map/ppermute | solution.py:436

commit v13 on v12

--- a/solution.py
+++ b/solution.py
@@ -482,7 +482,7 @@
             got, _ = lax.optimization_barrier((got, lags))
         spec = got.reshape(n_seg, n_pair * tiles, 2, rows, TILE)
         stack = stacks(me, table, spec, n_seg, n_pair, most)
-        blocks = exchange_plane(stack, n_pair, done[2:0:-1] or None)
+        blocks = exchange_plane(stack, n_pair, done[:1:-1] or None)
         lags = dft(me, tables, blocks, freq, n_seg, n_pair, most)
         done = exchange(lags, "seg", n_seg)
         parts += done[::-1]

time: 103 us -> 104 us (level)
  waiting for transfers between devices: 30.9 us -> 35.5 us
  starting transfers between devices: 31.1 us -> 27.9 us
    ppermute x6, waiting for transfers between devices: 6.63 us -> 10.2 us  [exchange(): lax.ppermute(blocks[k], axis, [(i, i ^ k) for i in range(size)])]
    ppermute x6, starting transfers between devices: 11.4 us -> 8.25 us  [exchange(): lax.ppermute(blocks[k], axis, [(i, i ^ k) for i in range(size)])]
  transfers between devices with their start and end apart: 22 -> 22, of which waited for: 8 -> 12; matrix products, arithmetic and copies ran while one was open for 1% -> 1% of each run, Pallas kernels for 19% -> 19%
where the time goes in v13:
time: 104 us
  waiting for transfers between devices  35.5 us (34%)
  Pallas kernels  29.4 us (28%)
  starting transfers between devices  27.9 us (27%)
  blocking collectives  8.35 us (8%)
  between operations  1.36 us (1%)
  local copies, waits for them, and re-layouts  1.09 us (1%)
    ppermute x6, waiting for transfers between devices, exchange_plane(): lax.ppermute(blocks[k], 'pair', [(i, i ^ 2 * k) for i in range(n_pair)])  13.1 us
    pallas_call x2, Pallas kernels, dft(): pl.pallas_call(functools.partial(dft_kernel, n_seg, n_pair, most), out_sh...  11.6 us
    all_to_all x2, starting transfers between devices, body(): lax.all_to_all(sent.reshape(n_seg * n_pair, tiles, 2, rows, TILE), ('seg'...  10.9 us
    ppermute x6, waiting for transfers between devices, exchange(): lax.ppermute(blocks[k], axis, [(i, i ^ k) for i in range(size)])  10.2 us
    all_to_all x2, waiting for transfers between devices, body(): lax.all_to_all(sent.reshape(n_seg * n_pair, tiles, 2, rows, TILE), ('seg'...  9.73 us
    unnamed x1, blocking collectives  8.35 us
    ppermute x6, starting transfers between devices, exchange(): lax.ppermute(blocks[k], axis, [(i, i ^ k) for i in range(size)])  8.25 us
    pallas_call x2, Pallas kernels, pack(): pl.pallas_call(functools.partial(pack_kernel, n_seg, chunk), out_shape=ja...  7.36 us
  transfers between devices with their start and end apart: 22, of which 12 were waited for; matrix products, arithmetic and copies ran while one was open for 1% of the time, Pallas kernels for 19%

profile of v13, /device:TPU:0, one launch (start us, length us, event | category | flops | bytes accessed | tf_op | source)
XLA Modules:
  0.0 103.8 jit_solution(13509351945676639982)
XLA Ops:
  0.0 3.7 %pack.3 = bf16[4,8,2,2,32,128]{5,4,3,2,1,0:T(8,128)(2,1)} custom-call(bf16[2,2048,256]{2,1,0:T(8,128)(2,1)} %bitcast.11), custom_call_target="tpu_custom_call" | custom-call | flops 1 | bytes 1 | tf_op jit(solution)/shard_map/pack/pallas_call | solution.py:131
  3.7 7.3 %all-to-all-start = ((bf16[32,2,2,32,128]{4,3,2,1,0:T(8,128)(2,1)}), bf16[32,2,2,32,128]{4,3,2,1,0:T(8,128)(2,1)S(1)}, u32[]{:S(2)}, u32[]{:S(2)}) async-start(bf16[32,2,2,32,128]{4,3,2,1,0:T(8,128)(2,1)} %bitcast.14), calls=%async_computation | async-start | bytes 2097152 | tf_op jit(solution)/shard_map/all_to_all | solution.py:474
  11.1 3.6 %pack.2 = bf16[4,8,2,2,32,128]{5,4,3,2,1,0:T(8,128)(2,1)} custom-call(bf16[2,2048,256]{2,1,0:T(8,128)(2,1)} %bitcast.12), custom_call_target="tpu_custom_call" | custom-call | flops 1 | bytes 1 | tf_op jit(solution)/shard_map/pack/pallas_call | solution.py:131
  14.7 2.1 %sums.1.tables_ref = bf16[98304,256]{1,0:T(8,128)(2,1)} custom-call(), custom_call_target="tpu_custom_call" | custom-call | flops 1 | bytes 1 | tf_op jit(solution)/shard_map/sums/pallas_call | solution.py:328
  17.7 0.6 dynamic-slice
  19.1 8.4 %all-reduce = s32[72]{0:T(128)S(1)} all-reduce(s32[72]{0:T(128)S(1)} %dynamic-update-slice), channel_id=2, replica_groups=mesh['seg'=4,'pair'=8] {'pair'}, use_global_device_ids=true, to_apply=%add | all-reduce | flops 72 | bytes 576
  27.6 9.7 %all-to-all-done = bf16[32,2,2,32,128]{4,3,2,1,0:T(8,128)(2,1)S(1)} async-done(((bf16[32,2,2,32,128]{4,3,2,1,0:T(8,128)(2,1)}), bf16[32,2,2,32,128]{4,3,2,1,0:T(8,128)(2,1)S(1)}, u32[]{:S(2)}, u32[]{:S(2)}) %all-to-all-start) | async-done | bytes 1048608 | tf_op jit(solution)/shard_map/all_to_all | solution.py:474
  37.3 3.6 %all-to-all-start.1 = ((bf16[32,2,2,32,128]{4,3,2,1,0:T(8,128)(2,1)}), bf16[32,2,2,32,128]{4,3,2,1,0:T(8,128)(2,1)S(1)}, u32[]{:S(2)}, u32[]{:S(2)}) async-start(bf16[32,2,2,32,128]{4,3,2,1,0:T(8,128)(2,1)} %bitcast.13), calls=%async_computation.1 | async-start | bytes 2097152 | tf_op jit(solution)/shard_map/all_to_all | solution.py:474
  41.0 2.3 %stack.14 = (s32[2,136,128]{2,1,0:T(8,128)S(1)}, s32[2,136,128]{2,1,0:T(8,128)S(1)}, s32[2,136,128]{2,1,0:T(8,128)S(1)}, s32[2,136,128]{2,1,0:T(8,128)S(1)}) custom-call(s32[2]{0:T(128)S(1)} %pad_add_fusion.me_ref, s32[8,9]{1,0:T(8,128)S(1)} %reshape.28.table_ref, bf16[4,16,2,32,128]{4,3,2,1,0:T(8,128)(2,1)S(1)} %bitcast.10), custom_call_target="tpu_custom_call" | custom-call | flops 1 | bytes 1 | tf_op jit(solution)/shard_map/stack/pallas_call | solution.py:205
  43.3 1.8 %collective-permute-start = (s32[2,136,128]{2,1,0:T(8,128)S(1)}, s32[2,136,128]{2,1,0:T(8,128)S(1)}, u32[]{:S(2)}, u32[]{:S(2)}) collective-permute-start(s32[2,136,128]{2,1,0:T(8,128)S(1)} %get-tuple-element.34), channel_id=1, source_target_pairs={{0,2},{1,3},{2,0},{3,1},{4,6},{5,7},{6,4},{7,5},{8,10},{9,11},{10,... | collective-permute-start | bytes 417800 | tf_op jit(solution)/shard_map/ppermute | solution.py:444
  45.2 1.5 %collective-permute-start.1 = (s32[2,136,128]{2,1,0:T(8,128)S(1)}, s32[2,136,128]{2,1,0:T(8,128)S(1)}, u32[]{:S(2)}, u32[]{:S(2)}) collective-permute-start(s32[2,136,128]{2,1,0:T(8,128)S(1)} %get-tuple-element.35), channel_id=1, source_target_pairs={{0,4},{1,5},{2,6},{3,7},{4,0},{5,1},{6,2},{7,3},{8,12},{9,13},{10,... | collective-permute-start | bytes 417800 | tf_op jit(solution)/shard_map/ppermute | solution.py:444
  46.9 9.0 %collective-permute-done.refs_1_ = s32[2,136,128]{2,1,0:T(8,128)S(1)} collective-permute-done((s32[2,136,128]{2,1,0:T(8,128)S(1)}, s32[2,136,128]{2,1,0:T(8,128)S(1)}, u32[]{:S(2)}, u32[]{:S(2)}) %collective-permute-start) | collective-permute-done | bytes 139296 | tf_op jit(solution)/shard_map/ppermute | solution.py:444
  55.9 0.5 collective-permute-start.5
  56.4 4.1 %collective-permute-done.2.refs_3_ = s32[2,136,128]{2,1,0:T(8,128)S(1)} collective-permute-done((s32[2,136,128]{2,1,0:T(8,128)S(1)}, s32[2,136,128]{2,1,0:T(8,128)S(1)}, u32[]{:S(2)}, u32[]{:S(2)}) %collective-permute-start.2) | collective-permute-done | bytes 139296 | tf_op jit(solution)/shard_map/ppermute | solution.py:444
  60.5 1.3 %collective-permute-done.6.refs_7_ = s32[2,136,128]{2,1,0:T(8,128)S(1)} collective-permute-done((s32[2,136,128]{2,1,0:T(8,128)S(1)}, s32[2,136,128]{2,1,0:T(8,128)S(1)}, u32[]{:S(2)}, u32[]{:S(2)}) %collective-permute-start.6) | collective-permute-done | bytes 139296 | tf_op jit(solution)/shard_map/ppermute | solution.py:450
  61.9 5.8 %dft.2 = (s32[136,128]{1,0:T(8,128)S(1)}, s32[136,128]{1,0:T(8,128)S(1)}, s32[136,128]{1,0:T(8,128)S(1)}, s32[136,128]{1,0:T(8,128)S(1)}) custom-call(s32[2]{0:T(128)S(1)} %pad_add_fusion.me_ref, bf16[1024,512]{1,0:T(8,128)(2,1)S(1)} %copy-done, f32[72,256]{1,0:T(8,128)S(1)} %copy-done.1, bf16[98304,256]{1,0:T(8,128)(2,1)} %sums.1.tables_ref, ...), custom_call_target="tpu_custom_call" | custom-call | flops 1 | bytes 1 | tf_op jit(solution)/shard_map/dft/pallas_call | solution.py:365
  67.7 2.5 %stack.15 = (s32[2,136,128]{2,1,0:T(8,128)S(1)}, s32[2,136,128]{2,1,0:T(8,128)S(1)}, s32[2,136,128]{2,1,0:T(8,128)S(1)}, s32[2,136,128]{2,1,0:T(8,128)S(1)}) custom-call(s32[2]{0:T(128)S(1)} %pad_add_fusion.me_ref, s32[8,9]{1,0:T(8,128)S(1)} %reshape.28.table_ref, bf16[4,16,2,32,128]{4,3,2,1,0:T(8,128)(2,1)S(1)} %bitcast.9), custom_call_target="tpu_custom_call" | custom-call | flops 1 | bytes 1 | tf_op jit(solution)/shard_map/stack/pallas_call | solution.py:205
  70.2 1.4 %collective-permute-start.10 = (s32[2,136,128]{2,1,0:T(8,128)S(1)}, s32[2,136,128]{2,1,0:T(8,128)S(1)}, u32[]{:S(2)}, u32[]{:S(2)}) collective-permute-start(s32[2,136,128]{2,1,0:T(8,128)S(1)} %get-tuple-element.44), channel_id=1, source_target_pairs={{0,2},{1,3},{2,0},{3,1},{4,6},{5,7},{6,4},{7,5},{8,10},{9,11},{10,... | collective-permute-start | bytes 417800 | tf_op jit(solution)/shard_map/ppermute | solution.py:444
  71.6 1.1 %collective-permute-start.11 = (s32[2,136,128]{2,1,0:T(8,128)S(1)}, s32[2,136,128]{2,1,0:T(8,128)S(1)}, u32[]{:S(2)}, u32[]{:S(2)}) collective-permute-start(s32[2,136,128]{2,1,0:T(8,128)S(1)} %get-tuple-element.45), channel_id=1, source_target_pairs={{0,4},{1,5},{2,6},{3,7},{4,0},{5,1},{6,2},{7,3},{8,12},{9,13},{10,... | collective-permute-start | bytes 417800 | tf_op jit(solution)/shard_map/ppermute | solution.py:444
  72.7 1.1 %collective-permute-start.12 = (s32[2,136,128]{2,1,0:T(8,128)S(1)}, s32[2,136,128]{2,1,0:T(8,128)S(1)}, u32[]{:S(2)}, u32[]{:S(2)}) collective-permute-start(s32[2,136,128]{2,1,0:T(8,128)S(1)} %get-tuple-element.46), channel_id=1, source_target_pairs={{0,6},{1,7},{2,4},{3,5},{4,2},{5,3},{6,0},{7,1},{8,14},{9,15},{10,... | collective-permute-start | bytes 417800 | tf_op jit(solution)/shard_map/ppermute | solution.py:444
  73.8 3.8 %collective-permute-start.7 = (s32[136,128]{1,0:T(8,128)S(1)}, s32[136,128]{1,0:T(8,128)S(1)}, u32[]{:S(2)}, u32[]{:S(2)}) collective-permute-start(s32[136,128]{1,0:T(8,128)S(1)} %get-tuple-element.37), channel_id=1, source_target_pairs={{0,24},{8,16},{16,8},{24,0},{1,25},{9,17},{17,9},{25,1},{2,26},{10... | collective-permute-start | bytes 208904 | tf_op jit(solution)/shard_map/ppermute | solution.py:436
  77.6 2.5 %collective-permute-done.7.refs_0_ = s32[136,128]{1,0:T(8,128)S(1)} collective-permute-done((s32[136,128]{1,0:T(8,128)S(1)}, s32[136,128]{1,0:T(8,128)S(1)}, u32[]{:S(2)}, u32[]{:S(2)}) %collective-permute-start.7) | collective-permute-done | bytes 69664 | tf_op jit(solution)/shard_map/ppermute | solution.py:436
  80.1 2.9 %collective-permute-done.8.refs_1_ = s32[136,128]{1,0:T(8,128)S(1)} collective-permute-done((s32[136,128]{1,0:T(8,128)S(1)}, s32[136,128]{1,0:T(8,128)S(1)}, u32[]{:S(2)}, u32[]{:S(2)}) %collective-permute-start.8) | collective-permute-done | bytes 69664 | tf_op jit(solution)/shard_map/ppermute | solution.py:436
  83.0 0.5 collective-permute-start.14
  83.6 0.4 collective-permute-start.16
  84.0 0.3 collective-permute-done.13.refs_4_
  85.1 5.8 %dft.3 = (s32[136,128]{1,0:T(8,128)S(1)}, s32[136,128]{1,0:T(8,128)S(1)}, s32[136,128]{1,0:T(8,128)S(1)}, s32[136,128]{1,0:T(8,128)S(1)}) custom-call(s32[2]{0:T(128)S(1)} %pad_add_fusion.me_ref, bf16[1024,512]{1,0:T(8,128)(2,1)S(1)} %copy-done, f32[72,256]{1,0:T(8,128)S(1)} %copy-done.1, bf16[98304,256]{1,0:T(8,128)(2,1)} %sums.1.tables_ref, ...), custom_call_target="tpu_custom_call" | custom-call | flops 1 | bytes 1 | tf_op jit(solution)/shard_map/dft/pallas_call | solution.py:365
  90.9 2.3 %collective-permute-start.17 = (s32[136,128]{1,0:T(8,128)S(1)}, s32[136,128]{1,0:T(8,128)S(1)}, u32[]{:S(2)}, u32[]{:S(2)}) collective-permute-start(s32[136,128]{1,0:T(8,128)S(1)} %get-tuple-element.51), channel_id=1, source_target_pairs={{0,24},{8,16},{16,8},{24,0},{1,25},{9,17},{17,9},{25,1},{2,26},{10... | collective-permute-start | bytes 208904 | tf_op jit(solution)/shard_map/ppermute | solution.py:436
  93.4 1.9 %collective-permute-start.19 = (s32[136,128]{1,0:T(8,128)S(1)}, s32[136,128]{1,0:T(8,128)S(1)}, u32[]{:S(2)}, u32[]{:S(2)}) collective-permute-start(s32[136,128]{1,0:T(8,128)S(1)} %get-tuple-element.53), channel_id=1, source_target_pairs={{0,8},{8,0},{16,24},{24,16},{1,9},{9,1},{17,25},{25,17},{2,10},{10... | collective-permute-start | bytes 208904 | tf_op jit(solution)/shard_map/ppermute | solution.py:436
  95.4 2.5 %collective-permute-done.17.refs_4_ = s32[136,128]{1,0:T(8,128)S(1)} collective-permute-done((s32[136,128]{1,0:T(8,128)S(1)}, s32[136,128]{1,0:T(8,128)S(1)}, u32[]{:S(2)}, u32[]{:S(2)}) %collective-permute-start.17) | collective-permute-done | bytes 69664 | tf_op jit(solution)/shard_map/ppermute | solution.py:436
  97.9 2.3 %collective-permute-done.18.refs_5_ = s32[136,128]{1,0:T(8,128)S(1)} collective-permute-done((s32[136,128]{1,0:T(8,128)S(1)}, s32[136,128]{1,0:T(8,128)S(1)}, u32[]{:S(2)}, u32[]{:S(2)}) %collective-permute-start.18) | collective-permute-done | bytes 69664 | tf_op jit(solution)/shard_map/ppermute | solution.py:436
  100.2 3.6 %unpack.1 = f32[2,256,4,128]{3,2,1,0:T(4,128)} custom-call(s32[2]{0:T(128)S(1)} %pad_add_fusion.me_ref, s32[136,128]{1,0:T(8,128)S(1)} %collective-permute-done.7.refs_0_, s32[136,128]{1,0:T(8,128)S(1)} %collective-permute-done.8.refs_1_, s32[136,128]{1,0:T(8,128)S(1)} %collective-permute-done.9.refs_2_, s32[136,128]{1,0:T(8,128)S(1)} %get-tuple-element.40.refs_3_, ...), custom_call_target="tpu_custom_call" | custom-call | flops 1 | bytes 1 | tf_op jit(solution)/shard_map/unpack/pallas_call | solution.py:420
  (37 shorter events, 2.0 us)
Async XLA Ops:
  0.0 17.7 %copy-start.3 = (u32[32]{0:T(128)S(1)}, u32[32]{0:T(128)}, u32[]{:S(2)}) copy-start(u32[32]{0:T(128)} %constant.19) | copy-start | bytes 388
  0.0 61.9 %copy-start.1 = (f32[72,256]{1,0:T(8,128)S(1)}, f32[72,256]{1,0:T(8,128)}, u32[]{:S(2)}) copy-start(f32[72,256]{1,0:T(8,128)} %constant.13.clone.phase_ref) | copy-start | bytes 221188
  0.0 61.9 %copy-start = (bf16[1024,512]{1,0:T(8,128)(2,1)S(1)}, bf16[1024,512]{1,0:T(8,128)(2,1)}, u32[]{:S(2)}) copy-start(bf16[1024,512]{1,0:T(8,128)(2,1)} %constant.12.clone.w_ref) | copy-start | bytes 3145732
  0.0 17.5 %copy-start.2 = (s32[4,2]{0,1:T(2,128)S(1)}, s32[4,2]{0,1:T(2,128)}, u32[]{:S(2)}) copy-start(s32[4,2]{0,1:T(2,128)} %param.6) | copy-start | bytes 100
  3.7 33.6 %all-to-all-start = ((bf16[32,2,2,32,128]{4,3,2,1,0:T(8,128)(2,1)}), bf16[32,2,2,32,128]{4,3,2,1,0:T(8,128)(2,1)S(1)}, u32[]{:S(2)}, u32[]{:S(2)}) async-start(bf16[32,2,2,32,128]{4,3,2,1,0:T(8,128)(2,1)} %bitcast.14), calls=%async_computation | async-start | bytes 2097152 | tf_op jit(solution)/shard_map/all_to_all | solution.py:474
  37.3 30.4 %all-to-all-start.1 = ((bf16[32,2,2,32,128]{4,3,2,1,0:T(8,128)(2,1)}), bf16[32,2,2,32,128]{4,3,2,1,0:T(8,128)(2,1)S(1)}, u32[]{:S(2)}, u32[]{:S(2)}) async-start(bf16[32,2,2,32,128]{4,3,2,1,0:T(8,128)(2,1)} %bitcast.13), calls=%async_computation.1 | async-start | bytes 2097152 | tf_op jit(solution)/shard_map/all_to_all | solution.py:474
  43.3 12.6 %collective-permute-start = (s32[2,136,128]{2,1,0:T(8,128)S(1)}, s32[2,136,128]{2,1,0:T(8,128)S(1)}, u32[]{:S(2)}, u32[]{:S(2)}) collective-permute-start(s32[2,136,128]{2,1,0:T(8,128)S(1)} %get-tuple-element.34), channel_id=1, source_target_pairs={{0,2},{1,3},{2,0},{3,1},{4,6},{5,7},{6,4},{7,5},{8,10},{9,11},{10,... | collective-permute-start | bytes 417800 | tf_op jit(solution)/shard_map/ppermute | solution.py:444
  45.2 10.7 %collective-permute-start.1 = (s32[2,136,128]{2,1,0:T(8,128)S(1)}, s32[2,136,128]{2,1,0:T(8,128)S(1)}, u32[]{:S(2)}, u32[]{:S(2)}) collective-permute-start(s32[2,136,128]{2,1,0:T(8,128)S(1)} %get-tuple-element.35), channel_id=1, source_target_pairs={{0,4},{1,5},{2,6},{3,7},{4,0},{5,1},{6,2},{7,3},{8,12},{9,13},{10,... | collective-permute-start | bytes 417800 | tf_op jit(solution)/shard_map/ppermute | solution.py:444
  46.6 13.9 %collective-permute-start.2 = (s32[2,136,128]{2,1,0:T(8,128)S(1)}, s32[2,136,128]{2,1,0:T(8,128)S(1)}, u32[]{:S(2)}, u32[]{:S(2)}) collective-permute-start(s32[2,136,128]{2,1,0:T(8,128)S(1)} %get-tuple-element.36), channel_id=1, source_target_pairs={{0,6},{1,7},{2,4},{3,5},{4,2},{5,3},{6,0},{7,1},{8,14},{9,15},{10,... | collective-permute-start | bytes 417800 | tf_op jit(solution)/shard_map/ppermute | solution.py:444
  46.9 13.6 %collective-permute-start.3 = (s32[2,136,128]{2,1,0:T(8,128)S(1)}, s32[2,136,128]{2,1,0:T(8,128)S(1)}, u32[]{:S(2)}, u32[]{:S(2)}) collective-permute-start(s32[2,136,128]{2,1,0:T(8,128)S(1)} %get-tuple-element.33.refs_0_), channel_id=1, source_target_pairs={{0,1},{1,0},{2,3},{3,2},{4,5},{5,4},{6,7},{7,6},{8,9},{9,8},{10,11... | collective-permute-start | bytes 417800 | tf_op jit(solution)/shard_map/ppermute | solution.py:450
  55.9 4.6 %collective-permute-start.4 = (s32[2,136,128]{2,1,0:T(8,128)S(1)}, s32[2,136,128]{2,1,0:T(8,128)S(1)}, u32[]{:S(2)}, u32[]{:S(2)}) collective-permute-start(s32[2,136,128]{2,1,0:T(8,128)S(1)} %collective-permute-done.refs_1_), channel_id=1, source_target_pairs={{0,1},{1,0},{2,3},{3,2},{4,5},{5,4},{6,7},{7,6},{8,9},{9,8},{10,11... | collective-permute-start | bytes 417800 | tf_op jit(solution)/shard_map/ppermute | solution.py:450
  55.9 4.6 %collective-permute-start.5 = (s32[2,136,128]{2,1,0:T(8,128)S(1)}, s32[2,136,128]{2,1,0:T(8,128)S(1)}, u32[]{:S(2)}, u32[]{:S(2)}) collective-permute-start(s32[2,136,128]{2,1,0:T(8,128)S(1)} %collective-permute-done.1.refs_2_), channel_id=1, source_target_pairs={{0,1},{1,0},{2,3},{3,2},{4,5},{5,4},{6,7},{7,6},{8,9},{9,8},{10,11... | collective-permute-start | bytes 417800 | tf_op jit(solution)/shard_map/ppermute | solution.py:450
  60.5 1.4 %collective-permute-start.6 = (s32[2,136,128]{2,1,0:T(8,128)S(1)}, s32[2,136,128]{2,1,0:T(8,128)S(1)}, u32[]{:S(2)}, u32[]{:S(2)}) collective-permute-start(s32[2,136,128]{2,1,0:T(8,128)S(1)} %collective-permute-done.2.refs_3_), channel_id=1, source_target_pairs={{0,1},{1,0},{2,3},{3,2},{4,5},{5,4},{6,7},{7,6},{8,9},{9,8},{10,11... | collective-permute-start | bytes 417800 | tf_op jit(solution)/shard_map/ppermute | solution.py:450
  70.2 12.7 %collective-permute-start.10 = (s32[2,136,128]{2,1,0:T(8,128)S(1)}, s32[2,136,128]{2,1,0:T(8,128)S(1)}, u32[]{:S(2)}, u32[]{:S(2)}) collective-permute-start(s32[2,136,128]{2,1,0:T(8,128)S(1)} %get-tuple-element.44), channel_id=1, source_target_pairs={{0,2},{1,3},{2,0},{3,1},{4,6},{5,7},{6,4},{7,5},{8,10},{9,11},{10,... | collective-permute-start | bytes 417800 | tf_op jit(solution)/shard_map/ppermute | solution.py:444
  71.6 11.4 %collective-permute-start.11 = (s32[2,136,128]{2,1,0:T(8,128)S(1)}, s32[2,136,128]{2,1,0:T(8,128)S(1)}, u32[]{:S(2)}, u32[]{:S(2)}) collective-permute-start(s32[2,136,128]{2,1,0:T(8,128)S(1)} %get-tuple-element.45), channel_id=1, source_target_pairs={{0,4},{1,5},{2,6},{3,7},{4,0},{5,1},{6,2},{7,3},{8,12},{9,13},{10,... | collective-permute-start | bytes 417800 | tf_op jit(solution)/shard_map/ppermute | solution.py:444
  72.7 10.3 %collective-permute-start.12 = (s32[2,136,128]{2,1,0:T(8,128)S(1)}, s32[2,136,128]{2,1,0:T(8,128)S(1)}, u32[]{:S(2)}, u32[]{:S(2)}) collective-permute-start(s32[2,136,128]{2,1,0:T(8,128)S(1)} %get-tuple-element.46), channel_id=1, source_target_pairs={{0,6},{1,7},{2,4},{3,5},{4,2},{5,3},{6,0},{7,1},{8,14},{9,15},{10,... | collective-permute-start | bytes 417800 | tf_op jit(solution)/shard_map/ppermute | solution.py:444
  73.8 6.3 %collective-permute-start.7 = (s32[136,128]{1,0:T(8,128)S(1)}, s32[136,128]{1,0:T(8,128)S(1)}, u32[]{:S(2)}, u32[]{:S(2)}) collective-permute-start(s32[136,128]{1,0:T(8,128)S(1)} %get-tuple-element.37), channel_id=1, source_target_pairs={{0,24},{8,16},{16,8},{24,0},{1,25},{9,17},{17,9},{25,1},{2,26},{10... | collective-permute-start | bytes 208904 | tf_op jit(solution)/shard_map/ppermute | solution.py:436
  77.6 5.4 %collective-permute-start.8 = (s32[136,128]{1,0:T(8,128)S(1)}, s32[136,128]{1,0:T(8,128)S(1)}, u32[]{:S(2)}, u32[]{:S(2)}) collective-permute-start(s32[136,128]{1,0:T(8,128)S(1)} %get-tuple-element.38), channel_id=1, source_target_pairs={{0,16},{8,24},{16,0},{24,8},{1,17},{9,25},{17,1},{25,9},{2,18},{10... | collective-permute-start | bytes 208904 | tf_op jit(solution)/shard_map/ppermute | solution.py:436
  83.0 1.4 %collective-permute-start.13 = (s32[2,136,128]{2,1,0:T(8,128)S(1)}, s32[2,136,128]{2,1,0:T(8,128)S(1)}, u32[]{:S(2)}, u32[]{:S(2)}) collective-permute-start(s32[2,136,128]{2,1,0:T(8,128)S(1)} %get-tuple-element.47.refs_0_), channel_id=1, source_target_pairs={{0,1},{1,0},{2,3},{3,2},{4,5},{5,4},{6,7},{7,6},{8,9},{9,8},{10,11... | collective-permute-start | bytes 417800 | tf_op jit(solution)/shard_map/ppermute | solution.py:450
  83.0 1.5 %collective-permute-start.14 = (s32[2,136,128]{2,1,0:T(8,128)S(1)}, s32[2,136,128]{2,1,0:T(8,128)S(1)}, u32[]{:S(2)}, u32[]{:S(2)}) collective-permute-start(s32[2,136,128]{2,1,0:T(8,128)S(1)} %collective-permute-done.10.refs_1_), channel_id=1, source_target_pairs={{0,1},{1,0},{2,3},{3,2},{4,5},{5,4},{6,7},{7,6},{8,9},{9,8},{10,11... | collective-permute-start | bytes 417800 | tf_op jit(solution)/shard_map/ppermute | solution.py:450
  83.5 1.4 %collective-permute-start.15 = (s32[2,136,128]{2,1,0:T(8,128)S(1)}, s32[2,136,128]{2,1,0:T(8,128)S(1)}, u32[]{:S(2)}, u32[]{:S(2)}) collective-permute-start(s32[2,136,128]{2,1,0:T(8,128)S(1)} %collective-permute-done.11.refs_2_), channel_id=1, source_target_pairs={{0,1},{1,0},{2,3},{3,2},{4,5},{5,4},{6,7},{7,6},{8,9},{9,8},{10,11... | collective-permute-start | bytes 417800 | tf_op jit(solution)/shard_map/ppermute | solution.py:450
  83.6 1.5 %collective-permute-start.16 = (s32[2,136,128]{2,1,0:T(8,128)S(1)}, s32[2,136,128]{2,1,0:T(8,128)S(1)}, u32[]{:S(2)}, u32[]{:S(2)}) collective-permute-start(s32[2,136,128]{2,1,0:T(8,128)S(1)} %collective-permute-done.12.refs_3_), channel_id=1, source_target_pairs={{0,1},{1,0},{2,3},{3,2},{4,5},{5,4},{6,7},{7,6},{8,9},{9,8},{10,11... | collective-permute-start | bytes 417800 | tf_op jit(solution)/shard_map/ppermute | solution.py:450
  84.0 11.3 %collective-permute-start.9 = (s32[136,128]{1,0:T(8,128)S(1)}, s32[136,128]{1,0:T(8,128)S(1)}, u32[]{:S(2)}, u32[]{:S(2)}) collective-permute-start(s32[136,128]{1,0:T(8,128)S(1)} %get-tuple-element.39), channel_id=1, source_target_pairs={{0,8},{8,0},{16,24},{24,16},{1,9},{9,1},{17,25},{25,17},{2,10},{10... | collective-permute-start | bytes 208904 | tf_op jit(solution)/shard_map/ppermute | solution.py:436
  90.9 7.0 %collective-permute-start.17 = (s32[136,128]{1,0:T(8,128)S(1)}, s32[136,128]{1,0:T(8,128)S(1)}, u32[]{:S(2)}, u32[]{:S(2)}) collective-permute-start(s32[136,128]{1,0:T(8,128)S(1)} %get-tuple-element.51), channel_id=1, source_target_pairs={{0,24},{8,16},{16,8},{24,0},{1,25},{9,17},{17,9},{25,1},{2,26},{10... | collective-permute-start | bytes 208904 | tf_op jit(solution)/shard_map/ppermute | solution.py:436
  93.2 7.0 %collective-permute-start.18 = (s32[136,128]{1,0:T(8,128)S(1)}, s32[136,128]{1,0:T(8,128)S(1)}, u32[]{:S(2)}, u32[]{:S(2)}) collective-permute-start(s32[136,128]{1,0:T(8,128)S(1)} %get-tuple-element.52), channel_id=1, source_target_pairs={{0,16},{8,24},{16,0},{24,8},{1,17},{9,25},{17,1},{25,9},{2,18},{10... | collective-permute-start | bytes 208904 | tf_op jit(solution)/shard_map/ppermute | solution.py:436
  93.4 6.8 %collective-permute-start.19 = (s32[136,128]{1,0:T(8,128)S(1)}, s32[136,128]{1,0:T(8,128)S(1)}, u32[]{:S(2)}, u32[]{:S(2)}) collective-permute-start(s32[136,128]{1,0:T(8,128)S(1)} %get-tuple-element.53), channel_id=1, source_target_pairs={{0,8},{8,0},{16,24},{24,16},{1,9},{9,1},{17,25},{25,17},{2,10},{10... | collective-permute-start | bytes 208904 | tf_op jit(solution)/shard_map/ppermute | solution.py:436

commit v14 on v12

--- a/solution.py
+++ b/solution.py
@@ -445,7 +445,8 @@
         for k in range(1, n_pair // 2)
     ]
     if between is not None:
-        direct, _ = lax.optimization_barrier((direct, between))
+        far, _ = lax.optimization_barrier((direct[1:], between))
+        direct = [direct[0]] + list(far)
     swap = [(i, i ^ 1) for i in range(n_pair)]
     return direct + [lax.ppermute(d, "pair", swap) for d in direct]
 

time: 103 us -> 103 us (level)
  no operation moved by 1% of the time
where the time goes in v14:
time: 103 us; the launch traced here: 102 us
  starting transfers between devices  30.9 us (30%)
  waiting for transfers between devices  30.9 us (30%)
  Pallas kernels  29.4 us (29%)
  blocking collectives  8.35 us (8%)
  between operations  1.37 us (1%)
  local copies, waits for them, and re-layouts  1.09 us (1%)
    ppermute x6, waiting for transfers between devices, exchange_plane(): lax.ppermute(blocks[k], 'pair', [(i, i ^ 2 * k) for i in range(n_pair)])  13.1 us
    ppermute x6, starting transfers between devices, exchange(): lax.ppermute(blocks[k], axis, [(i, i ^ k) for i in range(size)])  11.7 us
    pallas_call x2, Pallas kernels, dft(): pl.pallas_call(functools.partial(dft_kernel, n_seg, n_pair, most), out_sh...  11.6 us
    all_to_all x2, starting transfers between devices, body(): lax.all_to_all(sent.reshape(n_seg * n_pair, tiles, 2, rows, TILE), ('seg'...  10.9 us
    all_to_all x2, waiting for transfers between devices, body(): lax.all_to_all(sent.reshape(n_seg * n_pair, tiles, 2, rows, TILE), ('seg'...  9.73 us
    unnamed x1, blocking collectives  8.35 us
    pallas_call x2, Pallas kernels, pack(): pl.pallas_call(functools.partial(pack_kernel, n_seg, chunk), out_shape=ja...  7.36 us
    ppermute x6, starting transfers between devices, exchange_plane(): lax.ppermute(blocks[k], 'pair', [(i, i ^ 2 * k) for i in range(n_pair)])  7.11 us
  transfers between devices with their start and end apart: 22, of which 8 were waited for; matrix products, arithmetic and copies ran while one was open for 1% of the time, Pallas kernels for 19%

profile of v14, /device:TPU:0, one launch (start us, length us, event | category | flops | bytes accessed | tf_op | source)
XLA Modules:
  0.0 102.2 jit_solution(8032520230631773031)
XLA Ops:
  0.0 3.7 %pack.3 = bf16[4,8,2,2,32,128]{5,4,3,2,1,0:T(8,128)(2,1)} custom-call(bf16[2,2048,256]{2,1,0:T(8,128)(2,1)} %bitcast.11), custom_call_target="tpu_custom_call" | custom-call | flops 1 | bytes 1 | tf_op jit(solution)/shard_map/pack/pallas_call | solution.py:131
  3.7 7.3 %all-to-all-start = ((bf16[32,2,2,32,128]{4,3,2,1,0:T(8,128)(2,1)}), bf16[32,2,2,32,128]{4,3,2,1,0:T(8,128)(2,1)S(1)}, u32[]{:S(2)}, u32[]{:S(2)}) async-start(bf16[32,2,2,32,128]{4,3,2,1,0:T(8,128)(2,1)} %bitcast.14), calls=%async_computation | async-start | bytes 2097152 | tf_op jit(solution)/shard_map/all_to_all | solution.py:475
  11.1 3.6 %pack.2 = bf16[4,8,2,2,32,128]{5,4,3,2,1,0:T(8,128)(2,1)} custom-call(bf16[2,2048,256]{2,1,0:T(8,128)(2,1)} %bitcast.12), custom_call_target="tpu_custom_call" | custom-call | flops 1 | bytes 1 | tf_op jit(solution)/shard_map/pack/pallas_call | solution.py:131
  14.7 2.1 %sums.1.tables_ref = bf16[98304,256]{1,0:T(8,128)(2,1)} custom-call(), custom_call_target="tpu_custom_call" | custom-call | flops 1 | bytes 1 | tf_op jit(solution)/shard_map/sums/pallas_call | solution.py:328
  17.7 0.6 dynamic-slice
  19.1 8.4 %all-reduce = s32[72]{0:T(128)S(1)} all-reduce(s32[72]{0:T(128)S(1)} %dynamic-update-slice), channel_id=2, replica_groups=mesh['seg'=4,'pair'=8] {'pair'}, use_global_device_ids=true, to_apply=%add | all-reduce | flops 72 | bytes 576
  27.6 9.7 %all-to-all-done = bf16[32,2,2,32,128]{4,3,2,1,0:T(8,128)(2,1)S(1)} async-done(((bf16[32,2,2,32,128]{4,3,2,1,0:T(8,128)(2,1)}), bf16[32,2,2,32,128]{4,3,2,1,0:T(8,128)(2,1)S(1)}, u32[]{:S(2)}, u32[]{:S(2)}) %all-to-all-start) | async-done | bytes 1048608 | tf_op jit(solution)/shard_map/all_to_all | solution.py:475
  37.3 3.6 %all-to-all-start.1 = ((bf16[32,2,2,32,128]{4,3,2,1,0:T(8,128)(2,1)}), bf16[32,2,2,32,128]{4,3,2,1,0:T(8,128)(2,1)S(1)}, u32[]{:S(2)}, u32[]{:S(2)}) async-start(bf16[32,2,2,32,128]{4,3,2,1,0:T(8,128)(2,1)} %bitcast.13), calls=%async_computation.1 | async-start | bytes 2097152 | tf_op jit(solution)/shard_map/all_to_all | solution.py:475
  41.0 2.3 %stack.14 = (s32[2,136,128]{2,1,0:T(8,128)S(1)}, s32[2,136,128]{2,1,0:T(8,128)S(1)}, s32[2,136,128]{2,1,0:T(8,128)S(1)}, s32[2,136,128]{2,1,0:T(8,128)S(1)}) custom-call(s32[2]{0:T(128)S(1)} %pad_add_fusion.me_ref, s32[8,9]{1,0:T(8,128)S(1)} %reshape.28.table_ref, bf16[4,16,2,32,128]{4,3,2,1,0:T(8,128)(2,1)S(1)} %bitcast.10), custom_call_target="tpu_custom_call" | custom-call | flops 1 | bytes 1 | tf_op jit(solution)/shard_map/stack/pallas_call | solution.py:205
  43.3 1.8 %collective-permute-start = (s32[2,136,128]{2,1,0:T(8,128)S(1)}, s32[2,136,128]{2,1,0:T(8,128)S(1)}, u32[]{:S(2)}, u32[]{:S(2)}) collective-permute-start(s32[2,136,128]{2,1,0:T(8,128)S(1)} %get-tuple-element.33), channel_id=1, source_target_pairs={{0,2},{1,3},{2,0},{3,1},{4,6},{5,7},{6,4},{7,5},{8,10},{9,11},{10,... | collective-permute-start | bytes 417800 | tf_op jit(solution)/shard_map/ppermute | solution.py:444
  45.2 1.5 %collective-permute-start.1 = (s32[2,136,128]{2,1,0:T(8,128)S(1)}, s32[2,136,128]{2,1,0:T(8,128)S(1)}, u32[]{:S(2)}, u32[]{:S(2)}) collective-permute-start(s32[2,136,128]{2,1,0:T(8,128)S(1)} %get-tuple-element.34), channel_id=1, source_target_pairs={{0,4},{1,5},{2,6},{3,7},{4,0},{5,1},{6,2},{7,3},{8,12},{9,13},{10,... | collective-permute-start | bytes 417800 | tf_op jit(solution)/shard_map/ppermute | solution.py:444
  46.9 9.0 %collective-permute-done.refs_1_ = s32[2,136,128]{2,1,0:T(8,128)S(1)} collective-permute-done((s32[2,136,128]{2,1,0:T(8,128)S(1)}, s32[2,136,128]{2,1,0:T(8,128)S(1)}, u32[]{:S(2)}, u32[]{:S(2)}) %collective-permute-start) | collective-permute-done | bytes 139296 | tf_op jit(solution)/shard_map/ppermute | solution.py:444
  55.9 0.5 collective-permute-start.5
  56.4 4.1 %collective-permute-done.2.refs_3_ = s32[2,136,128]{2,1,0:T(8,128)S(1)} collective-permute-done((s32[2,136,128]{2,1,0:T(8,128)S(1)}, s32[2,136,128]{2,1,0:T(8,128)S(1)}, u32[]{:S(2)}, u32[]{:S(2)}) %collective-permute-start.2) | collective-permute-done | bytes 139296 | tf_op jit(solution)/shard_map/ppermute | solution.py:444
  60.5 1.3 %collective-permute-done.6.refs_7_ = s32[2,136,128]{2,1,0:T(8,128)S(1)} collective-permute-done((s32[2,136,128]{2,1,0:T(8,128)S(1)}, s32[2,136,128]{2,1,0:T(8,128)S(1)}, u32[]{:S(2)}, u32[]{:S(2)}) %collective-permute-start.6) | collective-permute-done | bytes 139296 | tf_op jit(solution)/shard_map/ppermute | solution.py:451
  61.9 5.8 %dft.2 = (s32[136,128]{1,0:T(8,128)S(1)}, s32[136,128]{1,0:T(8,128)S(1)}, s32[136,128]{1,0:T(8,128)S(1)}, s32[136,128]{1,0:T(8,128)S(1)}) custom-call(s32[2]{0:T(128)S(1)} %pad_add_fusion.me_ref, bf16[1024,512]{1,0:T(8,128)(2,1)S(1)} %copy-done, f32[72,256]{1,0:T(8,128)S(1)} %copy-done.1, bf16[98304,256]{1,0:T(8,128)(2,1)} %sums.1.tables_ref, ...), custom_call_target="tpu_custom_call" | custom-call | flops 1 | bytes 1 | tf_op jit(solution)/shard_map/dft/pallas_call | solution.py:365
  67.7 2.5 %stack.15 = (s32[2,136,128]{2,1,0:T(8,128)S(1)}, s32[2,136,128]{2,1,0:T(8,128)S(1)}, s32[2,136,128]{2,1,0:T(8,128)S(1)}, s32[2,136,128]{2,1,0:T(8,128)S(1)}) custom-call(s32[2]{0:T(128)S(1)} %pad_add_fusion.me_ref, s32[8,9]{1,0:T(8,128)S(1)} %reshape.28.table_ref, bf16[4,16,2,32,128]{4,3,2,1,0:T(8,128)(2,1)S(1)} %bitcast.9), custom_call_target="tpu_custom_call" | custom-call | flops 1 | bytes 1 | tf_op jit(solution)/shard_map/stack/pallas_call | solution.py:205
  70.2 1.4 %collective-permute-start.10 = (s32[2,136,128]{2,1,0:T(8,128)S(1)}, s32[2,136,128]{2,1,0:T(8,128)S(1)}, u32[]{:S(2)}, u32[]{:S(2)}) collective-permute-start(s32[2,136,128]{2,1,0:T(8,128)S(1)} %get-tuple-element.43), channel_id=1, source_target_pairs={{0,2},{1,3},{2,0},{3,1},{4,6},{5,7},{6,4},{7,5},{8,10},{9,11},{10,... | collective-permute-start | bytes 417800 | tf_op jit(solution)/shard_map/ppermute | solution.py:444
  71.6 1.1 %collective-permute-start.11 = (s32[2,136,128]{2,1,0:T(8,128)S(1)}, s32[2,136,128]{2,1,0:T(8,128)S(1)}, u32[]{:S(2)}, u32[]{:S(2)}) collective-permute-start(s32[2,136,128]{2,1,0:T(8,128)S(1)} %get-tuple-element.44), channel_id=1, source_target_pairs={{0,4},{1,5},{2,6},{3,7},{4,0},{5,1},{6,2},{7,3},{8,12},{9,13},{10,... | collective-permute-start | bytes 417800 | tf_op jit(solution)/shard_map/ppermute | solution.py:444
  72.7 1.1 %collective-permute-start.12 = (s32[2,136,128]{2,1,0:T(8,128)S(1)}, s32[2,136,128]{2,1,0:T(8,128)S(1)}, u32[]{:S(2)}, u32[]{:S(2)}) collective-permute-start(s32[2,136,128]{2,1,0:T(8,128)S(1)} %get-tuple-element.45), channel_id=1, source_target_pairs={{0,6},{1,7},{2,4},{3,5},{4,2},{5,3},{6,0},{7,1},{8,14},{9,15},{10,... | collective-permute-start | bytes 417800 | tf_op jit(solution)/shard_map/ppermute | solution.py:444
  73.8 1.8 %collective-permute-start.8 = (s32[136,128]{1,0:T(8,128)S(1)}, s32[136,128]{1,0:T(8,128)S(1)}, u32[]{:S(2)}, u32[]{:S(2)}) collective-permute-start(s32[136,128]{1,0:T(8,128)S(1)} %get-tuple-element.37), channel_id=1, source_target_pairs={{0,16},{8,24},{16,0},{24,8},{1,17},{9,25},{17,1},{25,9},{2,18},{10... | collective-permute-start | bytes 208904 | tf_op jit(solution)/shard_map/ppermute | solution.py:436
  75.5 2.6 %collective-permute-start.9 = (s32[136,128]{1,0:T(8,128)S(1)}, s32[136,128]{1,0:T(8,128)S(1)}, u32[]{:S(2)}, u32[]{:S(2)}) collective-permute-start(s32[136,128]{1,0:T(8,128)S(1)} %get-tuple-element.38), channel_id=1, source_target_pairs={{0,8},{8,0},{16,24},{24,16},{1,9},{9,1},{17,25},{25,17},{2,10},{10... | collective-permute-start | bytes 208904 | tf_op jit(solution)/shard_map/ppermute | solution.py:436
  78.1 1.2 %collective-permute-done.8.refs_1_ = s32[136,128]{1,0:T(8,128)S(1)} collective-permute-done((s32[136,128]{1,0:T(8,128)S(1)}, s32[136,128]{1,0:T(8,128)S(1)}, u32[]{:S(2)}, u32[]{:S(2)}) %collective-permute-start.8) | collective-permute-done | bytes 69664 | tf_op jit(solution)/shard_map/ppermute | solution.py:436
  79.3 1.1 %collective-permute-done.9.refs_2_ = s32[136,128]{1,0:T(8,128)S(1)} collective-permute-done((s32[136,128]{1,0:T(8,128)S(1)}, s32[136,128]{1,0:T(8,128)S(1)}, u32[]{:S(2)}, u32[]{:S(2)}) %collective-permute-start.9) | collective-permute-done | bytes 69664 | tf_op jit(solution)/shard_map/ppermute | solution.py:436
  81.1 2.9 %collective-permute-start.7 = (s32[136,128]{1,0:T(8,128)S(1)}, s32[136,128]{1,0:T(8,128)S(1)}, u32[]{:S(2)}, u32[]{:S(2)}) collective-permute-start(s32[136,128]{1,0:T(8,128)S(1)} %get-tuple-element.36), channel_id=1, source_target_pairs={{0,24},{8,16},{16,8},{24,0},{1,25},{9,17},{17,9},{25,1},{2,26},{10... | collective-permute-start | bytes 208904 | tf_op jit(solution)/shard_map/ppermute | solution.py:436
  84.0 5.8 %dft.3 = (s32[136,128]{1,0:T(8,128)S(1)}, s32[136,128]{1,0:T(8,128)S(1)}, s32[136,128]{1,0:T(8,128)S(1)}, s32[136,128]{1,0:T(8,128)S(1)}) custom-call(s32[2]{0:T(128)S(1)} %pad_add_fusion.me_ref, bf16[1024,512]{1,0:T(8,128)(2,1)S(1)} %copy-done, f32[72,256]{1,0:T(8,128)S(1)} %copy-done.1, bf16[98304,256]{1,0:T(8,128)(2,1)} %sums.1.tables_ref, ...), custom_call_target="tpu_custom_call" | custom-call | flops 1 | bytes 1 | tf_op jit(solution)/shard_map/dft/pallas_call | solution.py:365
  89.8 1.1 %collective-permute-start.17 = (s32[136,128]{1,0:T(8,128)S(1)}, s32[136,128]{1,0:T(8,128)S(1)}, u32[]{:S(2)}, u32[]{:S(2)}) collective-permute-start(s32[136,128]{1,0:T(8,128)S(1)} %get-tuple-element.49), channel_id=1, source_target_pairs={{0,24},{8,16},{16,8},{24,0},{1,25},{9,17},{17,9},{25,1},{2,26},{10... | collective-permute-start | bytes 208904 | tf_op jit(solution)/shard_map/ppermute | solution.py:436
  90.9 0.9 collective-permute-start.18
  91.7 2.5 %collective-permute-start.19 = (s32[136,128]{1,0:T(8,128)S(1)}, s32[136,128]{1,0:T(8,128)S(1)}, u32[]{:S(2)}, u32[]{:S(2)}) collective-permute-start(s32[136,128]{1,0:T(8,128)S(1)} %get-tuple-element.51), channel_id=1, source_target_pairs={{0,8},{8,0},{16,24},{24,16},{1,9},{9,1},{17,25},{25,17},{2,10},{10... | collective-permute-start | bytes 208904 | tf_op jit(solution)/shard_map/ppermute | solution.py:436
  94.2 2.5 %collective-permute-done.17.refs_4_ = s32[136,128]{1,0:T(8,128)S(1)} collective-permute-done((s32[136,128]{1,0:T(8,128)S(1)}, s32[136,128]{1,0:T(8,128)S(1)}, u32[]{:S(2)}, u32[]{:S(2)}) %collective-permute-start.17) | collective-permute-done | bytes 69664 | tf_op jit(solution)/shard_map/ppermute | solution.py:436
  96.8 1.8 %collective-permute-done.18.refs_5_ = s32[136,128]{1,0:T(8,128)S(1)} collective-permute-done((s32[136,128]{1,0:T(8,128)S(1)}, s32[136,128]{1,0:T(8,128)S(1)}, u32[]{:S(2)}, u32[]{:S(2)}) %collective-permute-start.18) | collective-permute-done | bytes 69664 | tf_op jit(solution)/shard_map/ppermute | solution.py:436
  98.6 3.6 %unpack.1 = f32[2,256,4,128]{3,2,1,0:T(4,128)} custom-call(s32[2]{0:T(128)S(1)} %pad_add_fusion.me_ref, s32[136,128]{1,0:T(8,128)S(1)} %collective-permute-done.7.refs_0_, s32[136,128]{1,0:T(8,128)S(1)} %collective-permute-done.8.refs_1_, s32[136,128]{1,0:T(8,128)S(1)} %collective-permute-done.9.refs_2_, s32[136,128]{1,0:T(8,128)S(1)} %get-tuple-element.39.refs_3_, ...), custom_call_target="tpu_custom_call" | custom-call | flops 1 | bytes 1 | tf_op jit(solution)/shard_map/unpack/pallas_call | solution.py:420
  (37 shorter events, 1.6 us)
Async XLA Ops:
  0.0 17.7 %copy-start.3 = (u32[32]{0:T(128)S(1)}, u32[32]{0:T(128)}, u32[]{:S(2)}) copy-start(u32[32]{0:T(128)} %constant.19) | copy-start | bytes 388
  0.0 61.9 %copy-start.1 = (f32[72,256]{1,0:T(8,128)S(1)}, f32[72,256]{1,0:T(8,128)}, u32[]{:S(2)}) copy-start(f32[72,256]{1,0:T(8,128)} %constant.13.clone.phase_ref) | copy-start | bytes 221188
  0.0 61.9 %copy-start = (bf16[1024,512]{1,0:T(8,128)(2,1)S(1)}, bf16[1024,512]{1,0:T(8,128)(2,1)}, u32[]{:S(2)}) copy-start(bf16[1024,512]{1,0:T(8,128)(2,1)} %constant.12.clone.w_ref) | copy-start | bytes 3145732
  0.0 17.5 %copy-start.2 = (s32[4,2]{0,1:T(2,128)S(1)}, s32[4,2]{0,1:T(2,128)}, u32[]{:S(2)}) copy-start(s32[4,2]{0,1:T(2,128)} %param.6) | copy-start | bytes 100
  3.7 33.6 %all-to-all-start = ((bf16[32,2,2,32,128]{4,3,2,1,0:T(8,128)(2,1)}), bf16[32,2,2,32,128]{4,3,2,1,0:T(8,128)(2,1)S(1)}, u32[]{:S(2)}, u32[]{:S(2)}) async-start(bf16[32,2,2,32,128]{4,3,2,1,0:T(8,128)(2,1)} %bitcast.14), calls=%async_computation | async-start | bytes 2097152 | tf_op jit(solution)/shard_map/all_to_all | solution.py:475
  37.3 30.4 %all-to-all-start.1 = ((bf16[32,2,2,32,128]{4,3,2,1,0:T(8,128)(2,1)}), bf16[32,2,2,32,128]{4,3,2,1,0:T(8,128)(2,1)S(1)}, u32[]{:S(2)}, u32[]{:S(2)}) async-start(bf16[32,2,2,32,128]{4,3,2,1,0:T(8,128)(2,1)} %bitcast.13), calls=%async_computation.1 | async-start | bytes 2097152 | tf_op jit(solution)/shard_map/all_to_all | solution.py:475
  43.3 12.6 %collective-permute-start = (s32[2,136,128]{2,1,0:T(8,128)S(1)}, s32[2,136,128]{2,1,0:T(8,128)S(1)}, u32[]{:S(2)}, u32[]{:S(2)}) collective-permute-start(s32[2,136,128]{2,1,0:T(8,128)S(1)} %get-tuple-element.33), channel_id=1, source_target_pairs={{0,2},{1,3},{2,0},{3,1},{4,6},{5,7},{6,4},{7,5},{8,10},{9,11},{10,... | collective-permute-start | bytes 417800 | tf_op jit(solution)/shard_map/ppermute | solution.py:444
  45.2 10.7 %collective-permute-start.1 = (s32[2,136,128]{2,1,0:T(8,128)S(1)}, s32[2,136,128]{2,1,0:T(8,128)S(1)}, u32[]{:S(2)}, u32[]{:S(2)}) collective-permute-start(s32[2,136,128]{2,1,0:T(8,128)S(1)} %get-tuple-element.34), channel_id=1, source_target_pairs={{0,4},{1,5},{2,6},{3,7},{4,0},{5,1},{6,2},{7,3},{8,12},{9,13},{10,... | collective-permute-start | bytes 417800 | tf_op jit(solution)/shard_map/ppermute | solution.py:444
  46.6 13.9 %collective-permute-start.2 = (s32[2,136,128]{2,1,0:T(8,128)S(1)}, s32[2,136,128]{2,1,0:T(8,128)S(1)}, u32[]{:S(2)}, u32[]{:S(2)}) collective-permute-start(s32[2,136,128]{2,1,0:T(8,128)S(1)} %get-tuple-element.35), channel_id=1, source_target_pairs={{0,6},{1,7},{2,4},{3,5},{4,2},{5,3},{6,0},{7,1},{8,14},{9,15},{10,... | collective-permute-start | bytes 417800 | tf_op jit(solution)/shard_map/ppermute | solution.py:444
  46.9 13.6 %collective-permute-start.3 = (s32[2,136,128]{2,1,0:T(8,128)S(1)}, s32[2,136,128]{2,1,0:T(8,128)S(1)}, u32[]{:S(2)}, u32[]{:S(2)}) collective-permute-start(s32[2,136,128]{2,1,0:T(8,128)S(1)} %get-tuple-element.32.refs_0_), channel_id=1, source_target_pairs={{0,1},{1,0},{2,3},{3,2},{4,5},{5,4},{6,7},{7,6},{8,9},{9,8},{10,11... | collective-permute-start | bytes 417800 | tf_op jit(solution)/shard_map/ppermute | solution.py:451
  55.9 4.6 %collective-permute-start.4 = (s32[2,136,128]{2,1,0:T(8,128)S(1)}, s32[2,136,128]{2,1,0:T(8,128)S(1)}, u32[]{:S(2)}, u32[]{:S(2)}) collective-permute-start(s32[2,136,128]{2,1,0:T(8,128)S(1)} %collective-permute-done.refs_1_), channel_id=1, source_target_pairs={{0,1},{1,0},{2,3},{3,2},{4,5},{5,4},{6,7},{7,6},{8,9},{9,8},{10,11... | collective-permute-start | bytes 417800 | tf_op jit(solution)/shard_map/ppermute | solution.py:451
  55.9 4.6 %collective-permute-start.5 = (s32[2,136,128]{2,1,0:T(8,128)S(1)}, s32[2,136,128]{2,1,0:T(8,128)S(1)}, u32[]{:S(2)}, u32[]{:S(2)}) collective-permute-start(s32[2,136,128]{2,1,0:T(8,128)S(1)} %collective-permute-done.1.refs_2_), channel_id=1, source_target_pairs={{0,1},{1,0},{2,3},{3,2},{4,5},{5,4},{6,7},{7,6},{8,9},{9,8},{10,11... | collective-permute-start | bytes 417800 | tf_op jit(solution)/shard_map/ppermute | solution.py:451
  60.5 1.4 %collective-permute-start.6 = (s32[2,136,128]{2,1,0:T(8,128)S(1)}, s32[2,136,128]{2,1,0:T(8,128)S(1)}, u32[]{:S(2)}, u32[]{:S(2)}) collective-permute-start(s32[2,136,128]{2,1,0:T(8,128)S(1)} %collective-permute-done.2.refs_3_), channel_id=1, source_target_pairs={{0,1},{1,0},{2,3},{3,2},{4,5},{5,4},{6,7},{7,6},{8,9},{9,8},{10,11... | collective-permute-start | bytes 417800 | tf_op jit(solution)/shard_map/ppermute | solution.py:451
  70.2 10.2 %collective-permute-start.10 = (s32[2,136,128]{2,1,0:T(8,128)S(1)}, s32[2,136,128]{2,1,0:T(8,128)S(1)}, u32[]{:S(2)}, u32[]{:S(2)}) collective-permute-start(s32[2,136,128]{2,1,0:T(8,128)S(1)} %get-tuple-element.43), channel_id=1, source_target_pairs={{0,2},{1,3},{2,0},{3,1},{4,6},{5,7},{6,4},{7,5},{8,10},{9,11},{10,... | collective-permute-start | bytes 417800 | tf_op jit(solution)/shard_map/ppermute | solution.py:444
  71.6 8.8 %collective-permute-start.11 = (s32[2,136,128]{2,1,0:T(8,128)S(1)}, s32[2,136,128]{2,1,0:T(8,128)S(1)}, u32[]{:S(2)}, u32[]{:S(2)}) collective-permute-start(s32[2,136,128]{2,1,0:T(8,128)S(1)} %get-tuple-element.44), channel_id=1, source_target_pairs={{0,4},{1,5},{2,6},{3,7},{4,0},{5,1},{6,2},{7,3},{8,12},{9,13},{10,... | collective-permute-start | bytes 417800 | tf_op jit(solution)/shard_map/ppermute | solution.py:444
  72.7 7.7 %collective-permute-start.12 = (s32[2,136,128]{2,1,0:T(8,128)S(1)}, s32[2,136,128]{2,1,0:T(8,128)S(1)}, u32[]{:S(2)}, u32[]{:S(2)}) collective-permute-start(s32[2,136,128]{2,1,0:T(8,128)S(1)} %get-tuple-element.45), channel_id=1, source_target_pairs={{0,6},{1,7},{2,4},{3,5},{4,2},{5,3},{6,0},{7,1},{8,14},{9,15},{10,... | collective-permute-start | bytes 417800 | tf_op jit(solution)/shard_map/ppermute | solution.py:444
  73.8 5.6 %collective-permute-start.8 = (s32[136,128]{1,0:T(8,128)S(1)}, s32[136,128]{1,0:T(8,128)S(1)}, u32[]{:S(2)}, u32[]{:S(2)}) collective-permute-start(s32[136,128]{1,0:T(8,128)S(1)} %get-tuple-element.37), channel_id=1, source_target_pairs={{0,16},{8,24},{16,0},{24,8},{1,17},{9,25},{17,1},{25,9},{2,18},{10... | collective-permute-start | bytes 208904 | tf_op jit(solution)/shard_map/ppermute | solution.py:436
  75.5 4.9 %collective-permute-start.9 = (s32[136,128]{1,0:T(8,128)S(1)}, s32[136,128]{1,0:T(8,128)S(1)}, u32[]{:S(2)}, u32[]{:S(2)}) collective-permute-start(s32[136,128]{1,0:T(8,128)S(1)} %get-tuple-element.38), channel_id=1, source_target_pairs={{0,8},{8,0},{16,24},{24,16},{1,9},{9,1},{17,25},{25,17},{2,10},{10... | collective-permute-start | bytes 208904 | tf_op jit(solution)/shard_map/ppermute | solution.py:436
  79.3 4.6 %collective-permute-start.13 = (s32[2,136,128]{2,1,0:T(8,128)S(1)}, s32[2,136,128]{2,1,0:T(8,128)S(1)}, u32[]{:S(2)}, u32[]{:S(2)}) collective-permute-start(s32[2,136,128]{2,1,0:T(8,128)S(1)} %get-tuple-element.42.refs_0_), channel_id=1, source_target_pairs={{0,1},{1,0},{2,3},{3,2},{4,5},{5,4},{6,7},{7,6},{8,9},{9,8},{10,11... | collective-permute-start | bytes 417800 | tf_op jit(solution)/shard_map/ppermute | solution.py:451
  80.4 3.5 %collective-permute-start.14 = (s32[2,136,128]{2,1,0:T(8,128)S(1)}, s32[2,136,128]{2,1,0:T(8,128)S(1)}, u32[]{:S(2)}, u32[]{:S(2)}) collective-permute-start(s32[2,136,128]{2,1,0:T(8,128)S(1)} %collective-permute-done.10.refs_1_), channel_id=1, source_target_pairs={{0,1},{1,0},{2,3},{3,2},{4,5},{5,4},{6,7},{7,6},{8,9},{9,8},{10,11... | collective-permute-start | bytes 417800 | tf_op jit(solution)/shard_map/ppermute | solution.py:451
  80.5 3.4 %collective-permute-start.15 = (s32[2,136,128]{2,1,0:T(8,128)S(1)}, s32[2,136,128]{2,1,0:T(8,128)S(1)}, u32[]{:S(2)}, u32[]{:S(2)}) collective-permute-start(s32[2,136,128]{2,1,0:T(8,128)S(1)} %collective-permute-done.11.refs_2_), channel_id=1, source_target_pairs={{0,1},{1,0},{2,3},{3,2},{4,5},{5,4},{6,7},{7,6},{8,9},{9,8},{10,11... | collective-permute-start | bytes 417800 | tf_op jit(solution)/shard_map/ppermute | solution.py:451
  81.0 3.0 %collective-permute-start.16 = (s32[2,136,128]{2,1,0:T(8,128)S(1)}, s32[2,136,128]{2,1,0:T(8,128)S(1)}, u32[]{:S(2)}, u32[]{:S(2)}) collective-permute-start(s32[2,136,128]{2,1,0:T(8,128)S(1)} %collective-permute-done.12.refs_3_), channel_id=1, source_target_pairs={{0,1},{1,0},{2,3},{3,2},{4,5},{5,4},{6,7},{7,6},{8,9},{9,8},{10,11... | collective-permute-start | bytes 417800 | tf_op jit(solution)/shard_map/ppermute | solution.py:451
  81.1 13.2 %collective-permute-start.7 = (s32[136,128]{1,0:T(8,128)S(1)}, s32[136,128]{1,0:T(8,128)S(1)}, u32[]{:S(2)}, u32[]{:S(2)}) collective-permute-start(s32[136,128]{1,0:T(8,128)S(1)} %get-tuple-element.36), channel_id=1, source_target_pairs={{0,24},{8,16},{16,8},{24,0},{1,25},{9,17},{17,9},{25,1},{2,26},{10... | collective-permute-start | bytes 208904 | tf_op jit(solution)/shard_map/ppermute | solution.py:436
  89.8 7.0 %collective-permute-start.17 = (s32[136,128]{1,0:T(8,128)S(1)}, s32[136,128]{1,0:T(8,128)S(1)}, u32[]{:S(2)}, u32[]{:S(2)}) collective-permute-start(s32[136,128]{1,0:T(8,128)S(1)} %get-tuple-element.49), channel_id=1, source_target_pairs={{0,24},{8,16},{16,8},{24,0},{1,25},{9,17},{17,9},{25,1},{2,26},{10... | collective-permute-start | bytes 208904 | tf_op jit(solution)/shard_map/ppermute | solution.py:436
  90.9 7.8 %collective-permute-start.18 = (s32[136,128]{1,0:T(8,128)S(1)}, s32[136,128]{1,0:T(8,128)S(1)}, u32[]{:S(2)}, u32[]{:S(2)}) collective-permute-start(s32[136,128]{1,0:T(8,128)S(1)} %get-tuple-element.50), channel_id=1, source_target_pairs={{0,16},{8,24},{16,0},{24,8},{1,17},{9,25},{17,1},{25,9},{2,18},{10... | collective-permute-start | bytes 208904 | tf_op jit(solution)/shard_map/ppermute | solution.py:436
  91.7 6.9 %collective-permute-start.19 = (s32[136,128]{1,0:T(8,128)S(1)}, s32[136,128]{1,0:T(8,128)S(1)}, u32[]{:S(2)}, u32[]{:S(2)}) collective-permute-start(s32[136,128]{1,0:T(8,128)S(1)} %get-tuple-element.51), channel_id=1, source_target_pairs={{0,8},{8,0},{16,24},{24,16},{1,9},{9,1},{17,25},{25,17},{2,10},{10... | collective-permute-start | bytes 208904 | tf_op jit(solution)/shard_map/ppermute | solution.py:436
